TPU v7x, 256 devices: a whole 4x4x8 slice. The times are simulated.
256 devices in a mesh: out: 32 (over z, x_hi, core), in: 8 (over y, x_lo).
Axes of the slice: x: 4 (x_hi: 2, x_lo: 2; x = x_hi * 2 + x_lo), y: 4, z: 8, core: 2. Of those that a mesh axis runs over, the one named last changes fastest.
Arguments:
- basis_out: bfloat16 [16384, 16384], P('in', 'out'), may hold values from -0.046875 to 0.046875
- corrected: float32 [16384, 26624], P('out', 'in'), may hold values from 0.5 to 2
- factor_table: float32 [32, 1664], replicated, may hold values from 0.5 to 2
- block_ids: int32 [16], replicated, may hold values from 0 to 31, as said below
- basis_in: bfloat16 [16, 1664, 1664], P('in', 'out'), may hold values from -0.15625 to 0.15625
- query_ids: int32 [4], replicated, may hold values from 0 to 5
- u_pool: bfloat16 [6, 16384, 64], P(None, 'in'), may hold values from -0.75 to 0.75
- v_pool: bfloat16 [6, 26624, 64], P(None, 'in'), may hold values from -6 to 6
- train_ids: int32 [4], replicated, may hold values from 0 to 7
- x_pool: bfloat16 [8, 32, 26624], P(None, 'out', 'in'), may hold values from -0.0390625 to 0.0390625
- delta_pool: bfloat16 [8, 32, 128], P(None, 'out'), may hold values from -0.09375 to 0.09375
Outputs:
- tiles: bfloat16 [4, 128, 26624], P(None, 'out', 'in')
- scores: float32 [4, 4], replicated
Inputs may be any that keep to these rules, and one draw needn't show every extreme that they name: `block_ids`: the 16 entries are distinct.
All inputs are finite; a program needn't handle non-finite values.
Results may differ from a plain program's by a relative error of at most 0.023.
Values may be sent and summed in bfloat16 or wider, within the bound.
No kernel may reach another device: no remote copies, remote signals or barrier semaphores. Data moves between devices by JAX's collectives and lax.ppermute only.
A program may use at most 128 MiB of HBM per device.

v0:
```python
import functools

import jax
import jax.numpy as jnp
from jax import lax
from jax.sharding import Mesh
from jax.sharding import PartitionSpec as P

WIN_ROWS = 16
OUT = ("out_0", "out_1", "out_2")
IN = ("in_0", "in_1")
OUT_IN = ("out_0", "out_1", "out_2", "in_0", "in_1")


def sent_to_all(value, axis):
    copies = jnp.broadcast_to(value, (lax.axis_size(axis), *value.shape))
    return lax.all_to_all(copies, axis, split_axis=0, concat_axis=0, tiled=True)


def taken_together(value, axis):
    return sent_to_all(value, axis).sum(axis=0)


def in_order(parts, dim):
    dims = list(parts.shape[1:])
    dims[dim] *= parts.shape[0]
    return jnp.moveaxis(parts, 0, dim).reshape(dims)


def collect(value, axis, dim):
    return in_order(sent_to_all(value, axis), dim)


def cut_along(value, dim, size):
    dims = value.shape
    parts = value.reshape(*dims[:dim], size, dims[dim] // size, *dims[dim + 1 :])
    return jnp.moveaxis(parts, dim, 0)


def sum_at_owner(value, axis, dim):
    size = lax.axis_size(axis)
    parts = lax.all_to_all(cut_along(value, dim, size), axis, 0, 0, tiled=True)
    return jnp.sum(parts.astype(jnp.float32), axis=0)


def sum_in_two_steps(value, axes, dim):
    far, near = axes
    own = sum_at_owner(cut_along(value, dim, lax.axis_size(far)), near, dim + 1)
    return jnp.sum(
        lax.all_to_all(own.astype(jnp.bfloat16), far, 0, 0, tiled=True).astype(jnp.float32), axis=0
    )


def sent_together(arrays, axis, dim, along):
    widths = [a.shape[along] for a in arrays]
    both = jnp.concatenate(arrays, axis=along)
    out = lax.all_gather(both, axis, axis=dim, tiled=True)
    return tuple(jnp.split(out, [sum(widths[:k]) for k in range(1, len(widths))], axis=along))


def over_axes(value, axes):
    return functools.reduce(lax.psum, axes, value)


def shards(
    basis_out,
    corrected,
    factor_table,
    block_ids,
    basis_in,
    query_ids,
    u_pool,
    v_pool,
    train_ids,
    x_pool,
    delta_pool,
):
    n_out = lax.axis_size(OUT)
    out_pos = lax.axis_index(OUT)
    in_pos = lax.axis_index(IN)
    queries = query_ids.shape[0]
    factor_rank = u_pool.shape[2]
    local_blocks, local_rows, block_width = basis_in.shape
    columns = local_blocks * block_width
    eigen_count = basis_out.shape[1]
    query_left = jnp.take(u_pool, query_ids, axis=0)
    left_flat = jnp.transpose(query_left, (1, 0, 2)).reshape(
        query_left.shape[1], queries * factor_rank
    )
    partial_out = lax.dot_general(
        basis_out, left_flat, (((0,), (0,)), ((), ())), preferred_element_type=jnp.float32
    )
    rotated_left = taken_together(partial_out, IN).astype(jnp.bfloat16)
    query_right = jnp.take(v_pool, query_ids, axis=0)
    right_blocks = jnp.transpose(query_right, (1, 0, 2)).reshape(
        local_blocks, block_width, queries * factor_rank
    )
    full_basis = lax.all_gather(basis_in, OUT, axis=1, tiled=True)
    rotated_right = jnp.einsum(
        "cij,cir->cjr", full_basis, right_blocks, preferred_element_type=jnp.float32
    ).astype(jnp.bfloat16)
    rotated_right = rotated_right.reshape(columns, queries, factor_rank)
    left_three = rotated_left.reshape(eigen_count, queries, factor_rank)
    chosen = lax.dynamic_slice_in_dim(block_ids, in_pos * local_blocks, local_blocks)
    onehot = (
        chosen[:, None] == jnp.arange(factor_table.shape[0], dtype=jnp.int32)[None, :]
    ).astype(jnp.float32)
    scale_row = jnp.dot(
        onehot, factor_table, precision=lax.Precision.HIGHEST, preferred_element_type=jnp.float32
    ).reshape(columns)
    divisor = corrected * scale_row[None, :]
    products = jnp.einsum(
        "kqr,jqr->kqj", left_three, rotated_right, preferred_element_type=jnp.float32
    )
    precond = (
        (products / divisor[:, None, :])
        .astype(jnp.bfloat16)
        .reshape(eigen_count, queries * columns)
    )
    window = collect(basis_out[:WIN_ROWS], IN, 0)
    own_rows = window.shape[0] // n_out
    half_back = sum_in_two_steps(
        jnp.dot(window, precond, preferred_element_type=jnp.float32).astype(jnp.bfloat16),
        (("out_0", "out_1"), "out_2"),
        0,
    ).astype(jnp.bfloat16)
    half_back = half_back.reshape(own_rows, queries, local_blocks, block_width)
    tile_out = jnp.einsum(
        "oqcj,cij->qoci", half_back, full_basis, preferred_element_type=jnp.float32
    )
    tile_out = tile_out.astype(jnp.bfloat16).reshape(queries, own_rows, columns)
    train_inputs = jnp.take(x_pool, train_ids, axis=0)
    train_deltas = jnp.take(delta_pool, train_ids, axis=0)
    input_rows, delta_rows = sent_together((train_inputs, train_deltas), OUT, 1, 2)
    delta_own = lax.dynamic_slice_in_dim(delta_rows, out_pos * own_rows, own_rows, 2).astype(
        jnp.float32
    )
    projected = jnp.einsum(
        "bsj,qoj->bsqo", input_rows, tile_out, preferred_element_type=jnp.float32
    )
    partial_value = jnp.einsum(
        "bsqo,bso->qb", projected, delta_own, precision=lax.Precision.HIGHEST
    )
    scores = over_axes(partial_value, OUT_IN)
    return (tile_out, scores)


def solution(mesh):
    split = Mesh(mesh.devices.reshape(8, 2, 2, 4, 2), ("out_0", "out_1", "out_2", "in_0", "in_1"))
    return jax.shard_map(
        shards,
        mesh=split,
        in_specs=(
            P(IN, OUT),
            P(OUT, IN),
            P(),
            P(),
            P(IN, OUT, None),
            P(),
            P(None, IN, None),
            P(None, IN, None),
            P(),
            P(None, OUT, IN),
            P(None, OUT, None),
        ),
        out_specs=(P(None, OUT, IN), P()),
        check_vma=False,
    )
```

profile of v0, /device:TPU:1, one launch (start us, length us, event | category | flops | bytes accessed | tf_op | source)
XLA Modules:
  0.0 328.6 jit_solution(12192890383082641452)
XLA Ops:
  7.2 0.0 copy-start
  7.2 0.0 copy-start.6
  7.2 0.0 all-gather.2.cloned.1.call-start
  7.2 0.7 all-gather.2.cloned.1.call-update
  7.9 0.7 compare_select_fusion.1
  8.6 3.0 gather_fusion.1
  11.6 0.0 copy-done.6
  11.6 1.4 broadcast_select_fusion
  13.0 3.1 convolution_bitcast_fusion
  16.1 1.2 copy.59
  17.4 2.3 broadcast_in_dim.58
  19.7 6.1 %all-to-all-start = ((f32[8,512,256]{2,1,0:T(8,128)}), f32[8,512,256]{2,1,0:T(8,128)}, u32[]{:S(2)}, u32[]{:S(2)}) async-start(f32[8,512,256]{2,1,0:T(8,128)} %broadcast_in_dim.58), calls=%async_computation | async-start | bytes 8388608 | tf_op jit(solution)/shard_map/all_to_all | solution.py:17
  25.8 0.0 copy-done.7
  25.8 0.1 dynamic_slice.6
  25.9 0.0 copy-done.4
  25.9 0.2 fusion.22
  26.1 6.4 %broadcast_multiply_fusion = f32[512,3328]{1,0:T(8,128)} fusion(f32[512,3328]{1,0:T(8,128)} %param.12, f32[3328]{0:T(1024)S(1)} %mul.27), kind=kLoop, calls=%fused_computation.13 | loop fusion | flops 1703936 | bytes 13644800 | tf_op jit(solution)/shard_map/mul | solution.py:111
  32.6 7.6 %copy.61 = f32[512,3328]{0,1:T(8,128)} copy(f32[512,3328]{1,0:T(8,128)} %broadcast_multiply_fusion) | data formatting | bytes 13631488 | tf_op jit(solution)/shard_map/mul | solution.py:111
  40.2 0.0 copy-done
  40.2 1.9 gather_fusion
  42.0 1.7 select_bitcast_fusion
  43.7 1.4 reshape.90
  45.1 37.5 %all-to-all-done = f32[8,512,256]{2,1,0:T(8,128)} async-done(((f32[8,512,256]{2,1,0:T(8,128)}), f32[8,512,256]{2,1,0:T(8,128)}, u32[]{:S(2)}, u32[]{:S(2)}) %all-to-all-start) | async-done | bytes 4194336 | tf_op jit(solution)/shard_map/all_to_all | solution.py:17
  82.7 0.7 broadcast_in_dim.59
  83.3 3.5 %all-to-all-start.1 = ((bf16[8,16,512]{2,1,0:T(8,128)(2,1)}), bf16[8,16,512]{2,1,0:T(8,128)(2,1)S(1)}, u32[]{:S(2)}, u32[]{:S(2)}) async-start(bf16[8,16,512]{2,1,0:T(8,128)(2,1)} %broadcast_in_dim.59), calls=%async_computation.1 | async-start | bytes 262144 | tf_op jit(solution)/shard_map/all_to_all | solution.py:17
  86.9 2.5 reduce_sum.33
  89.4 0.1 copy.60
  89.5 48.5 %all-gather.2.cloned.1.call-done = bf16[2,1664,1664]{2,0,1:T(2,128)(2,1)} async-done(((bf16[2,52,1664]{2,0,1:T(2,128)(2,1)}), bf16[2,1664,1664]{2,0,1:T(2,128)(2,1)}) %all-gather.2.cloned.1.call-update) | async-done | bytes 11075600 | tf_op jit(solution)/shard_map/all_gather | solution.py:98
  138.0 0.0 copy-done.2
  138.0 7.6 %fusion.9 = bf16[2,1664,256]{1,2,0:T(8,128)(2,1)S(1)} fusion(bf16[2,1664,1664]{2,0,1:T(2,128)(2,1)} %all-gather.2.cloned.1.call-done, bf16[2,1664,256]{1,0,2:T(2,128)(2,1)S(1)} %copy-done.2), kind=kOutput, calls=%fused_computation.15 | convolution fusion | flops 2836201472 | bytes 14483456 | tf_op jit(solution)/shard_map/cij,cir->cjr/dot_general | solution.py:99
  145.6 1.8 copy.58
  147.3 2.0 reshape.91
  149.4 9.4 %fusion = bf16[512,4,3328]{0,2,1:T(8,128)(2,1)} fusion(f32[512,3328]{0,1:T(8,128)} %copy.61, bf16[3328,4,64]{0,2,1:T(8,128)(2,1)} %reshape.91, bf16[512,4,64]{0,2,1:T(8,128)(2,1)S(1)} %bitcast.61), kind=kOutput, calls=%fused_computation.5 | convolution fusion | flops 886046720 | bytes 22413312 | tf_op jit(solution)/shard_map/kqr,jqr->kqj/dot_general | solution.py:112
  158.7 0.0 all-to-all-done.1
  158.8 11.2 %fusion.1 = bf16[128,13312]{1,0:T(8,128)(2,1)} fusion(bf16[512,13312]{0,1:T(8,128)(2,1)} %bitcast.56, bf16[128,512]{1,0:T(8,128)(2,1)S(1)} %bitcast.60), kind=kOutput, calls=%fused_computation.7 | convolution fusion | flops 1746534400 | bytes 17170432 | tf_op jit(solution)/shard_map/dot_general | solution.py:123
  169.9 6.1 %reshape_reshape.3 = bf16[16,2,4,13312]{3,2,1,0:T(4,128)(2,1)} reshape(bf16[128,13312]{1,0:T(8,128)(2,1)} %fusion.1) | data formatting | bytes 6815744 | tf_op jit(solution)/shard_map/reshape;reshape | solution.py:36
  176.1 3.1 copy.103
  179.2 7.3 %all_to_all.20 = bf16[2,16,4,13312]{3,2,1,0:T(4,128)(2,1)} all-to-all(bf16[2,16,4,13312]{3,2,1,0:T(4,128)(2,1)S(1)} %bitcast.57), channel_id=1, replica_groups=mesh['out_0'=8,'out_1'=2,'out_2'=2,'in_0'=4,'in_1'=2] {'out_2'}, dimensions={0} | all-to-all | bytes 6815744 | tf_op jit(solution)/shard_map/all_to_all | solution.py:42
  186.5 6.1 %reduce_sum.34 = bf16[16,4,13312]{2,1,0:T(4,128)(2,1)} reduce(bf16[2,16,4,13312]{3,2,1,0:T(4,128)(2,1)} %all_to_all.20, bf16[]{:T(256)} %constant.80.clone.1), dimensions={0}, to_apply=%region_1.2 | reduce | flops 851968 | bytes 5111810 | tf_op jit(solution)/shard_map/reduce_sum | solution.py:43
  192.7 4.1 %all-to-all-start.3 = ((bf16[16,4,13312]{2,1,0:T(4,128)(2,1)}), bf16[16,4,13312]{2,1,0:T(4,128)(2,1)S(1)}, u32[]{:S(2)}, u32[]{:S(2)}) async-start(bf16[16,4,13312]{2,1,0:T(4,128)(2,1)} %reduce_sum.34), calls=%async_computation.3 | async-start | bytes 3407872 | tf_op jit(solution)/shard_map/all_to_all | solution.py:50
  196.8 0.0 copy-done.8
  196.8 0.6 gather_fusion.3
  197.4 0.0 copy-done.3
  197.4 0.6 gather_fusion.2
  198.0 0.1 bitcast_select_fusion.1
  198.1 0.1 bitcast_select_fusion
  198.2 74.0 %all_gather.7 = bf16[4,32,3456]{2,0,1:T(4,128)(2,1)S(1)} all-gather(bf16[4,1,3456]{2,0,1:T(4,128)(2,1)S(1)} %pad_maximum_fusion), channel_id=1, replica_groups=mesh['out_0'=8,'out_1'=2,'out_2'=2,'in_0'=4,'in_1'=2] {'out_0','out_1','..., dimensions={1}, use_global_device_ids=true | all-gather | bytes 912384 | tf_op jit(solution)/shard_map/all_gather | solution.py:57
  272.2 0.3 split.9
  272.5 0.1 bitcast_convert_fusion
  272.6 0.1 copy.82
  272.7 0.0 all-to-all-done.3
  272.7 0.8 reduce_sum.35
  273.5 0.7 reshape.95
  274.2 7.4 %fusion.15 = bf16[4,4,2,1664]{3,0,1,2:T(4,128)(2,1)S(1)} fusion(bf16[2,1664,1664,1]{2,0,1,3:T(2,128)(2,1)} %bitcast.64, bf16[4,4,2,1664]{3,2,1,0:T(2,128)(2,1)} %reshape.95), kind=kOutput, calls=%fused_computation.17 | convolution fusion | flops 177262592 | bytes 11288576 | tf_op jit(solution)/shard_map/oqcj,cij->qoci/dot_general | solution.py:128
  281.6 0.1 copy.66
  281.7 0.7 reshape.96
  282.4 0.7 reshape.139
  283.1 1.8 fusion.20
  284.9 0.1 copy.77
  285.0 11.4 %psum.35 = f32[4,4]{1,0:T(4,128)S(1)} all-reduce(f32[4,4]{1,0:T(4,128)S(1)} %bitcast.63), channel_id=1, replica_groups=mesh['out_0'=8,'out_1'=2,'out_2'=2,'in_0'=4,'in_1'=2] {'out_0'}, use_global_device_ids=true, to_apply=%region_3.4 | all-reduce | flops 16 | bytes 128 | tf_op jit(solution)/shard_map/psum | solution.py:62
  296.4 5.3 %psum.36 = f32[4,4]{1,0:T(4,128)S(1)} all-reduce(f32[4,4]{1,0:T(4,128)S(1)} %psum.35), channel_id=1, replica_groups=mesh['out_0'=8,'out_1'=2,'out_2'=2,'in_0'=4,'in_1'=2] {'out_1'}, use_global_device_ids=true, to_apply=%region_4.5 | all-reduce | flops 16 | bytes 128 | tf_op jit(solution)/shard_map/psum | solution.py:62
  301.7 6.8 %psum.37 = f32[4,4]{1,0:T(4,128)S(1)} all-reduce(f32[4,4]{1,0:T(4,128)S(1)} %psum.36), channel_id=1, replica_groups=mesh['out_0'=8,'out_1'=2,'out_2'=2,'in_0'=4,'in_1'=2] {'out_2'}, use_global_device_ids=true, to_apply=%region_5.6 | all-reduce | flops 16 | bytes 128 | tf_op jit(solution)/shard_map/psum | solution.py:62
  308.5 8.9 %psum.38 = f32[4,4]{1,0:T(4,128)S(1)} all-reduce(f32[4,4]{1,0:T(4,128)S(1)} %psum.37), channel_id=1, replica_groups=mesh['out_0'=8,'out_1'=2,'out_2'=2,'in_0'=4,'in_1'=2] {'in_0'}, use_global_device_ids=true, to_apply=%region_6.7 | all-reduce | flops 16 | bytes 128 | tf_op jit(solution)/shard_map/psum | solution.py:62
  317.4 4.3 %psum.39 = f32[4,4]{1,0:T(4,128)} all-reduce(f32[4,4]{1,0:T(4,128)S(1)} %psum.38), channel_id=1, replica_groups=mesh['out_0'=8,'out_1'=2,'out_2'=2,'in_0'=4,'in_1'=2] {'in_1'}, use_global_device_ids=true, to_apply=%region_7.8 | all-reduce | flops 16 | bytes 128 | tf_op jit(solution)/shard_map/psum | solution.py:62
  (19 shorter events, 0.1 us)
Async XLA Ops:
  7.2 33.0 %copy-start = (bf16[6,3328,64]{1,2,0:T(8,128)(2,1)S(1)}, bf16[6,3328,64]{1,2,0:T(8,128)(2,1)}, u32[]{:S(2)}) copy-start(bf16[6,3328,64]{1,2,0:T(8,128)(2,1)} %param.18) | copy-start | bytes 7667716
  7.2 4.5 %copy-start.6 = (s32[4]{0:T(128)S(1)}, s32[4]{0:T(128)}, u32[]{:S(2)}) copy-start(s32[4]{0:T(128)} %param.16) | copy-start | bytes 52
  7.2 130.8 %all-gather.2.cloned.1.call-start = ((), (), s32[]{:S(2)}) async-start(), calls=%async_computation.4 | async-start | bytes 11421696 | tf_op jit(solution)/shard_map/all_gather | solution.py:98
  19.7 6.1 %copy-start.7 = (s32[16]{0:T(128)S(1)}, s32[16]{0:T(128)}, u32[]{:S(2)}) copy-start(s32[16]{0:T(128)} %param.14) | copy-start | bytes 196
  19.7 6.2 %copy-start.4 = (f32[32,1664]{1,0:T(8,128)S(1)}, f32[32,1664]{1,0:T(8,128)}, u32[]{:S(2)}) copy-start(f32[32,1664]{1,0:T(8,128)} %param.13) | copy-start | bytes 638980
  19.7 63.0 %all-to-all-start = ((f32[8,512,256]{2,1,0:T(8,128)}), f32[8,512,256]{2,1,0:T(8,128)}, u32[]{:S(2)}, u32[]{:S(2)}) async-start(f32[8,512,256]{2,1,0:T(8,128)} %broadcast_in_dim.58), calls=%async_computation | async-start | bytes 8388608 | tf_op jit(solution)/shard_map/all_to_all | solution.py:17
  42.0 40.6 %slice-start = ((bf16[2048,512]{1,0:T(8,128)(2,1)}), bf16[16,512]{1,0:T(8,128)(2,1)S(1)}, s32[]{:S(2)}) async-start(bf16[2048,512]{1,0:T(8,128)(2,1)} %param.11), calls=%async_computation.5 | async-start | bytes 32768 | tf_op jit(solution)/shard_map/slice | solution.py:120
  45.1 92.8 %copy-start.2 = (bf16[2,1664,256]{1,0,2:T(2,128)(2,1)S(1)}, bf16[2,1664,256]{1,0,2:T(2,128)(2,1)}, u32[]{:S(2)}) copy-start(bf16[2,1664,256]{1,0,2:T(2,128)(2,1)} %reshape.90) | copy-start | bytes 5111812
  83.3 75.4 %all-to-all-start.1 = ((bf16[8,16,512]{2,1,0:T(8,128)(2,1)}), bf16[8,16,512]{2,1,0:T(8,128)(2,1)S(1)}, u32[]{:S(2)}, u32[]{:S(2)}) async-start(bf16[8,16,512]{2,1,0:T(8,128)(2,1)} %broadcast_in_dim.59), calls=%async_computation.1 | async-start | bytes 262144 | tf_op jit(solution)/shard_map/all_to_all | solution.py:17
  186.5 10.2 %copy-start.8 = (s32[4]{0:T(128)S(1)}, s32[4]{0:T(128)}, u32[]{:S(2)}) copy-start(s32[4]{0:T(128)} %param.19) | copy-start | bytes 52
  186.5 10.3 %copy-start.5 = (bf16[8,1,128]{2,0,1:T(8,128)(2,1)S(1)}, bf16[8,1,128]{2,0,1:T(8,128)(2,1)}, u32[]{:S(2)}) copy-start(bf16[8,1,128]{2,0,1:T(8,128)(2,1)} %param.21) | copy-start | bytes 6148
  186.5 10.9 %copy-start.3 = (bf16[8,1,3328]{2,0,1:T(8,128)(2,1)S(1)}, bf16[8,1,3328]{2,0,1:T(8,128)(2,1)}, u32[]{:S(2)}) copy-start(bf16[8,1,3328]{2,0,1:T(8,128)(2,1)} %param.20) | copy-start | bytes 159748
  192.7 80.1 %all-to-all-start.3 = ((bf16[16,4,13312]{2,1,0:T(4,128)(2,1)}), bf16[16,4,13312]{2,1,0:T(4,128)(2,1)S(1)}, u32[]{:S(2)}, u32[]{:S(2)}) async-start(bf16[16,4,13312]{2,1,0:T(4,128)(2,1)} %reduce_sum.34), calls=%async_computation.3 | async-start | bytes 3407872 | tf_op jit(solution)/shard_map/all_to_all | solution.py:50
  274.2 47.5 %copy-start.1 = (bf16[6,3328,64]{1,2,0:T(8,128)(2,1)S(1)}, bf16[6,3328,64]{1,2,0:T(8,128)(2,1)}, u32[]{:S(2)}) copy-start(bf16[6,3328,64]{1,2,0:T(8,128)(2,1)} %param.18) | copy-start | bytes 7667716
Sparse Core Ops, SparseCore 0:
  10.7 127.2 all-gather.1
where the time goes:
time: 332 us; the launch traced here: 329 us
  blocking collectives  118 us (36%)
  waiting for transfers between devices  86.7 us (26%)
  matrix products  40.6 us (12%)
  local copies, waits for them, and re-layouts  35.3 us (11%)
  other arithmetic  19.9 us (6%)
  between operations  14.2 us (4%)
  starting transfers between devices  13.8 us (4%)
    all_gather x1, blocking collectives, sent_together(): out = lax.all_gather(both, axis, axis=dim, tiled=True)  74 us
    all_gather x1, waiting for transfers between devices, shards(): full_basis = lax.all_gather(basis_in, OUT, axis=1, tiled=True)  48.5 us
    all_to_all x2, waiting for transfers between devices, sent_to_all(): return lax.all_to_all(copies, axis, split_axis=0, concat_axis=0, tiled=True)  37.5 us
    psum x5, blocking collectives, over_axes(): return functools.reduce(lax.psum, axes, value)  36.7 us
    dot_general x1, matrix products, shards(): jnp.dot(window, precond, preferred_element_type=jnp.float32)  11.2 us
    all_to_all x2, starting transfers between devices, sent_to_all(): return lax.all_to_all(copies, axis, split_axis=0, concat_axis=0, tiled=True)  9.63 us
    dot_general x1, matrix products, shards(): jnp.einsum('kqr,jqr->kqj', left_three, rotated_right, preferred_element_t...  9.36 us
    another operation x2, local copies, waits for them, and re-layouts, cut_along(): parts = value.reshape(*dims[:dim], size, dims[dim] // size, *dims[dim + 1:])  9.26 us
  transfers between devices with their start and end apart: 4, of which 2 were waited for; matrix products, arithmetic and copies ran while one was open for 17% of the time, Pallas kernels for 0%

commit v1 on v0

v1 whole, which is shorter than its diff:
```python
import functools

import jax
import jax.numpy as jnp
from jax import lax
from jax.experimental import pallas as pl
from jax.experimental.pallas import tpu as pltpu
from jax.sharding import Mesh
from jax.sharding import PartitionSpec as P

WIN_ROWS = 16
OUT = ("z", "xh", "c")
IN = ("y", "xl")
QUAD = ("xh", "c")
PLANE = ("xh", "c", "y", "xl")
BF = jnp.bfloat16
F32 = jnp.float32
LANES = 128
VMEM_LIMIT = 56 * 2**20

VMEM_SPEC = pl.BlockSpec(memory_space=pltpu.VMEM)
SMEM_SPEC = pl.BlockSpec(memory_space=pltpu.SMEM)


def params():
    return pltpu.CompilerParams(vmem_limit_bytes=VMEM_LIMIT)


def dot(a, b, ca, cb):
    return lax.dot_general(a, b, (((ca,), (cb,)), ((), ())), preferred_element_type=F32)


def exchange(value, axis):
    return lax.all_to_all(value, axis, split_axis=0, concat_axis=0, tiled=True)


def copies(value, axis):
    return exchange(jnp.broadcast_to(value, (lax.axis_size(axis), *value.shape)), axis)


def swap(value, axis, mask=1):
    size = lax.axis_size(axis)
    return lax.ppermute(value, axis, [(i, i ^ mask) for i in range(size)])


def shift(value, step):
    size = lax.axis_size("z")
    return lax.ppermute(value, "z", [(i, (i + step) % size) for i in range(size)])


def left_body(ids, u0, u1, u2, u3, basis, out):
    left = jnp.concatenate([u[0] for u in (u0, u1, u2, u3)], axis=0)
    n_in, rows, width = out.shape
    part = dot(left, basis[...], 1, 0).astype(BF)
    out[:, : rows - WIN_ROWS, :] = part.reshape(n_in, rows - WIN_ROWS, width)
    out[:, rows - WIN_ROWS :, :] = jnp.broadcast_to(
        basis[:WIN_ROWS, :][None], (n_in, WIN_ROWS, width)
    )


def left_part(query_ids, u_t, basis_out, n_in):
    queries = query_ids.shape[0]
    _, rank, depth = u_t.shape
    eigen = basis_out.shape[1]
    rows = queries * rank // n_in + WIN_ROWS
    tile = 256
    specs = [
        pl.BlockSpec((1, rank, depth), functools.partial(lambda q, n, ids: (ids[q], 0, 0), q))
        for q in range(queries)
    ]
    return pl.pallas_call(
        left_body,
        out_shape=jax.ShapeDtypeStruct((n_in, rows, eigen), BF),
        grid_spec=pltpu.PrefetchScalarGridSpec(
            num_scalar_prefetch=1,
            grid=(eigen // tile,),
            in_specs=[*specs, pl.BlockSpec((depth, tile), lambda n, ids: (0, n))],
            out_specs=pl.BlockSpec((n_in, rows, tile), lambda n, ids: (0, 0, n)),
        ),
        compiler_params=params(),
        name="left",
    )(query_ids, u_t, u_t, u_t, u_t, basis_out)


def left_sum_body(parts, out, window):
    n_in, rows, _ = parts.shape
    own = rows - WIN_ROWS
    total = parts[0, :own, :].astype(F32)
    for i in range(1, n_in):
        total += parts[i, :own, :].astype(F32)
    total = total.astype(BF)
    for i in range(n_in):
        out[i] = total
        window[i * WIN_ROWS : (i + 1) * WIN_ROWS, :] = parts[i, own:, :]


def left_sum(parts):
    n_in, rows, eigen = parts.shape
    return pl.pallas_call(
        left_sum_body,
        out_shape=(
            jax.ShapeDtypeStruct((n_in, rows - WIN_ROWS, eigen), BF),
            jax.ShapeDtypeStruct((n_in * WIN_ROWS, eigen), BF),
        ),
        in_specs=[VMEM_SPEC],
        out_specs=(VMEM_SPEC, VMEM_SPEC),
        compiler_params=params(),
        name="left_sum",
    )(parts)


def inverse_body(offsets, corrected, *outs):
    for r, out in enumerate(outs):
        at = pl.multiple_of(offsets[r], LANES)
        out[...] = (1.0 / corrected[:, pl.ds(at, out.shape[1])]).astype(BF)


def inverse_quarters(offsets, corrected, width):
    rows, columns = corrected.shape
    tile = 64
    return pl.pallas_call(
        inverse_body,
        out_shape=tuple(jax.ShapeDtypeStruct((rows, width), BF) for _ in range(4)),
        grid_spec=pltpu.PrefetchScalarGridSpec(
            num_scalar_prefetch=1,
            grid=(rows // tile,),
            in_specs=[pl.BlockSpec((tile, columns), lambda n, o: (n, 0))],
            out_specs=tuple(pl.BlockSpec((tile, width), lambda n, o: (n, 0)) for _ in range(4)),
        ),
        compiler_params=params(),
        name="inverse",
    )(offsets, corrected)


def rotate_body(where, ids, v0, v1, v2, v3, *refs):
    chunks, (basis, right, tokens, delta) = refs[:-4], refs[-4:]
    n_z = len(chunks)
    slab = basis.shape[0] // n_z
    extra = (chunks[0].shape[0] - slab) // 2
    for k, chunk in enumerate(chunks):
        step = k if k <= n_z // 2 else k - n_z
        at = lax.rem(where[0] - step + n_z, n_z) * slab
        basis[pl.ds(pl.multiple_of(at, 16), slab), :] = chunk[:slab, :]
    factors = jnp.concatenate([v[0] for v in (v0, v1, v2, v3)], axis=0)
    whole = basis[...]
    right[...] = dot(factors, whole, 1, 0).astype(BF)
    width = whole.shape[1]
    rest = whole.shape[0] - width
    head = jnp.concatenate([c[slab : slab + extra, :] for c in chunks], axis=0)
    tail = jnp.concatenate([c[slab + extra :, :] for c in chunks], axis=0)
    rotated = dot(head, whole[:width, :], 1, 0) + dot(tail[:, :rest], whole[width:, :], 1, 0)
    tokens[...] = rotated.astype(BF)
    delta[...] = tail[:, rest:]


def rotate(where, query_ids, v_t, chunks, block_width):
    queries = query_ids.shape[0]
    rank = v_t.shape[1]
    rows, width = chunks[0].shape
    extra = (rows - block_width // len(chunks)) // 2
    specs = [
        pl.BlockSpec(
            (1, rank, block_width),
            functools.partial(lambda q, n, w, ids: (ids[q], 0, w[1]), q),
        )
        for q in range(queries)
    ]

    def full(shape):
        return pl.BlockSpec(shape, lambda n, w, ids: (0, 0))

    shapes = (
        (block_width, width),
        (queries * rank, width),
        (len(chunks) * extra, width),
        (len(chunks) * extra, 2 * width - block_width),
    )
    return pl.pallas_call(
        rotate_body,
        out_shape=tuple(jax.ShapeDtypeStruct(s, BF) for s in shapes),
        grid_spec=pltpu.PrefetchScalarGridSpec(
            num_scalar_prefetch=2,
            grid=(1,),
            in_specs=[*specs, *(full((rows, width)) for _ in chunks)],
            out_specs=tuple(full(s) for s in shapes),
        ),
        compiler_params=params(),
        name="rotate",
    )(where, query_ids, v_t, v_t, v_t, v_t, *chunks)


def back_body(where, factors, right, tokens, delta, *refs):
    lefts, windows, inverses, (out, score) = refs[:4], refs[4:8], refs[8:12], refs[12:]
    n_z, queries, rows, width = out.shape
    rank = right.shape[0] // queries
    valid = factors.shape[1] // 2
    skip = factors.shape[1] - width
    row = factors[pl.ds(where[2], 1), pl.ds(pl.multiple_of(where[3] * skip, LANES), width)]
    lane = lax.broadcasted_iota(jnp.int32, (1, width), 1)
    first = where[3] * (width - valid)
    mine = jnp.logical_and(lane >= first, lane < first + valid)
    scale = jnp.where(mine, 1.0 / row, 0.0)
    train = 4
    which = lax.rem(lax.broadcasted_iota(jnp.int32, (tokens.shape[0], 1), 0), train)
    for q in range(queries):
        at = slice(q * rank, (q + 1) * rank)
        total = None
        for left, window, inverse in zip(lefts, windows, inverses):
            product = dot(left[at, :], right[at, :], 0, 0)
            precond = (product * inverse[...].astype(F32)).astype(BF)
            term = dot(window[...], precond, 1, 0)
            total = term if total is None else total + term
        total = (total * scale).astype(BF)
        out[:, q] = total.reshape(n_z, rows, width)
        projected = dot(tokens[...], total, 1, 1) * delta[...].astype(F32)
        for b in range(train):
            part = jnp.where(which == b, projected, 0.0)
            score[q * train + b : q * train + b + 1, :] = jnp.sum(part, axis=0, keepdims=True)


def back(where, factors, right, tokens, delta, lefts, windows, inverses, n_z, queries):
    width = right.shape[1]
    win = windows[0].shape[0]
    return pl.pallas_call(
        back_body,
        out_shape=(
            jax.ShapeDtypeStruct((n_z, queries, win // n_z, width), BF),
            jax.ShapeDtypeStruct((queries * 4, win), F32),
        ),
        in_specs=[SMEM_SPEC, *([VMEM_SPEC] * (4 + 12))],
        out_specs=(VMEM_SPEC, VMEM_SPEC),
        compiler_params=params(),
        name="back",
    )(where, factors, right, tokens, delta, *lefts, *windows, *inverses)


def tile_body(parts, basis, out):
    n_z, rows, width = parts.shape
    owners, own, _ = out.shape
    queries = 4
    per = own // queries
    to = lax.broadcasted_iota(jnp.int32, (rows, n_z * rows), 0)
    at = lax.rem(lax.broadcasted_iota(jnp.int32, (rows, n_z * rows), 1), rows)
    query = at // (owners * per)
    owner = lax.rem(at // per, owners)
    goal = owner * own + query * per + lax.rem(at, per)
    select = jnp.where(goal == to, 1.0, 0.0).astype(BF)
    half = dot(select, parts[...].reshape(n_z * rows, width), 1, 0).astype(BF)
    tiles = dot(half, basis[...], 1, 1).astype(BF)
    out[...] = tiles.reshape(owners, own, tiles.shape[1])


def tile_part(parts, basis, owners):
    rows = parts.shape[1]
    return pl.pallas_call(
        tile_body,
        out_shape=jax.ShapeDtypeStruct((owners, rows // owners, basis.shape[0]), BF),
        in_specs=[VMEM_SPEC, VMEM_SPEC],
        out_specs=VMEM_SPEC,
        compiler_params=params(),
        name="tile",
    )(parts, basis)


def shards(
    basis_out,
    corrected,
    factor_table,
    block_ids,
    basis_in,
    query_ids,
    u_pool,
    v_pool,
    train_ids,
    x_pool,
    delta_pool,
):
    n_z, n_in = lax.axis_size("z"), lax.axis_size(IN)
    z, xh, c = lax.axis_index("z"), lax.axis_index("xh"), lax.axis_index("c")
    in_pos = lax.axis_index(IN)
    queries, train = query_ids.shape[0], train_ids.shape[0]
    _, local_rows, block = basis_in.shape
    width = -(-(block // 2) // LANES) * LANES
    skip = block - width
    me = 2 * xh + c

    parts = left_part(query_ids, jnp.transpose(u_pool, (0, 2, 1)), basis_out, n_in)
    spread, window = left_sum(exchange(parts, IN))
    left = exchange(spread, IN).reshape(-1, basis_out.shape[1])
    left_x, window_x = swap(left, "xh"), swap(window, "xh")
    lefts = (left, swap(left, "c"), left_x, swap(left_x, "c"))
    windows = (window, swap(window, "c"), window_x, swap(window_x, "c"))

    others = me ^ jnp.arange(4, dtype=jnp.int32)
    offsets = (others // 2) * block + (others % 2) * skip
    quarters = inverse_quarters(offsets, corrected, width)
    inverses = (
        quarters[0],
        swap(quarters[1], "c"),
        swap(quarters[2], "xh"),
        swap(quarters[3], QUAD, 3),
    )

    chosen = (train_ids[:, None] == jnp.arange(x_pool.shape[0])[None, :]).astype(BF)
    rows = jnp.concatenate([x_pool[:, 0], delta_pool[:, 0]], axis=1)
    rows = jnp.dot(chosen, rows, preferred_element_type=F32).astype(BF)
    deltas = rows[:, 2 * block :]
    send = []
    for p in range(4):
        blk, half = divmod(p, 2)
        cut = basis_in[blk, :, half * skip : half * skip + width]
        own = rows[:, blk * block : (blk + 1) * block]
        send.append(
            jnp.concatenate(
                [cut, own[:, :width], jnp.concatenate([own[:, width:], deltas], axis=1)], axis=0
            )
        )
    got = exchange(jnp.stack(send), QUAD)
    ends = (0, local_rows, local_rows + train, local_rows + 2 * train)
    own = jnp.concatenate(
        [got[:, a:b].reshape(-1, width) for a, b in zip(ends[:-1], ends[1:])], axis=0
    )
    ahead, behind = [own], []
    for step in range(n_z // 2):
        ahead.append(shift(ahead[-1], 1))
        if step < n_z // 2 - 1:
            behind.append(shift(behind[-1] if behind else own, -1))
    chunks = ahead + behind[::-1]

    block_id = lax.dynamic_index_in_dim(block_ids, in_pos * 2 + xh, keepdims=False)
    where = jnp.stack([z, xh, block_id, c]).astype(jnp.int32)
    basis, right, tokens, delta = rotate(
        where, query_ids, jnp.transpose(v_pool, (0, 2, 1)), chunks, block
    )
    parts, score = back(
        where, factor_table, right, tokens, delta, lefts, windows, inverses, n_z, queries
    )
    summed = exchange(parts.reshape(n_z, -1, width), "z")
    owned = exchange(tile_part(summed, basis, 4), QUAD).astype(F32)
    pairs = owned.reshape(2, 2, queries, -1, block)
    tiles = (pairs[:, 0] + pairs[:, 1]).astype(BF)
    tiles = jnp.moveaxis(tiles, 0, 2).reshape(queries, -1, 2 * block)

    score = copies(jnp.sum(score, axis=1)[None], "z").sum(axis=0)
    score = copies(score, PLANE).sum(axis=0)
    return tiles, score.reshape(queries, train)


def solution(mesh):
    split = Mesh(mesh.devices.reshape(8, 2, 2, 4, 2), ("z", "xh", "c", "y", "xl"))
    return jax.shard_map(
        shards,
        mesh=split,
        in_specs=(
            P(IN, OUT),
            P(OUT, IN),
            P(),
            P(),
            P(IN, OUT, None),
            P(),
            P(None, IN, None),
            P(None, IN, None),
            P(),
            P(None, OUT, IN),
            P(None, OUT, None),
        ),
        out_specs=(P(None, OUT, IN), P()),
        check_vma=False,
    )
```

time: 332 us -> 190 us (0.57)
  blocking collectives: 118 us -> 26.9 us
  matrix products: 40.6 us -> 1.04 us
  Pallas kernels: 0 us -> 34.1 us
  starting transfers between devices: 13.8 us -> 44.7 us
  local copies, waits for them, and re-layouts: 35.3 us -> 9.11 us
  waiting for transfers between devices: 86.7 us -> 69.8 us
  other arithmetic: 19.9 us -> 3.02 us
  between operations: 14.2 us -> 0.91 us
    all_gather x1 -> x0, blocking collectives: 74 us -> none  [sent_together(): out = lax.all_gather(both, axis, axis=dim, tiled=True)]
    all_gather x1 -> x0, waiting for transfers between devices: 48.5 us -> none  [shards(): full_basis = lax.all_gather(basis_in, OUT, axis=1, tiled=True)]
    dot_general x7 -> x1, matrix products: 40.6 us -> 1.04 us  [shards(): rows = jnp.dot(chosen, rows, preferred_element_type=F32).astype(BF)]
    psum x5 -> x0, blocking collectives: 36.7 us -> none  [over_axes(): return functools.reduce(lax.psum, axes, value)]
    pallas_call x0 -> x6, Pallas kernels: none -> 34.1 us  [the longest x1 10.9 us: back(): pl.pallas_call(back_body, out_shape=(jax.ShapeDtypeStruct((n_z, queries,...]
    ppermute x0 -> x16, waiting for transfers between devices: none -> 27.4 us  [the longest x9 14.2 us: swap(): return lax.ppermute(value, axis, [(i, i ^ mask) for i in range(size)])]
    ppermute x0 -> x16, starting transfers between devices: none -> 24.2 us  [the longest x7 12.9 us: shift(): lax.ppermute(value, 'z', [(i, (i + step) % size) for i in range(size)])]
    all_to_all x1 -> x2, blocking collectives: 7.33 us -> 26.9 us  [exchange(): return lax.all_to_all(value, axis, split_axis=0, concat_axis=0, tiled=True)]
  transfers between devices with their start and end apart: 4 -> 21, of which waited for: 2 -> 9; matrix products, arithmetic and copies ran while one was open for 17% -> 2% of each run, Pallas kernels for 0% -> 12%
where the time goes in v1:
time: 190 us
  waiting for transfers between devices  69.8 us (37%)
  starting transfers between devices  44.7 us (24%)
  Pallas kernels  34.1 us (18%)
  blocking collectives  26.9 us (14%)
  local copies, waits for them, and re-layouts  9.11 us (5%)
  other arithmetic  3.02 us (2%)
    all_to_all x5, waiting for transfers between devices, exchange(): return lax.all_to_all(value, axis, split_axis=0, concat_axis=0, tiled=True)  42.4 us
    all_to_all x2, blocking collectives, exchange(): return lax.all_to_all(value, axis, split_axis=0, concat_axis=0, tiled=True)  26.9 us
    all_to_all x5, starting transfers between devices, exchange(): return lax.all_to_all(value, axis, split_axis=0, concat_axis=0, tiled=True)  20.5 us
    ppermute x9, waiting for transfers between devices, swap(): return lax.ppermute(value, axis, [(i, i ^ mask) for i in range(size)])  14.2 us
    ppermute x7, waiting for transfers between devices, shift(): lax.ppermute(value, 'z', [(i, (i + step) % size) for i in range(size)])  13.2 us
    ppermute x7, starting transfers between devices, shift(): lax.ppermute(value, 'z', [(i, (i + step) % size) for i in range(size)])  12.9 us
    ppermute x9, starting transfers between devices, swap(): return lax.ppermute(value, axis, [(i, i ^ mask) for i in range(size)])  11.3 us
    pallas_call x1, Pallas kernels, back(): pl.pallas_call(back_body, out_shape=(jax.ShapeDtypeStruct((n_z, queries,...  10.9 us
  transfers between devices with their start and end apart: 21, of which 9 were waited for; matrix products, arithmetic and copies ran while one was open for 2% of the time, Pallas kernels for 12%

profile of v1, /device:TPU:1, one launch (start us, length us, event | category | flops | bytes accessed | tf_op | source)
XLA Modules:
  0.0 189.6 jit_solution(14968839141698564441)
XLA Ops:
  0.6 1.0 convolution_convert_fusion
  1.7 1.8 fusion.16
  3.7 0.1 fusion.1
  3.7 0.1 pad_maximum_fusion
  3.8 14.5 %all_to_all.35 = bf16[4,60,896]{2,1,0:T(8,128)(2,1)S(1)} all-to-all(bf16[4,60,896]{2,1,0:T(8,128)(2,1)S(1)} %pad_maximum_fusion), channel_id=1, replica_groups=mesh['z'=8,'xh'=2,'c'=2,'y'=4,'xl'=2] {'xh','c'}, dimensions={0} | all-to-all | bytes 860160 | tf_op jit(solution)/shard_map/all_to_all | solution.py:34
  18.4 0.1 reshape.39
  18.6 1.7 collective-permute-start
  20.3 4.1 %left.1 = bf16[8,48,512]{2,1,0:T(8,128)(2,1)} custom-call(s32[4]{0:T(128)} %ids.3, bf16[6,64,2048]{2,1,0:T(8,128)(2,1)} %bitcast.40, bf16[6,64,2048]{2,1,0:T(8,128)(2,1)} %bitcast.41, bf16[6,64,2048]{2,1,0:T(8,128)(2,1)} %bitcast.42, bf16[6,64,2048]{2,1,0:T(8,128)(2,1)} %bitcast.43, bf16[2048,512]{1,0:T(8,128)(2,1)} %basis.1), custom_call_target="tpu_custom_call" | custom-call | tf_op jit(solution)/shard_map/left/pallas_call | solution.py:71
  24.4 4.2 %all-to-all-start.1 = ((bf16[8,48,512]{2,1,0:T(8,128)(2,1)}), bf16[8,48,512]{2,1,0:T(8,128)(2,1)S(1)}, u32[]{:S(2)}, u32[]{:S(2)}) async-start(bf16[8,48,512]{2,1,0:T(8,128)(2,1)} %left.1), calls=%async_computation.1 | async-start | bytes 786432 | tf_op jit(solution)/shard_map/all_to_all | solution.py:34
  28.6 4.0 %collective-permute-start.4 = (bf16[240,896]{1,0:T(8,128)(2,1)S(1)}, bf16[240,896]{1,0:T(8,128)(2,1)}, u32[]{:S(2)}, u32[]{:S(2)}) collective-permute-start(bf16[240,896]{1,0:T(8,128)(2,1)S(1)} %constant_dynamic-update-slice_fusion.refs_0_), channel_id=1, source_target_pairs={{0,224},{32,0},{64,32},{96,64},{128,96},{160,128},{192,160},{224,1... | collective-permute-start | bytes 1290248 | tf_op jit(solution)/shard_map/ppermute | solution.py:48
  32.7 1.1 collective-permute-done.refs_1_
  33.8 2.3 %all-to-all-done.1.parts = bf16[8,48,512]{2,1,0:T(8,128)(2,1)S(1)} async-done(((bf16[8,48,512]{2,1,0:T(8,128)(2,1)}), bf16[8,48,512]{2,1,0:T(8,128)(2,1)S(1)}, u32[]{:S(2)}, u32[]{:S(2)}) %all-to-all-start.1) | async-done | bytes 393248 | tf_op jit(solution)/shard_map/all_to_all | solution.py:34
  36.0 0.7 copy-done.1
  36.8 1.8 left_sum.1
  38.6 3.4 %all-to-all-start.2 = ((bf16[8,32,512]{2,1,0:T(8,128)(2,1)}), bf16[8,32,512]{2,1,0:T(8,128)(2,1)S(1)}, u32[]{:S(2)}, u32[]{:S(2)}) async-start(bf16[8,32,512]{2,1,0:T(8,128)(2,1)} %get-tuple-element.17), calls=%async_computation.2 | async-start | bytes 524288 | tf_op jit(solution)/shard_map/all_to_all | solution.py:34
  42.0 0.5 collective-permute-start.11
  42.5 5.5 %all-to-all-done.2 = bf16[8,32,512]{2,1,0:T(8,128)(2,1)S(1)} async-done(((bf16[8,32,512]{2,1,0:T(8,128)(2,1)}), bf16[8,32,512]{2,1,0:T(8,128)(2,1)S(1)}, u32[]{:S(2)}, u32[]{:S(2)}) %all-to-all-start.2) | async-done | bytes 262176 | tf_op jit(solution)/shard_map/all_to_all | solution.py:34
  48.1 0.4 collective-permute-start.8
  48.5 0.0 collective-permute-done.4.refs_7_
  48.5 4.2 %collective-permute-start.5 = (bf16[240,896]{1,0:T(8,128)(2,1)}, bf16[240,896]{1,0:T(8,128)(2,1)}, u32[]{:S(2)}, u32[]{:S(2)}) collective-permute-start(bf16[240,896]{1,0:T(8,128)(2,1)} %collective-permute-done.4.refs_7_), channel_id=1, source_target_pairs={{0,224},{32,0},{64,32},{96,64},{128,96},{160,128},{192,160},{224,1... | collective-permute-start | bytes 1290248 | tf_op jit(solution)/shard_map/ppermute | solution.py:48
  52.8 0.0 collective-permute-done.1.refs_2_
  52.8 0.0 collective-permute-start.2
  52.8 4.6 %collective-permute-start.10 = (bf16[128,512]{1,0:T(8,128)(2,1)}, bf16[128,512]{1,0:T(8,128)(2,1)S(1)}, u32[]{:S(2)}, u32[]{:S(2)}) collective-permute-start(bf16[128,512]{1,0:T(8,128)(2,1)} %get-tuple-element.18.refs_4_), channel_id=1, source_target_pairs={{0,8},{8,0},{1,9},{9,1},{2,10},{10,2},{3,11},{11,3},{4,12},{12,4},... | collective-permute-start | bytes 393224 | tf_op jit(solution)/shard_map/ppermute | solution.py:43
  57.4 0.0 collective-permute-done.11.refs_6_
  57.4 0.1 collective-permute-start.12
  57.5 0.6 fusion.13.offsets
  58.1 7.9 %inverse.1 = (bf16[512,896]{1,0:T(8,128)(2,1)}, bf16[512,896]{1,0:T(8,128)(2,1)}, bf16[512,896]{1,0:T(8,128)(2,1)}, bf16[512,896]{1,0:T(8,128)(2,1)}) custom-call(s32[4]{0:T(128)} %fusion.13.offsets, f32[512,3328]{1,0:T(8,128)} %corrected.1), custom_call_target="tpu_custom_call" | custom-call | tf_op jit(solution)/shard_map/inverse/pallas_call | solution.py:121
  66.0 0.0 collective-permute-done.10.refs_5_
  66.0 0.5 collective-permute-start.13
  66.5 0.0 collective-permute-done.12.refs_7_
  66.5 0.1 copy-done.12
  66.6 0.7 copy-done.13
  67.3 2.3 %collective-permute-start.14 = (bf16[512,896]{1,0:T(8,128)(2,1)}, bf16[512,896]{1,0:T(8,128)(2,1)S(1)}, u32[]{:S(2)}, u32[]{:S(2)}) collective-permute-start(bf16[512,896]{1,0:T(8,128)(2,1)} %get-tuple-element.21), channel_id=1, source_target_pairs={{0,16},{16,0},{1,17},{17,1},{2,18},{18,2},{3,19},{19,3},{4,20},{20... | collective-permute-start | bytes 2752520 | tf_op jit(solution)/shard_map/ppermute | solution.py:43
  69.6 0.0 collective-permute-done.8.refs_2_
  69.6 0.7 copy-done.10
  70.3 1.2 collective-permute-start.15
  71.6 3.0 %collective-permute-start.6 = (bf16[240,896]{1,0:T(8,128)(2,1)}, bf16[240,896]{1,0:T(8,128)(2,1)S(1)}, u32[]{:S(2)}, u32[]{:S(2)}) collective-permute-start(bf16[240,896]{1,0:T(8,128)(2,1)} %collective-permute-done.5.refs_6_), channel_id=1, source_target_pairs={{0,224},{32,0},{64,32},{96,64},{128,96},{160,128},{192,160},{224,1... | collective-permute-start | bytes 1290248 | tf_op jit(solution)/shard_map/ppermute | solution.py:48
  74.5 9.8 %collective-permute-done.6.refs_5_ = bf16[240,896]{1,0:T(8,128)(2,1)S(1)} collective-permute-done((bf16[240,896]{1,0:T(8,128)(2,1)}, bf16[240,896]{1,0:T(8,128)(2,1)S(1)}, u32[]{:S(2)}, u32[]{:S(2)}) %collective-permute-start.6) | collective-permute-done | bytes 430112 | tf_op jit(solution)/shard_map/ppermute | solution.py:48
  84.3 0.7 collective-permute-start.7
  84.9 0.1 copy-done.8
  85.0 2.4 %collective-permute-done.3.refs_4_ = bf16[240,896]{1,0:T(8,128)(2,1)S(1)} collective-permute-done((bf16[240,896]{1,0:T(8,128)(2,1)}, bf16[240,896]{1,0:T(8,128)(2,1)S(1)}, u32[]{:S(2)}, u32[]{:S(2)}) %collective-permute-start.3) | collective-permute-done | bytes 430112 | tf_op jit(solution)/shard_map/ppermute | solution.py:48
  87.4 0.8 copy-done.9
  88.2 0.9 collective-permute-start.9
  89.1 0.7 dynamic_slice.4
  89.7 1.3 pad_add_fusion.where
  91.1 5.4 %rotate.1 = (bf16[1664,896]{1,0:T(8,128)(2,1)}, bf16[256,896]{1,0:T(8,128)(2,1)}, bf16[128,896]{1,0:T(8,128)(2,1)}, bf16[128,128]{1,0:T(8,128)(2,1)}) custom-call(s32[4]{0:T(128)} %pad_add_fusion.where, s32[4]{0:T(128)} %ids.3, bf16[6,64,3328]{2,1,0:T(8,128)(2,1)} %bitcast.36, bf16[6,64,3328]{2,1,0:T(8,128)(2,1)} %bitcast.37, bf16[6,64,3328]{2,1,0:T(8,128)(2,1)} %bitcast.38, ...), custom_call_target="tpu_custom_call" | custom-call | tf_op jit(solution)/shard_map/rotate/pallas_call | solution.py:178
  96.5 14.2 %collective-permute-done.15.refs_11_ = bf16[512,896]{1,0:T(8,128)(2,1)S(1)} collective-permute-done((bf16[512,896]{1,0:T(8,128)(2,1)}, bf16[512,896]{1,0:T(8,128)(2,1)S(1)}, u32[]{:S(2)}, u32[]{:S(2)}) %collective-permute-start.15) | collective-permute-done | bytes 917536 | tf_op jit(solution)/shard_map/ppermute | solution.py:43
  110.8 1.0 copy-done.6
  111.8 10.9 %back.1 = (bf16[8,4,16,896]{3,2,1,0:T(8,128)(2,1)}, f32[16,128]{1,0:T(8,128)}) custom-call(s32[4]{0:T(128)} %pad_add_fusion.where, f32[32,1664]{1,0:T(8,128)} %factors.1, bf16[256,896]{1,0:T(8,128)(2,1)} %get-tuple-element.14.right, bf16[128,896]{1,0:T(8,128)(2,1)} %get-tuple-element.15.tokens, bf16[128,128]{1,0:T(8,128)(2,1)} %get-tuple-element.16.delta, ...), custom_call_target="tpu_custom_call" | custom-call | tf_op jit(solution)/shard_map/back/pallas_call | solution.py:224
  122.7 0.8 reduce_sum.27
  123.5 12.4 %all_to_all.36 = f32[8,1,16]{2,1,0:T(1,128)S(1)} all-to-all(f32[8,1,16]{2,1,0:T(1,128)S(1)} %broadcast_in_dim.4), channel_id=1, replica_groups=mesh['z'=8,'xh'=2,'c'=2,'y'=4,'xl'=2] {'z'}, dimensions={0} | all-to-all | bytes 1024 | tf_op jit(solution)/shard_map/all_to_all | solution.py:34
  135.9 3.6 %all-to-all-start.3 = ((bf16[8,64,896]{2,1,0:T(8,128)(2,1)}), bf16[8,64,896]{2,1,0:T(8,128)(2,1)S(1)}, u32[]{:S(2)}, u32[]{:S(2)}) async-start(bf16[8,64,896]{2,1,0:T(8,128)(2,1)} %bitcast.47), calls=%async_computation.3 | async-start | bytes 1835008 | tf_op jit(solution)/shard_map/all_to_all | solution.py:34
  139.5 26.3 %all-to-all-done.3.parts = bf16[8,64,896]{2,1,0:T(8,128)(2,1)S(1)} async-done(((bf16[8,64,896]{2,1,0:T(8,128)(2,1)}), bf16[8,64,896]{2,1,0:T(8,128)(2,1)S(1)}, u32[]{:S(2)}, u32[]{:S(2)}) %all-to-all-start.3) | async-done | bytes 917536 | tf_op jit(solution)/shard_map/all_to_all | solution.py:34
  165.8 0.7 broadcast_in_dim.10
  166.4 5.3 %all-to-all-start.6 = ((f32[32,1,16]{2,1,0:T(1,128)}), f32[32,1,16]{2,1,0:T(1,128)S(1)}, u32[]{:S(2)}, u32[]{:S(2)}) async-start(f32[32,1,16]{2,1,0:T(1,128)} %broadcast_in_dim.10), calls=%async_computation.6 | async-start | bytes 32768 | tf_op jit(solution)/shard_map/all_to_all | solution.py:34
  171.7 4.0 %tile.1 = bf16[4,16,1664]{2,1,0:T(8,128)(2,1)} custom-call(bf16[8,64,896]{2,1,0:T(8,128)(2,1)} %copy-done, bf16[1664,896]{1,0:T(8,128)(2,1)} %get-tuple-element.24.basis), custom_call_target="tpu_custom_call" | custom-call | tf_op jit(solution)/shard_map/tile/pallas_call | solution.py:255
  175.7 2.9 %all-to-all-done.6 = f32[32,1,16]{2,1,0:T(1,128)S(1)} async-done(((f32[32,1,16]{2,1,0:T(1,128)}), f32[32,1,16]{2,1,0:T(1,128)S(1)}, u32[]{:S(2)}, u32[]{:S(2)}) %all-to-all-start.6) | async-done | bytes 2080 | tf_op jit(solution)/shard_map/all_to_all | solution.py:34
  178.6 4.0 %all-to-all-start.4 = ((bf16[4,16,1664]{2,1,0:T(8,128)(2,1)}), bf16[4,16,1664]{2,1,0:T(8,128)(2,1)S(1)}, u32[]{:S(2)}, u32[]{:S(2)}) async-start(bf16[4,16,1664]{2,1,0:T(8,128)(2,1)} %tile.1), calls=%async_computation.4 | async-start | bytes 425984 | tf_op jit(solution)/shard_map/all_to_all | solution.py:34
  182.6 0.1 reduce_sum.29
  182.6 0.7 reshape.47
  183.3 5.4 %all-to-all-done.4 = bf16[4,16,1664]{2,1,0:T(8,128)(2,1)S(1)} async-done(((bf16[4,16,1664]{2,1,0:T(8,128)(2,1)}), bf16[4,16,1664]{2,1,0:T(8,128)(2,1)S(1)}, u32[]{:S(2)}, u32[]{:S(2)}) %all-to-all-start.4) | async-done | bytes 213024 | tf_op jit(solution)/shard_map/all_to_all | solution.py:34
  188.7 0.1 reshape.49
  188.8 0.1 fusion.7
  188.9 0.7 copy.39
  (47 shorter events, 0.3 us)
Async XLA Ops:
  18.6 10.0 %copy-start.2 = (bf16[240,896]{1,0:T(8,128)(2,1)}, bf16[240,896]{1,0:T(8,128)(2,1)S(1)}, u32[]{:S(2)}) copy-start(bf16[240,896]{1,0:T(8,128)(2,1)S(1)} %constant_dynamic-update-slice_fusion.refs_0_) | copy-start | bytes 1290244
  18.6 15.2 %collective-permute-start = (bf16[240,896]{1,0:T(8,128)(2,1)S(1)}, bf16[240,896]{1,0:T(8,128)(2,1)S(1)}, u32[]{:S(2)}, u32[]{:S(2)}) collective-permute-start(bf16[240,896]{1,0:T(8,128)(2,1)S(1)} %constant_dynamic-update-slice_fusion.refs_0_), channel_id=1, source_target_pairs={{0,32},{32,64},{64,96},{96,128},{128,160},{160,192},{192,224},{224... | collective-permute-start | bytes 1290248 | tf_op jit(solution)/shard_map/ppermute | solution.py:48
  24.4 11.6 %all-to-all-start.1 = ((bf16[8,48,512]{2,1,0:T(8,128)(2,1)}), bf16[8,48,512]{2,1,0:T(8,128)(2,1)S(1)}, u32[]{:S(2)}, u32[]{:S(2)}) async-start(bf16[8,48,512]{2,1,0:T(8,128)(2,1)} %left.1), calls=%async_computation.1 | async-start | bytes 786432 | tf_op jit(solution)/shard_map/all_to_all | solution.py:34
  28.6 19.9 %collective-permute-start.4 = (bf16[240,896]{1,0:T(8,128)(2,1)S(1)}, bf16[240,896]{1,0:T(8,128)(2,1)}, u32[]{:S(2)}, u32[]{:S(2)}) collective-permute-start(bf16[240,896]{1,0:T(8,128)(2,1)S(1)} %constant_dynamic-update-slice_fusion.refs_0_), channel_id=1, source_target_pairs={{0,224},{32,0},{64,32},{96,64},{128,96},{160,128},{192,160},{224,1... | collective-permute-start | bytes 1290248 | tf_op jit(solution)/shard_map/ppermute | solution.py:48
  33.8 57.3 %copy-start.7 = (bf16[240,896]{1,0:T(8,128)(2,1)}, bf16[240,896]{1,0:T(8,128)(2,1)S(1)}, u32[]{:S(2)}) copy-start(bf16[240,896]{1,0:T(8,128)(2,1)S(1)} %collective-permute-done.refs_1_) | copy-start | bytes 1290244
  33.8 19.0 %collective-permute-start.1 = (bf16[240,896]{1,0:T(8,128)(2,1)S(1)}, bf16[240,896]{1,0:T(8,128)(2,1)}, u32[]{:S(2)}, u32[]{:S(2)}) collective-permute-start(bf16[240,896]{1,0:T(8,128)(2,1)S(1)} %collective-permute-done.refs_1_), channel_id=1, source_target_pairs={{0,32},{32,64},{64,96},{96,128},{128,160},{160,192},{192,224},{224... | collective-permute-start | bytes 1290248 | tf_op jit(solution)/shard_map/ppermute | solution.py:48
  36.0 0.7 copy-start.1
  38.6 9.5 %all-to-all-start.2 = ((bf16[8,32,512]{2,1,0:T(8,128)(2,1)}), bf16[8,32,512]{2,1,0:T(8,128)(2,1)S(1)}, u32[]{:S(2)}, u32[]{:S(2)}) async-start(bf16[8,32,512]{2,1,0:T(8,128)(2,1)} %get-tuple-element.17), calls=%async_computation.2 | async-start | bytes 524288 | tf_op jit(solution)/shard_map/all_to_all | solution.py:34
  42.0 15.4 %collective-permute-start.11 = (bf16[128,512]{1,0:T(8,128)(2,1)}, bf16[128,512]{1,0:T(8,128)(2,1)S(1)}, u32[]{:S(2)}, u32[]{:S(2)}) collective-permute-start(bf16[128,512]{1,0:T(8,128)(2,1)} %get-tuple-element.18.refs_4_), channel_id=1, source_target_pairs={{0,16},{16,0},{1,17},{17,1},{2,18},{18,2},{3,19},{19,3},{4,20},{20... | collective-permute-start | bytes 393224 | tf_op jit(solution)/shard_map/ppermute | solution.py:43
  48.1 36.2 %copy-start.3 = (bf16[8,32,512]{2,1,0:T(8,128)(2,1)}, bf16[8,32,512]{2,1,0:T(8,128)(2,1)S(1)}, u32[]{:S(2)}) copy-start(bf16[8,32,512]{2,1,0:T(8,128)(2,1)S(1)} %all-to-all-done.2) | copy-start | bytes 786436
  48.1 21.5 %collective-permute-start.8 = (bf16[256,512]{1,0:T(8,128)(2,1)S(1)}, bf16[256,512]{1,0:T(8,128)(2,1)S(1)}, u32[]{:S(2)}, u32[]{:S(2)}) collective-permute-start(bf16[256,512]{1,0:T(8,128)(2,1)S(1)} %bitcast.44), channel_id=1, source_target_pairs={{0,16},{16,0},{1,17},{17,1},{2,18},{18,2},{3,19},{19,3},{4,20},{20... | collective-permute-start | bytes 786440 | tf_op jit(solution)/shard_map/ppermute | solution.py:43
  48.5 23.0 %collective-permute-start.5 = (bf16[240,896]{1,0:T(8,128)(2,1)}, bf16[240,896]{1,0:T(8,128)(2,1)}, u32[]{:S(2)}, u32[]{:S(2)}) collective-permute-start(bf16[240,896]{1,0:T(8,128)(2,1)} %collective-permute-done.4.refs_7_), channel_id=1, source_target_pairs={{0,224},{32,0},{64,32},{96,64},{128,96},{160,128},{192,160},{224,1... | collective-permute-start | bytes 1290248 | tf_op jit(solution)/shard_map/ppermute | solution.py:48
  52.8 21.8 %collective-permute-start.2 = (bf16[240,896]{1,0:T(8,128)(2,1)}, bf16[240,896]{1,0:T(8,128)(2,1)}, u32[]{:S(2)}, u32[]{:S(2)}) collective-permute-start(bf16[240,896]{1,0:T(8,128)(2,1)} %collective-permute-done.1.refs_2_), channel_id=1, source_target_pairs={{0,32},{32,64},{64,96},{96,128},{128,160},{160,192},{192,224},{224... | collective-permute-start | bytes 1290248 | tf_op jit(solution)/shard_map/ppermute | solution.py:48
  52.8 13.2 %collective-permute-start.10 = (bf16[128,512]{1,0:T(8,128)(2,1)}, bf16[128,512]{1,0:T(8,128)(2,1)S(1)}, u32[]{:S(2)}, u32[]{:S(2)}) collective-permute-start(bf16[128,512]{1,0:T(8,128)(2,1)} %get-tuple-element.18.refs_4_), channel_id=1, source_target_pairs={{0,8},{8,0},{1,9},{9,1},{2,10},{10,2},{3,11},{11,3},{4,12},{12,4},... | collective-permute-start | bytes 393224 | tf_op jit(solution)/shard_map/ppermute | solution.py:43
  57.4 8.6 %copy-start.11 = (bf16[128,512]{1,0:T(8,128)(2,1)}, bf16[128,512]{1,0:T(8,128)(2,1)S(1)}, u32[]{:S(2)}) copy-start(bf16[128,512]{1,0:T(8,128)(2,1)S(1)} %collective-permute-done.11.refs_6_) | copy-start | bytes 393220
  57.4 9.1 %collective-permute-start.12 = (bf16[128,512]{1,0:T(8,128)(2,1)S(1)}, bf16[128,512]{1,0:T(8,128)(2,1)S(1)}, u32[]{:S(2)}, u32[]{:S(2)}) collective-permute-start(bf16[128,512]{1,0:T(8,128)(2,1)S(1)} %collective-permute-done.11.refs_6_), channel_id=1, source_target_pairs={{0,8},{8,0},{1,9},{9,1},{2,10},{10,2},{3,11},{11,3},{4,12},{12,4},... | collective-permute-start | bytes 393224 | tf_op jit(solution)/shard_map/ppermute | solution.py:43
  58.1 30.9 %copy-start.14 = (s32[16]{0:T(128)S(1)}, s32[16]{0:T(128)}, u32[]{:S(2)}) copy-start(s32[16]{0:T(128)} %param.14) | copy-start | bytes 196
  66.0 0.7 copy-start.12
  66.0 30.5 %collective-permute-start.13 = (bf16[512,896]{1,0:T(8,128)(2,1)}, bf16[512,896]{1,0:T(8,128)(2,1)S(1)}, u32[]{:S(2)}, u32[]{:S(2)}) collective-permute-start(bf16[512,896]{1,0:T(8,128)(2,1)} %get-tuple-element.20), channel_id=1, source_target_pairs={{0,8},{8,0},{1,9},{9,1},{2,10},{10,2},{3,11},{11,3},{4,12},{12,4},... | collective-permute-start | bytes 2752520 | tf_op jit(solution)/shard_map/ppermute | solution.py:43
  66.6 0.7 copy-start.13
  67.3 29.2 %collective-permute-start.14 = (bf16[512,896]{1,0:T(8,128)(2,1)}, bf16[512,896]{1,0:T(8,128)(2,1)S(1)}, u32[]{:S(2)}, u32[]{:S(2)}) collective-permute-start(bf16[512,896]{1,0:T(8,128)(2,1)} %get-tuple-element.21), channel_id=1, source_target_pairs={{0,16},{16,0},{1,17},{17,1},{2,18},{18,2},{3,19},{19,3},{4,20},{20... | collective-permute-start | bytes 2752520 | tf_op jit(solution)/shard_map/ppermute | solution.py:43
  69.6 0.7 copy-start.10
  70.3 40.4 %collective-permute-start.15 = (bf16[512,896]{1,0:T(8,128)(2,1)}, bf16[512,896]{1,0:T(8,128)(2,1)S(1)}, u32[]{:S(2)}, u32[]{:S(2)}) collective-permute-start(bf16[512,896]{1,0:T(8,128)(2,1)} %get-tuple-element.22), channel_id=1, source_target_pairs={{0,24},{8,16},{16,8},{24,0},{1,25},{9,17},{17,9},{25,1},{2,26},{10... | collective-permute-start | bytes 2752520 | tf_op jit(solution)/shard_map/ppermute | solution.py:43
  71.6 12.7 %collective-permute-start.6 = (bf16[240,896]{1,0:T(8,128)(2,1)}, bf16[240,896]{1,0:T(8,128)(2,1)S(1)}, u32[]{:S(2)}, u32[]{:S(2)}) collective-permute-start(bf16[240,896]{1,0:T(8,128)(2,1)} %collective-permute-done.5.refs_6_), channel_id=1, source_target_pairs={{0,224},{32,0},{64,32},{96,64},{128,96},{160,128},{192,160},{224,1... | collective-permute-start | bytes 1290248 | tf_op jit(solution)/shard_map/ppermute | solution.py:48
  74.5 12.9 %collective-permute-start.3 = (bf16[240,896]{1,0:T(8,128)(2,1)}, bf16[240,896]{1,0:T(8,128)(2,1)S(1)}, u32[]{:S(2)}, u32[]{:S(2)}) collective-permute-start(bf16[240,896]{1,0:T(8,128)(2,1)} %collective-permute-done.2.refs_3_), channel_id=1, source_target_pairs={{0,32},{32,64},{64,96},{96,128},{128,160},{160,192},{192,224},{224... | collective-permute-start | bytes 1290248 | tf_op jit(solution)/shard_map/ppermute | solution.py:48
  84.3 0.8 copy-start.8
  84.3 12.2 %collective-permute-start.7 = (bf16[256,512]{1,0:T(8,128)(2,1)S(1)}, bf16[256,512]{1,0:T(8,128)(2,1)}, u32[]{:S(2)}, u32[]{:S(2)}) collective-permute-start(bf16[256,512]{1,0:T(8,128)(2,1)S(1)} %bitcast.45), channel_id=1, source_target_pairs={{0,8},{8,0},{1,9},{9,1},{2,10},{10,2},{3,11},{11,3},{4,12},{12,4},... | collective-permute-start | bytes 786440 | tf_op jit(solution)/shard_map/ppermute | solution.py:43
  87.4 0.8 copy-start.9
  88.2 22.6 %collective-permute-start.9 = (bf16[256,512]{1,0:T(8,128)(2,1)}, bf16[256,512]{1,0:T(8,128)(2,1)}, u32[]{:S(2)}, u32[]{:S(2)}) collective-permute-start(bf16[256,512]{1,0:T(8,128)(2,1)} %copy-done.10), channel_id=1, source_target_pairs={{0,8},{8,0},{1,9},{9,1},{2,10},{10,2},{3,11},{11,3},{4,12},{12,4},... | collective-permute-start | bytes 786440 | tf_op jit(solution)/shard_map/ppermute | solution.py:43
  96.5 14.2 %copy-start.4 = (bf16[512,896]{1,0:T(8,128)(2,1)}, bf16[512,896]{1,0:T(8,128)(2,1)S(1)}, u32[]{:S(2)}) copy-start(bf16[512,896]{1,0:T(8,128)(2,1)S(1)} %collective-permute-done.13.refs_9_) | copy-start | bytes 2752516
  96.5 14.2 %copy-start.5 = (bf16[512,896]{1,0:T(8,128)(2,1)}, bf16[512,896]{1,0:T(8,128)(2,1)S(1)}, u32[]{:S(2)}) copy-start(bf16[512,896]{1,0:T(8,128)(2,1)S(1)} %collective-permute-done.14.refs_10_) | copy-start | bytes 2752516
  110.7 1.0 copy-start.6
  135.9 29.9 %all-to-all-start.3 = ((bf16[8,64,896]{2,1,0:T(8,128)(2,1)}), bf16[8,64,896]{2,1,0:T(8,128)(2,1)S(1)}, u32[]{:S(2)}, u32[]{:S(2)}) async-start(bf16[8,64,896]{2,1,0:T(8,128)(2,1)} %bitcast.47), calls=%async_computation.3 | async-start | bytes 1835008 | tf_op jit(solution)/shard_map/all_to_all | solution.py:34
  165.8 6.0 %copy-start = (bf16[8,64,896]{2,1,0:T(8,128)(2,1)}, bf16[8,64,896]{2,1,0:T(8,128)(2,1)S(1)}, u32[]{:S(2)}) copy-start(bf16[8,64,896]{2,1,0:T(8,128)(2,1)S(1)} %all-to-all-done.3.parts) | copy-start | bytes 2752516
  166.4 12.1 %all-to-all-start.6 = ((f32[32,1,16]{2,1,0:T(1,128)}), f32[32,1,16]{2,1,0:T(1,128)S(1)}, u32[]{:S(2)}, u32[]{:S(2)}) async-start(f32[32,1,16]{2,1,0:T(1,128)} %broadcast_in_dim.10), calls=%async_computation.6 | async-start | bytes 32768 | tf_op jit(solution)/shard_map/all_to_all | solution.py:34
  178.6 10.2 %all-to-all-start.4 = ((bf16[4,16,1664]{2,1,0:T(8,128)(2,1)}), bf16[4,16,1664]{2,1,0:T(8,128)(2,1)S(1)}, u32[]{:S(2)}, u32[]{:S(2)}) async-start(bf16[4,16,1664]{2,1,0:T(8,128)(2,1)} %tile.1), calls=%async_computation.4 | async-start | bytes 425984 | tf_op jit(solution)/shard_map/all_to_all | solution.py:34

commit v2 on v1

v2 whole, which is shorter than its diff:
```python
import functools

import jax
import jax.numpy as jnp
from jax import lax
from jax.experimental import pallas as pl
from jax.experimental.pallas import tpu as pltpu
from jax.sharding import Mesh
from jax.sharding import PartitionSpec as P

WIN_ROWS = 16
OUT = ("z", "xh", "c")
IN = ("y", "xl")
QUAD = ("xh", "c")
PLANE = ("xh", "c", "y", "xl")
BF = jnp.bfloat16
F32 = jnp.float32
LANES = 128
MIB = 2**20

VMEM_SPEC = pl.BlockSpec(memory_space=pltpu.VMEM)
SMEM_SPEC = pl.BlockSpec(memory_space=pltpu.SMEM)


def setup(mib, flops, nbytes):
    return {
        "compiler_params": pltpu.CompilerParams(vmem_limit_bytes=mib * MIB),
        "cost_estimate": pl.CostEstimate(flops=flops, bytes_accessed=nbytes, transcendentals=0),
    }


def dot(a, b, ca, cb):
    return lax.dot_general(a, b, (((ca,), (cb,)), ((), ())), preferred_element_type=F32)


def exchange(value, axis):
    return lax.all_to_all(value, axis, split_axis=0, concat_axis=0, tiled=True)


def swap(value, axis, mask=1):
    size = lax.axis_size(axis)
    return lax.ppermute(value, axis, [(i, i ^ mask) for i in range(size)])


def left_body(ids, u0, u1, u2, u3, basis, out):
    left = jnp.concatenate([u[0] for u in (u0, u1, u2, u3)], axis=0)
    n_in, rows, width = out.shape
    part = dot(left, basis[...], 1, 0).astype(BF)
    out[:, : rows - WIN_ROWS, :] = part.reshape(n_in, rows - WIN_ROWS, width)
    out[:, rows - WIN_ROWS :, :] = jnp.broadcast_to(
        basis[:WIN_ROWS, :][None], (n_in, WIN_ROWS, width)
    )


def left_part(query_ids, u_t, basis_out, n_in):
    queries = query_ids.shape[0]
    _, rank, depth = u_t.shape
    eigen = basis_out.shape[1]
    rows = queries * rank // n_in + WIN_ROWS
    tile = 256
    specs = [
        pl.BlockSpec((1, rank, depth), functools.partial(lambda q, n, ids: (ids[q], 0, 0), q))
        for q in range(queries)
    ]
    return pl.pallas_call(
        left_body,
        out_shape=jax.ShapeDtypeStruct((n_in, rows, eigen), BF),
        grid_spec=pltpu.PrefetchScalarGridSpec(
            num_scalar_prefetch=1,
            grid=(eigen // tile,),
            in_specs=[*specs, pl.BlockSpec((depth, tile), lambda n, ids: (0, n))],
            out_specs=pl.BlockSpec((n_in, rows, tile), lambda n, ids: (0, 0, n)),
        ),
        **setup(16, 2 * depth * eigen * rank * queries, 4 * MIB),
        name="left",
    )(query_ids, u_t, u_t, u_t, u_t, basis_out)


def left_sum_body(parts, out, window):
    n_in, rows, _ = parts.shape
    own = rows - WIN_ROWS
    total = parts[0, :own, :].astype(F32)
    for i in range(1, n_in):
        total += parts[i, :own, :].astype(F32)
    total = total.astype(BF)
    for i in range(n_in):
        out[i] = total
        window[i * WIN_ROWS : (i + 1) * WIN_ROWS, :] = parts[i, own:, :]


def left_sum(parts):
    n_in, rows, eigen = parts.shape
    return pl.pallas_call(
        left_sum_body,
        out_shape=(
            jax.ShapeDtypeStruct((n_in, rows - WIN_ROWS, eigen), BF),
            jax.ShapeDtypeStruct((n_in * WIN_ROWS, eigen), BF),
        ),
        in_specs=[VMEM_SPEC],
        out_specs=(VMEM_SPEC, VMEM_SPEC),
        **setup(4, 0, 2 * MIB),
        name="left_sum",
    )(parts)


def inverse_body(where, corrected, *outs):
    for r, out in enumerate(outs):
        half = where[3] ^ r
        skip = corrected.shape[1] - out.shape[1]
        at = pl.multiple_of(half * skip, LANES)
        out[...] = (1.0 / corrected[:, pl.ds(at, out.shape[1])]).astype(BF)


def inverse_halves(where, corrected, block, width, far):
    rows = corrected.shape[0]
    tile = 64
    return pl.pallas_call(
        inverse_body,
        out_shape=tuple(jax.ShapeDtypeStruct((rows, width), BF) for _ in range(2)),
        grid_spec=pltpu.PrefetchScalarGridSpec(
            num_scalar_prefetch=1,
            grid=(rows // tile,),
            in_specs=[pl.BlockSpec((tile, block), lambda n, w: (n, w[1] ^ far))],
            out_specs=tuple(pl.BlockSpec((tile, width), lambda n, w: (n, 0)) for _ in range(2)),
        ),
        **setup(8, 0, 12 * MIB),
        name="inverse",
    )(where, corrected)


def pack_body(where, train_ids, basis, tokens, delta, *outs):
    rows = basis.shape[1]
    train = train_ids.shape[0]
    for r, out in enumerate(outs):
        width = out.shape[1]
        block = basis.shape[2]
        skip = block - width
        blk, half = where[1] ^ (r // 2), where[3] ^ (r % 2)
        out[:rows, :] = basis[blk, :, pl.ds(pl.multiple_of(half * skip, LANES), width)]
        for b in range(train):
            row = train_ids[b]
            first = pl.multiple_of(blk * block, LANES)
            rest = pl.multiple_of(blk * block + width, LANES)
            out[rows + b : rows + b + 1, :] = tokens[row, :, pl.ds(first, width)]
            at = rows + train + b
            out[at : at + 1, :skip] = tokens[row, :, pl.ds(rest, skip)]
            out[at : at + 1, skip:] = delta[row]


def pack(where, train_ids, basis, tokens, delta, width):
    rows = basis.shape[1] + 2 * train_ids.shape[0]
    return pl.pallas_call(
        pack_body,
        out_shape=tuple(jax.ShapeDtypeStruct((rows, width), BF) for _ in range(4)),
        in_specs=[SMEM_SPEC, SMEM_SPEC, VMEM_SPEC, VMEM_SPEC, VMEM_SPEC],
        out_specs=tuple([VMEM_SPEC] * 4),
        **setup(4, 0, 2 * MIB),
        name="pack",
    )(where, train_ids, basis, tokens, delta)


def arrange_body(where, a0, a1, a2, a3, out, *, local, train):
    me = 2 * where[1] + where[3]
    rows = out.shape[0]
    each = local + 2 * train
    to = lax.broadcasted_iota(jnp.int32, (rows, each), 0)
    at = lax.broadcasted_iota(jnp.int32, (rows, each), 1)
    total = None
    for r, part in enumerate((a0, a1, a2, a3)):
        src = me ^ r
        head = src * local + at
        token = 4 * local + src * train + at - local
        other = 4 * local + 4 * train + src * train + at - local - train
        goal = jnp.where(at < local, head, jnp.where(at < local + train, token, other))
        term = dot(jnp.where(goal == to, 1.0, 0.0).astype(BF), part[...], 1, 0)
        total = term if total is None else total + term
    out[...] = total.astype(BF)


def arrange(where, parts, local, train):
    rows, width = parts[0].shape
    return pl.pallas_call(
        functools.partial(arrange_body, local=local, train=train),
        out_shape=jax.ShapeDtypeStruct((4 * rows, width), BF),
        in_specs=[SMEM_SPEC, *([VMEM_SPEC] * 4)],
        out_specs=VMEM_SPEC,
        **setup(8, 0, 2 * MIB),
        name="arrange",
    )(where, *parts)


def rotate_body(where, ids, v0, v1, v2, v3, gathered, basis, right, tokens, delta, *, n_z):
    each = gathered.shape[0] // n_z
    slab = basis.shape[0] // n_z
    extra = (each - slab) // 2
    for k in range(n_z):
        basis[k * slab : (k + 1) * slab, :] = gathered[k * each : k * each + slab, :]
    factors = jnp.concatenate([v[0] for v in (v0, v1, v2, v3)], axis=0)
    whole = basis[...]
    right[...] = dot(factors, whole, 1, 0).astype(BF)
    width = whole.shape[1]
    rest = whole.shape[0] - width
    head, tail = (
        jnp.concatenate(
            [gathered[k * each + a : k * each + a + extra, :] for k in range(n_z)], axis=0
        )
        for a in (slab, slab + extra)
    )
    rotated = dot(head, whole[:width, :], 1, 0) + dot(tail[:, :rest], whole[width:, :], 1, 0)
    tokens[...] = rotated.astype(BF)
    delta[...] = tail[:, rest:]


def rotate(where, query_ids, v_t, gathered, block, n_z):
    queries = query_ids.shape[0]
    rank = v_t.shape[1]
    rows, width = gathered.shape
    extra = (rows - block) // 2
    specs = [
        pl.BlockSpec(
            (1, rank, block), functools.partial(lambda q, n, w, ids: (ids[q], 0, w[1]), q)
        )
        for q in range(queries)
    ]

    def full(shape):
        return pl.BlockSpec(shape, lambda n, w, ids: (0, 0))

    shapes = (
        (block, width),
        (queries * rank, width),
        (extra, width),
        (extra, 2 * width - block),
    )
    return pl.pallas_call(
        functools.partial(rotate_body, n_z=n_z),
        out_shape=tuple(jax.ShapeDtypeStruct(s, BF) for s in shapes),
        grid_spec=pltpu.PrefetchScalarGridSpec(
            num_scalar_prefetch=2,
            grid=(1,),
            in_specs=[*specs, full((rows, width))],
            out_specs=tuple(full(s) for s in shapes),
        ),
        **setup(32, 2 * block * width * (queries * rank + extra), 8 * MIB),
        name="rotate",
    )(where, query_ids, v_t, v_t, v_t, v_t, gathered)


def back_body(where, factors, right, tokens, delta, *refs, queries, train):
    lefts, windows, inverses, out = refs[:4], refs[4:8], refs[8:12], refs[12]
    n_z, rows, width = out.shape
    win = windows[0].shape[0]
    per = win // n_z
    rank = right.shape[0] // queries
    valid = factors.shape[1] // 2
    skip = factors.shape[1] - width
    row = factors[pl.ds(where[2], 1), pl.ds(pl.multiple_of(where[3] * skip, LANES), width)]
    lane = lax.broadcasted_iota(jnp.int32, (1, width), 1)
    first = where[3] * (width - valid)
    mine = jnp.logical_and(lane >= first, lane < first + valid)
    scale = jnp.where(mine, 1.0 / row, 0.0)
    which = lax.rem(
        lax.broadcasted_iota(jnp.int32, (tokens.shape[0], 1), 0), train
    )
    scores = []
    for q in range(queries):
        at = slice(q * rank, (q + 1) * rank)
        total = None
        for left, window, inverse in zip(lefts, windows, inverses):
            product = dot(left[at, :], right[at, :], 0, 0)
            precond = (product * inverse[...].astype(F32)).astype(BF)
            term = dot(window[...], precond, 1, 0)
            total = term if total is None else total + term
        total = (total * scale).astype(BF)
        out[:, q * per : (q + 1) * per, :] = total.reshape(n_z, per, width)
        projected = dot(tokens[...], total, 1, 1) * delta[...].astype(F32)
        scores += [
            jnp.sum(jnp.where(which == b, projected, 0.0), axis=0, keepdims=True)
            for b in range(train)
        ]
    words = []
    for k in range(0, queries * train, 8):
        group = jnp.concatenate(scores[k : k + 8], axis=0)
        high = group.astype(BF)
        words += [high, (group - high.astype(F32)).astype(BF)]
    words.append(jnp.zeros((8, width - len(words) * win), BF))
    extra = jnp.concatenate(words, axis=1)
    for k in range(n_z):
        out[k, queries * per :, :] = extra


def back(where, factors, right, tokens, delta, lefts, windows, inverses, n_z, queries, train):
    width = right.shape[1]
    win, depth = windows[0].shape
    return pl.pallas_call(
        functools.partial(back_body, queries=queries, train=train),
        out_shape=jax.ShapeDtypeStruct((n_z, queries * win // n_z + 8, width), BF),
        in_specs=[SMEM_SPEC, *([VMEM_SPEC] * (4 + 12))],
        out_specs=VMEM_SPEC,
        **setup(32, 16 * depth * width * queries * win, 8 * MIB),
        name="back",
    )(where, factors, right, tokens, delta, *lefts, *windows, *inverses)


def tile_body(where, parts, basis, t0, t1, t2, t3, score, *, queries, train):
    n_z = parts.shape[0]
    me = 2 * where[1] + where[3]
    own = t0.shape[0]
    rows = 4 * own
    per = own // queries
    total = parts[0].astype(F32)
    for k in range(1, n_z):
        total += parts[k].astype(F32)
    to = lax.broadcasted_iota(jnp.int32, (rows, rows), 0)
    at = lax.broadcasted_iota(jnp.int32, (rows, rows), 1)
    query = at // own
    owner = lax.rem(at // per, 4)
    goal = (owner ^ me) * own + query * per + lax.rem(at, per)
    select = jnp.where(goal == to, 1.0, 0.0).astype(BF)
    half = dot(select, total[:rows].astype(BF), 1, 0).astype(BF)
    tiles = dot(half, basis[...], 1, 1).astype(BF)
    for r, out in enumerate((t0, t1, t2, t3)):
        out[...] = tiles[r * own : (r + 1) * own]
    words = total[rows:]
    line = lax.broadcasted_iota(jnp.int32, (8, LANES), 0)
    lane = lax.broadcasted_iota(jnp.int32, (8, LANES), 1)
    table = jnp.zeros((8, LANES), F32)
    for k in range(queries * train // 8):
        at = 2 * k * LANES
        sums = words[:, at : at + LANES] + words[:, at + LANES : at + 2 * LANES]
        sums = jnp.sum(sums, axis=1, keepdims=True)
        for i in range(8):
            q, b = divmod(8 * k + i, train)
            table = jnp.where(jnp.logical_and(line == q, lane == b), sums[i : i + 1], table)
    score[...] = jnp.broadcast_to(table[None], score.shape)


def tile_part(where, parts, basis, plane, queries, train):
    own = (parts.shape[1] - 8) // 4
    block = basis.shape[0]
    return pl.pallas_call(
        functools.partial(tile_body, queries=queries, train=train),
        out_shape=(
            *(jax.ShapeDtypeStruct((own, block), BF) for _ in range(4)),
            jax.ShapeDtypeStruct((plane, 8, LANES), F32),
        ),
        in_specs=[SMEM_SPEC, VMEM_SPEC, VMEM_SPEC],
        out_specs=tuple([VMEM_SPEC] * 5),
        **setup(24, 8 * own * block * basis.shape[1], 5 * MIB),
        name="tile",
    )(where, parts, basis)


def final_body(where, t0, t1, t2, t3, score, tiles, scores):
    queries, per, columns = tiles.shape
    block = columns // 2
    for r, (a, b) in enumerate(((t0, t1), (t2, t3))):
        total = (a[...].astype(F32) + b[...].astype(F32)).astype(BF)
        at = pl.multiple_of((where[1] ^ r) * block, LANES)
        for q in range(queries):
            tiles[q, :, pl.ds(at, block)] = total[q * per : (q + 1) * per]
    scores[...] = jnp.sum(score[...], axis=0)[: scores.shape[0], : scores.shape[1]]


def final(where, parts, score, queries, train):
    own, block = parts[0].shape
    return pl.pallas_call(
        final_body,
        out_shape=(
            jax.ShapeDtypeStruct((queries, own // queries, 2 * block), BF),
            jax.ShapeDtypeStruct((queries, train), F32),
        ),
        in_specs=[SMEM_SPEC, *([VMEM_SPEC] * 5)],
        out_specs=(VMEM_SPEC, VMEM_SPEC),
        **setup(4, 0, 1 * MIB),
        name="final",
    )(where, *parts, score)


def shards(
    basis_out,
    corrected,
    factor_table,
    block_ids,
    basis_in,
    query_ids,
    u_pool,
    v_pool,
    train_ids,
    x_pool,
    delta_pool,
):
    n_z, n_in = lax.axis_size("z"), lax.axis_size(IN)
    xh, c = lax.axis_index("xh"), lax.axis_index("c")
    in_pos = lax.axis_index(IN)
    queries, train = query_ids.shape[0], train_ids.shape[0]
    _, local_rows, block = basis_in.shape
    width = -(-(block // 2) // LANES) * LANES
    block_id = lax.dynamic_index_in_dim(block_ids, in_pos * 2 + xh, keepdims=False)
    where = jnp.stack([in_pos, xh, block_id, c]).astype(jnp.int32)

    packed = pack(where, train_ids, basis_in, x_pool, delta_pool, width)
    parts = (
        packed[0],
        swap(packed[1], "c"),
        swap(packed[2], "xh"),
        swap(packed[3], QUAD, 3),
    )
    own = arrange(where, parts, local_rows, train)
    gathered = lax.all_gather(own, "z", axis=0, tiled=True)

    far = inverse_halves(where, corrected, block, width, 1)
    near = inverse_halves(where, corrected, block, width, 0)
    inverses = (near[0], swap(near[1], "c"), swap(far[0], "xh"), swap(far[1], QUAD, 3))
    left_ids, _ = lax.optimization_barrier((query_ids, far[0]))

    parts = left_part(left_ids, jnp.transpose(u_pool, (0, 2, 1)), basis_out, n_in)
    spread, window = left_sum(exchange(parts, IN))
    left = exchange(spread, IN).reshape(-1, basis_out.shape[1])
    left_x, window_x = swap(left, "xh"), swap(window, "xh")
    lefts = (left, swap(left, "c"), left_x, swap(left_x, "c"))
    windows = (window, swap(window, "c"), window_x, swap(window_x, "c"))

    basis, right, tokens, delta = rotate(
        where, query_ids, jnp.transpose(v_pool, (0, 2, 1)), gathered, block, n_z
    )
    parts = back(
        where,
        factor_table,
        right,
        tokens,
        delta,
        lefts,
        windows,
        inverses,
        n_z,
        queries,
        train,
    )
    *parts, score = tile_part(
        where, exchange(parts, "z"), basis, lax.axis_size(PLANE), queries, train
    )
    parts = (
        parts[0],
        swap(parts[1], "c"),
        swap(parts[2], "xh"),
        swap(parts[3], QUAD, 3),
    )
    return final(where, parts, exchange(score, PLANE), queries, train)


def solution(mesh):
    split = Mesh(mesh.devices.reshape(8, 2, 2, 4, 2), ("z", "xh", "c", "y", "xl"))
    return jax.shard_map(
        shards,
        mesh=split,
        in_specs=(
            P(IN, OUT),
            P(OUT, IN),
            P(),
            P(),
            P(IN, OUT, None),
            P(),
            P(None, IN, None),
            P(None, IN, None),
            P(),
            P(None, OUT, IN),
            P(None, OUT, None),
        ),
        out_specs=(P(None, OUT, IN), P()),
        check_vma=False,
    )
```

time: 190 us -> 185 us (0.974)
  waiting for transfers between devices: 69.8 us -> 48.6 us
  between operations: 0.91 us -> 14.2 us
  blocking collectives: 26.9 us -> 36.9 us
  local copies, waits for them, and re-layouts: 9.11 us -> 15.3 us
  Pallas kernels: 34.1 us -> 28.2 us
  starting transfers between devices: 44.7 us -> 40.1 us
  other arithmetic: 3.02 us -> 0.71 us
    all_to_all x5 -> x3, waiting for transfers between devices: 42.4 us -> 0.01 us  [exchange(): return lax.all_to_all(value, axis, split_axis=0, concat_axis=0, tiled=True)]
    ppermute x9 -> x15, waiting for transfers between devices: 14.2 us -> 48.6 us  [swap(): return lax.ppermute(value, axis, [(i, i ^ mask) for i in range(size)])]
    ppermute x7 -> x0, waiting for transfers between devices: 13.2 us -> none  [shift(): lax.ppermute(value, 'z', [(i, (i + step) % size) for i in range(size)])]
    ppermute x7 -> x0, starting transfers between devices: 12.9 us -> none  [shift(): lax.ppermute(value, 'z', [(i, (i + step) % size) for i in range(size)])]
    ppermute x9 -> x15, starting transfers between devices: 11.3 us -> 23.7 us  [swap(): return lax.ppermute(value, axis, [(i, i ^ mask) for i in range(size)])]
    all_to_all x2 -> x1, blocking collectives: 26.9 us -> 36.9 us  [exchange(): return lax.all_to_all(value, axis, split_axis=0, concat_axis=0, tiled=True)]
    unnamed x36 -> x41, local copies, waits for them, and re-layouts: 4.3 us -> 14.1 us
    all_to_all x5 -> x3, starting transfers between devices: 20.5 us -> 16.3 us  [exchange(): return lax.all_to_all(value, axis, split_axis=0, concat_axis=0, tiled=True)]
  transfers between devices with their start and end apart: 21 -> 19, of which waited for: 9 -> 7; matrix products, arithmetic and copies ran while one was open for 2% -> 0% of each run, Pallas kernels for 12% -> 7%
where the time goes in v2:
time: 185 us; the launch traced here: 184 us
  waiting for transfers between devices  48.6 us (26%)
  starting transfers between devices  40.1 us (22%)
  blocking collectives  36.9 us (20%)
  Pallas kernels  28.2 us (15%)
  local copies, waits for them, and re-layouts  15.3 us (8%)
  between operations  14.2 us (8%)
    ppermute x15, waiting for transfers between devices, swap(): return lax.ppermute(value, axis, [(i, i ^ mask) for i in range(size)])  48.6 us
    all_to_all x1, blocking collectives, exchange(): return lax.all_to_all(value, axis, split_axis=0, concat_axis=0, tiled=True)  36.9 us
    ppermute x15, starting transfers between devices, swap(): return lax.ppermute(value, axis, [(i, i ^ mask) for i in range(size)])  23.7 us
    all_to_all x3, starting transfers between devices, exchange(): return lax.all_to_all(value, axis, split_axis=0, concat_axis=0, tiled=True)  16.3 us
    unnamed x41, local copies, waits for them, and re-layouts  14.1 us
    pallas_call x1, Pallas kernels, back(): pl.pallas_call(functools.partial(back_body, queries=queries, train=train)...  9.39 us
    pallas_call x2, Pallas kernels, inverse_halves(): pl.pallas_call(inverse_body, out_shape=tuple((jax.ShapeDtypeStruct((rows,...  7.33 us
  transfers between devices with their start and end apart: 19, of which 7 were waited for; matrix products, arithmetic and copies ran while one was open for 0% of the time, Pallas kernels for 7%

profile of v2, /device:TPU:1, one launch (start us, length us, event | category | flops | bytes accessed | tf_op | source)
XLA Modules:
  0.0 184.0 jit_solution(8900850506258878907)
XLA Ops:
  7.2 0.0 all-gather.2.cloned.1.call-start
  7.2 0.7 copy.15.delta
  7.9 0.9 copy.14.tokens
  8.8 1.0 copy.13.basis
  9.8 1.3 dynamic_slice.4
  11.1 0.7 pad_add_fusion.where
  11.8 0.7 copy-done.7
  12.5 0.7 pack.1
  13.1 3.3 %collective-permute-start = (bf16[60,896]{1,0:T(8,128)(2,1)S(1)}, bf16[60,896]{1,0:T(8,128)(2,1)S(1)}, u32[]{:S(2)}, u32[]{:S(2)}) collective-permute-start(bf16[60,896]{1,0:T(8,128)(2,1)S(1)} %get-tuple-element.23), channel_id=1, source_target_pairs={{0,8},{8,0},{1,9},{9,1},{2,10},{10,2},{3,11},{11,3},{4,12},{12,4},... | collective-permute-start | bytes 322568 | tf_op jit(solution)/shard_map/ppermute | solution.py:42
  16.5 1.0 collective-permute-start.1
  17.5 2.2 %collective-permute-start.2 = (bf16[60,896]{1,0:T(8,128)(2,1)S(1)}, bf16[60,896]{1,0:T(8,128)(2,1)S(1)}, u32[]{:S(2)}, u32[]{:S(2)}) collective-permute-start(bf16[60,896]{1,0:T(8,128)(2,1)S(1)} %get-tuple-element.25), channel_id=1, source_target_pairs={{0,24},{8,16},{16,8},{24,0},{1,25},{9,17},{17,9},{25,1},{2,26},{10... | collective-permute-start | bytes 322568 | tf_op jit(solution)/shard_map/ppermute | solution.py:42
  19.7 0.0 collective-permute-done.a1
  19.7 3.0 %collective-permute-done.1.a2 = bf16[60,896]{1,0:T(8,128)(2,1)S(1)} collective-permute-done((bf16[60,896]{1,0:T(8,128)(2,1)S(1)}, bf16[60,896]{1,0:T(8,128)(2,1)S(1)}, u32[]{:S(2)}, u32[]{:S(2)}) %collective-permute-start.1) | collective-permute-done | bytes 107552 | tf_op jit(solution)/shard_map/ppermute | solution.py:42
  22.7 2.6 %collective-permute-done.2.a3 = bf16[60,896]{1,0:T(8,128)(2,1)S(1)} collective-permute-done((bf16[60,896]{1,0:T(8,128)(2,1)S(1)}, bf16[60,896]{1,0:T(8,128)(2,1)S(1)}, u32[]{:S(2)}, u32[]{:S(2)}) %collective-permute-start.2) | collective-permute-done | bytes 107552 | tf_op jit(solution)/shard_map/ppermute | solution.py:42
  25.3 2.0 %arrange.1 = bf16[240,896]{1,0:T(8,128)(2,1)} custom-call(s32[4]{0:T(128)S(1)} %pad_add_fusion.where, bf16[60,896]{1,0:T(8,128)(2,1)S(1)} %get-tuple-element.22.a0, bf16[60,896]{1,0:T(8,128)(2,1)S(1)} %collective-permute-done.a1, bf16[60,896]{1,0:T(8,128)(2,1)S(1)} %collective-permute-done.1.a2, bf16[60,896]{1,0:T(8,128)(2,1)S(1)} %collective-permute-done.2.a3), custom_call_target="tpu_custom_call" | custom-call | bytes 2097152 | tf_op jit(solution)/shard_map/arrange/pallas_call | solution.py:182
  27.3 0.0 all-gather.2.cloned.1.call-update
  27.3 0.0 copy-start.1
  27.3 2.9 %copy-done.1 = f32[512,3328]{1,0:T(8,128)S(1)} copy-done((f32[512,3328]{1,0:T(8,128)S(1)}, f32[512,3328]{1,0:T(8,128)}, u32[]{:S(2)}) %copy-start.1) | copy-done | bytes 6815768
  30.2 3.8 %inverse.2 = (bf16[512,896]{1,0:T(8,128)(2,1)}, bf16[512,896]{1,0:T(8,128)(2,1)}) custom-call(s32[4]{0:T(128)S(1)} %pad_add_fusion.where, f32[512,3328]{1,0:T(8,128)S(1)} %copy-done.1), custom_call_target="tpu_custom_call" | custom-call | bytes 12582912 | tf_op jit(solution)/shard_map/inverse/pallas_call | solution.py:117
  34.0 2.3 %left.1 = bf16[8,48,512]{2,1,0:T(8,128)(2,1)} custom-call(s32[4]{0:T(128)S(1)} %copy-done.6, bf16[6,64,2048]{2,1,0:T(8,128)(2,1)S(1)} %bitcast.10, bf16[6,64,2048]{2,1,0:T(8,128)(2,1)S(1)} %bitcast.11, bf16[6,64,2048]{2,1,0:T(8,128)(2,1)S(1)} %bitcast.12, bf16[6,64,2048]{2,1,0:T(8,128)(2,1)S(1)} %bitcast.13, bf16[2048,512]{1,0:T(8,128)(2,1)S(1)} %copy-done.5), custom_call_target="tpu_custom_call" | custom-call | flops 536870912 | bytes 4194304 | tf_op jit(solution)/shard_map/left/pallas_call | solution.py:65
  36.4 3.5 %all-to-all-start = ((bf16[8,48,512]{2,1,0:T(8,128)(2,1)}), bf16[8,48,512]{2,1,0:T(8,128)(2,1)S(1)}, u32[]{:S(2)}, u32[]{:S(2)}) async-start(bf16[8,48,512]{2,1,0:T(8,128)(2,1)} %left.1), calls=%async_computation | async-start | bytes 786432 | tf_op jit(solution)/shard_map/all_to_all | solution.py:37
  39.8 0.0 copy-start.2
  39.8 2.9 %copy-done.2 = f32[512,3328]{1,0:T(8,128)S(1)} copy-done((f32[512,3328]{1,0:T(8,128)S(1)}, f32[512,3328]{1,0:T(8,128)}, u32[]{:S(2)}) %copy-start.2) | copy-done | bytes 6815768
  42.8 3.6 %inverse.3 = (bf16[512,896]{1,0:T(8,128)(2,1)S(1)}, bf16[512,896]{1,0:T(8,128)(2,1)}) custom-call(s32[4]{0:T(128)S(1)} %pad_add_fusion.where, f32[512,3328]{1,0:T(8,128)S(1)} %copy-done.2), custom_call_target="tpu_custom_call" | custom-call | bytes 12582912 | tf_op jit(solution)/shard_map/inverse/pallas_call | solution.py:117
  46.3 1.0 copy-done.8
  47.3 0.6 collective-permute-start.9
  47.9 2.2 %collective-permute-start.11 = (bf16[512,896]{1,0:T(8,128)(2,1)}, bf16[512,896]{1,0:T(8,128)(2,1)}, u32[]{:S(2)}, u32[]{:S(2)}) collective-permute-start(bf16[512,896]{1,0:T(8,128)(2,1)} %get-tuple-element.35), channel_id=1, source_target_pairs={{0,24},{8,16},{16,8},{24,0},{1,25},{9,17},{17,9},{25,1},{2,26},{10... | collective-permute-start | bytes 2752520 | tf_op jit(solution)/shard_map/ppermute | solution.py:42
  50.2 0.6 collective-permute-start.10
  50.8 0.0 all-to-all-done.parts
  50.8 0.8 left_sum.1
  51.5 5.4 %all-to-all-start.1 = ((bf16[8,32,512]{2,1,0:T(8,128)(2,1)}), bf16[8,32,512]{2,1,0:T(8,128)(2,1)S(1)}, u32[]{:S(2)}, u32[]{:S(2)}) async-start(bf16[8,32,512]{2,1,0:T(8,128)(2,1)} %get-tuple-element.31), calls=%async_computation.1 | async-start | bytes 524288 | tf_op jit(solution)/shard_map/all_to_all | solution.py:37
  57.0 2.3 %collective-permute-start.7 = (bf16[128,512]{1,0:T(8,128)(2,1)S(1)}, bf16[128,512]{1,0:T(8,128)(2,1)S(1)}, u32[]{:S(2)}, u32[]{:S(2)}) collective-permute-start(bf16[128,512]{1,0:T(8,128)(2,1)S(1)} %get-tuple-element.32.refs_4_), channel_id=1, source_target_pairs={{0,16},{16,0},{1,17},{17,1},{2,18},{18,2},{3,19},{19,3},{4,20},{20... | collective-permute-start | bytes 393224 | tf_op jit(solution)/shard_map/ppermute | solution.py:42
  59.2 1.3 collective-permute-start.6
  60.6 35.9 %collective-permute-done.7.refs_6_ = bf16[128,512]{1,0:T(8,128)(2,1)S(1)} collective-permute-done((bf16[128,512]{1,0:T(8,128)(2,1)S(1)}, bf16[128,512]{1,0:T(8,128)(2,1)S(1)}, u32[]{:S(2)}, u32[]{:S(2)}) %collective-permute-start.7) | collective-permute-done | bytes 131104 | tf_op jit(solution)/shard_map/ppermute | solution.py:42
  96.5 0.0 all-to-all-done.1
  96.5 2.4 %collective-permute-start.4 = (bf16[256,512]{1,0:T(8,128)(2,1)S(1)}, bf16[256,512]{1,0:T(8,128)(2,1)S(1)}, u32[]{:S(2)}, u32[]{:S(2)}) collective-permute-start(bf16[256,512]{1,0:T(8,128)(2,1)S(1)} %bitcast.14), channel_id=1, source_target_pairs={{0,16},{16,0},{1,17},{17,1},{2,18},{18,2},{3,19},{19,3},{4,20},{20... | collective-permute-start | bytes 786440 | tf_op jit(solution)/shard_map/ppermute | solution.py:42
  98.9 0.0 collective-permute-done.6.refs_5_
  99.0 0.6 copy-done.15
  99.6 1.3 collective-permute-start.8
  100.9 0.6 copy-done.13
  101.5 0.3 collective-permute-done.8.refs_7_
  101.8 0.6 copy-done.17
  102.5 0.4 collective-permute-start.3
  102.8 1.6 collective-permute-done.4.refs_2_
  104.4 2.3 %collective-permute-start.5 = (bf16[256,512]{1,0:T(8,128)(2,1)S(1)}, bf16[256,512]{1,0:T(8,128)(2,1)}, u32[]{:S(2)}, u32[]{:S(2)}) collective-permute-start(bf16[256,512]{1,0:T(8,128)(2,1)S(1)} %collective-permute-done.4.refs_2_), channel_id=1, source_target_pairs={{0,8},{8,0},{1,9},{9,1},{2,10},{10,2},{3,11},{11,3},{4,12},{12,4},... | collective-permute-start | bytes 786440 | tf_op jit(solution)/shard_map/ppermute | solution.py:42
  106.8 2.0 %copy-done.4 = bf16[1920,896]{1,0:T(8,128)(2,1)S(1)} copy-done((bf16[1920,896]{1,0:T(8,128)(2,1)S(1)}, bf16[1920,896]{1,0:T(8,128)(2,1)}, u32[]{:S(2)}) %copy-start.4) | copy-done | bytes 3440664
  108.8 2.2 %rotate.1 = (bf16[1664,896]{1,0:T(8,128)(2,1)S(1)}, bf16[256,896]{1,0:T(8,128)(2,1)S(1)}, bf16[128,896]{1,0:T(8,128)(2,1)S(1)}, bf16[128,128]{1,0:T(8,128)(2,1)S(1)}) custom-call(s32[4]{0:T(128)S(1)} %pad_add_fusion.where, s32[4]{0:T(128)S(1)} %copy-done.6, bf16[6,64,3328]{2,1,0:T(8,128)(2,1)S(1)} %bitcast.6, bf16[6,64,3328]{2,1,0:T(8,128)(2,1)S(1)} %bitcast.7, ...), custom_call_target="tpu_custom_call" | custom-call | flops 1145044992 | bytes 8388608 | tf_op jit(solution)/shard_map/rotate/pallas_call | solution.py:235
  111.0 0.0 collective-permute-done.3.refs_1_
  111.0 0.0 collective-permute-done.9.refs_9_
  111.0 0.0 collective-permute-done.11.refs_11_
  111.0 0.0 collective-permute-done.10.refs_10_
  111.0 0.0 collective-permute-done.5.refs_3_
  111.1 9.4 %back.1 = bf16[8,72,896]{2,1,0:T(8,128)(2,1)S(1)} custom-call(s32[4]{0:T(128)S(1)} %pad_add_fusion.where, f32[32,1664]{1,0:T(8,128)S(1)} %copy-done.10, bf16[256,896]{1,0:T(8,128)(2,1)S(1)} %get-tuple-element.26.right, bf16[128,896]{1,0:T(8,128)(2,1)S(1)} %get-tuple-element.27.tokens, bf16[128,128]{1,0:T(8,128)(2,1)S(1)} %get-tuple-element.28.delta, ...), custom_call_target="tpu_custom_call" | custom-call | flops 3758096384 | bytes 8388608 | tf_op jit(solution)/shard_map/back/pallas_call | solution.py:295
  120.5 36.9 %all_to_all.20.parts = bf16[8,72,896]{2,1,0:T(8,128)(2,1)S(1)} all-to-all(bf16[8,72,896]{2,1,0:T(8,128)(2,1)S(1)} %back.1), channel_id=1, replica_groups=mesh['z'=8,'xh'=2,'c'=2,'y'=4,'xl'=2] {'z'}, dimensions={0} | all-to-all | bytes 2064384 | tf_op jit(solution)/shard_map/all_to_all | solution.py:37
  157.4 2.3 %tile.1 = (bf16[16,1664]{1,0:T(8,128)(2,1)S(1)}, bf16[16,1664]{1,0:T(8,128)(2,1)S(1)}, bf16[16,1664]{1,0:T(8,128)(2,1)S(1)}, bf16[16,1664]{1,0:T(8,128)(2,1)S(1)}, f32[32,8,128]{2,1,0:T(8,128)}) custom-call(s32[4]{0:T(128)S(1)} %pad_add_fusion.where, bf16[8,72,896]{2,1,0:T(8,128)(2,1)S(1)} %all_to_all.20.parts, bf16[1664,896]{1,0:T(8,128)(2,1)S(1)} %get-tuple-element.36.basis), custom_call_target="tpu_custom_call" | custom-call | flops 190840832 | bytes 5242880 | tf_op jit(solution)/shard_map/tile/pallas_call | solution.py:341
  159.7 7.4 %all-to-all-start.3 = ((f32[32,8,128]{2,1,0:T(8,128)}), f32[32,8,128]{2,1,0:T(8,128)S(1)}, u32[]{:S(2)}, u32[]{:S(2)}) async-start(f32[32,8,128]{2,1,0:T(8,128)} %get-tuple-element.41), calls=%async_computation.3 | async-start | bytes 262144 | tf_op jit(solution)/shard_map/all_to_all | solution.py:37
  167.1 0.3 collective-permute-start.12
  167.4 3.0 %collective-permute-start.13 = (bf16[16,1664]{1,0:T(8,128)(2,1)S(1)}, bf16[16,1664]{1,0:T(8,128)(2,1)S(1)}, u32[]{:S(2)}, u32[]{:S(2)}) collective-permute-start(bf16[16,1664]{1,0:T(8,128)(2,1)S(1)} %get-tuple-element.39), channel_id=1, source_target_pairs={{0,16},{16,0},{1,17},{17,1},{2,18},{18,2},{3,19},{19,3},{4,20},{20... | collective-permute-start | bytes 159752 | tf_op jit(solution)/shard_map/ppermute | solution.py:42
  170.5 0.4 collective-permute-start.14
  170.8 0.0 collective-permute-done.12.t1
  170.8 2.6 %collective-permute-done.13.t2 = bf16[16,1664]{1,0:T(8,128)(2,1)S(1)} collective-permute-done((bf16[16,1664]{1,0:T(8,128)(2,1)S(1)}, bf16[16,1664]{1,0:T(8,128)(2,1)S(1)}, u32[]{:S(2)}, u32[]{:S(2)}) %collective-permute-start.13) | collective-permute-done | bytes 53280 | tf_op jit(solution)/shard_map/ppermute | solution.py:42
  173.5 2.5 %collective-permute-done.14.t3 = bf16[16,1664]{1,0:T(8,128)(2,1)S(1)} collective-permute-done((bf16[16,1664]{1,0:T(8,128)(2,1)S(1)}, bf16[16,1664]{1,0:T(8,128)(2,1)S(1)}, u32[]{:S(2)}, u32[]{:S(2)}) %collective-permute-start.14) | collective-permute-done | bytes 53280 | tf_op jit(solution)/shard_map/ppermute | solution.py:42
  175.9 0.0 all-to-all-done.3.score
  175.9 1.2 final.1
  (29 shorter events, 0.1 us)
Async XLA Ops:
  7.2 99.6 %all-gather.2.cloned.1.call-start = ((), (), s32[]{:S(2)}) async-start(), calls=%async_computation.4 | async-start | bytes 3870720 | tf_op jit(solution)/shard_map/all_gather | solution.py:410
  11.8 0.7 copy-start.7
  13.1 6.6 %collective-permute-start = (bf16[60,896]{1,0:T(8,128)(2,1)S(1)}, bf16[60,896]{1,0:T(8,128)(2,1)S(1)}, u32[]{:S(2)}, u32[]{:S(2)}) collective-permute-start(bf16[60,896]{1,0:T(8,128)(2,1)S(1)} %get-tuple-element.23), channel_id=1, source_target_pairs={{0,8},{8,0},{1,9},{9,1},{2,10},{10,2},{3,11},{11,3},{4,12},{12,4},... | collective-permute-start | bytes 322568 | tf_op jit(solution)/shard_map/ppermute | solution.py:42
  16.5 6.2 %collective-permute-start.1 = (bf16[60,896]{1,0:T(8,128)(2,1)S(1)}, bf16[60,896]{1,0:T(8,128)(2,1)S(1)}, u32[]{:S(2)}, u32[]{:S(2)}) collective-permute-start(bf16[60,896]{1,0:T(8,128)(2,1)S(1)} %get-tuple-element.24), channel_id=1, source_target_pairs={{0,16},{16,0},{1,17},{17,1},{2,18},{18,2},{3,19},{19,3},{4,20},{20... | collective-permute-start | bytes 322568 | tf_op jit(solution)/shard_map/ppermute | solution.py:42
  17.5 7.8 %collective-permute-start.2 = (bf16[60,896]{1,0:T(8,128)(2,1)S(1)}, bf16[60,896]{1,0:T(8,128)(2,1)S(1)}, u32[]{:S(2)}, u32[]{:S(2)}) collective-permute-start(bf16[60,896]{1,0:T(8,128)(2,1)S(1)} %get-tuple-element.25), channel_id=1, source_target_pairs={{0,24},{8,16},{16,8},{24,0},{1,25},{9,17},{17,9},{25,1},{2,26},{10... | collective-permute-start | bytes 322568 | tf_op jit(solution)/shard_map/ppermute | solution.py:42
  27.3 2.9 %copy-start.1 = (f32[512,3328]{1,0:T(8,128)S(1)}, f32[512,3328]{1,0:T(8,128)}, u32[]{:S(2)}) copy-start(f32[512,3328]{1,0:T(8,128)} %corrected.3) | copy-start | bytes 20447236
  30.2 3.8 %copy-start.3 = (bf16[6,2048,64]{1,2,0:T(8,128)(2,1)S(1)}, bf16[6,2048,64]{1,2,0:T(8,128)(2,1)}, u32[]{:S(2)}) copy-start(bf16[6,2048,64]{1,2,0:T(8,128)(2,1)} %param.17) | copy-start | bytes 4718596
  30.2 3.8 %copy-start.5 = (bf16[2048,512]{1,0:T(8,128)(2,1)S(1)}, bf16[2048,512]{1,0:T(8,128)(2,1)}, u32[]{:S(2)}) copy-start(bf16[2048,512]{1,0:T(8,128)(2,1)} %basis.2) | copy-start | bytes 6291460
  30.2 3.8 %copy-start.6 = (s32[4]{0:T(128)S(1)}, s32[4]{0:T(128)}, u32[]{:S(2)}) copy-start(s32[4]{0:T(128)} %ids.2) | copy-start | bytes 52
  36.4 14.4 %all-to-all-start = ((bf16[8,48,512]{2,1,0:T(8,128)(2,1)}), bf16[8,48,512]{2,1,0:T(8,128)(2,1)S(1)}, u32[]{:S(2)}, u32[]{:S(2)}) async-start(bf16[8,48,512]{2,1,0:T(8,128)(2,1)} %left.1), calls=%async_computation | async-start | bytes 786432 | tf_op jit(solution)/shard_map/all_to_all | solution.py:37
  39.8 2.9 %copy-start.2 = (f32[512,3328]{1,0:T(8,128)S(1)}, f32[512,3328]{1,0:T(8,128)}, u32[]{:S(2)}) copy-start(f32[512,3328]{1,0:T(8,128)} %corrected.3) | copy-start | bytes 20447236
  42.8 64.0 %copy-start = (bf16[6,3328,64]{1,2,0:T(8,128)(2,1)S(1)}, bf16[6,3328,64]{1,2,0:T(8,128)(2,1)}, u32[]{:S(2)}) copy-start(bf16[6,3328,64]{1,2,0:T(8,128)(2,1)} %param.18) | copy-start | bytes 7667716
  46.3 1.0 copy-start.8
  47.3 63.7 %collective-permute-start.9 = (bf16[512,896]{1,0:T(8,128)(2,1)}, bf16[512,896]{1,0:T(8,128)(2,1)}, u32[]{:S(2)}, u32[]{:S(2)}) collective-permute-start(bf16[512,896]{1,0:T(8,128)(2,1)} %get-tuple-element.34), channel_id=1, source_target_pairs={{0,8},{8,0},{1,9},{9,1},{2,10},{10,2},{3,11},{11,3},{4,12},{12,4},... | collective-permute-start | bytes 2752520 | tf_op jit(solution)/shard_map/ppermute | solution.py:42
  47.9 63.1 %collective-permute-start.11 = (bf16[512,896]{1,0:T(8,128)(2,1)}, bf16[512,896]{1,0:T(8,128)(2,1)}, u32[]{:S(2)}, u32[]{:S(2)}) collective-permute-start(bf16[512,896]{1,0:T(8,128)(2,1)} %get-tuple-element.35), channel_id=1, source_target_pairs={{0,24},{8,16},{16,8},{24,0},{1,25},{9,17},{17,9},{25,1},{2,26},{10... | collective-permute-start | bytes 2752520 | tf_op jit(solution)/shard_map/ppermute | solution.py:42
  50.2 60.9 %collective-permute-start.10 = (bf16[512,896]{1,0:T(8,128)(2,1)}, bf16[512,896]{1,0:T(8,128)(2,1)}, u32[]{:S(2)}, u32[]{:S(2)}) collective-permute-start(bf16[512,896]{1,0:T(8,128)(2,1)} %get-tuple-element.29), channel_id=1, source_target_pairs={{0,16},{16,0},{1,17},{17,1},{2,18},{18,2},{3,19},{19,3},{4,20},{20... | collective-permute-start | bytes 2752520 | tf_op jit(solution)/shard_map/ppermute | solution.py:42
  51.5 49.3 %copy-start.11 = (bf16[128,512]{1,0:T(8,128)(2,1)}, bf16[128,512]{1,0:T(8,128)(2,1)S(1)}, u32[]{:S(2)}) copy-start(bf16[128,512]{1,0:T(8,128)(2,1)S(1)} %get-tuple-element.32.refs_4_) | copy-start | bytes 393220
  51.5 45.0 %all-to-all-start.1 = ((bf16[8,32,512]{2,1,0:T(8,128)(2,1)}), bf16[8,32,512]{2,1,0:T(8,128)(2,1)S(1)}, u32[]{:S(2)}, u32[]{:S(2)}) async-start(bf16[8,32,512]{2,1,0:T(8,128)(2,1)} %get-tuple-element.31), calls=%async_computation.1 | async-start | bytes 524288 | tf_op jit(solution)/shard_map/all_to_all | solution.py:37
  57.0 39.6 %collective-permute-start.7 = (bf16[128,512]{1,0:T(8,128)(2,1)S(1)}, bf16[128,512]{1,0:T(8,128)(2,1)S(1)}, u32[]{:S(2)}, u32[]{:S(2)}) collective-permute-start(bf16[128,512]{1,0:T(8,128)(2,1)S(1)} %get-tuple-element.32.refs_4_), channel_id=1, source_target_pairs={{0,16},{16,0},{1,17},{17,1},{2,18},{18,2},{3,19},{19,3},{4,20},{20... | collective-permute-start | bytes 393224 | tf_op jit(solution)/shard_map/ppermute | solution.py:42
  59.2 39.7 %collective-permute-start.6 = (bf16[128,512]{1,0:T(8,128)(2,1)S(1)}, bf16[128,512]{1,0:T(8,128)(2,1)S(1)}, u32[]{:S(2)}, u32[]{:S(2)}) collective-permute-start(bf16[128,512]{1,0:T(8,128)(2,1)S(1)} %get-tuple-element.32.refs_4_), channel_id=1, source_target_pairs={{0,8},{8,0},{1,9},{9,1},{2,10},{10,2},{3,11},{11,3},{4,12},{12,4},... | collective-permute-start | bytes 393224 | tf_op jit(solution)/shard_map/ppermute | solution.py:42
  96.5 7.9 %collective-permute-start.4 = (bf16[256,512]{1,0:T(8,128)(2,1)S(1)}, bf16[256,512]{1,0:T(8,128)(2,1)S(1)}, u32[]{:S(2)}, u32[]{:S(2)}) collective-permute-start(bf16[256,512]{1,0:T(8,128)(2,1)S(1)} %bitcast.14), channel_id=1, source_target_pairs={{0,16},{16,0},{1,17},{17,1},{2,18},{18,2},{3,19},{19,3},{4,20},{20... | collective-permute-start | bytes 786440 | tf_op jit(solution)/shard_map/ppermute | solution.py:42
  99.0 0.6 copy-start.15
  99.6 2.2 %collective-permute-start.8 = (bf16[128,512]{1,0:T(8,128)(2,1)S(1)}, bf16[128,512]{1,0:T(8,128)(2,1)S(1)}, u32[]{:S(2)}, u32[]{:S(2)}) collective-permute-start(bf16[128,512]{1,0:T(8,128)(2,1)S(1)} %collective-permute-done.7.refs_6_), channel_id=1, source_target_pairs={{0,8},{8,0},{1,9},{9,1},{2,10},{10,2},{3,11},{11,3},{4,12},{12,4},... | collective-permute-start | bytes 393224 | tf_op jit(solution)/shard_map/ppermute | solution.py:42
  100.9 0.6 copy-start.13
  101.8 0.6 copy-start.17
  102.5 8.5 %collective-permute-start.3 = (bf16[256,512]{1,0:T(8,128)(2,1)S(1)}, bf16[256,512]{1,0:T(8,128)(2,1)S(1)}, u32[]{:S(2)}, u32[]{:S(2)}) collective-permute-start(bf16[256,512]{1,0:T(8,128)(2,1)S(1)} %bitcast.15), channel_id=1, source_target_pairs={{0,8},{8,0},{1,9},{9,1},{2,10},{10,2},{3,11},{11,3},{4,12},{12,4},... | collective-permute-start | bytes 786440 | tf_op jit(solution)/shard_map/ppermute | solution.py:42
  104.4 6.6 %collective-permute-start.5 = (bf16[256,512]{1,0:T(8,128)(2,1)S(1)}, bf16[256,512]{1,0:T(8,128)(2,1)}, u32[]{:S(2)}, u32[]{:S(2)}) collective-permute-start(bf16[256,512]{1,0:T(8,128)(2,1)S(1)} %collective-permute-done.4.refs_2_), channel_id=1, source_target_pairs={{0,8},{8,0},{1,9},{9,1},{2,10},{10,2},{3,11},{11,3},{4,12},{12,4},... | collective-permute-start | bytes 786440 | tf_op jit(solution)/shard_map/ppermute | solution.py:42
  106.8 2.0 %copy-start.4 = (bf16[1920,896]{1,0:T(8,128)(2,1)S(1)}, bf16[1920,896]{1,0:T(8,128)(2,1)}, u32[]{:S(2)}) copy-start(bf16[1920,896]{1,0:T(8,128)(2,1)} %all-gather.2.cloned.1.call-done.gathered) | copy-start | bytes 10321924
  108.7 2.3 %copy-start.9 = (bf16[512,896]{1,0:T(8,128)(2,1)S(1)}, bf16[512,896]{1,0:T(8,128)(2,1)}, u32[]{:S(2)}) copy-start(bf16[512,896]{1,0:T(8,128)(2,1)} %copy-done.8) | copy-start | bytes 2752516
  108.7 2.3 %copy-start.10 = (f32[32,1664]{1,0:T(8,128)S(1)}, f32[32,1664]{1,0:T(8,128)}, u32[]{:S(2)}) copy-start(f32[32,1664]{1,0:T(8,128)} %factors.1) | copy-start | bytes 638980
  108.7 2.3 %copy-start.12 = (bf16[128,512]{1,0:T(8,128)(2,1)S(1)}, bf16[128,512]{1,0:T(8,128)(2,1)}, u32[]{:S(2)}) copy-start(bf16[128,512]{1,0:T(8,128)(2,1)} %copy-done.11) | copy-start | bytes 393220
  108.7 2.3 %copy-start.14 = (bf16[128,512]{1,0:T(8,128)(2,1)S(1)}, bf16[128,512]{1,0:T(8,128)(2,1)}, u32[]{:S(2)}) copy-start(bf16[128,512]{1,0:T(8,128)(2,1)} %copy-done.13) | copy-start | bytes 393220
  108.7 2.4 %copy-start.16 = (bf16[128,512]{1,0:T(8,128)(2,1)S(1)}, bf16[128,512]{1,0:T(8,128)(2,1)}, u32[]{:S(2)}) copy-start(bf16[128,512]{1,0:T(8,128)(2,1)} %copy-done.15) | copy-start | bytes 393220
  108.8 2.4 %copy-start.18 = (bf16[128,512]{1,0:T(8,128)(2,1)S(1)}, bf16[128,512]{1,0:T(8,128)(2,1)}, u32[]{:S(2)}) copy-start(bf16[128,512]{1,0:T(8,128)(2,1)} %copy-done.17) | copy-start | bytes 393220
  159.7 16.3 %all-to-all-start.3 = ((f32[32,8,128]{2,1,0:T(8,128)}), f32[32,8,128]{2,1,0:T(8,128)S(1)}, u32[]{:S(2)}, u32[]{:S(2)}) async-start(f32[32,8,128]{2,1,0:T(8,128)} %get-tuple-element.41), calls=%async_computation.3 | async-start | bytes 262144 | tf_op jit(solution)/shard_map/all_to_all | solution.py:37
  167.1 3.7 %collective-permute-start.12 = (bf16[16,1664]{1,0:T(8,128)(2,1)S(1)}, bf16[16,1664]{1,0:T(8,128)(2,1)S(1)}, u32[]{:S(2)}, u32[]{:S(2)}) collective-permute-start(bf16[16,1664]{1,0:T(8,128)(2,1)S(1)} %get-tuple-element.38), channel_id=1, source_target_pairs={{0,8},{8,0},{1,9},{9,1},{2,10},{10,2},{3,11},{11,3},{4,12},{12,4},... | collective-permute-start | bytes 159752 | tf_op jit(solution)/shard_map/ppermute | solution.py:42
  167.4 6.0 %collective-permute-start.13 = (bf16[16,1664]{1,0:T(8,128)(2,1)S(1)}, bf16[16,1664]{1,0:T(8,128)(2,1)S(1)}, u32[]{:S(2)}, u32[]{:S(2)}) collective-permute-start(bf16[16,1664]{1,0:T(8,128)(2,1)S(1)} %get-tuple-element.39), channel_id=1, source_target_pairs={{0,16},{16,0},{1,17},{17,1},{2,18},{18,2},{3,19},{19,3},{4,20},{20... | collective-permute-start | bytes 159752 | tf_op jit(solution)/shard_map/ppermute | solution.py:42
  170.5 5.5 %collective-permute-start.14 = (bf16[16,1664]{1,0:T(8,128)(2,1)S(1)}, bf16[16,1664]{1,0:T(8,128)(2,1)S(1)}, u32[]{:S(2)}, u32[]{:S(2)}) collective-permute-start(bf16[16,1664]{1,0:T(8,128)(2,1)S(1)} %get-tuple-element.40), channel_id=1, source_target_pairs={{0,24},{8,16},{16,8},{24,0},{1,25},{9,17},{17,9},{25,1},{2,26},{10... | collective-permute-start | bytes 159752 | tf_op jit(solution)/shard_map/ppermute | solution.py:42
Sparse Core Ops, SparseCore 0:
  27.4 48.5 all-gather.1

commit v3 on v2

--- a/solution.py
+++ b/solution.py
@@ -22,11 +22,8 @@
 SMEM_SPEC = pl.BlockSpec(memory_space=pltpu.SMEM)
 
 
-def setup(mib, flops, nbytes):
-    return {
-        "compiler_params": pltpu.CompilerParams(vmem_limit_bytes=mib * MIB),
-        "cost_estimate": pl.CostEstimate(flops=flops, bytes_accessed=nbytes, transcendentals=0),
-    }
+def params(mib):
+    return pltpu.CompilerParams(vmem_limit_bytes=mib * MIB)
 
 
 def dot(a, b, ca, cb):
@@ -40,6 +37,15 @@
 def swap(value, axis, mask=1):
     size = lax.axis_size(axis)
     return lax.ppermute(value, axis, [(i, i ^ mask) for i in range(size)])
+
+
+def shift(value, step):
+    size = lax.axis_size("z")
+    return lax.ppermute(value, "z", [(i, (i + step) % size) for i in range(size)])
+
+
+def after(value, *others):
+    return lax.optimization_barrier((value, others))[0]
 
 
 def left_body(ids, u0, u1, u2, u3, basis, out):
@@ -71,7 +77,7 @@
             in_specs=[*specs, pl.BlockSpec((depth, tile), lambda n, ids: (0, n))],
             out_specs=pl.BlockSpec((n_in, rows, tile), lambda n, ids: (0, 0, n)),
         ),
-        **setup(16, 2 * depth * eigen * rank * queries, 4 * MIB),
+        compiler_params=params(16),
         name="left",
     )(query_ids, u_t, u_t, u_t, u_t, basis_out)
 
@@ -98,53 +104,60 @@
         ),
         in_specs=[VMEM_SPEC],
         out_specs=(VMEM_SPEC, VMEM_SPEC),
-        **setup(4, 0, 2 * MIB),
+        compiler_params=params(4),
         name="left_sum",
     )(parts)
 
 
-def inverse_body(where, corrected, *outs):
-    for r, out in enumerate(outs):
-        half = where[3] ^ r
-        skip = corrected.shape[1] - out.shape[1]
-        at = pl.multiple_of(half * skip, LANES)
-        out[...] = (1.0 / corrected[:, pl.ds(at, out.shape[1])]).astype(BF)
-
-
-def inverse_halves(where, corrected, block, width, far):
-    rows = corrected.shape[0]
-    tile = 64
-    return pl.pallas_call(
-        inverse_body,
+def inverse_body(where, corrected, out_0, out_1, values, done, *, far, part):
+    rows, block = values.shape
+    blk = where[1] ^ far
+    source = corrected.at[
+        pl.ds(part * rows, rows), pl.ds(pl.multiple_of(blk * block, LANES), block)
+    ]
+    copy = pltpu.make_async_copy(source, values, done)
+    copy.start()
+    copy.wait()
+    for r, out in enumerate((out_0, out_1)):
+        skip = block - out.shape[1]
+        at = pl.multiple_of((where[3] ^ r) * skip, LANES)
+        out[...] = (1.0 / values[:, pl.ds(at, out.shape[1])]).astype(BF)
+
+
+def inverse_halves(where, corrected, block, width, far, parts=1, part=0):
+    rows = corrected.shape[0] // parts
+    return pl.pallas_call(
+        functools.partial(inverse_body, far=far, part=part),
         out_shape=tuple(jax.ShapeDtypeStruct((rows, width), BF) for _ in range(2)),
-        grid_spec=pltpu.PrefetchScalarGridSpec(
-            num_scalar_prefetch=1,
-            grid=(rows // tile,),
-            in_specs=[pl.BlockSpec((tile, block), lambda n, w: (n, w[1] ^ far))],
-            out_specs=tuple(pl.BlockSpec((tile, width), lambda n, w: (n, 0)) for _ in range(2)),
-        ),
-        **setup(8, 0, 12 * MIB),
+        in_specs=[SMEM_SPEC, pl.BlockSpec(memory_space=pltpu.HBM)],
+        out_specs=(VMEM_SPEC, VMEM_SPEC),
+        scratch_shapes=[pltpu.VMEM((rows, block), F32), pltpu.SemaphoreType.DMA],
+        compiler_params=params(12),
         name="inverse",
     )(where, corrected)
 
 
 def pack_body(where, train_ids, basis, tokens, delta, *outs):
     rows = basis.shape[1]
-    train = train_ids.shape[0]
+    train, stored = train_ids.shape[0], tokens.shape[0]
+    line = lax.broadcasted_iota(jnp.int32, (stored, stored), 0)
+    lane = lax.broadcasted_iota(jnp.int32, (stored, stored), 1)
+    chosen = jnp.zeros((stored, stored), jnp.bool_)
+    for b in range(train):
+        chosen = jnp.logical_or(chosen, jnp.logical_and(line == b, lane == train_ids[b]))
+    chosen = jnp.where(chosen, 1.0, 0.0).astype(BF)
+    gradients = dot(chosen, delta[...], 1, 0).astype(BF)[:train]
     for r, out in enumerate(outs):
         width = out.shape[1]
         block = basis.shape[2]
         skip = block - width
         blk, half = where[1] ^ (r // 2), where[3] ^ (r % 2)
         out[:rows, :] = basis[blk, :, pl.ds(pl.multiple_of(half * skip, LANES), width)]
-        for b in range(train):
-            row = train_ids[b]
-            first = pl.multiple_of(blk * block, LANES)
-            rest = pl.multiple_of(blk * block + width, LANES)
-            out[rows + b : rows + b + 1, :] = tokens[row, :, pl.ds(first, width)]
-            at = rows + train + b
-            out[at : at + 1, :skip] = tokens[row, :, pl.ds(rest, skip)]
-            out[at : at + 1, skip:] = delta[row]
+        own = tokens[:, pl.ds(pl.multiple_of(blk * block, LANES), block)]
+        own = dot(chosen, own, 1, 0).astype(BF)[:train]
+        out[rows : rows + train, :] = own[:, :width]
+        out[rows + train :, :skip] = own[:, width:]
+        out[rows + train :, skip:] = gradients
 
 
 def pack(where, train_ids, basis, tokens, delta, width):
@@ -154,7 +167,7 @@
         out_shape=tuple(jax.ShapeDtypeStruct((rows, width), BF) for _ in range(4)),
         in_specs=[SMEM_SPEC, SMEM_SPEC, VMEM_SPEC, VMEM_SPEC, VMEM_SPEC],
         out_specs=tuple([VMEM_SPEC] * 4),
-        **setup(4, 0, 2 * MIB),
+        compiler_params=params(4),
         name="pack",
     )(where, train_ids, basis, tokens, delta)
 
@@ -184,38 +197,37 @@
         out_shape=jax.ShapeDtypeStruct((4 * rows, width), BF),
         in_specs=[SMEM_SPEC, *([VMEM_SPEC] * 4)],
         out_specs=VMEM_SPEC,
-        **setup(8, 0, 2 * MIB),
+        compiler_params=params(8),
         name="arrange",
     )(where, *parts)
 
 
-def rotate_body(where, ids, v0, v1, v2, v3, gathered, basis, right, tokens, delta, *, n_z):
-    each = gathered.shape[0] // n_z
+def rotate_body(where, ids, v0, v1, v2, v3, *refs):
+    chunks, (basis, right, tokens, delta) = refs[:-4], refs[-4:]
+    n_z = len(chunks)
     slab = basis.shape[0] // n_z
-    extra = (each - slab) // 2
-    for k in range(n_z):
-        basis[k * slab : (k + 1) * slab, :] = gathered[k * each : k * each + slab, :]
+    extra = (chunks[0].shape[0] - slab) // 2
+    for k, chunk in enumerate(chunks):
+        step = k if k <= n_z // 2 else k - n_z
+        at = lax.rem(where[0] - step + n_z, n_z) * slab
+        basis[pl.ds(pl.multiple_of(at, 16), slab), :] = chunk[:slab, :]
     factors = jnp.concatenate([v[0] for v in (v0, v1, v2, v3)], axis=0)
     whole = basis[...]
     right[...] = dot(factors, whole, 1, 0).astype(BF)
     width = whole.shape[1]
     rest = whole.shape[0] - width
-    head, tail = (
-        jnp.concatenate(
-            [gathered[k * each + a : k * each + a + extra, :] for k in range(n_z)], axis=0
-        )
-        for a in (slab, slab + extra)
-    )
+    head = jnp.concatenate([c[slab : slab + extra, :] for c in chunks], axis=0)
+    tail = jnp.concatenate([c[slab + extra :, :] for c in chunks], axis=0)
     rotated = dot(head, whole[:width, :], 1, 0) + dot(tail[:, :rest], whole[width:, :], 1, 0)
     tokens[...] = rotated.astype(BF)
     delta[...] = tail[:, rest:]
 
 
-def rotate(where, query_ids, v_t, gathered, block, n_z):
+def rotate(where, query_ids, v_t, chunks, block):
     queries = query_ids.shape[0]
     rank = v_t.shape[1]
-    rows, width = gathered.shape
-    extra = (rows - block) // 2
+    rows, width = chunks[0].shape
+    extra = (rows * len(chunks) - block) // 2
     specs = [
         pl.BlockSpec(
             (1, rank, block), functools.partial(lambda q, n, w, ids: (ids[q], 0, w[1]), q)
@@ -233,44 +245,74 @@
         (extra, 2 * width - block),
     )
     return pl.pallas_call(
-        functools.partial(rotate_body, n_z=n_z),
+        rotate_body,
         out_shape=tuple(jax.ShapeDtypeStruct(s, BF) for s in shapes),
         grid_spec=pltpu.PrefetchScalarGridSpec(
             num_scalar_prefetch=2,
             grid=(1,),
-            in_specs=[*specs, full((rows, width))],
+            in_specs=[*specs, *(full((rows, width)) for _ in chunks)],
             out_specs=tuple(full(s) for s in shapes),
         ),
-        **setup(32, 2 * block * width * (queries * rank + extra), 8 * MIB),
+        compiler_params=params(32),
         name="rotate",
-    )(where, query_ids, v_t, v_t, v_t, v_t, gathered)
-
-
-def back_body(where, factors, right, tokens, delta, *refs, queries, train):
-    lefts, windows, inverses, out = refs[:4], refs[4:8], refs[8:12], refs[12]
+    )(where, query_ids, v_t, v_t, v_t, v_t, *chunks)
+
+
+def back_terms(right, lefts, windows, inverses, rank, q):
+    at = slice(q * rank, (q + 1) * rank)
+    total = None
+    pieces = len(inverses) // 2
+    for k, (left, window) in enumerate(zip(lefts, windows)):
+        inverse = jnp.concatenate(
+            [i[...] for i in inverses[k * pieces : (k + 1) * pieces]], axis=0
+        )
+        product = dot(left[at, :], right[at, :], 0, 0)
+        precond = (product * inverse.astype(F32)).astype(BF)
+        term = dot(window[...], precond, 1, 0)
+        total = term if total is None else total + term
+    return total
+
+
+def back_first_body(right, *refs):
+    out = refs[6]
+    queries = out.shape[0]
+    rank = right.shape[0] // queries
+    for q in range(queries):
+        out[q] = back_terms(right, refs[:2], refs[2:4], refs[4:6], rank, q)
+
+
+def back_first(right, lefts, windows, inverses, queries):
+    width = right.shape[1]
+    win, depth = windows[0].shape
+    return pl.pallas_call(
+        back_first_body,
+        out_shape=jax.ShapeDtypeStruct((queries, win, width), F32),
+        in_specs=[VMEM_SPEC] * 7,
+        out_specs=VMEM_SPEC,
+        compiler_params=params(24),
+        name="back_first",
+    )(right, *lefts, *windows, *inverses)
+
+
+def back_body(where, block_ids, so_far, factors, right, tokens, delta, *refs, train):
+    out, refs = refs[-1], refs[:-1]
+    queries = so_far.shape[0]
     n_z, rows, width = out.shape
-    win = windows[0].shape[0]
+    win = so_far.shape[1]
     per = win // n_z
     rank = right.shape[0] // queries
     valid = factors.shape[1] // 2
     skip = factors.shape[1] - width
-    row = factors[pl.ds(where[2], 1), pl.ds(pl.multiple_of(where[3] * skip, LANES), width)]
+    chosen = block_ids[2 * where[2] + where[1]]
+    row = factors[pl.ds(chosen, 1), pl.ds(pl.multiple_of(where[3] * skip, LANES), width)]
     lane = lax.broadcasted_iota(jnp.int32, (1, width), 1)
     first = where[3] * (width - valid)
     mine = jnp.logical_and(lane >= first, lane < first + valid)
     scale = jnp.where(mine, 1.0 / row, 0.0)
-    which = lax.rem(
-        lax.broadcasted_iota(jnp.int32, (tokens.shape[0], 1), 0), train
-    )
+    which = lax.rem(lax.broadcasted_iota(jnp.int32, (tokens.shape[0], 1), 0), train)
     scores = []
     for q in range(queries):
-        at = slice(q * rank, (q + 1) * rank)
-        total = None
-        for left, window, inverse in zip(lefts, windows, inverses):
-            product = dot(left[at, :], right[at, :], 0, 0)
-            precond = (product * inverse[...].astype(F32)).astype(BF)
-            term = dot(window[...], precond, 1, 0)
-            total = term if total is None else total + term
+        total = so_far[q] + back_terms(right, refs[:2], refs[2:4], refs[4:], rank, q)
         total = (total * scale).astype(BF)
         out[:, q * per : (q + 1) * per, :] = total.reshape(n_z, per, width)
         projected = dot(tokens[...], total, 1, 1) * delta[...].astype(F32)
@@ -289,17 +331,17 @@
         out[k, queries * per :, :] = extra
 
 
-def back(where, factors, right, tokens, delta, lefts, windows, inverses, n_z, queries, train):
-    width = right.shape[1]
-    win, depth = windows[0].shape
-    return pl.pallas_call(
-        functools.partial(back_body, queries=queries, train=train),
+def back(where, block_ids, so_far, factors, right, tokens, delta, near, n_z, train):
+    queries, win, width = so_far.shape
+    depth = near[0].shape[1]
+    return pl.pallas_call(
+        functools.partial(back_body, train=train),
         out_shape=jax.ShapeDtypeStruct((n_z, queries * win // n_z + 8, width), BF),
-        in_specs=[SMEM_SPEC, *([VMEM_SPEC] * (4 + 12))],
+        in_specs=[SMEM_SPEC, SMEM_SPEC, *([VMEM_SPEC] * (5 + len(near)))],
         out_specs=VMEM_SPEC,
-        **setup(32, 16 * depth * width * queries * win, 8 * MIB),
+        compiler_params=params(24),
         name="back",
-    )(where, factors, right, tokens, delta, *lefts, *windows, *inverses)
+    )(where, block_ids, so_far, factors, right, tokens, delta, *near)
 
 
 def tile_body(where, parts, basis, t0, t1, t2, t3, score, *, queries, train):
@@ -322,16 +364,14 @@
     for r, out in enumerate((t0, t1, t2, t3)):
         out[...] = tiles[r * own : (r + 1) * own]
     words = total[rows:]
-    line = lax.broadcasted_iota(jnp.int32, (8, LANES), 0)
-    lane = lax.broadcasted_iota(jnp.int32, (8, LANES), 1)
-    table = jnp.zeros((8, LANES), F32)
+    lane = lax.broadcasted_iota(jnp.int32, (1, LANES), 1)
+    table = jnp.zeros((1, LANES), F32)
     for k in range(queries * train // 8):
         at = 2 * k * LANES
         sums = words[:, at : at + LANES] + words[:, at + LANES : at + 2 * LANES]
         sums = jnp.sum(sums, axis=1, keepdims=True)
         for i in range(8):
-            q, b = divmod(8 * k + i, train)
-            table = jnp.where(jnp.logical_and(line == q, lane == b), sums[i : i + 1], table)
+            table = jnp.where(lane == 8 * k + i, sums[i : i + 1], table)
     score[...] = jnp.broadcast_to(table[None], score.shape)
 
 
@@ -342,11 +382,11 @@
         functools.partial(tile_body, queries=queries, train=train),
         out_shape=(
             *(jax.ShapeDtypeStruct((own, block), BF) for _ in range(4)),
-            jax.ShapeDtypeStruct((plane, 8, LANES), F32),
+            jax.ShapeDtypeStruct((plane, 1, LANES), F32),
         ),
         in_specs=[SMEM_SPEC, VMEM_SPEC, VMEM_SPEC],
         out_specs=tuple([VMEM_SPEC] * 5),
-        **setup(24, 8 * own * block * basis.shape[1], 5 * MIB),
+        compiler_params=params(24),
         name="tile",
     )(where, parts, basis)
 
@@ -359,7 +399,10 @@
         at = pl.multiple_of((where[1] ^ r) * block, LANES)
         for q in range(queries):
             tiles[q, :, pl.ds(at, block)] = total[q * per : (q + 1) * per]
-    scores[...] = jnp.sum(score[...], axis=0)[: scores.shape[0], : scores.shape[1]]
+    sums = jnp.sum(score[...], axis=0)
+    train = scores.shape[1]
+    for q in range(queries):
+        scores[q : q + 1, :] = sums[:, q * train : (q + 1) * train]
 
 
 def final(where, parts, score, queries, train):
@@ -372,7 +415,7 @@
         ),
         in_specs=[SMEM_SPEC, *([VMEM_SPEC] * 5)],
         out_specs=(VMEM_SPEC, VMEM_SPEC),
-        **setup(4, 0, 1 * MIB),
+        compiler_params=params(4),
         name="final",
     )(where, *parts, score)
 
@@ -391,51 +434,56 @@
     delta_pool,
 ):
     n_z, n_in = lax.axis_size("z"), lax.axis_size(IN)
-    xh, c = lax.axis_index("xh"), lax.axis_index("c")
+    z, xh, c = lax.axis_index("z"), lax.axis_index("xh"), lax.axis_index("c")
     in_pos = lax.axis_index(IN)
     queries, train = query_ids.shape[0], train_ids.shape[0]
     _, local_rows, block = basis_in.shape
     width = -(-(block // 2) // LANES) * LANES
-    block_id = lax.dynamic_index_in_dim(block_ids, in_pos * 2 + xh, keepdims=False)
-    where = jnp.stack([in_pos, xh, block_id, c]).astype(jnp.int32)
-
-    packed = pack(where, train_ids, basis_in, x_pool, delta_pool, width)
+    where = jnp.stack([z, xh, in_pos, c]).astype(jnp.int32)
+
+    packed = pack(where, train_ids, basis_in, x_pool[:, 0], delta_pool[:, 0], width)
     parts = (
         packed[0],
         swap(packed[1], "c"),
         swap(packed[2], "xh"),
         swap(packed[3], QUAD, 3),
     )
-    own = arrange(where, parts, local_rows, train)
-    gathered = lax.all_gather(own, "z", axis=0, tiled=True)
-
-    far = inverse_halves(where, corrected, block, width, 1)
+    pieces = n_z // 2
+    far = [inverse_halves(where, corrected, block, width, 1, pieces, k) for k in range(pieces)]
+    own = arrange(where, (after(packed[0], far[0][0]), *parts[1:]), local_rows, train)
+    far = [(swap(a, "xh"), swap(b, QUAD, 3)) for a, b in far]
     near = inverse_halves(where, corrected, block, width, 0)
-    inverses = (near[0], swap(near[1], "c"), swap(far[0], "xh"), swap(far[1], QUAD, 3))
-    left_ids, _ = lax.optimization_barrier((query_ids, far[0]))
-
-    parts = left_part(left_ids, jnp.transpose(u_pool, (0, 2, 1)), basis_out, n_in)
-    spread, window = left_sum(exchange(parts, IN))
+    near = (near[0], swap(near[1], "c"))
+
+    partial = left_part(query_ids, jnp.transpose(u_pool, (0, 2, 1)), basis_out, n_in)
+    ahead, behind = [shift(own, 1)], [shift(own, -1)]
+    up, down = after((ahead[0], behind[0]), far[0], partial)
+    ahead.append(shift(up, 1))
+    behind.append(shift(down, -1))
+    spread, window = left_sum(exchange(partial, IN))
+    up, down = after((ahead[1], behind[1]), far[1], spread)
+    ahead.append(shift(up, 1))
+    behind.append(shift(down, -1))
     left = exchange(spread, IN).reshape(-1, basis_out.shape[1])
+    up, left, window = after((ahead[2], left, window), behind[2], far[2])
+    ahead.append(shift(up, 1))
     left_x, window_x = swap(left, "xh"), swap(window, "xh")
-    lefts = (left, swap(left, "c"), left_x, swap(left_x, "c"))
-    windows = (window, swap(window, "c"), window_x, swap(window_x, "c"))
+    lefts = (left, swap(left, "c"))
+    windows = (window, swap(window, "c"))
+    chunks = (own, *ahead[:3], after(ahead[3], far[3]), *behind[::-1])
 
     basis, right, tokens, delta = rotate(
-        where, query_ids, jnp.transpose(v_pool, (0, 2, 1)), gathered, block, n_z
+        where, query_ids, jnp.transpose(v_pool, (0, 2, 1)), chunks, block
+    )
+    so_far = back_first(right, lefts, windows, near, queries)
+    left_x, window_x = after((left_x, window_x), so_far)
+    far = (
+        *(left_x, swap(left_x, "c"), window_x, swap(window_x, "c")),
+        *(a for a, _ in far),
+        *(b for _, b in far),
     )
     parts = back(
-        where,
-        factor_table,
-        right,
-        tokens,
-        delta,
-        lefts,
-        windows,
-        inverses,
-        n_z,
-        queries,
-        train,
+        where, block_ids, so_far, factor_table, right, tokens, delta, far, n_z, train
     )
     *parts, score = tile_part(
         where, exchange(parts, "z"), basis, lax.axis_size(PLANE), queries, train

time: 185 us -> 179 us (0.968)
  between operations: 14.2 us -> 0.97 us
  starting transfers between devices: 40.1 us -> 52.7 us
  waiting for transfers between devices: 48.6 us -> 40.2 us
  blocking collectives: 36.9 us -> 43.6 us
  Pallas kernels: 28.2 us -> 25.5 us
    ppermute x15 -> x21, waiting for transfers between devices: 48.6 us -> 34.5 us  [swap(): return lax.ppermute(value, axis, [(i, i ^ mask) for i in range(size)])]
    ppermute x0 -> x7, starting transfers between devices: none -> 10 us  [shift(): lax.ppermute(value, 'z', [(i, (i + step) % size) for i in range(size)])]
    ppermute x15 -> x21, starting transfers between devices: 23.7 us -> 32.7 us  [swap(): return lax.ppermute(value, axis, [(i, i ^ mask) for i in range(size)])]
    all_to_all x1 -> x2, blocking collectives: 36.9 us -> 43.6 us  [exchange(): return lax.all_to_all(value, axis, split_axis=0, concat_axis=0, tiled=True)]
    all_to_all x3 -> x2, starting transfers between devices: 16.3 us -> 10 us  [exchange(): return lax.all_to_all(value, axis, split_axis=0, concat_axis=0, tiled=True)]
    all_to_all x3 -> x2, waiting for transfers between devices: 0.01 us -> 5.73 us  [exchange(): return lax.all_to_all(value, axis, split_axis=0, concat_axis=0, tiled=True)]
    unnamed x41 -> x45, local copies, waits for them, and re-layouts: 14.1 us -> 15.7 us
    pallas_call x4 -> x8, Pallas kernels: 19 us -> 18.3 us  [the longest x5 5.87 us: inverse_halves(): pl.pallas_call(functools.partial(inverse_body, far=far, part=part), out_s...]
  transfers between devices with their start and end apart: 19 -> 30, of which waited for: 7 -> 12; matrix products, arithmetic and copies ran while one was open for 0% -> 0% of each run, Pallas kernels for 7% -> 9%
where the time goes in v3:
time: 179 us
  starting transfers between devices  52.7 us (29%)
  blocking collectives  43.6 us (24%)
  waiting for transfers between devices  40.2 us (22%)
  Pallas kernels  25.5 us (14%)
  local copies, waits for them, and re-layouts  15.7 us (9%)
    all_to_all x2, blocking collectives, exchange(): return lax.all_to_all(value, axis, split_axis=0, concat_axis=0, tiled=True)  43.6 us
    ppermute x21, waiting for transfers between devices, swap(): return lax.ppermute(value, axis, [(i, i ^ mask) for i in range(size)])  34.5 us
    ppermute x21, starting transfers between devices, swap(): return lax.ppermute(value, axis, [(i, i ^ mask) for i in range(size)])  32.7 us
    unnamed x45, local copies, waits for them, and re-layouts  15.7 us
    all_to_all x2, starting transfers between devices, exchange(): return lax.all_to_all(value, axis, split_axis=0, concat_axis=0, tiled=True)  10 us
    ppermute x7, starting transfers between devices, shift(): lax.ppermute(value, 'z', [(i, (i + step) % size) for i in range(size)])  10 us
    pallas_call x5, Pallas kernels, inverse_halves(): pl.pallas_call(functools.partial(inverse_body, far=far, part=part), out_s...  5.87 us
    all_to_all x2, waiting for transfers between devices, exchange(): return lax.all_to_all(value, axis, split_axis=0, concat_axis=0, tiled=True)  5.73 us
  transfers between devices with their start and end apart: 30, of which 12 were waited for; matrix products, arithmetic and copies ran while one was open for 0% of the time, Pallas kernels for 9%

profile of v3, /device:TPU:1, one launch (start us, length us, event | category | flops | bytes accessed | tf_op | source)
XLA Modules:
  0.0 178.8 jit_solution(3298386840100218970)
XLA Ops:
  0.6 1.0 copy.13.basis
  1.7 0.1 pad_add_fusion.where
  1.8 0.8 copy-done.17
  2.6 0.7 copy-done.18
  3.2 0.7 copy-done.20
  3.9 0.7 pack.1
  4.6 3.3 %collective-permute-start = (bf16[60,896]{1,0:T(8,128)(2,1)S(1)}, bf16[60,896]{1,0:T(8,128)(2,1)S(1)}, u32[]{:S(2)}, u32[]{:S(2)}) collective-permute-start(bf16[60,896]{1,0:T(8,128)(2,1)S(1)} %get-tuple-element.41), channel_id=1, source_target_pairs={{0,8},{8,0},{1,9},{9,1},{2,10},{10,2},{3,11},{11,3},{4,12},{12,4},... | collective-permute-start | bytes 322568 | tf_op jit(solution)/shard_map/ppermute | solution.py:39
  8.0 1.0 collective-permute-start.1
  9.0 2.2 %collective-permute-start.2 = (bf16[60,896]{1,0:T(8,128)(2,1)S(1)}, bf16[60,896]{1,0:T(8,128)(2,1)S(1)}, u32[]{:S(2)}, u32[]{:S(2)}) collective-permute-start(bf16[60,896]{1,0:T(8,128)(2,1)S(1)} %get-tuple-element.43), channel_id=1, source_target_pairs={{0,24},{8,16},{16,8},{24,0},{1,25},{9,17},{17,9},{25,1},{2,26},{10... | collective-permute-start | bytes 322568 | tf_op jit(solution)/shard_map/ppermute | solution.py:39
  11.2 2.9 %copy-done = f32[512,3328]{1,0:T(8,128)S(1)} copy-done((f32[512,3328]{1,0:T(8,128)S(1)}, f32[512,3328]{1,0:T(8,128)}, u32[]{:S(2)}) %copy-start) | copy-done | bytes 6815768
  14.2 0.7 inverse.5
  14.9 1.9 %collective-permute-done.2.a3 = bf16[60,896]{1,0:T(8,128)(2,1)S(1)} collective-permute-done((bf16[60,896]{1,0:T(8,128)(2,1)S(1)}, bf16[60,896]{1,0:T(8,128)(2,1)S(1)}, u32[]{:S(2)}, u32[]{:S(2)}) %collective-permute-start.2) | collective-permute-done | bytes 107552 | tf_op jit(solution)/shard_map/ppermute | solution.py:39
  16.8 1.2 arrange.1.refs_0_
  18.0 0.5 collective-permute-start.3
  18.5 4.0 %collective-permute-start.4 = (bf16[240,896]{1,0:T(8,128)(2,1)S(1)}, bf16[240,896]{1,0:T(8,128)(2,1)S(1)}, u32[]{:S(2)}, u32[]{:S(2)}) collective-permute-start(bf16[240,896]{1,0:T(8,128)(2,1)S(1)} %arrange.1.refs_0_), channel_id=1, source_target_pairs={{0,224},{32,0},{64,32},{96,64},{128,96},{160,128},{192,160},{224,1... | collective-permute-start | bytes 1290248 | tf_op jit(solution)/shard_map/ppermute | solution.py:44
  22.6 2.2 %collective-permute-start.5 = (bf16[128,896]{1,0:T(8,128)(2,1)S(1)}, bf16[128,896]{1,0:T(8,128)(2,1)S(1)}, u32[]{:S(2)}, u32[]{:S(2)}) collective-permute-start(bf16[128,896]{1,0:T(8,128)(2,1)S(1)} %get-tuple-element.39), channel_id=1, source_target_pairs={{0,16},{16,0},{1,17},{17,1},{2,18},{18,2},{3,19},{19,3},{4,20},{20... | collective-permute-start | bytes 688136 | tf_op jit(solution)/shard_map/ppermute | solution.py:39
  24.8 1.6 collective-permute-start.6
  26.3 2.3 %left.1 = bf16[8,48,512]{2,1,0:T(8,128)(2,1)} custom-call(s32[4]{0:T(128)S(1)} %copy-done.19, bf16[6,64,2048]{2,1,0:T(8,128)(2,1)S(1)} %bitcast.13, bf16[6,64,2048]{2,1,0:T(8,128)(2,1)S(1)} %bitcast.14, bf16[6,64,2048]{2,1,0:T(8,128)(2,1)S(1)} %bitcast.15, bf16[6,64,2048]{2,1,0:T(8,128)(2,1)S(1)} %bitcast.16, bf16[2048,512]{1,0:T(8,128)(2,1)S(1)} %copy-done.6), custom_call_target="tpu_custom_call" | custom-call | tf_op jit(solution)/shard_map/left/pallas_call | solution.py:71
  28.7 1.9 %collective-permute-done.5.refs_4_ = bf16[128,896]{1,0:T(8,128)(2,1)S(1)} collective-permute-done((bf16[128,896]{1,0:T(8,128)(2,1)S(1)}, bf16[128,896]{1,0:T(8,128)(2,1)S(1)}, u32[]{:S(2)}, u32[]{:S(2)}) %collective-permute-start.5) | collective-permute-done | bytes 229408 | tf_op jit(solution)/shard_map/ppermute | solution.py:39
  30.6 5.7 %collective-permute-done.6.refs_8_ = bf16[128,896]{1,0:T(8,128)(2,1)S(1)} collective-permute-done((bf16[128,896]{1,0:T(8,128)(2,1)S(1)}, bf16[128,896]{1,0:T(8,128)(2,1)S(1)}, u32[]{:S(2)}, u32[]{:S(2)}) %collective-permute-start.6) | collective-permute-done | bytes 229408 | tf_op jit(solution)/shard_map/ppermute | solution.py:39
  36.3 0.1 collective-permute-start.7
  36.4 2.7 %collective-permute-start.8 = (bf16[240,896]{1,0:T(8,128)(2,1)S(1)}, bf16[240,896]{1,0:T(8,128)(2,1)}, u32[]{:S(2)}, u32[]{:S(2)}) collective-permute-start(bf16[240,896]{1,0:T(8,128)(2,1)S(1)} %collective-permute-done.4.refs_7_), channel_id=1, source_target_pairs={{0,224},{32,0},{64,32},{96,64},{128,96},{160,128},{192,160},{224,1... | collective-permute-start | bytes 1290248 | tf_op jit(solution)/shard_map/ppermute | solution.py:44
  39.1 4.6 %all-to-all-start = ((bf16[8,48,512]{2,1,0:T(8,128)(2,1)}), bf16[8,48,512]{2,1,0:T(8,128)(2,1)S(1)}, u32[]{:S(2)}, u32[]{:S(2)}) async-start(bf16[8,48,512]{2,1,0:T(8,128)(2,1)} %left.1), calls=%async_computation | async-start | bytes 786432 | tf_op jit(solution)/shard_map/all_to_all | solution.py:34
  43.7 2.9 %copy-done.1 = f32[512,3328]{1,0:T(8,128)S(1)} copy-done((f32[512,3328]{1,0:T(8,128)S(1)}, f32[512,3328]{1,0:T(8,128)}, u32[]{:S(2)}) %copy-start.1) | copy-done | bytes 6815768
  46.6 0.7 inverse.6
  47.4 3.0 %collective-permute-start.10 = (bf16[128,896]{1,0:T(8,128)(2,1)S(1)}, bf16[128,896]{1,0:T(8,128)(2,1)S(1)}, u32[]{:S(2)}, u32[]{:S(2)}) collective-permute-start(bf16[128,896]{1,0:T(8,128)(2,1)S(1)} %get-tuple-element.48), channel_id=1, source_target_pairs={{0,24},{8,16},{16,8},{24,0},{1,25},{9,17},{17,9},{25,1},{2,26},{10... | collective-permute-start | bytes 688136 | tf_op jit(solution)/shard_map/ppermute | solution.py:39
  50.4 0.3 collective-permute-start.9
  50.7 1.4 all-to-all-done.parts
  52.2 0.7 copy-done.7
  52.9 4.0 %collective-permute-done.10.refs_9_ = bf16[128,896]{1,0:T(8,128)(2,1)S(1)} collective-permute-done((bf16[128,896]{1,0:T(8,128)(2,1)S(1)}, bf16[128,896]{1,0:T(8,128)(2,1)S(1)}, u32[]{:S(2)}, u32[]{:S(2)}) %collective-permute-start.10) | collective-permute-done | bytes 229408 | tf_op jit(solution)/shard_map/ppermute | solution.py:39
  56.9 4.6 %collective-permute-done.9.refs_5_ = bf16[128,896]{1,0:T(8,128)(2,1)S(1)} collective-permute-done((bf16[128,896]{1,0:T(8,128)(2,1)S(1)}, bf16[128,896]{1,0:T(8,128)(2,1)S(1)}, u32[]{:S(2)}, u32[]{:S(2)}) %collective-permute-start.9) | collective-permute-done | bytes 229408 | tf_op jit(solution)/shard_map/ppermute | solution.py:39
  61.5 0.1 collective-permute-start.11
  61.5 2.7 %collective-permute-start.12 = (bf16[240,896]{1,0:T(8,128)(2,1)}, bf16[240,896]{1,0:T(8,128)(2,1)}, u32[]{:S(2)}, u32[]{:S(2)}) collective-permute-start(bf16[240,896]{1,0:T(8,128)(2,1)} %collective-permute-done.8.refs_6_), channel_id=1, source_target_pairs={{0,224},{32,0},{64,32},{96,64},{128,96},{160,128},{192,160},{224,1... | collective-permute-start | bytes 1290248 | tf_op jit(solution)/shard_map/ppermute | solution.py:44
  64.2 2.9 %copy-done.2 = f32[512,3328]{1,0:T(8,128)S(1)} copy-done((f32[512,3328]{1,0:T(8,128)S(1)}, f32[512,3328]{1,0:T(8,128)}, u32[]{:S(2)}) %copy-start.2) | copy-done | bytes 6815768
  67.2 2.1 %inverse.9 = (bf16[512,896]{1,0:T(8,128)(2,1)S(1)}, bf16[512,896]{1,0:T(8,128)(2,1)}) custom-call(s32[4]{0:T(128)S(1)} %pad_add_fusion.where, f32[512,3328]{1,0:T(8,128)S(1)} %copy-done.2), custom_call_target="tpu_custom_call" | custom-call | tf_op jit(solution)/shard_map/inverse/pallas_call | solution.py:129
  69.3 1.4 collective-permute-start.20
  70.7 1.5 inverse.7
  72.2 2.7 %collective-permute-start.13 = (bf16[128,896]{1,0:T(8,128)(2,1)}, bf16[128,896]{1,0:T(8,128)(2,1)}, u32[]{:S(2)}, u32[]{:S(2)}) collective-permute-start(bf16[128,896]{1,0:T(8,128)(2,1)} %get-tuple-element.53), channel_id=1, source_target_pairs={{0,16},{16,0},{1,17},{17,1},{2,18},{18,2},{3,19},{19,3},{4,20},{20... | collective-permute-start | bytes 688136 | tf_op jit(solution)/shard_map/ppermute | solution.py:39
  74.9 0.5 collective-permute-start.14
  75.4 5.4 %all-to-all-start.1 = ((bf16[8,32,512]{2,1,0:T(8,128)(2,1)}), bf16[8,32,512]{2,1,0:T(8,128)(2,1)S(1)}, u32[]{:S(2)}, u32[]{:S(2)}) async-start(bf16[8,32,512]{2,1,0:T(8,128)(2,1)} %copy-done.7), calls=%async_computation.1 | async-start | bytes 524288 | tf_op jit(solution)/shard_map/all_to_all | solution.py:34
  80.8 0.5 collective-permute-done.13.refs_6_
  81.3 5.6 %collective-permute-done.14.refs_10_ = bf16[128,896]{1,0:T(8,128)(2,1)} collective-permute-done((bf16[128,896]{1,0:T(8,128)(2,1)}, bf16[128,896]{1,0:T(8,128)(2,1)}, u32[]{:S(2)}, u32[]{:S(2)}) %collective-permute-start.14) | collective-permute-done | bytes 229408 | tf_op jit(solution)/shard_map/ppermute | solution.py:39
  86.9 4.3 %all-to-all-done.1 = bf16[8,32,512]{2,1,0:T(8,128)(2,1)S(1)} async-done(((bf16[8,32,512]{2,1,0:T(8,128)(2,1)}), bf16[8,32,512]{2,1,0:T(8,128)(2,1)S(1)}, u32[]{:S(2)}, u32[]{:S(2)}) %all-to-all-start.1) | async-done | bytes 262176 | tf_op jit(solution)/shard_map/all_to_all | solution.py:34
  91.2 2.9 %copy-done.3 = f32[512,3328]{1,0:T(8,128)S(1)} copy-done((f32[512,3328]{1,0:T(8,128)S(1)}, f32[512,3328]{1,0:T(8,128)}, u32[]{:S(2)}) %copy-start.3) | copy-done | bytes 6815768
  94.2 0.7 inverse.8
  94.9 2.0 %collective-permute-start.16 = (bf16[128,896]{1,0:T(8,128)(2,1)S(1)}, bf16[128,896]{1,0:T(8,128)(2,1)S(1)}, u32[]{:S(2)}, u32[]{:S(2)}) collective-permute-start(bf16[128,896]{1,0:T(8,128)(2,1)S(1)} %get-tuple-element.56), channel_id=1, source_target_pairs={{0,16},{16,0},{1,17},{17,1},{2,18},{18,2},{3,19},{19,3},{4,20},{20... | collective-permute-start | bytes 688136 | tf_op jit(solution)/shard_map/ppermute | solution.py:39
  96.9 2.3 %collective-permute-start.17 = (bf16[128,896]{1,0:T(8,128)(2,1)S(1)}, bf16[128,896]{1,0:T(8,128)(2,1)S(1)}, u32[]{:S(2)}, u32[]{:S(2)}) collective-permute-start(bf16[128,896]{1,0:T(8,128)(2,1)S(1)} %get-tuple-element.57), channel_id=1, source_target_pairs={{0,24},{8,16},{16,8},{24,0},{1,25},{9,17},{17,9},{25,1},{2,26},{10... | collective-permute-start | bytes 688136 | tf_op jit(solution)/shard_map/ppermute | solution.py:39
  99.3 3.3 %collective-permute-done.16.refs_7_ = bf16[128,896]{1,0:T(8,128)(2,1)S(1)} collective-permute-done((bf16[128,896]{1,0:T(8,128)(2,1)S(1)}, bf16[128,896]{1,0:T(8,128)(2,1)S(1)}, u32[]{:S(2)}, u32[]{:S(2)}) %collective-permute-start.16) | collective-permute-done | bytes 229408 | tf_op jit(solution)/shard_map/ppermute | solution.py:39
  102.5 1.9 %collective-permute-start.21 = (bf16[256,512]{1,0:T(8,128)(2,1)S(1)}, bf16[256,512]{1,0:T(8,128)(2,1)S(1)}, u32[]{:S(2)}, u32[]{:S(2)}) collective-permute-start(bf16[256,512]{1,0:T(8,128)(2,1)S(1)} %bitcast.18), channel_id=1, source_target_pairs={{0,16},{16,0},{1,17},{17,1},{2,18},{18,2},{3,19},{19,3},{4,20},{20... | collective-permute-start | bytes 786440 | tf_op jit(solution)/shard_map/ppermute | solution.py:39
  104.4 6.0 %collective-permute-done.17.refs_11_ = bf16[128,896]{1,0:T(8,128)(2,1)S(1)} collective-permute-done((bf16[128,896]{1,0:T(8,128)(2,1)S(1)}, bf16[128,896]{1,0:T(8,128)(2,1)S(1)}, u32[]{:S(2)}, u32[]{:S(2)}) %collective-permute-start.17) | collective-permute-done | bytes 229408 | tf_op jit(solution)/shard_map/ppermute | solution.py:39
  110.4 1.9 %collective-permute-start.22 = (bf16[128,512]{1,0:T(8,128)(2,1)S(1)}, bf16[128,512]{1,0:T(8,128)(2,1)S(1)}, u32[]{:S(2)}, u32[]{:S(2)}) collective-permute-start(bf16[128,512]{1,0:T(8,128)(2,1)S(1)} %get-tuple-element.61.refs_2_), channel_id=1, source_target_pairs={{0,16},{16,0},{1,17},{17,1},{2,18},{18,2},{3,19},{19,3},{4,20},{20... | collective-permute-start | bytes 393224 | tf_op jit(solution)/shard_map/ppermute | solution.py:39
  112.3 3.8 %rotate.1 = (bf16[1664,896]{1,0:T(8,128)(2,1)S(1)}, bf16[256,896]{1,0:T(8,128)(2,1)S(1)}, bf16[128,896]{1,0:T(8,128)(2,1)S(1)}, bf16[128,128]{1,0:T(8,128)(2,1)S(1)}) custom-call(s32[4]{0:T(128)S(1)} %pad_add_fusion.where, s32[4]{0:T(128)S(1)} %copy-done.19, bf16[6,64,3328]{2,1,0:T(8,128)(2,1)S(1)} %bitcast.9, bf16[6,64,3328]{2,1,0:T(8,128)(2,1)S(1)} %bitcast.10, ...), custom_call_target="tpu_custom_call" | custom-call | tf_op jit(solution)/shard_map/rotate/pallas_call | solution.py:247
  116.2 3.4 %back_first.1.so_far = f32[4,128,896]{2,1,0:T(8,128)S(1)} custom-call(bf16[256,896]{1,0:T(8,128)(2,1)S(1)} %get-tuple-element.59.right, bf16[256,512]{1,0:T(8,128)(2,1)S(1)} %bitcast.19, bf16[256,512]{1,0:T(8,128)(2,1)S(1)} %collective-permute-done.18.refs_1_, bf16[128,512]{1,0:T(8,128)(2,1)S(1)} %get-tuple-element.61.refs_2_, ...), custom_call_target="tpu_custom_call" | custom-call | tf_op jit(solution)/shard_map/back_first/pallas_call | solution.py:287
  119.6 0.9 collective-permute-start.23
  120.4 0.3 collective-permute-start.24
  120.8 1.0 collective-permute-done.24.refs_3_
  121.8 5.3 %back.1 = bf16[8,72,896]{2,1,0:T(8,128)(2,1)S(1)} custom-call(s32[4]{0:T(128)S(1)} %pad_add_fusion.where, s32[16]{0:T(128)S(1)} %copy-done.21, f32[4,128,896]{2,1,0:T(8,128)S(1)} %back_first.1.so_far, f32[32,1664]{1,0:T(8,128)S(1)} %copy-done.16, bf16[256,896]{1,0:T(8,128)(2,1)S(1)} %get-tuple-element.59.right, ...), custom_call_target="tpu_custom_call" | custom-call | tf_op jit(solution)/shard_map/back/pallas_call | solution.py:337
  127.1 32.7 %all_to_all.20.parts = bf16[8,72,896]{2,1,0:T(8,128)(2,1)S(1)} all-to-all(bf16[8,72,896]{2,1,0:T(8,128)(2,1)S(1)} %back.1), channel_id=1, replica_groups=mesh['z'=8,'xh'=2,'c'=2,'y'=4,'xl'=2] {'z'}, dimensions={0} | all-to-all | bytes 2064384 | tf_op jit(solution)/shard_map/all_to_all | solution.py:34
  159.8 1.7 tile.1
  161.5 1.9 %collective-permute-start.25 = (bf16[16,1664]{1,0:T(8,128)(2,1)S(1)}, bf16[16,1664]{1,0:T(8,128)(2,1)S(1)}, u32[]{:S(2)}, u32[]{:S(2)}) collective-permute-start(bf16[16,1664]{1,0:T(8,128)(2,1)S(1)} %get-tuple-element.70), channel_id=1, source_target_pairs={{0,8},{8,0},{1,9},{9,1},{2,10},{10,2},{3,11},{11,3},{4,12},{12,4},... | collective-permute-start | bytes 159752 | tf_op jit(solution)/shard_map/ppermute | solution.py:39
  163.4 1.4 collective-permute-start.26
  164.8 1.8 %collective-permute-start.27 = (bf16[16,1664]{1,0:T(8,128)(2,1)S(1)}, bf16[16,1664]{1,0:T(8,128)(2,1)S(1)}, u32[]{:S(2)}, u32[]{:S(2)}) collective-permute-start(bf16[16,1664]{1,0:T(8,128)(2,1)S(1)} %get-tuple-element.72), channel_id=1, source_target_pairs={{0,24},{8,16},{16,8},{24,0},{1,25},{9,17},{17,9},{25,1},{2,26},{10... | collective-permute-start | bytes 159752 | tf_op jit(solution)/shard_map/ppermute | solution.py:39
  166.7 10.9 %all_to_all.21.score = f32[32,1,128]{2,1,0:T(1,128)S(1)} all-to-all(f32[32,1,128]{2,1,0:T(1,128)S(1)} %get-tuple-element.73), channel_id=1, replica_groups=mesh['z'=8,'xh'=2,'c'=2,'y'=4,'xl'=2] {'xh','c','y','xl'}, dimensions={0} | all-to-all | bytes 32768 | tf_op jit(solution)/shard_map/all_to_all | solution.py:34
  177.6 1.2 final.1
  (58 shorter events, 0.2 us)
Async XLA Ops:
  1.8 0.8 copy-start.17
  2.6 0.7 copy-start.18
  3.2 0.7 copy-start.20
  4.6 10.3 %collective-permute-start = (bf16[60,896]{1,0:T(8,128)(2,1)S(1)}, bf16[60,896]{1,0:T(8,128)(2,1)S(1)}, u32[]{:S(2)}, u32[]{:S(2)}) collective-permute-start(bf16[60,896]{1,0:T(8,128)(2,1)S(1)} %get-tuple-element.41), channel_id=1, source_target_pairs={{0,8},{8,0},{1,9},{9,1},{2,10},{10,2},{3,11},{11,3},{4,12},{12,4},... | collective-permute-start | bytes 322568 | tf_op jit(solution)/shard_map/ppermute | solution.py:39
  8.0 7.0 %collective-permute-start.1 = (bf16[60,896]{1,0:T(8,128)(2,1)S(1)}, bf16[60,896]{1,0:T(8,128)(2,1)S(1)}, u32[]{:S(2)}, u32[]{:S(2)}) collective-permute-start(bf16[60,896]{1,0:T(8,128)(2,1)S(1)} %get-tuple-element.42), channel_id=1, source_target_pairs={{0,16},{16,0},{1,17},{17,1},{2,18},{18,2},{3,19},{19,3},{4,20},{20... | collective-permute-start | bytes 322568 | tf_op jit(solution)/shard_map/ppermute | solution.py:39
  9.0 7.8 %collective-permute-start.2 = (bf16[60,896]{1,0:T(8,128)(2,1)S(1)}, bf16[60,896]{1,0:T(8,128)(2,1)S(1)}, u32[]{:S(2)}, u32[]{:S(2)}) collective-permute-start(bf16[60,896]{1,0:T(8,128)(2,1)S(1)} %get-tuple-element.43), channel_id=1, source_target_pairs={{0,24},{8,16},{16,8},{24,0},{1,25},{9,17},{17,9},{25,1},{2,26},{10... | collective-permute-start | bytes 322568 | tf_op jit(solution)/shard_map/ppermute | solution.py:39
  11.2 2.9 %copy-start = (f32[512,3328]{1,0:T(8,128)S(1)}, f32[512,3328]{1,0:T(8,128)}, u32[]{:S(2)}) copy-start(f32[512,3328]{1,0:T(8,128)} %corrected.9) | copy-start | bytes 20447236
  14.2 12.2 %copy-start.5 = (bf16[6,2048,64]{1,2,0:T(8,128)(2,1)S(1)}, bf16[6,2048,64]{1,2,0:T(8,128)(2,1)}, u32[]{:S(2)}) copy-start(bf16[6,2048,64]{1,2,0:T(8,128)(2,1)} %param.17) | copy-start | bytes 4718596
  14.2 12.2 %copy-start.6 = (bf16[2048,512]{1,0:T(8,128)(2,1)S(1)}, bf16[2048,512]{1,0:T(8,128)(2,1)}, u32[]{:S(2)}) copy-start(bf16[2048,512]{1,0:T(8,128)(2,1)} %basis.2) | copy-start | bytes 6291460
  14.2 12.2 %copy-start.19 = (s32[4]{0:T(128)S(1)}, s32[4]{0:T(128)}, u32[]{:S(2)}) copy-start(s32[4]{0:T(128)} %ids.3) | copy-start | bytes 52
  18.0 18.3 %collective-permute-start.3 = (bf16[240,896]{1,0:T(8,128)(2,1)S(1)}, bf16[240,896]{1,0:T(8,128)(2,1)S(1)}, u32[]{:S(2)}, u32[]{:S(2)}) collective-permute-start(bf16[240,896]{1,0:T(8,128)(2,1)S(1)} %arrange.1.refs_0_), channel_id=1, source_target_pairs={{0,32},{32,64},{64,96},{96,128},{128,160},{160,192},{192,224},{224... | collective-permute-start | bytes 1290248 | tf_op jit(solution)/shard_map/ppermute | solution.py:44
  18.5 17.8 %collective-permute-start.4 = (bf16[240,896]{1,0:T(8,128)(2,1)S(1)}, bf16[240,896]{1,0:T(8,128)(2,1)S(1)}, u32[]{:S(2)}, u32[]{:S(2)}) collective-permute-start(bf16[240,896]{1,0:T(8,128)(2,1)S(1)} %arrange.1.refs_0_), channel_id=1, source_target_pairs={{0,224},{32,0},{64,32},{96,64},{128,96},{160,128},{192,160},{224,1... | collective-permute-start | bytes 1290248 | tf_op jit(solution)/shard_map/ppermute | solution.py:44
  22.6 8.0 %collective-permute-start.5 = (bf16[128,896]{1,0:T(8,128)(2,1)S(1)}, bf16[128,896]{1,0:T(8,128)(2,1)S(1)}, u32[]{:S(2)}, u32[]{:S(2)}) collective-permute-start(bf16[128,896]{1,0:T(8,128)(2,1)S(1)} %get-tuple-element.39), channel_id=1, source_target_pairs={{0,16},{16,0},{1,17},{17,1},{2,18},{18,2},{3,19},{19,3},{4,20},{20... | collective-permute-start | bytes 688136 | tf_op jit(solution)/shard_map/ppermute | solution.py:39
  24.8 11.5 %collective-permute-start.6 = (bf16[128,896]{1,0:T(8,128)(2,1)S(1)}, bf16[128,896]{1,0:T(8,128)(2,1)S(1)}, u32[]{:S(2)}, u32[]{:S(2)}) collective-permute-start(bf16[128,896]{1,0:T(8,128)(2,1)S(1)} %get-tuple-element.44), channel_id=1, source_target_pairs={{0,24},{8,16},{16,8},{24,0},{1,25},{9,17},{17,9},{25,1},{2,26},{10... | collective-permute-start | bytes 688136 | tf_op jit(solution)/shard_map/ppermute | solution.py:39
  30.6 8.5 %copy-start.8 = (bf16[128,896]{1,0:T(8,128)(2,1)}, bf16[128,896]{1,0:T(8,128)(2,1)S(1)}, u32[]{:S(2)}) copy-start(bf16[128,896]{1,0:T(8,128)(2,1)S(1)} %collective-permute-done.5.refs_4_) | copy-start | bytes 688132
  36.3 2.8 %copy-start.10 = (bf16[128,896]{1,0:T(8,128)(2,1)}, bf16[128,896]{1,0:T(8,128)(2,1)S(1)}, u32[]{:S(2)}) copy-start(bf16[128,896]{1,0:T(8,128)(2,1)S(1)} %collective-permute-done.6.refs_8_) | copy-start | bytes 688132
  36.3 25.1 %collective-permute-start.7 = (bf16[240,896]{1,0:T(8,128)(2,1)S(1)}, bf16[240,896]{1,0:T(8,128)(2,1)}, u32[]{:S(2)}, u32[]{:S(2)}) collective-permute-start(bf16[240,896]{1,0:T(8,128)(2,1)S(1)} %collective-permute-done.3.refs_1_), channel_id=1, source_target_pairs={{0,32},{32,64},{64,96},{96,128},{128,160},{160,192},{192,224},{224... | collective-permute-start | bytes 1290248 | tf_op jit(solution)/shard_map/ppermute | solution.py:44
  36.4 25.0 %collective-permute-start.8 = (bf16[240,896]{1,0:T(8,128)(2,1)S(1)}, bf16[240,896]{1,0:T(8,128)(2,1)}, u32[]{:S(2)}, u32[]{:S(2)}) collective-permute-start(bf16[240,896]{1,0:T(8,128)(2,1)S(1)} %collective-permute-done.4.refs_7_), channel_id=1, source_target_pairs={{0,224},{32,0},{64,32},{96,64},{128,96},{160,128},{192,160},{224,1... | collective-permute-start | bytes 1290248 | tf_op jit(solution)/shard_map/ppermute | solution.py:44
  39.1 13.1 %all-to-all-start = ((bf16[8,48,512]{2,1,0:T(8,128)(2,1)}), bf16[8,48,512]{2,1,0:T(8,128)(2,1)S(1)}, u32[]{:S(2)}, u32[]{:S(2)}) async-start(bf16[8,48,512]{2,1,0:T(8,128)(2,1)} %left.1), calls=%async_computation | async-start | bytes 786432 | tf_op jit(solution)/shard_map/all_to_all | solution.py:34
  43.7 2.9 %copy-start.1 = (f32[512,3328]{1,0:T(8,128)S(1)}, f32[512,3328]{1,0:T(8,128)}, u32[]{:S(2)}) copy-start(f32[512,3328]{1,0:T(8,128)} %corrected.9) | copy-start | bytes 20447236
  47.4 9.5 %collective-permute-start.10 = (bf16[128,896]{1,0:T(8,128)(2,1)S(1)}, bf16[128,896]{1,0:T(8,128)(2,1)S(1)}, u32[]{:S(2)}, u32[]{:S(2)}) collective-permute-start(bf16[128,896]{1,0:T(8,128)(2,1)S(1)} %get-tuple-element.48), channel_id=1, source_target_pairs={{0,24},{8,16},{16,8},{24,0},{1,25},{9,17},{17,9},{25,1},{2,26},{10... | collective-permute-start | bytes 688136 | tf_op jit(solution)/shard_map/ppermute | solution.py:39
  50.4 11.1 %collective-permute-start.9 = (bf16[128,896]{1,0:T(8,128)(2,1)S(1)}, bf16[128,896]{1,0:T(8,128)(2,1)S(1)}, u32[]{:S(2)}, u32[]{:S(2)}) collective-permute-start(bf16[128,896]{1,0:T(8,128)(2,1)S(1)} %get-tuple-element.47), channel_id=1, source_target_pairs={{0,16},{16,0},{1,17},{17,1},{2,18},{18,2},{3,19},{19,3},{4,20},{20... | collective-permute-start | bytes 688136 | tf_op jit(solution)/shard_map/ppermute | solution.py:39
  52.2 0.7 copy-start.7
  56.9 12.4 %copy-start.12 = (bf16[128,896]{1,0:T(8,128)(2,1)}, bf16[128,896]{1,0:T(8,128)(2,1)S(1)}, u32[]{:S(2)}) copy-start(bf16[128,896]{1,0:T(8,128)(2,1)S(1)} %collective-permute-done.10.refs_9_) | copy-start | bytes 688132
  61.4 7.9 %copy-start.14 = (bf16[128,896]{1,0:T(8,128)(2,1)}, bf16[128,896]{1,0:T(8,128)(2,1)S(1)}, u32[]{:S(2)}) copy-start(bf16[128,896]{1,0:T(8,128)(2,1)S(1)} %collective-permute-done.9.refs_5_) | copy-start | bytes 688132
  61.5 29.8 %collective-permute-start.11 = (bf16[240,896]{1,0:T(8,128)(2,1)}, bf16[240,896]{1,0:T(8,128)(2,1)}, u32[]{:S(2)}, u32[]{:S(2)}) collective-permute-start(bf16[240,896]{1,0:T(8,128)(2,1)} %collective-permute-done.7.refs_2_), channel_id=1, source_target_pairs={{0,32},{32,64},{64,96},{96,128},{128,160},{160,192},{192,224},{224... | collective-permute-start | bytes 1290248 | tf_op jit(solution)/shard_map/ppermute | solution.py:44
  61.5 29.7 %collective-permute-start.12 = (bf16[240,896]{1,0:T(8,128)(2,1)}, bf16[240,896]{1,0:T(8,128)(2,1)}, u32[]{:S(2)}, u32[]{:S(2)}) collective-permute-start(bf16[240,896]{1,0:T(8,128)(2,1)} %collective-permute-done.8.refs_6_), channel_id=1, source_target_pairs={{0,224},{32,0},{64,32},{96,64},{128,96},{160,128},{192,160},{224,1... | collective-permute-start | bytes 1290248 | tf_op jit(solution)/shard_map/ppermute | solution.py:44
  64.2 2.9 %copy-start.2 = (f32[512,3328]{1,0:T(8,128)S(1)}, f32[512,3328]{1,0:T(8,128)}, u32[]{:S(2)}) copy-start(f32[512,3328]{1,0:T(8,128)} %corrected.9) | copy-start | bytes 20447236
  69.3 46.8 %collective-permute-start.20 = (bf16[512,896]{1,0:T(8,128)(2,1)}, bf16[512,896]{1,0:T(8,128)(2,1)S(1)}, u32[]{:S(2)}, u32[]{:S(2)}) collective-permute-start(bf16[512,896]{1,0:T(8,128)(2,1)} %get-tuple-element.63), channel_id=1, source_target_pairs={{0,8},{8,0},{1,9},{9,1},{2,10},{10,2},{3,11},{11,3},{4,12},{12,4},... | collective-permute-start | bytes 2752520 | tf_op jit(solution)/shard_map/ppermute | solution.py:39
  72.2 9.1 %collective-permute-start.13 = (bf16[128,896]{1,0:T(8,128)(2,1)}, bf16[128,896]{1,0:T(8,128)(2,1)}, u32[]{:S(2)}, u32[]{:S(2)}) collective-permute-start(bf16[128,896]{1,0:T(8,128)(2,1)} %get-tuple-element.53), channel_id=1, source_target_pairs={{0,16},{16,0},{1,17},{17,1},{2,18},{18,2},{3,19},{19,3},{4,20},{20... | collective-permute-start | bytes 688136 | tf_op jit(solution)/shard_map/ppermute | solution.py:39
  74.9 12.0 %collective-permute-start.14 = (bf16[128,896]{1,0:T(8,128)(2,1)}, bf16[128,896]{1,0:T(8,128)(2,1)}, u32[]{:S(2)}, u32[]{:S(2)}) collective-permute-start(bf16[128,896]{1,0:T(8,128)(2,1)} %get-tuple-element.54), channel_id=1, source_target_pairs={{0,24},{8,16},{16,8},{24,0},{1,25},{9,17},{17,9},{25,1},{2,26},{10... | collective-permute-start | bytes 688136 | tf_op jit(solution)/shard_map/ppermute | solution.py:39
  75.4 15.8 %all-to-all-start.1 = ((bf16[8,32,512]{2,1,0:T(8,128)(2,1)}), bf16[8,32,512]{2,1,0:T(8,128)(2,1)S(1)}, u32[]{:S(2)}, u32[]{:S(2)}) async-start(bf16[8,32,512]{2,1,0:T(8,128)(2,1)} %copy-done.7), calls=%async_computation.1 | async-start | bytes 524288 | tf_op jit(solution)/shard_map/all_to_all | solution.py:34
  91.2 19.2 %collective-permute-start.15 = (bf16[240,896]{1,0:T(8,128)(2,1)}, bf16[240,896]{1,0:T(8,128)(2,1)S(1)}, u32[]{:S(2)}, u32[]{:S(2)}) collective-permute-start(bf16[240,896]{1,0:T(8,128)(2,1)} %collective-permute-done.11.refs_3_), channel_id=1, source_target_pairs={{0,32},{32,64},{64,96},{96,128},{128,160},{160,192},{192,224},{224... | collective-permute-start | bytes 1290248 | tf_op jit(solution)/shard_map/ppermute | solution.py:44
  91.2 2.9 %copy-start.3 = (f32[512,3328]{1,0:T(8,128)S(1)}, f32[512,3328]{1,0:T(8,128)}, u32[]{:S(2)}) copy-start(f32[512,3328]{1,0:T(8,128)} %corrected.9) | copy-start | bytes 20447236
  94.2 18.1 %copy-start.4 = (bf16[6,3328,64]{1,2,0:T(8,128)(2,1)S(1)}, bf16[6,3328,64]{1,2,0:T(8,128)(2,1)}, u32[]{:S(2)}) copy-start(bf16[6,3328,64]{1,2,0:T(8,128)(2,1)} %param.18) | copy-start | bytes 7667716
  94.9 7.6 %collective-permute-start.16 = (bf16[128,896]{1,0:T(8,128)(2,1)S(1)}, bf16[128,896]{1,0:T(8,128)(2,1)S(1)}, u32[]{:S(2)}, u32[]{:S(2)}) collective-permute-start(bf16[128,896]{1,0:T(8,128)(2,1)S(1)} %get-tuple-element.56), channel_id=1, source_target_pairs={{0,16},{16,0},{1,17},{17,1},{2,18},{18,2},{3,19},{19,3},{4,20},{20... | collective-permute-start | bytes 688136 | tf_op jit(solution)/shard_map/ppermute | solution.py:39
  96.9 13.5 %collective-permute-start.17 = (bf16[128,896]{1,0:T(8,128)(2,1)S(1)}, bf16[128,896]{1,0:T(8,128)(2,1)S(1)}, u32[]{:S(2)}, u32[]{:S(2)}) collective-permute-start(bf16[128,896]{1,0:T(8,128)(2,1)S(1)} %get-tuple-element.57), channel_id=1, source_target_pairs={{0,24},{8,16},{16,8},{24,0},{1,25},{9,17},{17,9},{25,1},{2,26},{10... | collective-permute-start | bytes 688136 | tf_op jit(solution)/shard_map/ppermute | solution.py:39
  99.2 16.9 %collective-permute-start.18 = (bf16[256,512]{1,0:T(8,128)(2,1)S(1)}, bf16[256,512]{1,0:T(8,128)(2,1)S(1)}, u32[]{:S(2)}, u32[]{:S(2)}) collective-permute-start(bf16[256,512]{1,0:T(8,128)(2,1)S(1)} %bitcast.17), channel_id=1, source_target_pairs={{0,8},{8,0},{1,9},{9,1},{2,10},{10,2},{3,11},{11,3},{4,12},{12,4},... | collective-permute-start | bytes 786440 | tf_op jit(solution)/shard_map/ppermute | solution.py:39
  102.5 17.0 %collective-permute-start.21 = (bf16[256,512]{1,0:T(8,128)(2,1)S(1)}, bf16[256,512]{1,0:T(8,128)(2,1)S(1)}, u32[]{:S(2)}, u32[]{:S(2)}) collective-permute-start(bf16[256,512]{1,0:T(8,128)(2,1)S(1)} %bitcast.18), channel_id=1, source_target_pairs={{0,16},{16,0},{1,17},{17,1},{2,18},{18,2},{3,19},{19,3},{4,20},{20... | collective-permute-start | bytes 786440 | tf_op jit(solution)/shard_map/ppermute | solution.py:39
  110.4 5.8 %collective-permute-start.19 = (bf16[128,512]{1,0:T(8,128)(2,1)S(1)}, bf16[128,512]{1,0:T(8,128)(2,1)S(1)}, u32[]{:S(2)}, u32[]{:S(2)}) collective-permute-start(bf16[128,512]{1,0:T(8,128)(2,1)S(1)} %get-tuple-element.61.refs_2_), channel_id=1, source_target_pairs={{0,8},{8,0},{1,9},{9,1},{2,10},{10,2},{3,11},{11,3},{4,12},{12,4},... | collective-permute-start | bytes 393224 | tf_op jit(solution)/shard_map/ppermute | solution.py:39
  110.4 9.2 %collective-permute-start.22 = (bf16[128,512]{1,0:T(8,128)(2,1)S(1)}, bf16[128,512]{1,0:T(8,128)(2,1)S(1)}, u32[]{:S(2)}, u32[]{:S(2)}) collective-permute-start(bf16[128,512]{1,0:T(8,128)(2,1)S(1)} %get-tuple-element.61.refs_2_), channel_id=1, source_target_pairs={{0,16},{16,0},{1,17},{17,1},{2,18},{18,2},{3,19},{19,3},{4,20},{20... | collective-permute-start | bytes 393224 | tf_op jit(solution)/shard_map/ppermute | solution.py:39
  116.1 5.7 %copy-start.9 = (bf16[128,896]{1,0:T(8,128)(2,1)S(1)}, bf16[128,896]{1,0:T(8,128)(2,1)}, u32[]{:S(2)}) copy-start(bf16[128,896]{1,0:T(8,128)(2,1)} %copy-done.8) | copy-start | bytes 688132
  116.1 5.7 %copy-start.11 = (bf16[128,896]{1,0:T(8,128)(2,1)S(1)}, bf16[128,896]{1,0:T(8,128)(2,1)}, u32[]{:S(2)}) copy-start(bf16[128,896]{1,0:T(8,128)(2,1)} %copy-done.10) | copy-start | bytes 688132
  116.1 5.7 %copy-start.13 = (bf16[128,896]{1,0:T(8,128)(2,1)S(1)}, bf16[128,896]{1,0:T(8,128)(2,1)}, u32[]{:S(2)}) copy-start(bf16[128,896]{1,0:T(8,128)(2,1)} %copy-done.12) | copy-start | bytes 688132
  116.1 5.7 %copy-start.15 = (bf16[128,896]{1,0:T(8,128)(2,1)S(1)}, bf16[128,896]{1,0:T(8,128)(2,1)}, u32[]{:S(2)}) copy-start(bf16[128,896]{1,0:T(8,128)(2,1)} %copy-done.14) | copy-start | bytes 688132
  116.1 5.7 %copy-start.16 = (f32[32,1664]{1,0:T(8,128)S(1)}, f32[32,1664]{1,0:T(8,128)}, u32[]{:S(2)}) copy-start(f32[32,1664]{1,0:T(8,128)} %factors.1) | copy-start | bytes 638980
  116.1 5.7 %copy-start.21 = (s32[16]{0:T(128)S(1)}, s32[16]{0:T(128)}, u32[]{:S(2)}) copy-start(s32[16]{0:T(128)} %block_ids.1) | copy-start | bytes 196
  119.6 2.2 %collective-permute-start.23 = (bf16[256,512]{1,0:T(8,128)(2,1)S(1)}, bf16[256,512]{1,0:T(8,128)(2,1)S(1)}, u32[]{:S(2)}, u32[]{:S(2)}) collective-permute-start(bf16[256,512]{1,0:T(8,128)(2,1)S(1)} %collective-permute-done.21.refs_0_), channel_id=1, source_target_pairs={{0,8},{8,0},{1,9},{9,1},{2,10},{10,2},{3,11},{11,3},{4,12},{12,4},... | collective-permute-start | bytes 786440 | tf_op jit(solution)/shard_map/ppermute | solution.py:39
  120.4 1.3 collective-permute-start.24
  161.5 16.0 %collective-permute-start.25 = (bf16[16,1664]{1,0:T(8,128)(2,1)S(1)}, bf16[16,1664]{1,0:T(8,128)(2,1)S(1)}, u32[]{:S(2)}, u32[]{:S(2)}) collective-permute-start(bf16[16,1664]{1,0:T(8,128)(2,1)S(1)} %get-tuple-element.70), channel_id=1, source_target_pairs={{0,8},{8,0},{1,9},{9,1},{2,10},{10,2},{3,11},{11,3},{4,12},{12,4},... | collective-permute-start | bytes 159752 | tf_op jit(solution)/shard_map/ppermute | solution.py:39
  163.4 14.1 %collective-permute-start.26 = (bf16[16,1664]{1,0:T(8,128)(2,1)S(1)}, bf16[16,1664]{1,0:T(8,128)(2,1)S(1)}, u32[]{:S(2)}, u32[]{:S(2)}) collective-permute-start(bf16[16,1664]{1,0:T(8,128)(2,1)S(1)} %get-tuple-element.71), channel_id=1, source_target_pairs={{0,16},{16,0},{1,17},{17,1},{2,18},{18,2},{3,19},{19,3},{4,20},{20... | collective-permute-start | bytes 159752 | tf_op jit(solution)/shard_map/ppermute | solution.py:39
  164.8 12.7 %collective-permute-start.27 = (bf16[16,1664]{1,0:T(8,128)(2,1)S(1)}, bf16[16,1664]{1,0:T(8,128)(2,1)S(1)}, u32[]{:S(2)}, u32[]{:S(2)}) collective-permute-start(bf16[16,1664]{1,0:T(8,128)(2,1)S(1)} %get-tuple-element.72), channel_id=1, source_target_pairs={{0,24},{8,16},{16,8},{24,0},{1,25},{9,17},{17,9},{25,1},{2,26},{10... | collective-permute-start | bytes 159752 | tf_op jit(solution)/shard_map/ppermute | solution.py:39

commit v4 on v3

--- a/solution.py
+++ b/solution.py
@@ -109,32 +109,49 @@
     )(parts)
 
 
-def inverse_body(where, corrected, out_0, out_1, values, done, *, far, part):
-    rows, block = values.shape
-    blk = where[1] ^ far
-    source = corrected.at[
-        pl.ds(part * rows, rows), pl.ds(pl.multiple_of(blk * block, LANES), block)
-    ]
-    copy = pltpu.make_async_copy(source, values, done)
-    copy.start()
-    copy.wait()
-    for r, out in enumerate((out_0, out_1)):
-        skip = block - out.shape[1]
-        at = pl.multiple_of((where[3] ^ r) * skip, LANES)
-        out[...] = (1.0 / values[:, pl.ds(at, out.shape[1])]).astype(BF)
-
-
-def inverse_halves(where, corrected, block, width, far, parts=1, part=0):
-    rows = corrected.shape[0] // parts
-    return pl.pallas_call(
-        functools.partial(inverse_body, far=far, part=part),
-        out_shape=tuple(jax.ShapeDtypeStruct((rows, width), BF) for _ in range(2)),
-        in_specs=[SMEM_SPEC, pl.BlockSpec(memory_space=pltpu.HBM)],
-        out_specs=(VMEM_SPEC, VMEM_SPEC),
-        scratch_shapes=[pltpu.VMEM((rows, block), F32), pltpu.SemaphoreType.DMA],
-        compiler_params=params(12),
+def inverse_body(where, corrected, *outs):
+    width = outs[0].shape[1]
+    skip = corrected.shape[1] - width
+    for r, out in enumerate(outs):
+        at = pl.multiple_of((where[3] ^ r) * skip, LANES) if skip else 0
+        out[...] = (1.0 / corrected[:, pl.ds(at, width)]).astype(BF)
+
+
+def inverse_block(where, corrected, block, far, width, count):
+    rows = corrected.shape[0]
+    tile = 128
+    return pl.pallas_call(
+        inverse_body,
+        out_shape=tuple(jax.ShapeDtypeStruct((rows, width), BF) for _ in range(count)),
+        grid_spec=pltpu.PrefetchScalarGridSpec(
+            num_scalar_prefetch=1,
+            grid=(rows // tile,),
+            in_specs=[pl.BlockSpec((tile, block), lambda n, w: (n, w[1] ^ far))],
+            out_specs=tuple(
+                pl.BlockSpec((tile, width), lambda n, w: (n, 0)) for _ in range(count)
+            ),
+        ),
+        compiler_params=params(58),
         name="inverse",
     )(where, corrected)
+
+
+def halves_body(where, block, own, other):
+    width = own.shape[1]
+    skip = block.shape[1] - width
+    for r, out in enumerate((own, other)):
+        out[...] = block[:, pl.ds(pl.multiple_of((where[3] ^ r) * skip, LANES), width)]
+
+
+def halves(where, block, width):
+    return pl.pallas_call(
+        halves_body,
+        out_shape=tuple(jax.ShapeDtypeStruct((block.shape[0], width), BF) for _ in range(2)),
+        in_specs=[SMEM_SPEC, VMEM_SPEC],
+        out_specs=(VMEM_SPEC, VMEM_SPEC),
+        compiler_params=params(10),
+        name="halves",
+    )(where, block)
 
 
 def pack_body(where, train_ids, basis, tokens, delta, *outs):
@@ -448,40 +465,36 @@
         swap(packed[2], "xh"),
         swap(packed[3], QUAD, 3),
     )
-    pieces = n_z // 2
-    far = [inverse_halves(where, corrected, block, width, 1, pieces, k) for k in range(pieces)]
-    own = arrange(where, (after(packed[0], far[0][0]), *parts[1:]), local_rows, train)
-    far = [(swap(a, "xh"), swap(b, QUAD, 3)) for a, b in far]
-    near = inverse_halves(where, corrected, block, width, 0)
+    (far,) = inverse_block(where, corrected, block, 1, block, 1)
+    own = arrange(where, (after(packed[0], far), *parts[1:]), local_rows, train)
+    far = swap(far, "xh")
+    near = inverse_block(where, corrected, block, 0, width, 2)
     near = (near[0], swap(near[1], "c"))
 
     partial = left_part(query_ids, jnp.transpose(u_pool, (0, 2, 1)), basis_out, n_in)
     ahead, behind = [shift(own, 1)], [shift(own, -1)]
-    up, down = after((ahead[0], behind[0]), far[0], partial)
+    up, down = after((ahead[0], behind[0]), partial)
     ahead.append(shift(up, 1))
     behind.append(shift(down, -1))
     spread, window = left_sum(exchange(partial, IN))
-    up, down = after((ahead[1], behind[1]), far[1], spread)
+    up, down = after((ahead[1], behind[1]), spread)
     ahead.append(shift(up, 1))
     behind.append(shift(down, -1))
     left = exchange(spread, IN).reshape(-1, basis_out.shape[1])
-    up, left, window = after((ahead[2], left, window), behind[2], far[2])
+    up, left, window = after((ahead[2], left, window), behind[2])
     ahead.append(shift(up, 1))
     left_x, window_x = swap(left, "xh"), swap(window, "xh")
     lefts = (left, swap(left, "c"))
     windows = (window, swap(window, "c"))
-    chunks = (own, *ahead[:3], after(ahead[3], far[3]), *behind[::-1])
+    chunks = (own, *ahead, *behind[::-1])
 
     basis, right, tokens, delta = rotate(
         where, query_ids, jnp.transpose(v_pool, (0, 2, 1)), chunks, block
     )
     so_far = back_first(right, lefts, windows, near, queries)
-    left_x, window_x = after((left_x, window_x), so_far)
-    far = (
-        *(left_x, swap(left_x, "c"), window_x, swap(window_x, "c")),
-        *(a for a, _ in far),
-        *(b for _, b in far),
-    )
+    left_x, window_x, far = after((left_x, window_x, far), so_far)
+    far = halves(where, far, width)
+    far = (left_x, swap(left_x, "c"), window_x, swap(window_x, "c"), far[0], swap(far[1], "c"))
     parts = back(
         where, block_ids, so_far, factor_table, right, tokens, delta, far, n_z, train
     )

time: 179 us -> 165 us (0.922)
  local copies, waits for them, and re-layouts: 15.7 us -> 3.86 us
  starting transfers between devices: 52.7 us -> 41.6 us
  blocking collectives: 43.6 us -> 51.6 us
  Pallas kernels: 25.5 us -> 31.6 us
  waiting for transfers between devices: 40.2 us -> 35.2 us
    ppermute x21 -> x15, waiting for transfers between devices: 34.5 us -> 2.83 us  [swap(): return lax.ppermute(value, axis, [(i, i ^ mask) for i in range(size)])]
    all_to_all x2 -> x1, waiting for transfers between devices: 5.73 us -> 22.3 us  [exchange(): return lax.all_to_all(value, axis, split_axis=0, concat_axis=0, tiled=True)]
    unnamed x45 -> x27, local copies, waits for them, and re-layouts: 15.7 us -> 3.86 us
    ppermute x7, waiting for transfers between devices: 0.02 us -> 10.1 us  [shift(): lax.ppermute(value, 'z', [(i, (i + step) % size) for i in range(size)])]
    all_to_all x2 -> x3, blocking collectives: 43.6 us -> 51.6 us  [exchange(): return lax.all_to_all(value, axis, split_axis=0, concat_axis=0, tiled=True)]
    ppermute x21 -> x15, starting transfers between devices: 32.7 us -> 27 us  [swap(): return lax.ppermute(value, axis, [(i, i ^ mask) for i in range(size)])]
    pallas_call x5 -> x3, Pallas kernels: 5.87 us -> 11.4 us  [the longest x2 9.84 us: inverse_block(): pl.pallas_call(inverse_body, out_shape=tuple((jax.ShapeDtypeStruct((rows,...]
    all_to_all x2 -> x1, starting transfers between devices: 10 us -> 4.55 us  [exchange(): return lax.all_to_all(value, axis, split_axis=0, concat_axis=0, tiled=True)]
  transfers between devices with their start and end apart: 30 -> 23, of which waited for: 12 -> 6; matrix products, arithmetic and copies ran while one was open for 0% -> 0% of each run, Pallas kernels for 9% -> 12%
where the time goes in v4:
time: 165 us
  blocking collectives  51.6 us (31%)
  starting transfers between devices  41.6 us (25%)
  waiting for transfers between devices  35.2 us (21%)
  Pallas kernels  31.6 us (19%)
  local copies, waits for them, and re-layouts  3.86 us (2%)
    all_to_all x3, blocking collectives, exchange(): return lax.all_to_all(value, axis, split_axis=0, concat_axis=0, tiled=True)  51.6 us
    ppermute x15, starting transfers between devices, swap(): return lax.ppermute(value, axis, [(i, i ^ mask) for i in range(size)])  27 us
    all_to_all x1, waiting for transfers between devices, exchange(): return lax.all_to_all(value, axis, split_axis=0, concat_axis=0, tiled=True)  22.3 us
    ppermute x7, waiting for transfers between devices, shift(): lax.ppermute(value, 'z', [(i, (i + step) % size) for i in range(size)])  10.1 us
    ppermute x7, starting transfers between devices, shift(): lax.ppermute(value, 'z', [(i, (i + step) % size) for i in range(size)])  9.97 us
    pallas_call x2, Pallas kernels, inverse_block(): pl.pallas_call(inverse_body, out_shape=tuple((jax.ShapeDtypeStruct((rows,...  9.84 us
    pallas_call x1, Pallas kernels, back(): pl.pallas_call(functools.partial(back_body, train=train), out_shape=jax.S...  4.73 us
    all_to_all x1, starting transfers between devices, exchange(): return lax.all_to_all(value, axis, split_axis=0, concat_axis=0, tiled=True)  4.55 us
  transfers between devices with their start and end apart: 23, of which 6 were waited for; matrix products, arithmetic and copies ran while one was open for 0% of the time, Pallas kernels for 12%

profile of v4, /device:TPU:1, one launch (start us, length us, event | category | flops | bytes accessed | tf_op | source)
XLA Modules:
  0.0 164.7 jit_solution(17626100671043289973)
XLA Ops:
  0.6 1.0 copy.13.basis
  1.7 0.1 pad_add_fusion.where
  1.8 0.8 copy-done.5
  2.6 0.7 copy-done.9
  3.2 0.7 copy-done.11
  3.9 0.7 pack.1
  4.7 3.3 %collective-permute-start = (bf16[60,896]{1,0:T(8,128)(2,1)S(1)}, bf16[60,896]{1,0:T(8,128)(2,1)S(1)}, u32[]{:S(2)}, u32[]{:S(2)}) collective-permute-start(bf16[60,896]{1,0:T(8,128)(2,1)S(1)} %get-tuple-element.34), channel_id=1, source_target_pairs={{0,8},{8,0},{1,9},{9,1},{2,10},{10,2},{3,11},{11,3},{4,12},{12,4},... | collective-permute-start | bytes 322568 | tf_op jit(solution)/shard_map/ppermute | solution.py:39
  8.0 1.0 collective-permute-start.1
  9.0 2.2 %collective-permute-start.2 = (bf16[60,896]{1,0:T(8,128)(2,1)S(1)}, bf16[60,896]{1,0:T(8,128)(2,1)S(1)}, u32[]{:S(2)}, u32[]{:S(2)}) collective-permute-start(bf16[60,896]{1,0:T(8,128)(2,1)S(1)} %get-tuple-element.36), channel_id=1, source_target_pairs={{0,24},{8,16},{16,8},{24,0},{1,25},{9,17},{17,9},{25,1},{2,26},{10... | collective-permute-start | bytes 322568 | tf_op jit(solution)/shard_map/ppermute | solution.py:39
  11.2 5.0 %inverse.2 = bf16[512,1664]{1,0:T(8,128)(2,1)} custom-call(s32[4]{0:T(128)} %copy-done.6, f32[512,3328]{1,0:T(8,128)} %corrected.3), custom_call_target="tpu_custom_call" | custom-call | tf_op jit(solution)/shard_map/inverse/pallas_call | solution.py:123
  16.2 0.0 collective-permute-done.a1
  16.2 0.0 collective-permute-done.1.a2
  16.2 0.6 collective-permute-done.2.a3
  16.8 0.7 copy-done.7
  17.5 1.2 arrange.1.refs_0_
  18.7 0.5 collective-permute-start.3
  19.2 4.0 %collective-permute-start.4 = (bf16[240,896]{1,0:T(8,128)(2,1)S(1)}, bf16[240,896]{1,0:T(8,128)(2,1)}, u32[]{:S(2)}, u32[]{:S(2)}) collective-permute-start(bf16[240,896]{1,0:T(8,128)(2,1)S(1)} %arrange.1.refs_0_), channel_id=1, source_target_pairs={{0,224},{32,0},{64,32},{96,64},{128,96},{160,128},{192,160},{224,1... | collective-permute-start | bytes 1290248 | tf_op jit(solution)/shard_map/ppermute | solution.py:44
  23.2 2.2 %collective-permute-start.15 = (bf16[512,1664]{1,0:T(8,128)(2,1)}, bf16[512,1664]{1,0:T(8,128)(2,1)}, u32[]{:S(2)}, u32[]{:S(2)}) collective-permute-start(bf16[512,1664]{1,0:T(8,128)(2,1)} %inverse.2), channel_id=1, source_target_pairs={{0,16},{16,0},{1,17},{17,1},{2,18},{18,2},{3,19},{19,3},{4,20},{20... | collective-permute-start | bytes 5111816 | tf_op jit(solution)/shard_map/ppermute | solution.py:39
  25.4 2.3 %left.1 = bf16[8,48,512]{2,1,0:T(8,128)(2,1)} custom-call(s32[4]{0:T(128)S(1)} %copy-done.10, bf16[6,64,2048]{2,1,0:T(8,128)(2,1)S(1)} %bitcast.13, bf16[6,64,2048]{2,1,0:T(8,128)(2,1)S(1)} %bitcast.14, bf16[6,64,2048]{2,1,0:T(8,128)(2,1)S(1)} %bitcast.15, bf16[6,64,2048]{2,1,0:T(8,128)(2,1)S(1)} %bitcast.16, bf16[2048,512]{1,0:T(8,128)(2,1)S(1)} %copy-done.2), custom_call_target="tpu_custom_call" | custom-call | tf_op jit(solution)/shard_map/left/pallas_call | solution.py:71
  27.7 5.5 %collective-permute-done.3.refs_1_ = bf16[240,896]{1,0:T(8,128)(2,1)} collective-permute-done((bf16[240,896]{1,0:T(8,128)(2,1)S(1)}, bf16[240,896]{1,0:T(8,128)(2,1)}, u32[]{:S(2)}, u32[]{:S(2)}) %collective-permute-start.3) | collective-permute-done | bytes 430112 | tf_op jit(solution)/shard_map/ppermute | solution.py:44
  33.2 0.0 collective-permute-done.4.refs_7_
  33.2 0.0 collective-permute-start.5
  33.2 2.7 %collective-permute-start.6 = (bf16[240,896]{1,0:T(8,128)(2,1)}, bf16[240,896]{1,0:T(8,128)(2,1)}, u32[]{:S(2)}, u32[]{:S(2)}) collective-permute-start(bf16[240,896]{1,0:T(8,128)(2,1)} %collective-permute-done.4.refs_7_), channel_id=1, source_target_pairs={{0,224},{32,0},{64,32},{96,64},{128,96},{160,128},{192,160},{224,1... | collective-permute-start | bytes 1290248 | tf_op jit(solution)/shard_map/ppermute | solution.py:44
  35.9 4.5 %all-to-all-start = ((bf16[8,48,512]{2,1,0:T(8,128)(2,1)}), bf16[8,48,512]{2,1,0:T(8,128)(2,1)S(1)}, u32[]{:S(2)}, u32[]{:S(2)}) async-start(bf16[8,48,512]{2,1,0:T(8,128)(2,1)} %left.1), calls=%async_computation | async-start | bytes 786432 | tf_op jit(solution)/shard_map/all_to_all | solution.py:34
  40.5 0.0 copy-start.8
  40.5 4.9 %inverse.3 = (bf16[512,896]{1,0:T(8,128)(2,1)}, bf16[512,896]{1,0:T(8,128)(2,1)}) custom-call(s32[4]{0:T(128)} %copy-done.6, f32[512,3328]{1,0:T(8,128)} %corrected.3), custom_call_target="tpu_custom_call" | custom-call | tf_op jit(solution)/shard_map/inverse/pallas_call | solution.py:123
  45.4 1.8 %collective-permute-start.12 = (bf16[512,896]{1,0:T(8,128)(2,1)}, bf16[512,896]{1,0:T(8,128)(2,1)}, u32[]{:S(2)}, u32[]{:S(2)}) collective-permute-start(bf16[512,896]{1,0:T(8,128)(2,1)} %get-tuple-element.48), channel_id=1, source_target_pairs={{0,8},{8,0},{1,9},{9,1},{2,10},{10,2},{3,11},{11,3},{4,12},{12,4},... | collective-permute-start | bytes 2752520 | tf_op jit(solution)/shard_map/ppermute | solution.py:39
  47.1 22.3 %all-to-all-done.parts = bf16[8,48,512]{2,1,0:T(8,128)(2,1)S(1)} async-done(((bf16[8,48,512]{2,1,0:T(8,128)(2,1)}), bf16[8,48,512]{2,1,0:T(8,128)(2,1)S(1)}, u32[]{:S(2)}, u32[]{:S(2)}) %all-to-all-start) | async-done | bytes 393248 | tf_op jit(solution)/shard_map/all_to_all | solution.py:34
  69.4 0.0 collective-permute-done.5.refs_2_
  69.4 0.0 collective-permute-done.6.refs_6_
  69.5 0.1 collective-permute-start.7
  69.5 2.7 %collective-permute-start.8 = (bf16[240,896]{1,0:T(8,128)(2,1)}, bf16[240,896]{1,0:T(8,128)(2,1)S(1)}, u32[]{:S(2)}, u32[]{:S(2)}) collective-permute-start(bf16[240,896]{1,0:T(8,128)(2,1)} %collective-permute-done.6.refs_6_), channel_id=1, source_target_pairs={{0,224},{32,0},{64,32},{96,64},{128,96},{160,128},{192,160},{224,1... | collective-permute-start | bytes 1290248 | tf_op jit(solution)/shard_map/ppermute | solution.py:44
  72.2 8.6 %all_to_all.20 = bf16[8,32,512]{2,1,0:T(8,128)(2,1)S(1)} all-to-all(bf16[8,32,512]{2,1,0:T(8,128)(2,1)S(1)} %get-tuple-element.39), channel_id=1, replica_groups=mesh['z'=8,'xh'=2,'c'=2,'y'=4,'xl'=2] {'y','xl'}, dimensions={0} | all-to-all | bytes 524288 | tf_op jit(solution)/shard_map/all_to_all | solution.py:34
  80.8 0.2 collective-permute-done.7.refs_3_
  81.0 0.0 collective-permute-done.8.refs_5_
  81.0 0.0 collective-permute-start.9
  81.0 3.2 %collective-permute-start.10 = (bf16[256,512]{1,0:T(8,128)(2,1)S(1)}, bf16[256,512]{1,0:T(8,128)(2,1)S(1)}, u32[]{:S(2)}, u32[]{:S(2)}) collective-permute-start(bf16[256,512]{1,0:T(8,128)(2,1)S(1)} %bitcast.17), channel_id=1, source_target_pairs={{0,8},{8,0},{1,9},{9,1},{2,10},{10,2},{3,11},{11,3},{4,12},{12,4},... | collective-permute-start | bytes 786440 | tf_op jit(solution)/shard_map/ppermute | solution.py:39
  84.2 1.5 collective-permute-start.13
  85.7 0.0 collective-permute-done.12.refs_5_
  85.7 0.4 collective-permute-start.11
  86.1 4.4 %collective-permute-done.9.refs_4_ = bf16[240,896]{1,0:T(8,128)(2,1)S(1)} collective-permute-done((bf16[240,896]{1,0:T(8,128)(2,1)S(1)}, bf16[240,896]{1,0:T(8,128)(2,1)S(1)}, u32[]{:S(2)}, u32[]{:S(2)}) %collective-permute-start.9) | collective-permute-done | bytes 430112 | tf_op jit(solution)/shard_map/ppermute | solution.py:44
  90.4 1.3 collective-permute-start.14
  91.8 3.8 %rotate.1 = (bf16[1664,896]{1,0:T(8,128)(2,1)S(1)}, bf16[256,896]{1,0:T(8,128)(2,1)S(1)}, bf16[128,896]{1,0:T(8,128)(2,1)S(1)}, bf16[128,128]{1,0:T(8,128)(2,1)S(1)}) custom-call(s32[4]{0:T(128)S(1)} %copy-done.8, s32[4]{0:T(128)S(1)} %copy-done.10, bf16[6,64,3328]{2,1,0:T(8,128)(2,1)S(1)} %bitcast.9, bf16[6,64,3328]{2,1,0:T(8,128)(2,1)S(1)} %bitcast.10, ...), custom_call_target="tpu_custom_call" | custom-call | tf_op jit(solution)/shard_map/rotate/pallas_call | solution.py:264
  95.5 0.0 collective-permute-done.10.refs_1_
  95.6 0.0 copy-start.4
  95.6 0.0 copy-start.12
  95.6 4.5 %back_first.1.so_far = f32[4,128,896]{2,1,0:T(8,128)S(1)} custom-call(bf16[256,896]{1,0:T(8,128)(2,1)S(1)} %get-tuple-element.44.right, bf16[256,512]{1,0:T(8,128)(2,1)S(1)} %bitcast.19, bf16[256,512]{1,0:T(8,128)(2,1)S(1)} %collective-permute-done.10.refs_1_, bf16[128,512]{1,0:T(8,128)(2,1)S(1)} %get-tuple-element.46.refs_2_, ...), custom_call_target="tpu_custom_call" | custom-call | tf_op jit(solution)/shard_map/back_first/pallas_call | solution.py:304
  100.1 0.0 collective-permute-done.13.refs_0_
  100.1 0.0 collective-permute-done.15.block
  100.1 1.6 halves.1
  101.7 4.5 %collective-permute-start.18 = (bf16[512,896]{1,0:T(8,128)(2,1)S(1)}, bf16[512,896]{1,0:T(8,128)(2,1)S(1)}, u32[]{:S(2)}, u32[]{:S(2)}) collective-permute-start(bf16[512,896]{1,0:T(8,128)(2,1)S(1)} %get-tuple-element.55), channel_id=1, source_target_pairs={{0,8},{8,0},{1,9},{9,1},{2,10},{10,2},{3,11},{11,3},{4,12},{12,4},... | collective-permute-start | bytes 2752520 | tf_op jit(solution)/shard_map/ppermute | solution.py:39
  106.2 0.1 collective-permute-start.16
  106.3 0.4 collective-permute-start.17
  106.7 2.2 %collective-permute-done.17.refs_3_ = bf16[128,512]{1,0:T(8,128)(2,1)S(1)} collective-permute-done((bf16[128,512]{1,0:T(8,128)(2,1)S(1)}, bf16[128,512]{1,0:T(8,128)(2,1)S(1)}, u32[]{:S(2)}, u32[]{:S(2)}) %collective-permute-start.17) | collective-permute-done | bytes 131104 | tf_op jit(solution)/shard_map/ppermute | solution.py:39
  108.9 4.7 %back.1 = bf16[8,72,896]{2,1,0:T(8,128)(2,1)S(1)} custom-call(s32[4]{0:T(128)S(1)} %copy-done.8, s32[16]{0:T(128)S(1)} %copy-done.12, f32[4,128,896]{2,1,0:T(8,128)S(1)} %back_first.1.so_far, f32[32,1664]{1,0:T(8,128)S(1)} %copy-done.4, bf16[256,896]{1,0:T(8,128)(2,1)S(1)} %get-tuple-element.44.right, bf16[128,896]{1,0:T(8,128)(2,1)S(1)} %get-tuple-element.49.tokens, ...), custom_call_target="tpu_custom_call" | custom-call | tf_op jit(solution)/shard_map/back/pallas_call | solution.py:354
  113.6 32.2 %all_to_all.21.parts = bf16[8,72,896]{2,1,0:T(8,128)(2,1)S(1)} all-to-all(bf16[8,72,896]{2,1,0:T(8,128)(2,1)S(1)} %back.1), channel_id=1, replica_groups=mesh['z'=8,'xh'=2,'c'=2,'y'=4,'xl'=2] {'z'}, dimensions={0} | all-to-all | bytes 2064384 | tf_op jit(solution)/shard_map/all_to_all | solution.py:34
  145.8 1.7 %tile.1 = (bf16[16,1664]{1,0:T(8,128)(2,1)S(1)}, bf16[16,1664]{1,0:T(8,128)(2,1)S(1)}, bf16[16,1664]{1,0:T(8,128)(2,1)S(1)}, bf16[16,1664]{1,0:T(8,128)(2,1)S(1)}, f32[32,1,128]{2,1,0:T(1,128)S(1)}) custom-call(s32[4]{0:T(128)S(1)} %copy-done.8, bf16[8,72,896]{2,1,0:T(8,128)(2,1)S(1)} %all_to_all.21.parts, bf16[1664,896]{1,0:T(8,128)(2,1)S(1)} %get-tuple-element.56.basis), custom_call_target="tpu_custom_call" | custom-call | tf_op jit(solution)/shard_map/tile/pallas_call | solution.py:398
  147.5 1.9 %collective-permute-start.19 = (bf16[16,1664]{1,0:T(8,128)(2,1)S(1)}, bf16[16,1664]{1,0:T(8,128)(2,1)S(1)}, u32[]{:S(2)}, u32[]{:S(2)}) collective-permute-start(bf16[16,1664]{1,0:T(8,128)(2,1)S(1)} %get-tuple-element.58), channel_id=1, source_target_pairs={{0,8},{8,0},{1,9},{9,1},{2,10},{10,2},{3,11},{11,3},{4,12},{12,4},... | collective-permute-start | bytes 159752 | tf_op jit(solution)/shard_map/ppermute | solution.py:39
  149.4 1.4 collective-permute-start.20
  150.8 1.8 %collective-permute-start.21 = (bf16[16,1664]{1,0:T(8,128)(2,1)S(1)}, bf16[16,1664]{1,0:T(8,128)(2,1)S(1)}, u32[]{:S(2)}, u32[]{:S(2)}) collective-permute-start(bf16[16,1664]{1,0:T(8,128)(2,1)S(1)} %get-tuple-element.60), channel_id=1, source_target_pairs={{0,24},{8,16},{16,8},{24,0},{1,25},{9,17},{17,9},{25,1},{2,26},{10... | collective-permute-start | bytes 159752 | tf_op jit(solution)/shard_map/ppermute | solution.py:39
  152.6 10.9 %all_to_all.22.score = f32[32,1,128]{2,1,0:T(1,128)S(1)} all-to-all(f32[32,1,128]{2,1,0:T(1,128)S(1)} %get-tuple-element.61), channel_id=1, replica_groups=mesh['z'=8,'xh'=2,'c'=2,'y'=4,'xl'=2] {'xh','c','y','xl'}, dimensions={0} | all-to-all | bytes 32768 | tf_op jit(solution)/shard_map/all_to_all | solution.py:34
  163.5 0.0 collective-permute-done.19.t1
  163.5 0.0 collective-permute-done.20.t2
  163.5 1.2 final.1
  (25 shorter events, 0.1 us)
Async XLA Ops:
  1.8 9.5 %copy-start.6 = (s32[4]{0:T(128)}, s32[4]{0:T(128)S(1)}, u32[]{:S(2)}) copy-start(s32[4]{0:T(128)S(1)} %pad_add_fusion.where) | copy-start | bytes 52
  1.8 0.8 copy-start.5
  2.6 0.7 copy-start.9
  3.2 0.7 copy-start.11
  4.7 11.5 %collective-permute-start = (bf16[60,896]{1,0:T(8,128)(2,1)S(1)}, bf16[60,896]{1,0:T(8,128)(2,1)S(1)}, u32[]{:S(2)}, u32[]{:S(2)}) collective-permute-start(bf16[60,896]{1,0:T(8,128)(2,1)S(1)} %get-tuple-element.34), channel_id=1, source_target_pairs={{0,8},{8,0},{1,9},{9,1},{2,10},{10,2},{3,11},{11,3},{4,12},{12,4},... | collective-permute-start | bytes 322568 | tf_op jit(solution)/shard_map/ppermute | solution.py:39
  8.0 8.2 %collective-permute-start.1 = (bf16[60,896]{1,0:T(8,128)(2,1)S(1)}, bf16[60,896]{1,0:T(8,128)(2,1)S(1)}, u32[]{:S(2)}, u32[]{:S(2)}) collective-permute-start(bf16[60,896]{1,0:T(8,128)(2,1)S(1)} %get-tuple-element.35), channel_id=1, source_target_pairs={{0,16},{16,0},{1,17},{17,1},{2,18},{18,2},{3,19},{19,3},{4,20},{20... | collective-permute-start | bytes 322568 | tf_op jit(solution)/shard_map/ppermute | solution.py:39
  9.0 16.4 %copy-start.1 = (bf16[6,2048,64]{1,2,0:T(8,128)(2,1)S(1)}, bf16[6,2048,64]{1,2,0:T(8,128)(2,1)}, u32[]{:S(2)}) copy-start(bf16[6,2048,64]{1,2,0:T(8,128)(2,1)} %param.17) | copy-start | bytes 4718596
  9.0 16.4 %copy-start.10 = (s32[4]{0:T(128)S(1)}, s32[4]{0:T(128)}, u32[]{:S(2)}) copy-start(s32[4]{0:T(128)} %ids.3) | copy-start | bytes 52
  9.0 7.8 %collective-permute-start.2 = (bf16[60,896]{1,0:T(8,128)(2,1)S(1)}, bf16[60,896]{1,0:T(8,128)(2,1)S(1)}, u32[]{:S(2)}, u32[]{:S(2)}) collective-permute-start(bf16[60,896]{1,0:T(8,128)(2,1)S(1)} %get-tuple-element.36), channel_id=1, source_target_pairs={{0,24},{8,16},{16,8},{24,0},{1,25},{9,17},{17,9},{25,1},{2,26},{10... | collective-permute-start | bytes 322568 | tf_op jit(solution)/shard_map/ppermute | solution.py:39
  11.2 14.2 %copy-start.2 = (bf16[2048,512]{1,0:T(8,128)(2,1)S(1)}, bf16[2048,512]{1,0:T(8,128)(2,1)}, u32[]{:S(2)}) copy-start(bf16[2048,512]{1,0:T(8,128)(2,1)} %basis.2) | copy-start | bytes 6291460
  16.8 0.7 copy-start.7
  18.7 14.5 %collective-permute-start.3 = (bf16[240,896]{1,0:T(8,128)(2,1)S(1)}, bf16[240,896]{1,0:T(8,128)(2,1)}, u32[]{:S(2)}, u32[]{:S(2)}) collective-permute-start(bf16[240,896]{1,0:T(8,128)(2,1)S(1)} %arrange.1.refs_0_), channel_id=1, source_target_pairs={{0,32},{32,64},{64,96},{96,128},{128,160},{160,192},{192,224},{224... | collective-permute-start | bytes 1290248 | tf_op jit(solution)/shard_map/ppermute | solution.py:44
  19.2 14.0 %collective-permute-start.4 = (bf16[240,896]{1,0:T(8,128)(2,1)S(1)}, bf16[240,896]{1,0:T(8,128)(2,1)}, u32[]{:S(2)}, u32[]{:S(2)}) collective-permute-start(bf16[240,896]{1,0:T(8,128)(2,1)S(1)} %arrange.1.refs_0_), channel_id=1, source_target_pairs={{0,224},{32,0},{64,32},{96,64},{128,96},{160,128},{192,160},{224,1... | collective-permute-start | bytes 1290248 | tf_op jit(solution)/shard_map/ppermute | solution.py:44
  23.2 76.9 %collective-permute-start.15 = (bf16[512,1664]{1,0:T(8,128)(2,1)}, bf16[512,1664]{1,0:T(8,128)(2,1)}, u32[]{:S(2)}, u32[]{:S(2)}) collective-permute-start(bf16[512,1664]{1,0:T(8,128)(2,1)} %inverse.2), channel_id=1, source_target_pairs={{0,16},{16,0},{1,17},{17,1},{2,18},{18,2},{3,19},{19,3},{4,20},{20... | collective-permute-start | bytes 5111816 | tf_op jit(solution)/shard_map/ppermute | solution.py:39
  33.2 36.2 %collective-permute-start.5 = (bf16[240,896]{1,0:T(8,128)(2,1)}, bf16[240,896]{1,0:T(8,128)(2,1)}, u32[]{:S(2)}, u32[]{:S(2)}) collective-permute-start(bf16[240,896]{1,0:T(8,128)(2,1)} %collective-permute-done.3.refs_1_), channel_id=1, source_target_pairs={{0,32},{32,64},{64,96},{96,128},{128,160},{160,192},{192,224},{224... | collective-permute-start | bytes 1290248 | tf_op jit(solution)/shard_map/ppermute | solution.py:44
  33.2 36.2 %collective-permute-start.6 = (bf16[240,896]{1,0:T(8,128)(2,1)}, bf16[240,896]{1,0:T(8,128)(2,1)}, u32[]{:S(2)}, u32[]{:S(2)}) collective-permute-start(bf16[240,896]{1,0:T(8,128)(2,1)} %collective-permute-done.4.refs_7_), channel_id=1, source_target_pairs={{0,224},{32,0},{64,32},{96,64},{128,96},{160,128},{192,160},{224,1... | collective-permute-start | bytes 1290248 | tf_op jit(solution)/shard_map/ppermute | solution.py:44
  35.9 33.5 %all-to-all-start = ((bf16[8,48,512]{2,1,0:T(8,128)(2,1)}), bf16[8,48,512]{2,1,0:T(8,128)(2,1)S(1)}, u32[]{:S(2)}, u32[]{:S(2)}) async-start(bf16[8,48,512]{2,1,0:T(8,128)(2,1)} %left.1), calls=%async_computation | async-start | bytes 786432 | tf_op jit(solution)/shard_map/all_to_all | solution.py:34
  40.5 51.3 %copy-start = (bf16[6,3328,64]{1,2,0:T(8,128)(2,1)S(1)}, bf16[6,3328,64]{1,2,0:T(8,128)(2,1)}, u32[]{:S(2)}) copy-start(bf16[6,3328,64]{1,2,0:T(8,128)(2,1)} %param.18) | copy-start | bytes 7667716
  40.5 51.3 %copy-start.8 = (s32[4]{0:T(128)S(1)}, s32[4]{0:T(128)}, u32[]{:S(2)}) copy-start(s32[4]{0:T(128)} %copy-done.6) | copy-start | bytes 52
  45.4 40.3 %collective-permute-start.12 = (bf16[512,896]{1,0:T(8,128)(2,1)}, bf16[512,896]{1,0:T(8,128)(2,1)}, u32[]{:S(2)}, u32[]{:S(2)}) collective-permute-start(bf16[512,896]{1,0:T(8,128)(2,1)} %get-tuple-element.48), channel_id=1, source_target_pairs={{0,8},{8,0},{1,9},{9,1},{2,10},{10,2},{3,11},{11,3},{4,12},{12,4},... | collective-permute-start | bytes 2752520 | tf_op jit(solution)/shard_map/ppermute | solution.py:39
  69.5 11.5 %collective-permute-start.7 = (bf16[240,896]{1,0:T(8,128)(2,1)}, bf16[240,896]{1,0:T(8,128)(2,1)S(1)}, u32[]{:S(2)}, u32[]{:S(2)}) collective-permute-start(bf16[240,896]{1,0:T(8,128)(2,1)} %collective-permute-done.5.refs_2_), channel_id=1, source_target_pairs={{0,32},{32,64},{64,96},{96,128},{128,160},{160,192},{192,224},{224... | collective-permute-start | bytes 1290248 | tf_op jit(solution)/shard_map/ppermute | solution.py:44
  69.5 11.4 %collective-permute-start.8 = (bf16[240,896]{1,0:T(8,128)(2,1)}, bf16[240,896]{1,0:T(8,128)(2,1)S(1)}, u32[]{:S(2)}, u32[]{:S(2)}) collective-permute-start(bf16[240,896]{1,0:T(8,128)(2,1)} %collective-permute-done.6.refs_6_), channel_id=1, source_target_pairs={{0,224},{32,0},{64,32},{96,64},{128,96},{160,128},{192,160},{224,1... | collective-permute-start | bytes 1290248 | tf_op jit(solution)/shard_map/ppermute | solution.py:44
  81.0 9.5 %collective-permute-start.9 = (bf16[240,896]{1,0:T(8,128)(2,1)S(1)}, bf16[240,896]{1,0:T(8,128)(2,1)S(1)}, u32[]{:S(2)}, u32[]{:S(2)}) collective-permute-start(bf16[240,896]{1,0:T(8,128)(2,1)S(1)} %collective-permute-done.7.refs_3_), channel_id=1, source_target_pairs={{0,32},{32,64},{64,96},{96,128},{128,160},{160,192},{192,224},{224... | collective-permute-start | bytes 1290248 | tf_op jit(solution)/shard_map/ppermute | solution.py:44
  81.0 14.6 %collective-permute-start.10 = (bf16[256,512]{1,0:T(8,128)(2,1)S(1)}, bf16[256,512]{1,0:T(8,128)(2,1)S(1)}, u32[]{:S(2)}, u32[]{:S(2)}) collective-permute-start(bf16[256,512]{1,0:T(8,128)(2,1)S(1)} %bitcast.17), channel_id=1, source_target_pairs={{0,8},{8,0},{1,9},{9,1},{2,10},{10,2},{3,11},{11,3},{4,12},{12,4},... | collective-permute-start | bytes 786440 | tf_op jit(solution)/shard_map/ppermute | solution.py:39
  84.2 15.9 %collective-permute-start.13 = (bf16[256,512]{1,0:T(8,128)(2,1)S(1)}, bf16[256,512]{1,0:T(8,128)(2,1)S(1)}, u32[]{:S(2)}, u32[]{:S(2)}) collective-permute-start(bf16[256,512]{1,0:T(8,128)(2,1)S(1)} %bitcast.18), channel_id=1, source_target_pairs={{0,16},{16,0},{1,17},{17,1},{2,18},{18,2},{3,19},{19,3},{4,20},{20... | collective-permute-start | bytes 786440 | tf_op jit(solution)/shard_map/ppermute | solution.py:39
  85.7 9.8 %collective-permute-start.11 = (bf16[128,512]{1,0:T(8,128)(2,1)S(1)}, bf16[128,512]{1,0:T(8,128)(2,1)S(1)}, u32[]{:S(2)}, u32[]{:S(2)}) collective-permute-start(bf16[128,512]{1,0:T(8,128)(2,1)S(1)} %get-tuple-element.46.refs_2_), channel_id=1, source_target_pairs={{0,8},{8,0},{1,9},{9,1},{2,10},{10,2},{3,11},{11,3},{4,12},{12,4},... | collective-permute-start | bytes 393224 | tf_op jit(solution)/shard_map/ppermute | solution.py:39
  90.4 9.6 %collective-permute-start.14 = (bf16[128,512]{1,0:T(8,128)(2,1)S(1)}, bf16[128,512]{1,0:T(8,128)(2,1)S(1)}, u32[]{:S(2)}, u32[]{:S(2)}) collective-permute-start(bf16[128,512]{1,0:T(8,128)(2,1)S(1)} %get-tuple-element.46.refs_2_), channel_id=1, source_target_pairs={{0,16},{16,0},{1,17},{17,1},{2,18},{18,2},{3,19},{19,3},{4,20},{20... | collective-permute-start | bytes 393224 | tf_op jit(solution)/shard_map/ppermute | solution.py:39
  91.8 3.8 %copy-start.3 = (bf16[512,896]{1,0:T(8,128)(2,1)S(1)}, bf16[512,896]{1,0:T(8,128)(2,1)}, u32[]{:S(2)}) copy-start(bf16[512,896]{1,0:T(8,128)(2,1)} %get-tuple-element.47.refs_4_) | copy-start | bytes 2752516
  95.6 13.3 %copy-start.4 = (f32[32,1664]{1,0:T(8,128)S(1)}, f32[32,1664]{1,0:T(8,128)}, u32[]{:S(2)}) copy-start(f32[32,1664]{1,0:T(8,128)} %factors.1) | copy-start | bytes 638980
  95.6 13.3 %copy-start.12 = (s32[16]{0:T(128)S(1)}, s32[16]{0:T(128)}, u32[]{:S(2)}) copy-start(s32[16]{0:T(128)} %block_ids.1) | copy-start | bytes 196
  101.7 7.2 %collective-permute-start.18 = (bf16[512,896]{1,0:T(8,128)(2,1)S(1)}, bf16[512,896]{1,0:T(8,128)(2,1)S(1)}, u32[]{:S(2)}, u32[]{:S(2)}) collective-permute-start(bf16[512,896]{1,0:T(8,128)(2,1)S(1)} %get-tuple-element.55), channel_id=1, source_target_pairs={{0,8},{8,0},{1,9},{9,1},{2,10},{10,2},{3,11},{11,3},{4,12},{12,4},... | collective-permute-start | bytes 2752520 | tf_op jit(solution)/shard_map/ppermute | solution.py:39
  106.2 2.7 %collective-permute-start.16 = (bf16[256,512]{1,0:T(8,128)(2,1)S(1)}, bf16[256,512]{1,0:T(8,128)(2,1)S(1)}, u32[]{:S(2)}, u32[]{:S(2)}) collective-permute-start(bf16[256,512]{1,0:T(8,128)(2,1)S(1)} %collective-permute-done.13.refs_0_), channel_id=1, source_target_pairs={{0,8},{8,0},{1,9},{9,1},{2,10},{10,2},{3,11},{11,3},{4,12},{12,4},... | collective-permute-start | bytes 786440 | tf_op jit(solution)/shard_map/ppermute | solution.py:39
  106.3 2.6 %collective-permute-start.17 = (bf16[128,512]{1,0:T(8,128)(2,1)S(1)}, bf16[128,512]{1,0:T(8,128)(2,1)S(1)}, u32[]{:S(2)}, u32[]{:S(2)}) collective-permute-start(bf16[128,512]{1,0:T(8,128)(2,1)S(1)} %collective-permute-done.14.refs_2_), channel_id=1, source_target_pairs={{0,8},{8,0},{1,9},{9,1},{2,10},{10,2},{3,11},{11,3},{4,12},{12,4},... | collective-permute-start | bytes 393224 | tf_op jit(solution)/shard_map/ppermute | solution.py:39
  147.5 16.0 %collective-permute-start.19 = (bf16[16,1664]{1,0:T(8,128)(2,1)S(1)}, bf16[16,1664]{1,0:T(8,128)(2,1)S(1)}, u32[]{:S(2)}, u32[]{:S(2)}) collective-permute-start(bf16[16,1664]{1,0:T(8,128)(2,1)S(1)} %get-tuple-element.58), channel_id=1, source_target_pairs={{0,8},{8,0},{1,9},{9,1},{2,10},{10,2},{3,11},{11,3},{4,12},{12,4},... | collective-permute-start | bytes 159752 | tf_op jit(solution)/shard_map/ppermute | solution.py:39
  149.4 14.1 %collective-permute-start.20 = (bf16[16,1664]{1,0:T(8,128)(2,1)S(1)}, bf16[16,1664]{1,0:T(8,128)(2,1)S(1)}, u32[]{:S(2)}, u32[]{:S(2)}) collective-permute-start(bf16[16,1664]{1,0:T(8,128)(2,1)S(1)} %get-tuple-element.59), channel_id=1, source_target_pairs={{0,16},{16,0},{1,17},{17,1},{2,18},{18,2},{3,19},{19,3},{4,20},{20... | collective-permute-start | bytes 159752 | tf_op jit(solution)/shard_map/ppermute | solution.py:39
  150.8 12.7 %collective-permute-start.21 = (bf16[16,1664]{1,0:T(8,128)(2,1)S(1)}, bf16[16,1664]{1,0:T(8,128)(2,1)S(1)}, u32[]{:S(2)}, u32[]{:S(2)}) collective-permute-start(bf16[16,1664]{1,0:T(8,128)(2,1)S(1)} %get-tuple-element.60), channel_id=1, source_target_pairs={{0,24},{8,16},{16,8},{24,0},{1,25},{9,17},{17,9},{25,1},{2,26},{10... | collective-permute-start | bytes 159752 | tf_op jit(solution)/shard_map/ppermute | solution.py:39

commit v5 on v4

--- a/solution.py
+++ b/solution.py
@@ -117,16 +117,17 @@
         out[...] = (1.0 / corrected[:, pl.ds(at, width)]).astype(BF)
 
 
-def inverse_block(where, corrected, block, far, width, count):
-    rows = corrected.shape[0]
-    tile = 128
+def inverse_block(where, corrected, block, far, width, count, start=0, stop=None):
+    tile = 64
+    first = start // tile
+    rows = (stop or corrected.shape[0]) - start
     return pl.pallas_call(
         inverse_body,
         out_shape=tuple(jax.ShapeDtypeStruct((rows, width), BF) for _ in range(count)),
         grid_spec=pltpu.PrefetchScalarGridSpec(
             num_scalar_prefetch=1,
             grid=(rows // tile,),
-            in_specs=[pl.BlockSpec((tile, block), lambda n, w: (n, w[1] ^ far))],
+            in_specs=[pl.BlockSpec((tile, block), lambda n, w: (first + n, w[1] ^ far))],
             out_specs=tuple(
                 pl.BlockSpec((tile, width), lambda n, w: (n, 0)) for _ in range(count)
             ),
@@ -136,22 +137,28 @@
     )(where, corrected)
 
 
-def halves_body(where, block, own, other):
+def halves_body(where, *refs):
+    pieces, (own, other) = refs[:-2], refs[-2:]
     width = own.shape[1]
-    skip = block.shape[1] - width
-    for r, out in enumerate((own, other)):
-        out[...] = block[:, pl.ds(pl.multiple_of((where[3] ^ r) * skip, LANES), width)]
-
-
-def halves(where, block, width):
+    first = 0
+    for piece in pieces:
+        rows, block = piece.shape
+        for r, out in enumerate((own, other)):
+            at = pl.multiple_of((where[3] ^ r) * (block - width), LANES)
+            out[first : first + rows, :] = piece[:, pl.ds(at, width)]
+        first += rows
+
+
+def halves(where, pieces, width):
+    rows = sum(p.shape[0] for p in pieces)
     return pl.pallas_call(
         halves_body,
-        out_shape=tuple(jax.ShapeDtypeStruct((block.shape[0], width), BF) for _ in range(2)),
-        in_specs=[SMEM_SPEC, VMEM_SPEC],
+        out_shape=tuple(jax.ShapeDtypeStruct((rows, width), BF) for _ in range(2)),
+        in_specs=[SMEM_SPEC, *([VMEM_SPEC] * len(pieces))],
         out_specs=(VMEM_SPEC, VMEM_SPEC),
         compiler_params=params(10),
         name="halves",
-    )(where, block)
+    )(where, *pieces)
 
 
 def pack_body(where, train_ids, basis, tokens, delta, *outs):
@@ -465,24 +472,31 @@
         swap(packed[2], "xh"),
         swap(packed[3], QUAD, 3),
     )
-    (far,) = inverse_block(where, corrected, block, 1, block, 1)
-    own = arrange(where, (after(packed[0], far), *parts[1:]), local_rows, train)
-    far = swap(far, "xh")
+    rows = corrected.shape[0]
+    ends = (0, 3 * rows // 8, 3 * rows // 4, rows)
+    far = [
+        inverse_block(where, corrected, block, 1, block, 1, a, b)[0]
+        for a, b in zip(ends[:-1], ends[1:])
+    ]
+    partial = left_part(query_ids, jnp.transpose(u_pool, (0, 2, 1)), basis_out, n_in)
+    own = arrange(where, (after(packed[0], far[0], partial), *parts[1:]), local_rows, train)
     near = inverse_block(where, corrected, block, 0, width, 2)
     near = (near[0], swap(near[1], "c"))
 
-    partial = left_part(query_ids, jnp.transpose(u_pool, (0, 2, 1)), basis_out, n_in)
     ahead, behind = [shift(own, 1)], [shift(own, -1)]
-    up, down = after((ahead[0], behind[0]), partial)
-    ahead.append(shift(up, 1))
-    behind.append(shift(down, -1))
+    far[0] = swap(far[0], "xh")
     spread, window = left_sum(exchange(partial, IN))
-    up, down = after((ahead[1], behind[1]), spread)
+    up, down = after((ahead[0], behind[0]), spread)
+    far[1] = swap(after(far[1], ahead[0], spread), "xh")
     ahead.append(shift(up, 1))
     behind.append(shift(down, -1))
     left = exchange(spread, IN).reshape(-1, basis_out.shape[1])
-    up, left, window = after((ahead[2], left, window), behind[2])
+    up, down, left = after((ahead[1], behind[1], left), far[0])
     ahead.append(shift(up, 1))
+    behind.append(shift(down, -1))
+    up = after(ahead[2], behind[2], far[1])
+    ahead.append(shift(up, 1))
+    far[2] = swap(after(far[2], left), "xh")
     left_x, window_x = swap(left, "xh"), swap(window, "xh")
     lefts = (left, swap(left, "c"))
     windows = (window, swap(window, "c"))
@@ -492,7 +506,7 @@
         where, query_ids, jnp.transpose(v_pool, (0, 2, 1)), chunks, block
     )
     so_far = back_first(right, lefts, windows, near, queries)
-    left_x, window_x, far = after((left_x, window_x, far), so_far)
+    left_x, window_x, *far = after((left_x, window_x, *far), so_far)
     far = halves(where, far, width)
     far = (left_x, swap(left_x, "c"), window_x, swap(window_x, "c"), far[0], swap(far[1], "c"))
     parts = back(

time: 165 us -> 151 us (0.915)
  waiting for transfers between devices: 35.2 us -> 13.4 us
  starting transfers between devices: 41.6 us -> 50.2 us
  blocking collectives: 51.6 us -> 44.5 us
  Pallas kernels: 31.6 us -> 37.2 us
    all_to_all x1 -> x2, waiting for transfers between devices: 22.3 us -> 8.71 us  [exchange(): return lax.all_to_all(value, axis, split_axis=0, concat_axis=0, tiled=True)]
    ppermute x7, waiting for transfers between devices: 10.1 us -> 1.52 us  [shift(): lax.ppermute(value, 'z', [(i, (i + step) % size) for i in range(size)])]
    all_to_all x3 -> x2, blocking collectives: 51.6 us -> 44.5 us  [exchange(): return lax.all_to_all(value, axis, split_axis=0, concat_axis=0, tiled=True)]
    pallas_call x2 -> x4, Pallas kernels: 9.84 us -> 16.5 us  [inverse_block(): pl.pallas_call(inverse_body, out_shape=tuple((jax.ShapeDtypeStruct((rows,...]
    ppermute x15 -> x17, starting transfers between devices: 27 us -> 32.1 us  [swap(): return lax.ppermute(value, axis, [(i, i ^ mask) for i in range(size)])]
    all_to_all x1 -> x2, starting transfers between devices: 4.55 us -> 8.4 us  [exchange(): return lax.all_to_all(value, axis, split_axis=0, concat_axis=0, tiled=True)]
    unnamed x27 -> x31, local copies, waits for them, and re-layouts: 3.86 us -> 4.23 us
  transfers between devices with their start and end apart: 23 -> 26, of which waited for: 6 -> 5; matrix products, arithmetic and copies ran while one was open for 0% -> 0% of each run, Pallas kernels for 12% -> 18%
where the time goes in v5:
time: 151 us; the launch traced here: 150 us
  starting transfers between devices  50.2 us (33%)
  blocking collectives  44.5 us (29%)
  Pallas kernels  37.2 us (25%)
  waiting for transfers between devices  13.4 us (9%)
  local copies, waits for them, and re-layouts  4.23 us (3%)
    all_to_all x2, blocking collectives, exchange(): return lax.all_to_all(value, axis, split_axis=0, concat_axis=0, tiled=True)  44.5 us
    ppermute x17, starting transfers between devices, swap(): return lax.ppermute(value, axis, [(i, i ^ mask) for i in range(size)])  32.1 us
    pallas_call x4, Pallas kernels, inverse_block(): pl.pallas_call(inverse_body, out_shape=tuple((jax.ShapeDtypeStruct((rows,...  16.5 us
    ppermute x7, starting transfers between devices, shift(): lax.ppermute(value, 'z', [(i, (i + step) % size) for i in range(size)])  9.71 us
    all_to_all x2, waiting for transfers between devices, exchange(): return lax.all_to_all(value, axis, split_axis=0, concat_axis=0, tiled=True)  8.71 us
    all_to_all x2, starting transfers between devices, exchange(): return lax.all_to_all(value, axis, split_axis=0, concat_axis=0, tiled=True)  8.4 us
    pallas_call x1, Pallas kernels, back(): pl.pallas_call(functools.partial(back_body, train=train), out_shape=jax.S...  4.79 us
    unnamed x31, local copies, waits for them, and re-layouts  4.23 us
  transfers between devices with their start and end apart: 26, of which 5 were waited for; matrix products, arithmetic and copies ran while one was open for 0% of the time, Pallas kernels for 18%

profile of v5, /device:TPU:1, one launch (start us, length us, event | category | flops | bytes accessed | tf_op | source)
XLA Modules:
  0.0 150.5 jit_solution(15903048598207974651)
XLA Ops:
  0.6 1.0 copy.13.basis
  1.7 0.1 pad_add_fusion.where
  1.8 0.8 copy-done.10
  2.6 0.7 copy-done.11
  3.2 0.7 copy-done.13
  3.9 0.7 pack.1
  4.7 3.3 %collective-permute-start = (bf16[60,896]{1,0:T(8,128)(2,1)S(1)}, bf16[60,896]{1,0:T(8,128)(2,1)S(1)}, u32[]{:S(2)}, u32[]{:S(2)}) collective-permute-start(bf16[60,896]{1,0:T(8,128)(2,1)S(1)} %get-tuple-element.37), channel_id=1, source_target_pairs={{0,8},{8,0},{1,9},{9,1},{2,10},{10,2},{3,11},{11,3},{4,12},{12,4},... | collective-permute-start | bytes 322568 | tf_op jit(solution)/shard_map/ppermute | solution.py:39
  8.0 1.0 collective-permute-start.1
  9.0 2.2 %collective-permute-start.2 = (bf16[60,896]{1,0:T(8,128)(2,1)S(1)}, bf16[60,896]{1,0:T(8,128)(2,1)S(1)}, u32[]{:S(2)}, u32[]{:S(2)}) collective-permute-start(bf16[60,896]{1,0:T(8,128)(2,1)S(1)} %get-tuple-element.39), channel_id=1, source_target_pairs={{0,24},{8,16},{16,8},{24,0},{1,25},{9,17},{17,9},{25,1},{2,26},{10... | collective-permute-start | bytes 322568 | tf_op jit(solution)/shard_map/ppermute | solution.py:39
  11.2 3.7 %inverse.4 = bf16[192,1664]{1,0:T(8,128)(2,1)} custom-call(s32[4]{0:T(128)} %copy-done.7, f32[512,3328]{1,0:T(8,128)} %corrected.7), custom_call_target="tpu_custom_call" | custom-call | tf_op jit(solution)/shard_map/inverse/pallas_call | solution.py:124
  14.9 0.0 copy-start.8
  14.9 2.3 %left.1 = bf16[8,48,512]{2,1,0:T(8,128)(2,1)} custom-call(s32[4]{0:T(128)S(1)} %copy-done.12, bf16[6,64,2048]{2,1,0:T(8,128)(2,1)S(1)} %bitcast.13, bf16[6,64,2048]{2,1,0:T(8,128)(2,1)S(1)} %bitcast.14, bf16[6,64,2048]{2,1,0:T(8,128)(2,1)S(1)} %bitcast.15, bf16[6,64,2048]{2,1,0:T(8,128)(2,1)S(1)} %bitcast.16, bf16[2048,512]{1,0:T(8,128)(2,1)S(1)} %copy-done.2), custom_call_target="tpu_custom_call" | custom-call | tf_op jit(solution)/shard_map/left/pallas_call | solution.py:71
  17.2 0.0 collective-permute-done.a1
  17.2 0.0 collective-permute-done.1.a2
  17.2 0.0 collective-permute-done.2.a3
  17.3 1.2 arrange.1.refs_0_
  18.5 0.1 collective-permute-start.3
  18.6 4.0 %collective-permute-start.4 = (bf16[240,896]{1,0:T(8,128)(2,1)S(1)}, bf16[240,896]{1,0:T(8,128)(2,1)S(1)}, u32[]{:S(2)}, u32[]{:S(2)}) collective-permute-start(bf16[240,896]{1,0:T(8,128)(2,1)S(1)} %arrange.1.refs_0_), channel_id=1, source_target_pairs={{0,224},{32,0},{64,32},{96,64},{128,96},{160,128},{192,160},{224,1... | collective-permute-start | bytes 1290248 | tf_op jit(solution)/shard_map/ppermute | solution.py:44
  22.6 5.0 %all-to-all-start = ((bf16[8,48,512]{2,1,0:T(8,128)(2,1)}), bf16[8,48,512]{2,1,0:T(8,128)(2,1)S(1)}, u32[]{:S(2)}, u32[]{:S(2)}) async-start(bf16[8,48,512]{2,1,0:T(8,128)(2,1)} %left.1), calls=%async_computation | async-start | bytes 786432 | tf_op jit(solution)/shard_map/all_to_all | solution.py:34
  27.6 2.5 %collective-permute-start.7 = (bf16[192,1664]{1,0:T(8,128)(2,1)}, bf16[192,1664]{1,0:T(8,128)(2,1)S(1)}, u32[]{:S(2)}, u32[]{:S(2)}) collective-permute-start(bf16[192,1664]{1,0:T(8,128)(2,1)} %inverse.4), channel_id=1, source_target_pairs={{0,16},{16,0},{1,17},{17,1},{2,18},{18,2},{3,19},{19,3},{4,20},{20... | collective-permute-start | bytes 1916936 | tf_op jit(solution)/shard_map/ppermute | solution.py:39
  30.0 5.6 %all-to-all-done.parts = bf16[8,48,512]{2,1,0:T(8,128)(2,1)S(1)} async-done(((bf16[8,48,512]{2,1,0:T(8,128)(2,1)}), bf16[8,48,512]{2,1,0:T(8,128)(2,1)S(1)}, u32[]{:S(2)}, u32[]{:S(2)}) %all-to-all-start) | async-done | bytes 393248 | tf_op jit(solution)/shard_map/all_to_all | solution.py:34
  35.6 0.7 left_sum.1
  36.4 0.0 collective-permute-done.3.refs_1_
  36.4 0.0 collective-permute-done.4.refs_7_
  36.4 0.1 collective-permute-start.5
  36.5 2.7 %collective-permute-start.6 = (bf16[240,896]{1,0:T(8,128)(2,1)S(1)}, bf16[240,896]{1,0:T(8,128)(2,1)}, u32[]{:S(2)}, u32[]{:S(2)}) collective-permute-start(bf16[240,896]{1,0:T(8,128)(2,1)S(1)} %collective-permute-done.4.refs_7_), channel_id=1, source_target_pairs={{0,224},{32,0},{64,32},{96,64},{128,96},{160,128},{192,160},{224,1... | collective-permute-start | bytes 1290248 | tf_op jit(solution)/shard_map/ppermute | solution.py:44
  39.1 3.4 %all-to-all-start.1 = ((bf16[8,32,512]{2,1,0:T(8,128)(2,1)}), bf16[8,32,512]{2,1,0:T(8,128)(2,1)S(1)}, u32[]{:S(2)}, u32[]{:S(2)}) async-start(bf16[8,32,512]{2,1,0:T(8,128)(2,1)} %get-tuple-element.40), calls=%async_computation.1 | async-start | bytes 524288 | tf_op jit(solution)/shard_map/all_to_all | solution.py:34
  42.5 3.7 %inverse.5 = bf16[192,1664]{1,0:T(8,128)(2,1)} custom-call(s32[4]{0:T(128)} %copy-done.7, f32[512,3328]{1,0:T(8,128)} %corrected.7), custom_call_target="tpu_custom_call" | custom-call | tf_op jit(solution)/shard_map/inverse/pallas_call | solution.py:124
  46.2 2.5 %collective-permute-start.10 = (bf16[192,1664]{1,0:T(8,128)(2,1)}, bf16[192,1664]{1,0:T(8,128)(2,1)S(1)}, u32[]{:S(2)}, u32[]{:S(2)}) collective-permute-start(bf16[192,1664]{1,0:T(8,128)(2,1)} %inverse.5), channel_id=1, source_target_pairs={{0,16},{16,0},{1,17},{17,1},{2,18},{18,2},{3,19},{19,3},{4,20},{20... | collective-permute-start | bytes 1916936 | tf_op jit(solution)/shard_map/ppermute | solution.py:39
  48.7 3.1 %all-to-all-done.1 = bf16[8,32,512]{2,1,0:T(8,128)(2,1)S(1)} async-done(((bf16[8,32,512]{2,1,0:T(8,128)(2,1)}), bf16[8,32,512]{2,1,0:T(8,128)(2,1)S(1)}, u32[]{:S(2)}, u32[]{:S(2)}) %all-to-all-start.1) | async-done | bytes 262176 | tf_op jit(solution)/shard_map/all_to_all | solution.py:34
  51.8 0.0 collective-permute-done.5.refs_2_
  51.8 0.0 collective-permute-done.6.refs_6_
  51.8 0.1 collective-permute-start.8
  51.9 2.7 %collective-permute-start.9 = (bf16[240,896]{1,0:T(8,128)(2,1)}, bf16[240,896]{1,0:T(8,128)(2,1)}, u32[]{:S(2)}, u32[]{:S(2)}) collective-permute-start(bf16[240,896]{1,0:T(8,128)(2,1)} %collective-permute-done.6.refs_6_), channel_id=1, source_target_pairs={{0,224},{32,0},{64,32},{96,64},{128,96},{160,128},{192,160},{224,1... | collective-permute-start | bytes 1290248 | tf_op jit(solution)/shard_map/ppermute | solution.py:44
  54.6 6.6 %inverse.6 = (bf16[512,896]{1,0:T(8,128)(2,1)}, bf16[512,896]{1,0:T(8,128)(2,1)}) custom-call(s32[4]{0:T(128)} %copy-done.7, f32[512,3328]{1,0:T(8,128)} %corrected.7), custom_call_target="tpu_custom_call" | custom-call | tf_op jit(solution)/shard_map/inverse/pallas_call | solution.py:124
  61.2 2.7 %collective-permute-start.14 = (bf16[512,896]{1,0:T(8,128)(2,1)}, bf16[512,896]{1,0:T(8,128)(2,1)S(1)}, u32[]{:S(2)}, u32[]{:S(2)}) collective-permute-start(bf16[512,896]{1,0:T(8,128)(2,1)} %get-tuple-element.51), channel_id=1, source_target_pairs={{0,8},{8,0},{1,9},{9,1},{2,10},{10,2},{3,11},{11,3},{4,12},{12,4},... | collective-permute-start | bytes 2752520 | tf_op jit(solution)/shard_map/ppermute | solution.py:39
  63.9 0.0 collective-permute-done.9.refs_5_
  63.9 0.1 collective-permute-start.11
  64.0 2.6 %inverse.7 = bf16[128,1664]{1,0:T(8,128)(2,1)} custom-call(s32[4]{0:T(128)} %copy-done.7, f32[512,3328]{1,0:T(8,128)} %corrected.7), custom_call_target="tpu_custom_call" | custom-call | tf_op jit(solution)/shard_map/inverse/pallas_call | solution.py:124
  66.6 3.2 %collective-permute-start.17 = (bf16[128,1664]{1,0:T(8,128)(2,1)}, bf16[128,1664]{1,0:T(8,128)(2,1)S(1)}, u32[]{:S(2)}, u32[]{:S(2)}) collective-permute-start(bf16[128,1664]{1,0:T(8,128)(2,1)} %inverse.7), channel_id=1, source_target_pairs={{0,16},{16,0},{1,17},{17,1},{2,18},{18,2},{3,19},{19,3},{4,20},{20... | collective-permute-start | bytes 1277960 | tf_op jit(solution)/shard_map/ppermute | solution.py:39
  69.8 1.3 collective-permute-start.13
  71.1 0.0 collective-permute-start.12
  71.1 1.0 collective-permute-done.13.refs_3_
  72.1 1.1 collective-permute-start.15
  73.1 1.5 %collective-permute-done.11.refs_4_ = bf16[240,896]{1,0:T(8,128)(2,1)} collective-permute-done((bf16[240,896]{1,0:T(8,128)(2,1)}, bf16[240,896]{1,0:T(8,128)(2,1)}, u32[]{:S(2)}, u32[]{:S(2)}) %collective-permute-start.11) | collective-permute-done | bytes 430112 | tf_op jit(solution)/shard_map/ppermute | solution.py:44
  74.6 4.4 %collective-permute-start.16 = (bf16[128,512]{1,0:T(8,128)(2,1)S(1)}, bf16[128,512]{1,0:T(8,128)(2,1)S(1)}, u32[]{:S(2)}, u32[]{:S(2)}) collective-permute-start(bf16[128,512]{1,0:T(8,128)(2,1)S(1)} %get-tuple-element.49.refs_2_), channel_id=1, source_target_pairs={{0,16},{16,0},{1,17},{17,1},{2,18},{18,2},{3,19},{19,3},{4,20},{20... | collective-permute-start | bytes 393224 | tf_op jit(solution)/shard_map/ppermute | solution.py:39
  79.0 1.0 copy-done.5
  80.1 3.9 %rotate.1 = (bf16[1664,896]{1,0:T(8,128)(2,1)S(1)}, bf16[256,896]{1,0:T(8,128)(2,1)S(1)}, bf16[128,896]{1,0:T(8,128)(2,1)S(1)}, bf16[128,128]{1,0:T(8,128)(2,1)S(1)}) custom-call(s32[4]{0:T(128)S(1)} %copy-done.9, s32[4]{0:T(128)S(1)} %copy-done.12, bf16[6,64,3328]{2,1,0:T(8,128)(2,1)S(1)} %bitcast.9, bf16[6,64,3328]{2,1,0:T(8,128)(2,1)S(1)} %bitcast.10, ...), custom_call_target="tpu_custom_call" | custom-call | tf_op jit(solution)/shard_map/rotate/pallas_call | solution.py:271
  84.0 0.0 copy-start.6
  84.0 0.0 copy-start.14
  84.0 3.4 %back_first.1.so_far = f32[4,128,896]{2,1,0:T(8,128)S(1)} custom-call(bf16[256,896]{1,0:T(8,128)(2,1)S(1)} %get-tuple-element.47.right, bf16[256,512]{1,0:T(8,128)(2,1)S(1)} %bitcast.19, bf16[256,512]{1,0:T(8,128)(2,1)S(1)} %collective-permute-done.12.refs_1_, bf16[128,512]{1,0:T(8,128)(2,1)S(1)} %get-tuple-element.49.refs_2_, ...), custom_call_target="tpu_custom_call" | custom-call | tf_op jit(solution)/shard_map/back_first/pallas_call | solution.py:311
  87.4 0.7 halves.1
  88.1 2.3 %collective-permute-start.20 = (bf16[512,896]{1,0:T(8,128)(2,1)S(1)}, bf16[512,896]{1,0:T(8,128)(2,1)S(1)}, u32[]{:S(2)}, u32[]{:S(2)}) collective-permute-start(bf16[512,896]{1,0:T(8,128)(2,1)S(1)} %get-tuple-element.61), channel_id=1, source_target_pairs={{0,8},{8,0},{1,9},{9,1},{2,10},{10,2},{3,11},{11,3},{4,12},{12,4},... | collective-permute-start | bytes 2752520 | tf_op jit(solution)/shard_map/ppermute | solution.py:39
  90.5 0.1 collective-permute-start.18
  90.6 0.4 collective-permute-start.19
  91.0 2.2 %collective-permute-done.19.refs_3_ = bf16[128,512]{1,0:T(8,128)(2,1)S(1)} collective-permute-done((bf16[128,512]{1,0:T(8,128)(2,1)S(1)}, bf16[128,512]{1,0:T(8,128)(2,1)S(1)}, u32[]{:S(2)}, u32[]{:S(2)}) %collective-permute-start.19) | collective-permute-done | bytes 131104 | tf_op jit(solution)/shard_map/ppermute | solution.py:39
  93.1 4.8 %back.1 = bf16[8,72,896]{2,1,0:T(8,128)(2,1)S(1)} custom-call(s32[4]{0:T(128)S(1)} %copy-done.9, s32[16]{0:T(128)S(1)} %copy-done.14, f32[4,128,896]{2,1,0:T(8,128)S(1)} %back_first.1.so_far, f32[32,1664]{1,0:T(8,128)S(1)} %copy-done.6, bf16[256,896]{1,0:T(8,128)(2,1)S(1)} %get-tuple-element.47.right, bf16[128,896]{1,0:T(8,128)(2,1)S(1)} %get-tuple-element.52.tokens, ...), custom_call_target="tpu_custom_call" | custom-call | tf_op jit(solution)/shard_map/back/pallas_call | solution.py:361
  97.9 32.9 %all_to_all.20.parts = bf16[8,72,896]{2,1,0:T(8,128)(2,1)S(1)} all-to-all(bf16[8,72,896]{2,1,0:T(8,128)(2,1)S(1)} %back.1), channel_id=1, replica_groups=mesh['z'=8,'xh'=2,'c'=2,'y'=4,'xl'=2] {'z'}, dimensions={0} | all-to-all | bytes 2064384 | tf_op jit(solution)/shard_map/all_to_all | solution.py:34
  130.8 1.7 %tile.1 = (bf16[16,1664]{1,0:T(8,128)(2,1)S(1)}, bf16[16,1664]{1,0:T(8,128)(2,1)S(1)}, bf16[16,1664]{1,0:T(8,128)(2,1)S(1)}, bf16[16,1664]{1,0:T(8,128)(2,1)S(1)}, f32[32,1,128]{2,1,0:T(1,128)S(1)}) custom-call(s32[4]{0:T(128)S(1)} %copy-done.9, bf16[8,72,896]{2,1,0:T(8,128)(2,1)S(1)} %all_to_all.20.parts, bf16[1664,896]{1,0:T(8,128)(2,1)S(1)} %get-tuple-element.62.basis), custom_call_target="tpu_custom_call" | custom-call | tf_op jit(solution)/shard_map/tile/pallas_call | solution.py:405
  132.5 1.8 %collective-permute-start.21 = (bf16[16,1664]{1,0:T(8,128)(2,1)S(1)}, bf16[16,1664]{1,0:T(8,128)(2,1)S(1)}, u32[]{:S(2)}, u32[]{:S(2)}) collective-permute-start(bf16[16,1664]{1,0:T(8,128)(2,1)S(1)} %get-tuple-element.64), channel_id=1, source_target_pairs={{0,8},{8,0},{1,9},{9,1},{2,10},{10,2},{3,11},{11,3},{4,12},{12,4},... | collective-permute-start | bytes 159752 | tf_op jit(solution)/shard_map/ppermute | solution.py:39
  134.4 2.7 %collective-permute-start.22 = (bf16[16,1664]{1,0:T(8,128)(2,1)S(1)}, bf16[16,1664]{1,0:T(8,128)(2,1)S(1)}, u32[]{:S(2)}, u32[]{:S(2)}) collective-permute-start(bf16[16,1664]{1,0:T(8,128)(2,1)S(1)} %get-tuple-element.65), channel_id=1, source_target_pairs={{0,16},{16,0},{1,17},{17,1},{2,18},{18,2},{3,19},{19,3},{4,20},{20... | collective-permute-start | bytes 159752 | tf_op jit(solution)/shard_map/ppermute | solution.py:39
  137.1 0.5 collective-permute-start.23
  137.6 11.6 %all_to_all.21.score = f32[32,1,128]{2,1,0:T(1,128)S(1)} all-to-all(f32[32,1,128]{2,1,0:T(1,128)S(1)} %get-tuple-element.67), channel_id=1, replica_groups=mesh['z'=8,'xh'=2,'c'=2,'y'=4,'xl'=2] {'xh','c','y','xl'}, dimensions={0} | all-to-all | bytes 32768 | tf_op jit(solution)/shard_map/all_to_all | solution.py:34
  149.2 1.2 final.1
  (36 shorter events, 0.1 us)
Async XLA Ops:
  1.8 9.5 %copy-start.7 = (s32[4]{0:T(128)}, s32[4]{0:T(128)S(1)}, u32[]{:S(2)}) copy-start(s32[4]{0:T(128)S(1)} %pad_add_fusion.where) | copy-start | bytes 52
  1.8 0.8 copy-start.10
  2.6 0.7 copy-start.11
  3.2 0.7 copy-start.13
  4.7 12.6 %collective-permute-start = (bf16[60,896]{1,0:T(8,128)(2,1)S(1)}, bf16[60,896]{1,0:T(8,128)(2,1)S(1)}, u32[]{:S(2)}, u32[]{:S(2)}) collective-permute-start(bf16[60,896]{1,0:T(8,128)(2,1)S(1)} %get-tuple-element.37), channel_id=1, source_target_pairs={{0,8},{8,0},{1,9},{9,1},{2,10},{10,2},{3,11},{11,3},{4,12},{12,4},... | collective-permute-start | bytes 322568 | tf_op jit(solution)/shard_map/ppermute | solution.py:39
  8.0 9.3 %collective-permute-start.1 = (bf16[60,896]{1,0:T(8,128)(2,1)S(1)}, bf16[60,896]{1,0:T(8,128)(2,1)S(1)}, u32[]{:S(2)}, u32[]{:S(2)}) collective-permute-start(bf16[60,896]{1,0:T(8,128)(2,1)S(1)} %get-tuple-element.38), channel_id=1, source_target_pairs={{0,16},{16,0},{1,17},{17,1},{2,18},{18,2},{3,19},{19,3},{4,20},{20... | collective-permute-start | bytes 322568 | tf_op jit(solution)/shard_map/ppermute | solution.py:39
  9.0 5.9 %copy-start.1 = (bf16[6,2048,64]{1,2,0:T(8,128)(2,1)S(1)}, bf16[6,2048,64]{1,2,0:T(8,128)(2,1)}, u32[]{:S(2)}) copy-start(bf16[6,2048,64]{1,2,0:T(8,128)(2,1)} %param.17) | copy-start | bytes 4718596
  9.0 5.9 %copy-start.2 = (bf16[2048,512]{1,0:T(8,128)(2,1)S(1)}, bf16[2048,512]{1,0:T(8,128)(2,1)}, u32[]{:S(2)}) copy-start(bf16[2048,512]{1,0:T(8,128)(2,1)} %basis.2) | copy-start | bytes 6291460
  9.0 5.9 %copy-start.12 = (s32[4]{0:T(128)S(1)}, s32[4]{0:T(128)}, u32[]{:S(2)}) copy-start(s32[4]{0:T(128)} %ids.3) | copy-start | bytes 52
  9.0 8.2 %collective-permute-start.2 = (bf16[60,896]{1,0:T(8,128)(2,1)S(1)}, bf16[60,896]{1,0:T(8,128)(2,1)S(1)}, u32[]{:S(2)}, u32[]{:S(2)}) collective-permute-start(bf16[60,896]{1,0:T(8,128)(2,1)S(1)} %get-tuple-element.39), channel_id=1, source_target_pairs={{0,24},{8,16},{16,8},{24,0},{1,25},{9,17},{17,9},{25,1},{2,26},{10... | collective-permute-start | bytes 322568 | tf_op jit(solution)/shard_map/ppermute | solution.py:39
  14.9 2.3 %copy-start.8 = (s32[4]{0:T(128)S(1)}, s32[4]{0:T(128)}, u32[]{:S(2)}) copy-start(s32[4]{0:T(128)} %copy-done.7) | copy-start | bytes 52
  18.5 17.9 %collective-permute-start.3 = (bf16[240,896]{1,0:T(8,128)(2,1)S(1)}, bf16[240,896]{1,0:T(8,128)(2,1)S(1)}, u32[]{:S(2)}, u32[]{:S(2)}) collective-permute-start(bf16[240,896]{1,0:T(8,128)(2,1)S(1)} %arrange.1.refs_0_), channel_id=1, source_target_pairs={{0,32},{32,64},{64,96},{96,128},{128,160},{160,192},{192,224},{224... | collective-permute-start | bytes 1290248 | tf_op jit(solution)/shard_map/ppermute | solution.py:44
  18.6 17.8 %collective-permute-start.4 = (bf16[240,896]{1,0:T(8,128)(2,1)S(1)}, bf16[240,896]{1,0:T(8,128)(2,1)S(1)}, u32[]{:S(2)}, u32[]{:S(2)}) collective-permute-start(bf16[240,896]{1,0:T(8,128)(2,1)S(1)} %arrange.1.refs_0_), channel_id=1, source_target_pairs={{0,224},{32,0},{64,32},{96,64},{128,96},{160,128},{192,160},{224,1... | collective-permute-start | bytes 1290248 | tf_op jit(solution)/shard_map/ppermute | solution.py:44
  22.6 13.0 %all-to-all-start = ((bf16[8,48,512]{2,1,0:T(8,128)(2,1)}), bf16[8,48,512]{2,1,0:T(8,128)(2,1)S(1)}, u32[]{:S(2)}, u32[]{:S(2)}) async-start(bf16[8,48,512]{2,1,0:T(8,128)(2,1)} %left.1), calls=%async_computation | async-start | bytes 786432 | tf_op jit(solution)/shard_map/all_to_all | solution.py:34
  27.6 24.2 %collective-permute-start.7 = (bf16[192,1664]{1,0:T(8,128)(2,1)}, bf16[192,1664]{1,0:T(8,128)(2,1)S(1)}, u32[]{:S(2)}, u32[]{:S(2)}) collective-permute-start(bf16[192,1664]{1,0:T(8,128)(2,1)} %inverse.4), channel_id=1, source_target_pairs={{0,16},{16,0},{1,17},{17,1},{2,18},{18,2},{3,19},{19,3},{4,20},{20... | collective-permute-start | bytes 1916936 | tf_op jit(solution)/shard_map/ppermute | solution.py:39
  36.4 9.9 %copy-start.4 = (bf16[240,896]{1,0:T(8,128)(2,1)}, bf16[240,896]{1,0:T(8,128)(2,1)S(1)}, u32[]{:S(2)}) copy-start(bf16[240,896]{1,0:T(8,128)(2,1)S(1)} %collective-permute-done.4.refs_7_) | copy-start | bytes 1290244
  36.4 15.5 %collective-permute-start.5 = (bf16[240,896]{1,0:T(8,128)(2,1)S(1)}, bf16[240,896]{1,0:T(8,128)(2,1)}, u32[]{:S(2)}, u32[]{:S(2)}) collective-permute-start(bf16[240,896]{1,0:T(8,128)(2,1)S(1)} %collective-permute-done.3.refs_1_), channel_id=1, source_target_pairs={{0,32},{32,64},{64,96},{96,128},{128,160},{160,192},{192,224},{224... | collective-permute-start | bytes 1290248 | tf_op jit(solution)/shard_map/ppermute | solution.py:44
  36.5 15.4 %collective-permute-start.6 = (bf16[240,896]{1,0:T(8,128)(2,1)S(1)}, bf16[240,896]{1,0:T(8,128)(2,1)}, u32[]{:S(2)}, u32[]{:S(2)}) collective-permute-start(bf16[240,896]{1,0:T(8,128)(2,1)S(1)} %collective-permute-done.4.refs_7_), channel_id=1, source_target_pairs={{0,224},{32,0},{64,32},{96,64},{128,96},{160,128},{192,160},{224,1... | collective-permute-start | bytes 1290248 | tf_op jit(solution)/shard_map/ppermute | solution.py:44
  39.1 12.7 %all-to-all-start.1 = ((bf16[8,32,512]{2,1,0:T(8,128)(2,1)}), bf16[8,32,512]{2,1,0:T(8,128)(2,1)S(1)}, u32[]{:S(2)}, u32[]{:S(2)}) async-start(bf16[8,32,512]{2,1,0:T(8,128)(2,1)} %get-tuple-element.40), calls=%async_computation.1 | async-start | bytes 524288 | tf_op jit(solution)/shard_map/all_to_all | solution.py:34
  46.2 17.7 %collective-permute-start.10 = (bf16[192,1664]{1,0:T(8,128)(2,1)}, bf16[192,1664]{1,0:T(8,128)(2,1)S(1)}, u32[]{:S(2)}, u32[]{:S(2)}) collective-permute-start(bf16[192,1664]{1,0:T(8,128)(2,1)} %inverse.5), channel_id=1, source_target_pairs={{0,16},{16,0},{1,17},{17,1},{2,18},{18,2},{3,19},{19,3},{4,20},{20... | collective-permute-start | bytes 1916936 | tf_op jit(solution)/shard_map/ppermute | solution.py:39
  51.8 12.1 %collective-permute-start.8 = (bf16[240,896]{1,0:T(8,128)(2,1)}, bf16[240,896]{1,0:T(8,128)(2,1)}, u32[]{:S(2)}, u32[]{:S(2)}) collective-permute-start(bf16[240,896]{1,0:T(8,128)(2,1)} %collective-permute-done.5.refs_2_), channel_id=1, source_target_pairs={{0,32},{32,64},{64,96},{96,128},{128,160},{160,192},{192,224},{224... | collective-permute-start | bytes 1290248 | tf_op jit(solution)/shard_map/ppermute | solution.py:44
  51.9 12.0 %collective-permute-start.9 = (bf16[240,896]{1,0:T(8,128)(2,1)}, bf16[240,896]{1,0:T(8,128)(2,1)}, u32[]{:S(2)}, u32[]{:S(2)}) collective-permute-start(bf16[240,896]{1,0:T(8,128)(2,1)} %collective-permute-done.6.refs_6_), channel_id=1, source_target_pairs={{0,224},{32,0},{64,32},{96,64},{128,96},{160,128},{192,160},{224,1... | collective-permute-start | bytes 1290248 | tf_op jit(solution)/shard_map/ppermute | solution.py:44
  61.2 17.9 %copy-start = (bf16[6,3328,64]{1,2,0:T(8,128)(2,1)S(1)}, bf16[6,3328,64]{1,2,0:T(8,128)(2,1)}, u32[]{:S(2)}) copy-start(bf16[6,3328,64]{1,2,0:T(8,128)(2,1)} %param.18) | copy-start | bytes 7667716
  61.2 17.9 %copy-start.9 = (s32[4]{0:T(128)S(1)}, s32[4]{0:T(128)}, u32[]{:S(2)}) copy-start(s32[4]{0:T(128)} %copy-done.7) | copy-start | bytes 52
  61.2 22.8 %collective-permute-start.14 = (bf16[512,896]{1,0:T(8,128)(2,1)}, bf16[512,896]{1,0:T(8,128)(2,1)S(1)}, u32[]{:S(2)}, u32[]{:S(2)}) collective-permute-start(bf16[512,896]{1,0:T(8,128)(2,1)} %get-tuple-element.51), channel_id=1, source_target_pairs={{0,8},{8,0},{1,9},{9,1},{2,10},{10,2},{3,11},{11,3},{4,12},{12,4},... | collective-permute-start | bytes 2752520 | tf_op jit(solution)/shard_map/ppermute | solution.py:39
  63.9 10.7 %collective-permute-start.11 = (bf16[240,896]{1,0:T(8,128)(2,1)}, bf16[240,896]{1,0:T(8,128)(2,1)}, u32[]{:S(2)}, u32[]{:S(2)}) collective-permute-start(bf16[240,896]{1,0:T(8,128)(2,1)} %collective-permute-done.8.refs_3_), channel_id=1, source_target_pairs={{0,32},{32,64},{64,96},{96,128},{128,160},{160,192},{192,224},{224... | collective-permute-start | bytes 1290248 | tf_op jit(solution)/shard_map/ppermute | solution.py:44
  66.6 20.8 %collective-permute-start.17 = (bf16[128,1664]{1,0:T(8,128)(2,1)}, bf16[128,1664]{1,0:T(8,128)(2,1)S(1)}, u32[]{:S(2)}, u32[]{:S(2)}) collective-permute-start(bf16[128,1664]{1,0:T(8,128)(2,1)} %inverse.7), channel_id=1, source_target_pairs={{0,16},{16,0},{1,17},{17,1},{2,18},{18,2},{3,19},{19,3},{4,20},{20... | collective-permute-start | bytes 1277960 | tf_op jit(solution)/shard_map/ppermute | solution.py:39
  69.8 2.3 %collective-permute-start.13 = (bf16[128,512]{1,0:T(8,128)(2,1)S(1)}, bf16[128,512]{1,0:T(8,128)(2,1)S(1)}, u32[]{:S(2)}, u32[]{:S(2)}) collective-permute-start(bf16[128,512]{1,0:T(8,128)(2,1)S(1)} %get-tuple-element.49.refs_2_), channel_id=1, source_target_pairs={{0,8},{8,0},{1,9},{9,1},{2,10},{10,2},{3,11},{11,3},{4,12},{12,4},... | collective-permute-start | bytes 393224 | tf_op jit(solution)/shard_map/ppermute | solution.py:39
  71.1 12.9 %collective-permute-start.12 = (bf16[256,512]{1,0:T(8,128)(2,1)S(1)}, bf16[256,512]{1,0:T(8,128)(2,1)S(1)}, u32[]{:S(2)}, u32[]{:S(2)}) collective-permute-start(bf16[256,512]{1,0:T(8,128)(2,1)S(1)} %bitcast.17), channel_id=1, source_target_pairs={{0,8},{8,0},{1,9},{9,1},{2,10},{10,2},{3,11},{11,3},{4,12},{12,4},... | collective-permute-start | bytes 786440 | tf_op jit(solution)/shard_map/ppermute | solution.py:39
  72.1 15.4 %collective-permute-start.15 = (bf16[256,512]{1,0:T(8,128)(2,1)S(1)}, bf16[256,512]{1,0:T(8,128)(2,1)S(1)}, u32[]{:S(2)}, u32[]{:S(2)}) collective-permute-start(bf16[256,512]{1,0:T(8,128)(2,1)S(1)} %bitcast.18), channel_id=1, source_target_pairs={{0,16},{16,0},{1,17},{17,1},{2,18},{18,2},{3,19},{19,3},{4,20},{20... | collective-permute-start | bytes 786440 | tf_op jit(solution)/shard_map/ppermute | solution.py:39
  74.6 12.8 %collective-permute-start.16 = (bf16[128,512]{1,0:T(8,128)(2,1)S(1)}, bf16[128,512]{1,0:T(8,128)(2,1)S(1)}, u32[]{:S(2)}, u32[]{:S(2)}) collective-permute-start(bf16[128,512]{1,0:T(8,128)(2,1)S(1)} %get-tuple-element.49.refs_2_), channel_id=1, source_target_pairs={{0,16},{16,0},{1,17},{17,1},{2,18},{18,2},{3,19},{19,3},{4,20},{20... | collective-permute-start | bytes 393224 | tf_op jit(solution)/shard_map/ppermute | solution.py:39
  79.0 1.0 copy-start.5
  80.1 3.9 %copy-start.3 = (bf16[512,896]{1,0:T(8,128)(2,1)S(1)}, bf16[512,896]{1,0:T(8,128)(2,1)}, u32[]{:S(2)}) copy-start(bf16[512,896]{1,0:T(8,128)(2,1)} %get-tuple-element.50.refs_4_) | copy-start | bytes 2752516
  84.0 9.1 %copy-start.6 = (f32[32,1664]{1,0:T(8,128)S(1)}, f32[32,1664]{1,0:T(8,128)}, u32[]{:S(2)}) copy-start(f32[32,1664]{1,0:T(8,128)} %factors.1) | copy-start | bytes 638980
  84.0 9.1 %copy-start.14 = (s32[16]{0:T(128)S(1)}, s32[16]{0:T(128)}, u32[]{:S(2)}) copy-start(s32[16]{0:T(128)} %block_ids.1) | copy-start | bytes 196
  88.1 5.0 %collective-permute-start.20 = (bf16[512,896]{1,0:T(8,128)(2,1)S(1)}, bf16[512,896]{1,0:T(8,128)(2,1)S(1)}, u32[]{:S(2)}, u32[]{:S(2)}) collective-permute-start(bf16[512,896]{1,0:T(8,128)(2,1)S(1)} %get-tuple-element.61), channel_id=1, source_target_pairs={{0,8},{8,0},{1,9},{9,1},{2,10},{10,2},{3,11},{11,3},{4,12},{12,4},... | collective-permute-start | bytes 2752520 | tf_op jit(solution)/shard_map/ppermute | solution.py:39
  90.5 2.7 %collective-permute-start.18 = (bf16[256,512]{1,0:T(8,128)(2,1)S(1)}, bf16[256,512]{1,0:T(8,128)(2,1)S(1)}, u32[]{:S(2)}, u32[]{:S(2)}) collective-permute-start(bf16[256,512]{1,0:T(8,128)(2,1)S(1)} %collective-permute-done.15.refs_0_), channel_id=1, source_target_pairs={{0,8},{8,0},{1,9},{9,1},{2,10},{10,2},{3,11},{11,3},{4,12},{12,4},... | collective-permute-start | bytes 786440 | tf_op jit(solution)/shard_map/ppermute | solution.py:39
  90.6 2.6 %collective-permute-start.19 = (bf16[128,512]{1,0:T(8,128)(2,1)S(1)}, bf16[128,512]{1,0:T(8,128)(2,1)S(1)}, u32[]{:S(2)}, u32[]{:S(2)}) collective-permute-start(bf16[128,512]{1,0:T(8,128)(2,1)S(1)} %collective-permute-done.16.refs_2_), channel_id=1, source_target_pairs={{0,8},{8,0},{1,9},{9,1},{2,10},{10,2},{3,11},{11,3},{4,12},{12,4},... | collective-permute-start | bytes 393224 | tf_op jit(solution)/shard_map/ppermute | solution.py:39
  132.5 16.7 %collective-permute-start.21 = (bf16[16,1664]{1,0:T(8,128)(2,1)S(1)}, bf16[16,1664]{1,0:T(8,128)(2,1)S(1)}, u32[]{:S(2)}, u32[]{:S(2)}) collective-permute-start(bf16[16,1664]{1,0:T(8,128)(2,1)S(1)} %get-tuple-element.64), channel_id=1, source_target_pairs={{0,8},{8,0},{1,9},{9,1},{2,10},{10,2},{3,11},{11,3},{4,12},{12,4},... | collective-permute-start | bytes 159752 | tf_op jit(solution)/shard_map/ppermute | solution.py:39
  134.4 14.9 %collective-permute-start.22 = (bf16[16,1664]{1,0:T(8,128)(2,1)S(1)}, bf16[16,1664]{1,0:T(8,128)(2,1)S(1)}, u32[]{:S(2)}, u32[]{:S(2)}) collective-permute-start(bf16[16,1664]{1,0:T(8,128)(2,1)S(1)} %get-tuple-element.65), channel_id=1, source_target_pairs={{0,16},{16,0},{1,17},{17,1},{2,18},{18,2},{3,19},{19,3},{4,20},{20... | collective-permute-start | bytes 159752 | tf_op jit(solution)/shard_map/ppermute | solution.py:39
  137.1 12.1 %collective-permute-start.23 = (bf16[16,1664]{1,0:T(8,128)(2,1)S(1)}, bf16[16,1664]{1,0:T(8,128)(2,1)S(1)}, u32[]{:S(2)}, u32[]{:S(2)}) collective-permute-start(bf16[16,1664]{1,0:T(8,128)(2,1)S(1)} %get-tuple-element.66), channel_id=1, source_target_pairs={{0,24},{8,16},{16,8},{24,0},{1,25},{9,17},{17,9},{25,1},{2,26},{10... | collective-permute-start | bytes 159752 | tf_op jit(solution)/shard_map/ppermute | solution.py:39

commit v6 on v5

--- a/solution.py
+++ b/solution.py
@@ -12,7 +12,6 @@
 OUT = ("z", "xh", "c")
 IN = ("y", "xl")
 QUAD = ("xh", "c")
-PLANE = ("xh", "c", "y", "xl")
 BF = jnp.bfloat16
 F32 = jnp.float32
 LANES = 128
@@ -50,19 +49,16 @@
 
 def left_body(ids, u0, u1, u2, u3, basis, out):
     left = jnp.concatenate([u[0] for u in (u0, u1, u2, u3)], axis=0)
-    n_in, rows, width = out.shape
-    part = dot(left, basis[...], 1, 0).astype(BF)
-    out[:, : rows - WIN_ROWS, :] = part.reshape(n_in, rows - WIN_ROWS, width)
-    out[:, rows - WIN_ROWS :, :] = jnp.broadcast_to(
-        basis[:WIN_ROWS, :][None], (n_in, WIN_ROWS, width)
-    )
-
-
-def left_part(query_ids, u_t, basis_out, n_in):
+    rows = left.shape[0]
+    out[:rows, :] = dot(left, basis[...], 1, 0).astype(BF)
+    out[rows:, :] = basis[:WIN_ROWS, :]
+
+
+def left_part(query_ids, u_t, basis_out):
     queries = query_ids.shape[0]
     _, rank, depth = u_t.shape
     eigen = basis_out.shape[1]
-    rows = queries * rank // n_in + WIN_ROWS
+    rows = queries * rank + WIN_ROWS
     tile = 256
     specs = [
         pl.BlockSpec((1, rank, depth), functools.partial(lambda q, n, ids: (ids[q], 0, 0), q))
@@ -70,41 +66,70 @@
     ]
     return pl.pallas_call(
         left_body,
-        out_shape=jax.ShapeDtypeStruct((n_in, rows, eigen), BF),
+        out_shape=jax.ShapeDtypeStruct((rows, eigen), BF),
         grid_spec=pltpu.PrefetchScalarGridSpec(
             num_scalar_prefetch=1,
             grid=(eigen // tile,),
             in_specs=[*specs, pl.BlockSpec((depth, tile), lambda n, ids: (0, n))],
-            out_specs=pl.BlockSpec((n_in, rows, tile), lambda n, ids: (0, 0, n)),
-        ),
-        compiler_params=params(16),
+            out_specs=pl.BlockSpec((rows, tile), lambda n, ids: (0, n)),
+        ),
+        compiler_params=params(10),
         name="left",
     )(query_ids, u_t, u_t, u_t, u_t, basis_out)
 
 
+def left_pair_body(where, own, other, out):
+    n_y, rows, _ = out.shape
+    each = rows - 2 * WIN_ROWS
+    near = lax.rem(where[2], 2)
+    last = n_y * each
+    for k in range(n_y):
+        at = slice(k * each, (k + 1) * each)
+        out[k, :each, :] = (own[at, :].astype(F32) + other[at, :].astype(F32)).astype(BF)
+        for part, place in ((own, near), (other, 1 - near)):
+            first = pl.multiple_of(each + place * WIN_ROWS, WIN_ROWS)
+            out[k, pl.ds(first, WIN_ROWS), :] = part[last:, :]
+
+
+def left_pair(where, own, other, n_y):
+    rows, eigen = own.shape
+    return pl.pallas_call(
+        left_pair_body,
+        out_shape=jax.ShapeDtypeStruct(
+            (n_y, (rows - WIN_ROWS) // n_y + 2 * WIN_ROWS, eigen), BF
+        ),
+        in_specs=[SMEM_SPEC, VMEM_SPEC, VMEM_SPEC],
+        out_specs=VMEM_SPEC,
+        compiler_params=params(3),
+        name="left_pair",
+    )(where, own, other)
+
+
 def left_sum_body(parts, out, window):
-    n_in, rows, _ = parts.shape
-    own = rows - WIN_ROWS
+    n_y, rows, _ = parts.shape
+    wins = 2 * WIN_ROWS
+    own = rows - wins
     total = parts[0, :own, :].astype(F32)
-    for i in range(1, n_in):
+    for i in range(1, n_y):
         total += parts[i, :own, :].astype(F32)
     total = total.astype(BF)
-    for i in range(n_in):
+    for i in range(n_y):
         out[i] = total
-        window[i * WIN_ROWS : (i + 1) * WIN_ROWS, :] = parts[i, own:, :]
+        window[i * wins : (i + 1) * wins, :] = parts[i, own:, :]
 
 
 def left_sum(parts):
-    n_in, rows, eigen = parts.shape
+    n_y, rows, eigen = parts.shape
+    wins = 2 * WIN_ROWS
     return pl.pallas_call(
         left_sum_body,
         out_shape=(
-            jax.ShapeDtypeStruct((n_in, rows - WIN_ROWS, eigen), BF),
-            jax.ShapeDtypeStruct((n_in * WIN_ROWS, eigen), BF),
+            jax.ShapeDtypeStruct((n_y, rows - wins, eigen), BF),
+            jax.ShapeDtypeStruct((n_y * wins, eigen), BF),
         ),
         in_specs=[VMEM_SPEC],
         out_specs=(VMEM_SPEC, VMEM_SPEC),
-        compiler_params=params(4),
+        compiler_params=params(3),
         name="left_sum",
     )(parts)
 
@@ -118,9 +143,11 @@
 
 
 def inverse_block(where, corrected, block, far, width, count, start=0, stop=None):
-    tile = 64
+    rows = (stop or corrected.shape[0]) - start
+    tile = min(rows, 256)
+    while start % tile or rows % tile:
+        tile -= 64
     first = start // tile
-    rows = (stop or corrected.shape[0]) - start
     return pl.pallas_call(
         inverse_body,
         out_shape=tuple(jax.ShapeDtypeStruct((rows, width), BF) for _ in range(count)),
@@ -156,7 +183,7 @@
         out_shape=tuple(jax.ShapeDtypeStruct((rows, width), BF) for _ in range(2)),
         in_specs=[SMEM_SPEC, *([VMEM_SPEC] * len(pieces))],
         out_specs=(VMEM_SPEC, VMEM_SPEC),
-        compiler_params=params(10),
+        compiler_params=params(6),
         name="halves",
     )(where, *pieces)
 
@@ -221,7 +248,7 @@
         out_shape=jax.ShapeDtypeStruct((4 * rows, width), BF),
         in_specs=[SMEM_SPEC, *([VMEM_SPEC] * 4)],
         out_specs=VMEM_SPEC,
-        compiler_params=params(8),
+        compiler_params=params(3),
         name="arrange",
     )(where, *parts)
 
@@ -277,7 +304,7 @@
             in_specs=[*specs, *(full((rows, width)) for _ in chunks)],
             out_specs=tuple(full(s) for s in shapes),
         ),
-        compiler_params=params(32),
+        compiler_params=params(20),
         name="rotate",
     )(where, query_ids, v_t, v_t, v_t, v_t, *chunks)
 
@@ -313,17 +340,16 @@
         out_shape=jax.ShapeDtypeStruct((queries, win, width), F32),
         in_specs=[VMEM_SPEC] * 7,
         out_specs=VMEM_SPEC,
-        compiler_params=params(24),
+        compiler_params=params(10),
         name="back_first",
     )(right, *lefts, *windows, *inverses)
 
 
 def back_body(where, block_ids, so_far, factors, right, tokens, delta, *refs, train):
-    out, refs = refs[-1], refs[:-1]
+    refs, (out, score) = refs[:-2], refs[-2:]
     queries = so_far.shape[0]
     n_z, rows, width = out.shape
-    win = so_far.shape[1]
-    per = win // n_z
+    per = rows // queries
     rank = right.shape[0] // queries
     valid = factors.shape[1] // 2
     skip = factors.shape[1] - width
@@ -334,45 +360,39 @@
     mine = jnp.logical_and(lane >= first, lane < first + valid)
     scale = jnp.where(mine, 1.0 / row, 0.0)
     which = lax.rem(lax.broadcasted_iota(jnp.int32, (tokens.shape[0], 1), 0), train)
-    scores = []
+    place = lax.broadcasted_iota(jnp.int32, (1, LANES), 1)
+    table = jnp.zeros((1, LANES), F32)
     for q in range(queries):
         total = so_far[q] + back_terms(right, refs[:2], refs[2:4], refs[4:], rank, q)
         total = (total * scale).astype(BF)
         out[:, q * per : (q + 1) * per, :] = total.reshape(n_z, per, width)
         projected = dot(tokens[...], total, 1, 1) * delta[...].astype(F32)
-        scores += [
-            jnp.sum(jnp.where(which == b, projected, 0.0), axis=0, keepdims=True)
-            for b in range(train)
-        ]
-    words = []
-    for k in range(0, queries * train, 8):
-        group = jnp.concatenate(scores[k : k + 8], axis=0)
-        high = group.astype(BF)
-        words += [high, (group - high.astype(F32)).astype(BF)]
-    words.append(jnp.zeros((8, width - len(words) * win), BF))
-    extra = jnp.concatenate(words, axis=1)
-    for k in range(n_z):
-        out[k, queries * per :, :] = extra
-
-
-def back(where, block_ids, so_far, factors, right, tokens, delta, near, n_z, train):
+        for b in range(train):
+            part = jnp.sum(jnp.where(which == b, projected, 0.0), axis=0, keepdims=True)
+            part = jnp.sum(part, axis=1, keepdims=True)
+            table = jnp.where(place == q * train + b, part, table)
+    score[...] = table
+
+
+def back(where, block_ids, so_far, factors, right, tokens, delta, far, n_z, train):
     queries, win, width = so_far.shape
-    depth = near[0].shape[1]
     return pl.pallas_call(
         functools.partial(back_body, train=train),
-        out_shape=jax.ShapeDtypeStruct((n_z, queries * win // n_z + 8, width), BF),
-        in_specs=[SMEM_SPEC, SMEM_SPEC, *([VMEM_SPEC] * (5 + len(near)))],
-        out_specs=VMEM_SPEC,
-        compiler_params=params(24),
+        out_shape=(
+            jax.ShapeDtypeStruct((n_z, queries * win // n_z, width), BF),
+            jax.ShapeDtypeStruct((1, LANES), F32),
+        ),
+        in_specs=[SMEM_SPEC, SMEM_SPEC, *([VMEM_SPEC] * (5 + len(far)))],
+        out_specs=(VMEM_SPEC, VMEM_SPEC),
+        compiler_params=params(12),
         name="back",
-    )(where, block_ids, so_far, factors, right, tokens, delta, *near)
-
-
-def tile_body(where, parts, basis, t0, t1, t2, t3, score, *, queries, train):
-    n_z = parts.shape[0]
+    )(where, block_ids, so_far, factors, right, tokens, delta, *far)
+
+
+def tile_body(where, parts, basis, *outs, queries):
+    n_z, rows, _ = parts.shape
     me = 2 * where[1] + where[3]
-    own = t0.shape[0]
-    rows = 4 * own
+    own = rows // 4
     per = own // queries
     total = parts[0].astype(F32)
     for k in range(1, n_z):
@@ -383,34 +403,20 @@
     owner = lax.rem(at // per, 4)
     goal = (owner ^ me) * own + query * per + lax.rem(at, per)
     select = jnp.where(goal == to, 1.0, 0.0).astype(BF)
-    half = dot(select, total[:rows].astype(BF), 1, 0).astype(BF)
+    half = dot(select, total.astype(BF), 1, 0).astype(BF)
     tiles = dot(half, basis[...], 1, 1).astype(BF)
-    for r, out in enumerate((t0, t1, t2, t3)):
+    for r, out in enumerate(outs):
         out[...] = tiles[r * own : (r + 1) * own]
-    words = total[rows:]
-    lane = lax.broadcasted_iota(jnp.int32, (1, LANES), 1)
-    table = jnp.zeros((1, LANES), F32)
-    for k in range(queries * train // 8):
-        at = 2 * k * LANES
-        sums = words[:, at : at + LANES] + words[:, at + LANES : at + 2 * LANES]
-        sums = jnp.sum(sums, axis=1, keepdims=True)
-        for i in range(8):
-            table = jnp.where(lane == 8 * k + i, sums[i : i + 1], table)
-    score[...] = jnp.broadcast_to(table[None], score.shape)
-
-
-def tile_part(where, parts, basis, plane, queries, train):
-    own = (parts.shape[1] - 8) // 4
-    block = basis.shape[0]
-    return pl.pallas_call(
-        functools.partial(tile_body, queries=queries, train=train),
-        out_shape=(
-            *(jax.ShapeDtypeStruct((own, block), BF) for _ in range(4)),
-            jax.ShapeDtypeStruct((plane, 1, LANES), F32),
-        ),
+
+
+def tile_part(where, parts, basis, queries):
+    own = parts.shape[1] // 4
+    return pl.pallas_call(
+        functools.partial(tile_body, queries=queries),
+        out_shape=tuple(jax.ShapeDtypeStruct((own, basis.shape[0]), BF) for _ in range(4)),
         in_specs=[SMEM_SPEC, VMEM_SPEC, VMEM_SPEC],
-        out_specs=tuple([VMEM_SPEC] * 5),
-        compiler_params=params(24),
+        out_specs=tuple([VMEM_SPEC] * 4),
+        compiler_params=params(8),
         name="tile",
     )(where, parts, basis)
 
@@ -439,7 +445,7 @@
         ),
         in_specs=[SMEM_SPEC, *([VMEM_SPEC] * 5)],
         out_specs=(VMEM_SPEC, VMEM_SPEC),
-        compiler_params=params(4),
+        compiler_params=params(3),
         name="final",
     )(where, *parts, score)
 
@@ -457,7 +463,7 @@
     x_pool,
     delta_pool,
 ):
-    n_z, n_in = lax.axis_size("z"), lax.axis_size(IN)
+    n_z = lax.axis_size("z")
     z, xh, c = lax.axis_index("z"), lax.axis_index("xh"), lax.axis_index("c")
     in_pos = lax.axis_index(IN)
     queries, train = query_ids.shape[0], train_ids.shape[0]
@@ -472,56 +478,64 @@
         swap(packed[2], "xh"),
         swap(packed[3], QUAD, 3),
     )
+    partial = left_part(
+        after(query_ids, packed[0]), jnp.transpose(u_pool, (0, 2, 1)), basis_out
+    )
+    other = swap(partial, "xl")
     rows = corrected.shape[0]
     ends = (0, 3 * rows // 8, 3 * rows // 4, rows)
     far = [
-        inverse_block(where, corrected, block, 1, block, 1, a, b)[0]
+        inverse_block(after(where, partial), corrected, block, 1, block, 1, a, b)[0]
         for a, b in zip(ends[:-1], ends[1:])
     ]
-    partial = left_part(query_ids, jnp.transpose(u_pool, (0, 2, 1)), basis_out, n_in)
-    own = arrange(where, (after(packed[0], far[0], partial), *parts[1:]), local_rows, train)
+    own = arrange(where, (after(packed[0], far[0]), *parts[1:]), local_rows, train)
     near = inverse_block(where, corrected, block, 0, width, 2)
     near = (near[0], swap(near[1], "c"))
 
+    partial = left_pair(where, partial, other, lax.axis_size("y"))
     ahead, behind = [shift(own, 1)], [shift(own, -1)]
-    far[0] = swap(far[0], "xh")
-    spread, window = left_sum(exchange(partial, IN))
-    up, down = after((ahead[0], behind[0]), spread)
-    far[1] = swap(after(far[1], ahead[0], spread), "xh")
+    far[0] = swap(after(far[0], other), "xh")
+    up, down = after((ahead[0], behind[0]), far[0])
+    spread, window = left_sum(exchange(partial, "y"))
+    far[1] = swap(after(far[1], ahead[0]), "xh")
     ahead.append(shift(up, 1))
     behind.append(shift(down, -1))
-    left = exchange(spread, IN).reshape(-1, basis_out.shape[1])
-    up, down, left = after((ahead[1], behind[1], left), far[0])
+    left = exchange(spread, "y").reshape(-1, basis_out.shape[1])
+    up, down, left = after((ahead[1], behind[1], left), far[1])
     ahead.append(shift(up, 1))
     behind.append(shift(down, -1))
-    up = after(ahead[2], behind[2], far[1])
-    ahead.append(shift(up, 1))
     far[2] = swap(after(far[2], left), "xh")
     left_x, window_x = swap(left, "xh"), swap(window, "xh")
     lefts = (left, swap(left, "c"))
     windows = (window, swap(window, "c"))
-    chunks = (own, *ahead, *behind[::-1])
+    up, left_x, window_x = after((ahead[2], left_x, window_x), behind[2])
+    ahead.append(shift(up, 1))
+    far = halves(where, far, width)
+    last, *far = after((ahead[3], *far))
+    chunks = (own, *ahead[:3], last, *behind[::-1])
 
     basis, right, tokens, delta = rotate(
         where, query_ids, jnp.transpose(v_pool, (0, 2, 1)), chunks, block
     )
-    so_far = back_first(right, lefts, windows, near, queries)
-    left_x, window_x, *far = after((left_x, window_x, *far), so_far)
-    far = halves(where, far, width)
-    far = (left_x, swap(left_x, "c"), window_x, swap(window_x, "c"), far[0], swap(far[1], "c"))
-    parts = back(
+    left_x, window_x, right_x = after((left_x, window_x, right))
+    left_d, window_d = swap(left_x, "c"), swap(window_x, "c")
+    so_far = back_first(right_x, lefts, windows, near, queries)
+    far = (left_x, left_d, window_x, window_d, far[0], swap(far[1], "c"))
+    parts, score = back(
         where, block_ids, so_far, factor_table, right, tokens, delta, far, n_z, train
     )
-    *parts, score = tile_part(
-        where, exchange(parts, "z"), basis, lax.axis_size(PLANE), queries, train
-    )
+    for axis, mask in (("c", 1), ("xl", 1), ("y", 1), ("y", 2), ("xh", 1)):
+        score = score + swap(score, axis, mask)
+    parts, score = after((exchange(parts, "z"), score))
+    parts = tile_part(where, parts, basis, queries)
+    score = exchange(jnp.broadcast_to(score, (n_z, *score.shape)), "z")
     parts = (
         parts[0],
         swap(parts[1], "c"),
         swap(parts[2], "xh"),
         swap(parts[3], QUAD, 3),
     )
-    return final(where, parts, exchange(score, PLANE), queries, train)
+    return final(where, parts, score, queries, train)
 
 
 def solution(mesh):

time: 151 us -> 162 us (1.073)
  waiting for transfers between devices: 13.4 us -> 46.2 us
  blocking collectives: 44.5 us -> 16.8 us
  local copies, waits for them, and re-layouts: 4.23 us -> 11.2 us
  Pallas kernels: 37.2 us -> 34.3 us
    all_to_all x2, blocking collectives: 44.5 us -> 16.8 us  [exchange(): return lax.all_to_all(value, axis, split_axis=0, concat_axis=0, tiled=True)]
    ppermute x17 -> x23, waiting for transfers between devices: 3.17 us -> 23.6 us  [swap(): return lax.ppermute(value, axis, [(i, i ^ mask) for i in range(size)])]
    all_to_all x2, waiting for transfers between devices: 8.71 us -> 16 us  [exchange(): return lax.all_to_all(value, axis, split_axis=0, concat_axis=0, tiled=True)]
    unnamed x31 -> x43, local copies, waits for them, and re-layouts: 4.23 us -> 11.2 us
    ppermute x7, waiting for transfers between devices: 1.52 us -> 6.58 us  [shift(): lax.ppermute(value, 'z', [(i, (i + step) % size) for i in range(size)])]
    pallas_call x4, Pallas kernels: 16.5 us -> 12.6 us  [inverse_block(): pl.pallas_call(inverse_body, out_shape=tuple((jax.ShapeDtypeStruct((rows,...]
    ppermute x17 -> x23, starting transfers between devices: 32.1 us -> 29.7 us  [swap(): return lax.ppermute(value, axis, [(i, i ^ mask) for i in range(size)])]
    all_to_all x2, starting transfers between devices: 8.4 us -> 10.3 us  [exchange(): return lax.all_to_all(value, axis, split_axis=0, concat_axis=0, tiled=True)]
  transfers between devices with their start and end apart: 26 -> 32, of which waited for: 5 -> 11; matrix products, arithmetic and copies ran while one was open for 0% -> 0% of each run, Pallas kernels for 18% -> 15%
where the time goes in v6:
time: 162 us; the launch traced here: 161 us
  starting transfers between devices  51.3 us (32%)
  waiting for transfers between devices  46.2 us (29%)
  Pallas kernels  34.3 us (21%)
  blocking collectives  16.8 us (10%)
  local copies, waits for them, and re-layouts  11.2 us (7%)
    ppermute x23, starting transfers between devices, swap(): return lax.ppermute(value, axis, [(i, i ^ mask) for i in range(size)])  29.7 us
    ppermute x23, waiting for transfers between devices, swap(): return lax.ppermute(value, axis, [(i, i ^ mask) for i in range(size)])  23.6 us
    all_to_all x2, blocking collectives, exchange(): return lax.all_to_all(value, axis, split_axis=0, concat_axis=0, tiled=True)  16.8 us
    all_to_all x2, waiting for transfers between devices, exchange(): return lax.all_to_all(value, axis, split_axis=0, concat_axis=0, tiled=True)  16 us
    pallas_call x4, Pallas kernels, inverse_block(): pl.pallas_call(inverse_body, out_shape=tuple((jax.ShapeDtypeStruct((rows,...  12.6 us
    ppermute x7, starting transfers between devices, shift(): lax.ppermute(value, 'z', [(i, (i + step) % size) for i in range(size)])  11.3 us
    unnamed x43, local copies, waits for them, and re-layouts  11.2 us
    all_to_all x2, starting transfers between devices, exchange(): return lax.all_to_all(value, axis, split_axis=0, concat_axis=0, tiled=True)  10.3 us
  transfers between devices with their start and end apart: 32, of which 11 were waited for; matrix products, arithmetic and copies ran while one was open for 0% of the time, Pallas kernels for 15%

profile of v6, /device:TPU:1, one launch (start us, length us, event | category | flops | bytes accessed | tf_op | source)
XLA Modules:
  0.0 160.8 jit_solution(7907613937753520557)
XLA Ops:
  0.6 1.0 copy.13.basis
  1.8 0.8 copy-done.15
  2.6 0.7 copy-done.16
  3.2 0.7 copy-done.19
  3.9 0.7 pack.1
  4.7 1.4 copy-done.1
  6.1 1.6 copy-done.4
  7.7 0.7 copy-done.17
  8.3 1.6 %left.1.own = bf16[272,512]{1,0:T(8,128)(2,1)S(1)} custom-call(s32[4]{0:T(128)S(1)} %copy-done.17, bf16[6,64,2048]{2,1,0:T(8,128)(2,1)S(1)} %bitcast.14, bf16[6,64,2048]{2,1,0:T(8,128)(2,1)S(1)} %bitcast.15, bf16[6,64,2048]{2,1,0:T(8,128)(2,1)S(1)} %bitcast.16, bf16[6,64,2048]{2,1,0:T(8,128)(2,1)S(1)} %bitcast.17, bf16[2048,512]{1,0:T(8,128)(2,1)S(1)} %copy-done.4), custom_call_target="tpu_custom_call" | custom-call | tf_op jit(solution)/shard_map/left/pallas_call | solution.py:67
  10.0 2.1 %collective-permute-start.5 = (bf16[272,512]{1,0:T(8,128)(2,1)S(1)}, bf16[272,512]{1,0:T(8,128)(2,1)S(1)}, u32[]{:S(2)}, u32[]{:S(2)}) collective-permute-start(bf16[272,512]{1,0:T(8,128)(2,1)S(1)} %left.1.own), channel_id=1, source_target_pairs={{0,1},{1,0},{2,3},{3,2},{4,5},{5,4},{6,7},{7,6},{8,9},{9,8},{10,11... | collective-permute-start | bytes 835592 | tf_op jit(solution)/shard_map/ppermute | solution.py:38
  12.1 1.3 collective-permute-start
  13.4 2.1 %collective-permute-start.1 = (bf16[60,896]{1,0:T(8,128)(2,1)S(1)}, bf16[60,896]{1,0:T(8,128)(2,1)S(1)}, u32[]{:S(2)}, u32[]{:S(2)}) collective-permute-start(bf16[60,896]{1,0:T(8,128)(2,1)S(1)} %get-tuple-element.49), channel_id=1, source_target_pairs={{0,16},{16,0},{1,17},{17,1},{2,18},{18,2},{3,19},{19,3},{4,20},{20... | collective-permute-start | bytes 322568 | tf_op jit(solution)/shard_map/ppermute | solution.py:38
  15.5 1.1 collective-permute-start.2
  16.6 3.0 %inverse.4 = bf16[192,1664]{1,0:T(8,128)(2,1)} custom-call(s32[4]{0:T(128)} %copy-done.11, f32[512,3328]{1,0:T(8,128)} %corrected.7), custom_call_target="tpu_custom_call" | custom-call | tf_op jit(solution)/shard_map/inverse/pallas_call | solution.py:151
  19.6 3.4 %collective-permute-done.1.a2 = bf16[60,896]{1,0:T(8,128)(2,1)S(1)} collective-permute-done((bf16[60,896]{1,0:T(8,128)(2,1)S(1)}, bf16[60,896]{1,0:T(8,128)(2,1)S(1)}, u32[]{:S(2)}, u32[]{:S(2)}) %collective-permute-start.1) | collective-permute-done | bytes 107552 | tf_op jit(solution)/shard_map/ppermute | solution.py:38
  23.1 3.3 %collective-permute-done.2.a3 = bf16[60,896]{1,0:T(8,128)(2,1)S(1)} collective-permute-done((bf16[60,896]{1,0:T(8,128)(2,1)S(1)}, bf16[60,896]{1,0:T(8,128)(2,1)S(1)}, u32[]{:S(2)}, u32[]{:S(2)}) %collective-permute-start.2) | collective-permute-done | bytes 107552 | tf_op jit(solution)/shard_map/ppermute | solution.py:38
  26.4 1.2 arrange.1.refs_0_
  27.6 1.7 %collective-permute-start.3 = (bf16[240,896]{1,0:T(8,128)(2,1)S(1)}, bf16[240,896]{1,0:T(8,128)(2,1)S(1)}, u32[]{:S(2)}, u32[]{:S(2)}) collective-permute-start(bf16[240,896]{1,0:T(8,128)(2,1)S(1)} %arrange.1.refs_0_), channel_id=1, source_target_pairs={{0,32},{32,64},{64,96},{96,128},{128,160},{160,192},{192,224},{224... | collective-permute-start | bytes 1290248 | tf_op jit(solution)/shard_map/ppermute | solution.py:43
  29.3 0.5 collective-permute-start.6
  29.8 4.0 %collective-permute-start.4 = (bf16[240,896]{1,0:T(8,128)(2,1)S(1)}, bf16[240,896]{1,0:T(8,128)(2,1)S(1)}, u32[]{:S(2)}, u32[]{:S(2)}) collective-permute-start(bf16[240,896]{1,0:T(8,128)(2,1)S(1)} %arrange.1.refs_0_), channel_id=1, source_target_pairs={{0,224},{32,0},{64,32},{96,64},{128,96},{160,128},{192,160},{224,1... | collective-permute-start | bytes 1290248 | tf_op jit(solution)/shard_map/ppermute | solution.py:43
  33.9 3.0 %inverse.5 = bf16[192,1664]{1,0:T(8,128)(2,1)} custom-call(s32[4]{0:T(128)} %copy-done.11, f32[512,3328]{1,0:T(8,128)} %corrected.7), custom_call_target="tpu_custom_call" | custom-call | tf_op jit(solution)/shard_map/inverse/pallas_call | solution.py:151
  36.9 6.6 %collective-permute-done.3.refs_1_ = bf16[240,896]{1,0:T(8,128)(2,1)S(1)} collective-permute-done((bf16[240,896]{1,0:T(8,128)(2,1)S(1)}, bf16[240,896]{1,0:T(8,128)(2,1)S(1)}, u32[]{:S(2)}, u32[]{:S(2)}) %collective-permute-start.3) | collective-permute-done | bytes 430112 | tf_op jit(solution)/shard_map/ppermute | solution.py:43
  43.4 0.4 collective-permute-start.9
  43.8 1.4 left_pair.1
  45.2 4.2 %all-to-all-start = ((bf16[4,96,512]{2,1,0:T(8,128)(2,1)}), bf16[4,96,512]{2,1,0:T(8,128)(2,1)S(1)}, u32[]{:S(2)}, u32[]{:S(2)}) async-start(bf16[4,96,512]{2,1,0:T(8,128)(2,1)} %left_pair.1), calls=%async_computation | async-start | bytes 786432 | tf_op jit(solution)/shard_map/all_to_all | solution.py:33
  49.4 2.7 %collective-permute-start.8 = (bf16[240,896]{1,0:T(8,128)(2,1)S(1)}, bf16[240,896]{1,0:T(8,128)(2,1)}, u32[]{:S(2)}, u32[]{:S(2)}) collective-permute-start(bf16[240,896]{1,0:T(8,128)(2,1)S(1)} %collective-permute-done.4.refs_7_), channel_id=1, source_target_pairs={{0,224},{32,0},{64,32},{96,64},{128,96},{160,128},{192,160},{224,1... | collective-permute-start | bytes 1290248 | tf_op jit(solution)/shard_map/ppermute | solution.py:43
  52.1 4.5 %all-to-all-done.parts = bf16[4,96,512]{2,1,0:T(8,128)(2,1)S(1)} async-done(((bf16[4,96,512]{2,1,0:T(8,128)(2,1)}), bf16[4,96,512]{2,1,0:T(8,128)(2,1)S(1)}, u32[]{:S(2)}, u32[]{:S(2)}) %all-to-all-start) | async-done | bytes 393248 | tf_op jit(solution)/shard_map/all_to_all | solution.py:33
  56.7 7.9 %all_to_all.20 = bf16[4,64,512]{2,1,0:T(8,128)(2,1)S(1)} all-to-all(bf16[4,64,512]{2,1,0:T(8,128)(2,1)S(1)} %get-tuple-element.54), channel_id=1, replica_groups=mesh['z'=8,'xh'=2,'c'=2,'y'=4,'xl'=2] {'y'}, dimensions={0} | all-to-all | bytes 524288 | tf_op jit(solution)/shard_map/all_to_all | solution.py:33
  64.7 2.7 %collective-permute-start.13 = (bf16[240,896]{1,0:T(8,128)(2,1)}, bf16[240,896]{1,0:T(8,128)(2,1)S(1)}, u32[]{:S(2)}, u32[]{:S(2)}) collective-permute-start(bf16[240,896]{1,0:T(8,128)(2,1)} %collective-permute-done.8.refs_6_), channel_id=1, source_target_pairs={{0,224},{32,0},{64,32},{96,64},{128,96},{160,128},{192,160},{224,1... | collective-permute-start | bytes 1290248 | tf_op jit(solution)/shard_map/ppermute | solution.py:43
  67.4 2.6 %collective-permute-start.11 = (bf16[256,512]{1,0:T(8,128)(2,1)S(1)}, bf16[256,512]{1,0:T(8,128)(2,1)S(1)}, u32[]{:S(2)}, u32[]{:S(2)}) collective-permute-start(bf16[256,512]{1,0:T(8,128)(2,1)S(1)} %bitcast.18), channel_id=1, source_target_pairs={{0,16},{16,0},{1,17},{17,1},{2,18},{18,2},{3,19},{19,3},{4,20},{20... | collective-permute-start | bytes 786440 | tf_op jit(solution)/shard_map/ppermute | solution.py:38
  69.9 0.4 collective-permute-start.12
  70.3 5.7 %collective-permute-done.12.refs_2_ = bf16[128,512]{1,0:T(8,128)(2,1)S(1)} collective-permute-done((bf16[128,512]{1,0:T(8,128)(2,1)S(1)}, bf16[128,512]{1,0:T(8,128)(2,1)S(1)}, u32[]{:S(2)}, u32[]{:S(2)}) %collective-permute-start.12) | collective-permute-done | bytes 131104 | tf_op jit(solution)/shard_map/ppermute | solution.py:38
  76.1 0.7 copy-done.8
  76.8 0.7 copy-done.6
  77.5 2.7 %inverse.6 = bf16[128,1664]{1,0:T(8,128)(2,1)} custom-call(s32[4]{0:T(128)} %copy-done.11, f32[512,3328]{1,0:T(8,128)} %corrected.7), custom_call_target="tpu_custom_call" | custom-call | tf_op jit(solution)/shard_map/inverse/pallas_call | solution.py:151
  80.2 2.6 %collective-permute-start.15 = (bf16[128,1664]{1,0:T(8,128)(2,1)}, bf16[128,1664]{1,0:T(8,128)(2,1)}, u32[]{:S(2)}, u32[]{:S(2)}) collective-permute-start(bf16[128,1664]{1,0:T(8,128)(2,1)} %inverse.6), channel_id=1, source_target_pairs={{0,16},{16,0},{1,17},{17,1},{2,18},{18,2},{3,19},{19,3},{4,20},{20... | collective-permute-start | bytes 1277960 | tf_op jit(solution)/shard_map/ppermute | solution.py:38
  82.8 3.9 %inverse.7 = (bf16[512,896]{1,0:T(8,128)(2,1)}, bf16[512,896]{1,0:T(8,128)(2,1)}) custom-call(s32[4]{0:T(128)} %copy-done.11, f32[512,3328]{1,0:T(8,128)} %corrected.7), custom_call_target="tpu_custom_call" | custom-call | tf_op jit(solution)/shard_map/inverse/pallas_call | solution.py:151
  86.7 4.6 %collective-permute-start.18 = (bf16[512,896]{1,0:T(8,128)(2,1)}, bf16[512,896]{1,0:T(8,128)(2,1)S(1)}, u32[]{:S(2)}, u32[]{:S(2)}) collective-permute-start(bf16[512,896]{1,0:T(8,128)(2,1)} %get-tuple-element.70), channel_id=1, source_target_pairs={{0,8},{8,0},{1,9},{9,1},{2,10},{10,2},{3,11},{11,3},{4,12},{12,4},... | collective-permute-start | bytes 2752520 | tf_op jit(solution)/shard_map/ppermute | solution.py:38
  91.3 1.2 halves.1
  92.5 3.3 %collective-permute-start.21 = (bf16[512,896]{1,0:T(8,128)(2,1)S(1)}, bf16[512,896]{1,0:T(8,128)(2,1)S(1)}, u32[]{:S(2)}, u32[]{:S(2)}) collective-permute-start(bf16[512,896]{1,0:T(8,128)(2,1)S(1)} %get-tuple-element.76), channel_id=1, source_target_pairs={{0,8},{8,0},{1,9},{9,1},{2,10},{10,2},{3,11},{11,3},{4,12},{12,4},... | collective-permute-start | bytes 2752520 | tf_op jit(solution)/shard_map/ppermute | solution.py:38
  95.9 0.4 collective-permute-start.16
  96.3 1.0 copy-done.7
  97.3 3.7 %rotate.1 = (bf16[1664,896]{1,0:T(8,128)(2,1)S(1)}, bf16[256,896]{1,0:T(8,128)(2,1)S(1)}, bf16[128,896]{1,0:T(8,128)(2,1)S(1)}, bf16[128,128]{1,0:T(8,128)(2,1)S(1)}) custom-call(s32[4]{0:T(128)S(1)} %copy-done.14, s32[4]{0:T(128)S(1)} %copy-done.18, bf16[6,64,3328]{2,1,0:T(8,128)(2,1)S(1)} %bitcast.10, bf16[6,64,3328]{2,1,0:T(8,128)(2,1)S(1)} %bitcast.11, ...), custom_call_target="tpu_custom_call" | custom-call | tf_op jit(solution)/shard_map/rotate/pallas_call | solution.py:298
  101.2 0.4 collective-permute-start.20
  101.7 3.3 %back_first.1.so_far = f32[4,128,896]{2,1,0:T(8,128)S(1)} custom-call(bf16[256,896]{1,0:T(8,128)(2,1)S(1)} %get-tuple-element.68.right, bf16[256,512]{1,0:T(8,128)(2,1)S(1)} %bitcast.20, bf16[256,512]{1,0:T(8,128)(2,1)S(1)} %collective-permute-done.16.refs_1_, bf16[128,512]{1,0:T(8,128)(2,1)S(1)} %get-tuple-element.58.refs_2_, ...), custom_call_target="tpu_custom_call" | custom-call | tf_op jit(solution)/shard_map/back_first/pallas_call | solution.py:338
  105.1 5.7 %back.1 = (bf16[8,64,896]{2,1,0:T(8,128)(2,1)}, f32[1,128]{1,0:T(1,128)S(1)}) custom-call(s32[4]{0:T(128)S(1)} %copy-done.14, s32[16]{0:T(128)S(1)} %copy-done.20, f32[4,128,896]{2,1,0:T(8,128)S(1)} %back_first.1.so_far, f32[32,1664]{1,0:T(8,128)S(1)} %copy-done.10, bf16[256,896]{1,0:T(8,128)(2,1)S(1)} %get-tuple-element.68.right, ...), custom_call_target="tpu_custom_call" | custom-call | tf_op jit(solution)/shard_map/back/pallas_call | solution.py:379
  110.8 6.2 %all-to-all-start.2 = ((bf16[8,64,896]{2,1,0:T(8,128)(2,1)}), bf16[8,64,896]{2,1,0:T(8,128)(2,1)S(1)}, u32[]{:S(2)}, u32[]{:S(2)}) async-start(bf16[8,64,896]{2,1,0:T(8,128)(2,1)} %get-tuple-element.77), calls=%async_computation.2 | async-start | bytes 1835008 | tf_op jit(solution)/shard_map/all_to_all | solution.py:33
  117.0 0.4 collective-permute-start.22
  117.3 0.8 collective-permute-done.22
  118.2 2.6 %collective-permute-done.23 = f32[1,128]{1,0:T(1,128)S(1)} collective-permute-done((f32[1,128]{1,0:T(1,128)S(1)}, f32[1,128]{1,0:T(1,128)S(1)}, u32[]{:S(2)}, u32[]{:S(2)}) %collective-permute-start.23) | collective-permute-done | bytes 544 | tf_op jit(solution)/shard_map/ppermute | solution.py:38
  120.8 0.3 collective-permute-start.24
  121.1 2.4 %collective-permute-done.24 = f32[1,128]{1,0:T(1,128)S(1)} collective-permute-done((f32[1,128]{1,0:T(1,128)S(1)}, f32[1,128]{1,0:T(1,128)S(1)}, u32[]{:S(2)}, u32[]{:S(2)}) %collective-permute-start.24) | collective-permute-done | bytes 544 | tf_op jit(solution)/shard_map/ppermute | solution.py:38
  123.5 0.8 collective-permute-start.25
  124.4 3.3 %collective-permute-done.25 = f32[1,128]{1,0:T(1,128)S(1)} collective-permute-done((f32[1,128]{1,0:T(1,128)S(1)}, f32[1,128]{1,0:T(1,128)S(1)}, u32[]{:S(2)}, u32[]{:S(2)}) %collective-permute-start.25) | collective-permute-done | bytes 544 | tf_op jit(solution)/shard_map/ppermute | solution.py:38
  127.7 2.3 %collective-permute-start.26 = (f32[1,128]{1,0:T(1,128)S(1)}, f32[1,128]{1,0:T(1,128)S(1)}, u32[]{:S(2)}, u32[]{:S(2)}) collective-permute-start(f32[1,128]{1,0:T(1,128)S(1)} %add.22), channel_id=1, source_target_pairs={{0,16},{16,0},{1,17},{17,1},{2,18},{18,2},{3,19},{19,3},{4,20},{20... | collective-permute-start | bytes 1544 | tf_op jit(solution)/shard_map/ppermute | solution.py:38
  130.0 1.9 %collective-permute-done.26 = f32[1,128]{1,0:T(1,128)S(1)} collective-permute-done((f32[1,128]{1,0:T(1,128)S(1)}, f32[1,128]{1,0:T(1,128)S(1)}, u32[]{:S(2)}, u32[]{:S(2)}) %collective-permute-start.26) | collective-permute-done | bytes 544 | tf_op jit(solution)/shard_map/ppermute | solution.py:38
  131.9 11.5 %all-to-all-done.2.parts = bf16[8,64,896]{2,1,0:T(8,128)(2,1)S(1)} async-done(((bf16[8,64,896]{2,1,0:T(8,128)(2,1)}), bf16[8,64,896]{2,1,0:T(8,128)(2,1)S(1)}, u32[]{:S(2)}, u32[]{:S(2)}) %all-to-all-start.2) | async-done | bytes 917536 | tf_op jit(solution)/shard_map/all_to_all | solution.py:33
  143.4 1.8 %copy-done.3 = bf16[1664,896]{1,0:T(8,128)(2,1)S(1)} copy-done((bf16[1664,896]{1,0:T(8,128)(2,1)S(1)}, bf16[1664,896]{1,0:T(8,128)(2,1)}, u32[]{:S(2)}) %copy-start.3) | copy-done | bytes 2981912
  145.2 1.7 %tile.1 = (bf16[16,1664]{1,0:T(8,128)(2,1)S(1)}, bf16[16,1664]{1,0:T(8,128)(2,1)S(1)}, bf16[16,1664]{1,0:T(8,128)(2,1)S(1)}, bf16[16,1664]{1,0:T(8,128)(2,1)S(1)}) custom-call(s32[4]{0:T(128)S(1)} %copy-done.14, bf16[8,64,896]{2,1,0:T(8,128)(2,1)S(1)} %all-to-all-done.2.parts, bf16[1664,896]{1,0:T(8,128)(2,1)S(1)} %copy-done.3), custom_call_target="tpu_custom_call" | custom-call | tf_op jit(solution)/shard_map/tile/pallas_call | solution.py:414
  146.9 0.6 collective-permute-start.27
  147.4 2.3 %collective-permute-start.28 = (bf16[16,1664]{1,0:T(8,128)(2,1)S(1)}, bf16[16,1664]{1,0:T(8,128)(2,1)S(1)}, u32[]{:S(2)}, u32[]{:S(2)}) collective-permute-start(bf16[16,1664]{1,0:T(8,128)(2,1)S(1)} %get-tuple-element.83), channel_id=1, source_target_pairs={{0,16},{16,0},{1,17},{17,1},{2,18},{18,2},{3,19},{19,3},{4,20},{20... | collective-permute-start | bytes 159752 | tf_op jit(solution)/shard_map/ppermute | solution.py:38
  149.7 0.9 collective-permute-start.29
  150.7 8.9 %all_to_all.21.score = f32[8,1,128]{2,1,0:T(1,128)S(1)} all-to-all(f32[8,1,128]{2,1,0:T(1,128)S(1)} %broadcast_in_dim.3), channel_id=1, replica_groups=mesh['z'=8,'xh'=2,'c'=2,'y'=4,'xl'=2] {'z'}, dimensions={0} | all-to-all | bytes 8192 | tf_op jit(solution)/shard_map/all_to_all | solution.py:33
  159.6 1.2 final.1
  (67 shorter events, 0.8 us)
Async XLA Ops:
  1.8 8.2 %copy-start.11 = (s32[4]{0:T(128)}, s32[4]{0:T(128)S(1)}, u32[]{:S(2)}) copy-start(s32[4]{0:T(128)S(1)} %pad_add_fusion.where) | copy-start | bytes 52
  1.8 0.8 copy-start.15
  2.6 0.7 copy-start.16
  3.2 0.7 copy-start.19
  4.7 1.4 copy-start.1
  6.1 1.6 copy-start.4
  7.7 0.7 copy-start.17
  10.0 19.3 %collective-permute-start.5 = (bf16[272,512]{1,0:T(8,128)(2,1)S(1)}, bf16[272,512]{1,0:T(8,128)(2,1)S(1)}, u32[]{:S(2)}, u32[]{:S(2)}) collective-permute-start(bf16[272,512]{1,0:T(8,128)(2,1)S(1)} %left.1.own), channel_id=1, source_target_pairs={{0,1},{1,0},{2,3},{3,2},{4,5},{5,4},{6,7},{7,6},{8,9},{9,8},{10,11... | collective-permute-start | bytes 835592 | tf_op jit(solution)/shard_map/ppermute | solution.py:38
  12.1 7.5 %collective-permute-start = (bf16[60,896]{1,0:T(8,128)(2,1)S(1)}, bf16[60,896]{1,0:T(8,128)(2,1)S(1)}, u32[]{:S(2)}, u32[]{:S(2)}) collective-permute-start(bf16[60,896]{1,0:T(8,128)(2,1)S(1)} %get-tuple-element.48), channel_id=1, source_target_pairs={{0,8},{8,0},{1,9},{9,1},{2,10},{10,2},{3,11},{11,3},{4,12},{12,4},... | collective-permute-start | bytes 322568 | tf_op jit(solution)/shard_map/ppermute | solution.py:38
  13.4 9.7 %collective-permute-start.1 = (bf16[60,896]{1,0:T(8,128)(2,1)S(1)}, bf16[60,896]{1,0:T(8,128)(2,1)S(1)}, u32[]{:S(2)}, u32[]{:S(2)}) collective-permute-start(bf16[60,896]{1,0:T(8,128)(2,1)S(1)} %get-tuple-element.49), channel_id=1, source_target_pairs={{0,16},{16,0},{1,17},{17,1},{2,18},{18,2},{3,19},{19,3},{4,20},{20... | collective-permute-start | bytes 322568 | tf_op jit(solution)/shard_map/ppermute | solution.py:38
  15.5 10.9 %copy-start.12 = (s32[4]{0:T(128)S(1)}, s32[4]{0:T(128)}, u32[]{:S(2)}) copy-start(s32[4]{0:T(128)} %copy-done.11) | copy-start | bytes 52
  15.5 10.9 %collective-permute-start.2 = (bf16[60,896]{1,0:T(8,128)(2,1)S(1)}, bf16[60,896]{1,0:T(8,128)(2,1)S(1)}, u32[]{:S(2)}, u32[]{:S(2)}) collective-permute-start(bf16[60,896]{1,0:T(8,128)(2,1)S(1)} %get-tuple-element.50), channel_id=1, source_target_pairs={{0,24},{8,16},{16,8},{24,0},{1,25},{9,17},{17,9},{25,1},{2,26},{10... | collective-permute-start | bytes 322568 | tf_op jit(solution)/shard_map/ppermute | solution.py:38
  27.6 16.2 %copy-start.13 = (s32[4]{0:T(128)S(1)}, s32[4]{0:T(128)}, u32[]{:S(2)}) copy-start(s32[4]{0:T(128)} %copy-done.11) | copy-start | bytes 52
  27.6 15.8 %collective-permute-start.3 = (bf16[240,896]{1,0:T(8,128)(2,1)S(1)}, bf16[240,896]{1,0:T(8,128)(2,1)S(1)}, u32[]{:S(2)}, u32[]{:S(2)}) collective-permute-start(bf16[240,896]{1,0:T(8,128)(2,1)S(1)} %arrange.1.refs_0_), channel_id=1, source_target_pairs={{0,32},{32,64},{64,96},{96,128},{128,160},{160,192},{192,224},{224... | collective-permute-start | bytes 1290248 | tf_op jit(solution)/shard_map/ppermute | solution.py:43
  29.3 20.0 %collective-permute-start.6 = (bf16[192,1664]{1,0:T(8,128)(2,1)}, bf16[192,1664]{1,0:T(8,128)(2,1)S(1)}, u32[]{:S(2)}, u32[]{:S(2)}) collective-permute-start(bf16[192,1664]{1,0:T(8,128)(2,1)} %inverse.4), channel_id=1, source_target_pairs={{0,16},{16,0},{1,17},{17,1},{2,18},{18,2},{3,19},{19,3},{4,20},{20... | collective-permute-start | bytes 1916936 | tf_op jit(solution)/shard_map/ppermute | solution.py:38
  29.8 19.5 %collective-permute-start.4 = (bf16[240,896]{1,0:T(8,128)(2,1)S(1)}, bf16[240,896]{1,0:T(8,128)(2,1)S(1)}, u32[]{:S(2)}, u32[]{:S(2)}) collective-permute-start(bf16[240,896]{1,0:T(8,128)(2,1)S(1)} %arrange.1.refs_0_), channel_id=1, source_target_pairs={{0,224},{32,0},{64,32},{96,64},{128,96},{160,128},{192,160},{224,1... | collective-permute-start | bytes 1290248 | tf_op jit(solution)/shard_map/ppermute | solution.py:43
  43.4 21.2 %collective-permute-start.9 = (bf16[192,1664]{1,0:T(8,128)(2,1)}, bf16[192,1664]{1,0:T(8,128)(2,1)S(1)}, u32[]{:S(2)}, u32[]{:S(2)}) collective-permute-start(bf16[192,1664]{1,0:T(8,128)(2,1)} %inverse.5), channel_id=1, source_target_pairs={{0,16},{16,0},{1,17},{17,1},{2,18},{18,2},{3,19},{19,3},{4,20},{20... | collective-permute-start | bytes 1916936 | tf_op jit(solution)/shard_map/ppermute | solution.py:38
  45.2 11.5 %all-to-all-start = ((bf16[4,96,512]{2,1,0:T(8,128)(2,1)}), bf16[4,96,512]{2,1,0:T(8,128)(2,1)S(1)}, u32[]{:S(2)}, u32[]{:S(2)}) async-start(bf16[4,96,512]{2,1,0:T(8,128)(2,1)} %left_pair.1), calls=%async_computation | async-start | bytes 786432 | tf_op jit(solution)/shard_map/all_to_all | solution.py:33
  49.4 15.3 %collective-permute-start.7 = (bf16[240,896]{1,0:T(8,128)(2,1)S(1)}, bf16[240,896]{1,0:T(8,128)(2,1)S(1)}, u32[]{:S(2)}, u32[]{:S(2)}) collective-permute-start(bf16[240,896]{1,0:T(8,128)(2,1)S(1)} %collective-permute-done.3.refs_1_), channel_id=1, source_target_pairs={{0,32},{32,64},{64,96},{96,128},{128,160},{160,192},{192,224},{224... | collective-permute-start | bytes 1290248 | tf_op jit(solution)/shard_map/ppermute | solution.py:43
  49.4 15.2 %collective-permute-start.8 = (bf16[240,896]{1,0:T(8,128)(2,1)S(1)}, bf16[240,896]{1,0:T(8,128)(2,1)}, u32[]{:S(2)}, u32[]{:S(2)}) collective-permute-start(bf16[240,896]{1,0:T(8,128)(2,1)S(1)} %collective-permute-done.4.refs_7_), channel_id=1, source_target_pairs={{0,224},{32,0},{64,32},{96,64},{128,96},{160,128},{192,160},{224,1... | collective-permute-start | bytes 1290248 | tf_op jit(solution)/shard_map/ppermute | solution.py:43
  64.6 11.4 %collective-permute-start.10 = (bf16[240,896]{1,0:T(8,128)(2,1)S(1)}, bf16[240,896]{1,0:T(8,128)(2,1)}, u32[]{:S(2)}, u32[]{:S(2)}) collective-permute-start(bf16[240,896]{1,0:T(8,128)(2,1)S(1)} %collective-permute-done.7.refs_2_), channel_id=1, source_target_pairs={{0,32},{32,64},{64,96},{96,128},{128,160},{160,192},{192,224},{224... | collective-permute-start | bytes 1290248 | tf_op jit(solution)/shard_map/ppermute | solution.py:43
  64.7 11.4 %collective-permute-start.13 = (bf16[240,896]{1,0:T(8,128)(2,1)}, bf16[240,896]{1,0:T(8,128)(2,1)S(1)}, u32[]{:S(2)}, u32[]{:S(2)}) collective-permute-start(bf16[240,896]{1,0:T(8,128)(2,1)} %collective-permute-done.8.refs_6_), channel_id=1, source_target_pairs={{0,224},{32,0},{64,32},{96,64},{128,96},{160,128},{192,160},{224,1... | collective-permute-start | bytes 1290248 | tf_op jit(solution)/shard_map/ppermute | solution.py:43
  67.4 8.7 %collective-permute-start.11 = (bf16[256,512]{1,0:T(8,128)(2,1)S(1)}, bf16[256,512]{1,0:T(8,128)(2,1)S(1)}, u32[]{:S(2)}, u32[]{:S(2)}) collective-permute-start(bf16[256,512]{1,0:T(8,128)(2,1)S(1)} %bitcast.18), channel_id=1, source_target_pairs={{0,16},{16,0},{1,17},{17,1},{2,18},{18,2},{3,19},{19,3},{4,20},{20... | collective-permute-start | bytes 786440 | tf_op jit(solution)/shard_map/ppermute | solution.py:38
  69.9 6.1 %collective-permute-start.12 = (bf16[128,512]{1,0:T(8,128)(2,1)S(1)}, bf16[128,512]{1,0:T(8,128)(2,1)S(1)}, u32[]{:S(2)}, u32[]{:S(2)}) collective-permute-start(bf16[128,512]{1,0:T(8,128)(2,1)S(1)} %get-tuple-element.58.refs_2_), channel_id=1, source_target_pairs={{0,16},{16,0},{1,17},{17,1},{2,18},{18,2},{3,19},{19,3},{4,20},{20... | collective-permute-start | bytes 393224 | tf_op jit(solution)/shard_map/ppermute | solution.py:38
  76.1 0.7 copy-start.8
  76.8 0.8 copy-start.6
  77.5 15.0 %collective-permute-start.14 = (bf16[240,896]{1,0:T(8,128)(2,1)}, bf16[240,896]{1,0:T(8,128)(2,1)}, u32[]{:S(2)}, u32[]{:S(2)}) collective-permute-start(bf16[240,896]{1,0:T(8,128)(2,1)} %collective-permute-done.10.refs_3_), channel_id=1, source_target_pairs={{0,32},{32,64},{64,96},{96,128},{128,160},{160,192},{192,224},{224... | collective-permute-start | bytes 1290248 | tf_op jit(solution)/shard_map/ppermute | solution.py:43
  80.2 11.1 %copy-start.14 = (s32[4]{0:T(128)S(1)}, s32[4]{0:T(128)}, u32[]{:S(2)}) copy-start(s32[4]{0:T(128)} %copy-done.11) | copy-start | bytes 52
  80.2 16.1 %copy-start.18 = (s32[4]{0:T(128)S(1)}, s32[4]{0:T(128)}, u32[]{:S(2)}) copy-start(s32[4]{0:T(128)} %ids.2) | copy-start | bytes 52
  80.2 11.1 %collective-permute-start.15 = (bf16[128,1664]{1,0:T(8,128)(2,1)}, bf16[128,1664]{1,0:T(8,128)(2,1)}, u32[]{:S(2)}, u32[]{:S(2)}) collective-permute-start(bf16[128,1664]{1,0:T(8,128)(2,1)} %inverse.6), channel_id=1, source_target_pairs={{0,16},{16,0},{1,17},{17,1},{2,18},{18,2},{3,19},{19,3},{4,20},{20... | collective-permute-start | bytes 1277960 | tf_op jit(solution)/shard_map/ppermute | solution.py:38
  82.8 13.5 %copy-start = (bf16[6,3328,64]{1,2,0:T(8,128)(2,1)S(1)}, bf16[6,3328,64]{1,2,0:T(8,128)(2,1)}, u32[]{:S(2)}) copy-start(bf16[6,3328,64]{1,2,0:T(8,128)(2,1)} %param.18) | copy-start | bytes 7667716
  86.7 14.9 %collective-permute-start.18 = (bf16[512,896]{1,0:T(8,128)(2,1)}, bf16[512,896]{1,0:T(8,128)(2,1)S(1)}, u32[]{:S(2)}, u32[]{:S(2)}) collective-permute-start(bf16[512,896]{1,0:T(8,128)(2,1)} %get-tuple-element.70), channel_id=1, source_target_pairs={{0,8},{8,0},{1,9},{9,1},{2,10},{10,2},{3,11},{11,3},{4,12},{12,4},... | collective-permute-start | bytes 2752520 | tf_op jit(solution)/shard_map/ppermute | solution.py:38
  92.5 12.5 %collective-permute-start.21 = (bf16[512,896]{1,0:T(8,128)(2,1)S(1)}, bf16[512,896]{1,0:T(8,128)(2,1)S(1)}, u32[]{:S(2)}, u32[]{:S(2)}) collective-permute-start(bf16[512,896]{1,0:T(8,128)(2,1)S(1)} %get-tuple-element.76), channel_id=1, source_target_pairs={{0,8},{8,0},{1,9},{9,1},{2,10},{10,2},{3,11},{11,3},{4,12},{12,4},... | collective-permute-start | bytes 2752520 | tf_op jit(solution)/shard_map/ppermute | solution.py:38
  95.8 5.4 %collective-permute-start.17 = (bf16[128,512]{1,0:T(8,128)(2,1)S(1)}, bf16[128,512]{1,0:T(8,128)(2,1)S(1)}, u32[]{:S(2)}, u32[]{:S(2)}) collective-permute-start(bf16[128,512]{1,0:T(8,128)(2,1)S(1)} %get-tuple-element.58.refs_2_), channel_id=1, source_target_pairs={{0,8},{8,0},{1,9},{9,1},{2,10},{10,2},{3,11},{11,3},{4,12},{12,4},... | collective-permute-start | bytes 393224 | tf_op jit(solution)/shard_map/ppermute | solution.py:38
  95.9 5.7 %collective-permute-start.16 = (bf16[256,512]{1,0:T(8,128)(2,1)S(1)}, bf16[256,512]{1,0:T(8,128)(2,1)S(1)}, u32[]{:S(2)}, u32[]{:S(2)}) collective-permute-start(bf16[256,512]{1,0:T(8,128)(2,1)S(1)} %bitcast.19), channel_id=1, source_target_pairs={{0,8},{8,0},{1,9},{9,1},{2,10},{10,2},{3,11},{11,3},{4,12},{12,4},... | collective-permute-start | bytes 786440 | tf_op jit(solution)/shard_map/ppermute | solution.py:38
  96.3 1.0 copy-start.7
  97.3 3.7 %copy-start.9 = (bf16[256,512]{1,0:T(8,128)(2,1)S(1)}, bf16[256,512]{1,0:T(8,128)(2,1)}, u32[]{:S(2)}) copy-start(bf16[256,512]{1,0:T(8,128)(2,1)} %copy-done.8) | copy-start | bytes 786436
  97.3 4.3 %copy-start.5 = (bf16[512,896]{1,0:T(8,128)(2,1)S(1)}, bf16[512,896]{1,0:T(8,128)(2,1)}, u32[]{:S(2)}) copy-start(bf16[512,896]{1,0:T(8,128)(2,1)} %get-tuple-element.69.refs_4_) | copy-start | bytes 2752516
  101.0 9.8 %copy-start.2 = (bf16[1664,896]{1,0:T(8,128)(2,1)}, bf16[1664,896]{1,0:T(8,128)(2,1)S(1)}, u32[]{:S(2)}) copy-start(bf16[1664,896]{1,0:T(8,128)(2,1)S(1)} %get-tuple-element.80.basis) | copy-start | bytes 8945668
  101.0 4.0 %copy-start.10 = (f32[32,1664]{1,0:T(8,128)S(1)}, f32[32,1664]{1,0:T(8,128)}, u32[]{:S(2)}) copy-start(f32[32,1664]{1,0:T(8,128)} %factors.1) | copy-start | bytes 638980
  101.0 4.0 %copy-start.20 = (s32[16]{0:T(128)S(1)}, s32[16]{0:T(128)}, u32[]{:S(2)}) copy-start(s32[16]{0:T(128)} %block_ids.1) | copy-start | bytes 196
  101.1 4.0 %collective-permute-start.19 = (bf16[256,512]{1,0:T(8,128)(2,1)S(1)}, bf16[256,512]{1,0:T(8,128)(2,1)S(1)}, u32[]{:S(2)}, u32[]{:S(2)}) collective-permute-start(bf16[256,512]{1,0:T(8,128)(2,1)S(1)} %copy-done.9), channel_id=1, source_target_pairs={{0,8},{8,0},{1,9},{9,1},{2,10},{10,2},{3,11},{11,3},{4,12},{12,4},... | collective-permute-start | bytes 786440 | tf_op jit(solution)/shard_map/ppermute | solution.py:38
  101.2 3.8 %collective-permute-start.20 = (bf16[128,512]{1,0:T(8,128)(2,1)S(1)}, bf16[128,512]{1,0:T(8,128)(2,1)S(1)}, u32[]{:S(2)}, u32[]{:S(2)}) collective-permute-start(bf16[128,512]{1,0:T(8,128)(2,1)S(1)} %collective-permute-done.12.refs_2_), channel_id=1, source_target_pairs={{0,8},{8,0},{1,9},{9,1},{2,10},{10,2},{3,11},{11,3},{4,12},{12,4},... | collective-permute-start | bytes 393224 | tf_op jit(solution)/shard_map/ppermute | solution.py:38
  110.8 32.6 %all-to-all-start.2 = ((bf16[8,64,896]{2,1,0:T(8,128)(2,1)}), bf16[8,64,896]{2,1,0:T(8,128)(2,1)S(1)}, u32[]{:S(2)}, u32[]{:S(2)}) async-start(bf16[8,64,896]{2,1,0:T(8,128)(2,1)} %get-tuple-element.77), calls=%async_computation.2 | async-start | bytes 1835008 | tf_op jit(solution)/shard_map/all_to_all | solution.py:33
  117.0 1.2 collective-permute-start.22
  118.1 2.7 %collective-permute-start.23 = (f32[1,128]{1,0:T(1,128)S(1)}, f32[1,128]{1,0:T(1,128)S(1)}, u32[]{:S(2)}, u32[]{:S(2)}) collective-permute-start(f32[1,128]{1,0:T(1,128)S(1)} %add.19), channel_id=1, source_target_pairs={{0,1},{1,0},{2,3},{3,2},{4,5},{5,4},{6,7},{7,6},{8,9},{9,8},{10,11... | collective-permute-start | bytes 1544 | tf_op jit(solution)/shard_map/ppermute | solution.py:38
  120.8 2.7 %collective-permute-start.24 = (f32[1,128]{1,0:T(1,128)S(1)}, f32[1,128]{1,0:T(1,128)S(1)}, u32[]{:S(2)}, u32[]{:S(2)}) collective-permute-start(f32[1,128]{1,0:T(1,128)S(1)} %add.20), channel_id=1, source_target_pairs={{0,2},{2,0},{4,6},{6,4},{1,3},{3,1},{5,7},{7,5},{8,10},{10,8},{12,... | collective-permute-start | bytes 1544 | tf_op jit(solution)/shard_map/ppermute | solution.py:38
  123.5 4.2 %collective-permute-start.25 = (f32[1,128]{1,0:T(1,128)S(1)}, f32[1,128]{1,0:T(1,128)S(1)}, u32[]{:S(2)}, u32[]{:S(2)}) collective-permute-start(f32[1,128]{1,0:T(1,128)S(1)} %add.21), channel_id=1, source_target_pairs={{0,4},{2,6},{4,0},{6,2},{1,5},{3,7},{5,1},{7,3},{8,12},{10,14},{12... | collective-permute-start | bytes 1544 | tf_op jit(solution)/shard_map/ppermute | solution.py:38
  127.7 4.2 %collective-permute-start.26 = (f32[1,128]{1,0:T(1,128)S(1)}, f32[1,128]{1,0:T(1,128)S(1)}, u32[]{:S(2)}, u32[]{:S(2)}) collective-permute-start(f32[1,128]{1,0:T(1,128)S(1)} %add.22), channel_id=1, source_target_pairs={{0,16},{16,0},{1,17},{17,1},{2,18},{18,2},{3,19},{19,3},{4,20},{20... | collective-permute-start | bytes 1544 | tf_op jit(solution)/shard_map/ppermute | solution.py:38
  143.4 1.8 %copy-start.3 = (bf16[1664,896]{1,0:T(8,128)(2,1)S(1)}, bf16[1664,896]{1,0:T(8,128)(2,1)}, u32[]{:S(2)}) copy-start(bf16[1664,896]{1,0:T(8,128)(2,1)} %copy-done.2) | copy-start | bytes 8945668
  146.9 12.7 %collective-permute-start.27 = (bf16[16,1664]{1,0:T(8,128)(2,1)S(1)}, bf16[16,1664]{1,0:T(8,128)(2,1)S(1)}, u32[]{:S(2)}, u32[]{:S(2)}) collective-permute-start(bf16[16,1664]{1,0:T(8,128)(2,1)S(1)} %get-tuple-element.82), channel_id=1, source_target_pairs={{0,8},{8,0},{1,9},{9,1},{2,10},{10,2},{3,11},{11,3},{4,12},{12,4},... | collective-permute-start | bytes 159752 | tf_op jit(solution)/shard_map/ppermute | solution.py:38
  147.4 12.1 %collective-permute-start.28 = (bf16[16,1664]{1,0:T(8,128)(2,1)S(1)}, bf16[16,1664]{1,0:T(8,128)(2,1)S(1)}, u32[]{:S(2)}, u32[]{:S(2)}) collective-permute-start(bf16[16,1664]{1,0:T(8,128)(2,1)S(1)} %get-tuple-element.83), channel_id=1, source_target_pairs={{0,16},{16,0},{1,17},{17,1},{2,18},{18,2},{3,19},{19,3},{4,20},{20... | collective-permute-start | bytes 159752 | tf_op jit(solution)/shard_map/ppermute | solution.py:38
  149.7 9.8 %collective-permute-start.29 = (bf16[16,1664]{1,0:T(8,128)(2,1)S(1)}, bf16[16,1664]{1,0:T(8,128)(2,1)S(1)}, u32[]{:S(2)}, u32[]{:S(2)}) collective-permute-start(bf16[16,1664]{1,0:T(8,128)(2,1)S(1)} %get-tuple-element.84), channel_id=1, source_target_pairs={{0,24},{8,16},{16,8},{24,0},{1,25},{9,17},{17,9},{25,1},{2,26},{10... | collective-permute-start | bytes 159752 | tf_op jit(solution)/shard_map/ppermute | solution.py:38

commit v7 on v6

--- a/solution.py
+++ b/solution.py
@@ -12,6 +12,7 @@
 OUT = ("z", "xh", "c")
 IN = ("y", "xl")
 QUAD = ("xh", "c")
+PLANE = ("xh", "c", "y", "xl")
 BF = jnp.bfloat16
 F32 = jnp.float32
 LANES = 128
@@ -49,16 +50,19 @@
 
 def left_body(ids, u0, u1, u2, u3, basis, out):
     left = jnp.concatenate([u[0] for u in (u0, u1, u2, u3)], axis=0)
-    rows = left.shape[0]
-    out[:rows, :] = dot(left, basis[...], 1, 0).astype(BF)
-    out[rows:, :] = basis[:WIN_ROWS, :]
-
-
-def left_part(query_ids, u_t, basis_out):
+    n_in, rows, width = out.shape
+    part = dot(left, basis[...], 1, 0).astype(BF)
+    out[:, : rows - WIN_ROWS, :] = part.reshape(n_in, rows - WIN_ROWS, width)
+    out[:, rows - WIN_ROWS :, :] = jnp.broadcast_to(
+        basis[:WIN_ROWS, :][None], (n_in, WIN_ROWS, width)
+    )
+
+
+def left_part(query_ids, u_t, basis_out, n_in):
     queries = query_ids.shape[0]
     _, rank, depth = u_t.shape
     eigen = basis_out.shape[1]
-    rows = queries * rank + WIN_ROWS
+    rows = queries * rank // n_in + WIN_ROWS
     tile = 256
     specs = [
         pl.BlockSpec((1, rank, depth), functools.partial(lambda q, n, ids: (ids[q], 0, 0), q))
@@ -66,70 +70,41 @@
     ]
     return pl.pallas_call(
         left_body,
-        out_shape=jax.ShapeDtypeStruct((rows, eigen), BF),
+        out_shape=jax.ShapeDtypeStruct((n_in, rows, eigen), BF),
         grid_spec=pltpu.PrefetchScalarGridSpec(
             num_scalar_prefetch=1,
             grid=(eigen // tile,),
             in_specs=[*specs, pl.BlockSpec((depth, tile), lambda n, ids: (0, n))],
-            out_specs=pl.BlockSpec((rows, tile), lambda n, ids: (0, n)),
-        ),
-        compiler_params=params(10),
+            out_specs=pl.BlockSpec((n_in, rows, tile), lambda n, ids: (0, 0, n)),
+        ),
+        compiler_params=params(16),
         name="left",
     )(query_ids, u_t, u_t, u_t, u_t, basis_out)
 
 
-def left_pair_body(where, own, other, out):
-    n_y, rows, _ = out.shape
-    each = rows - 2 * WIN_ROWS
-    near = lax.rem(where[2], 2)
-    last = n_y * each
-    for k in range(n_y):
-        at = slice(k * each, (k + 1) * each)
-        out[k, :each, :] = (own[at, :].astype(F32) + other[at, :].astype(F32)).astype(BF)
-        for part, place in ((own, near), (other, 1 - near)):
-            first = pl.multiple_of(each + place * WIN_ROWS, WIN_ROWS)
-            out[k, pl.ds(first, WIN_ROWS), :] = part[last:, :]
-
-
-def left_pair(where, own, other, n_y):
-    rows, eigen = own.shape
-    return pl.pallas_call(
-        left_pair_body,
-        out_shape=jax.ShapeDtypeStruct(
-            (n_y, (rows - WIN_ROWS) // n_y + 2 * WIN_ROWS, eigen), BF
-        ),
-        in_specs=[SMEM_SPEC, VMEM_SPEC, VMEM_SPEC],
-        out_specs=VMEM_SPEC,
-        compiler_params=params(3),
-        name="left_pair",
-    )(where, own, other)
-
-
 def left_sum_body(parts, out, window):
-    n_y, rows, _ = parts.shape
-    wins = 2 * WIN_ROWS
-    own = rows - wins
+    n_in, rows, _ = parts.shape
+    own = rows - WIN_ROWS
     total = parts[0, :own, :].astype(F32)
-    for i in range(1, n_y):
+    for i in range(1, n_in):
         total += parts[i, :own, :].astype(F32)
     total = total.astype(BF)
-    for i in range(n_y):
+    for i in range(n_in):
         out[i] = total
-        window[i * wins : (i + 1) * wins, :] = parts[i, own:, :]
+        window[i * WIN_ROWS : (i + 1) * WIN_ROWS, :] = parts[i, own:, :]
 
 
 def left_sum(parts):
-    n_y, rows, eigen = parts.shape
-    wins = 2 * WIN_ROWS
+    n_in, rows, eigen = parts.shape
     return pl.pallas_call(
         left_sum_body,
         out_shape=(
-            jax.ShapeDtypeStruct((n_y, rows - wins, eigen), BF),
-            jax.ShapeDtypeStruct((n_y * wins, eigen), BF),
+            jax.ShapeDtypeStruct((n_in, rows - WIN_ROWS, eigen), BF),
+            jax.ShapeDtypeStruct((n_in * WIN_ROWS, eigen), BF),
         ),
         in_specs=[VMEM_SPEC],
         out_specs=(VMEM_SPEC, VMEM_SPEC),
-        compiler_params=params(3),
+        compiler_params=params(4),
         name="left_sum",
     )(parts)
 
@@ -463,7 +438,7 @@
     x_pool,
     delta_pool,
 ):
-    n_z = lax.axis_size("z")
+    n_z, n_in = lax.axis_size("z"), lax.axis_size(IN)
     z, xh, c = lax.axis_index("z"), lax.axis_index("xh"), lax.axis_index("c")
     in_pos = lax.axis_index(IN)
     queries, train = query_ids.shape[0], train_ids.shape[0]
@@ -478,37 +453,33 @@
         swap(packed[2], "xh"),
         swap(packed[3], QUAD, 3),
     )
-    partial = left_part(
-        after(query_ids, packed[0]), jnp.transpose(u_pool, (0, 2, 1)), basis_out
-    )
-    other = swap(partial, "xl")
     rows = corrected.shape[0]
     ends = (0, 3 * rows // 8, 3 * rows // 4, rows)
     far = [
-        inverse_block(after(where, partial), corrected, block, 1, block, 1, a, b)[0]
+        inverse_block(where, corrected, block, 1, block, 1, a, b)[0]
         for a, b in zip(ends[:-1], ends[1:])
     ]
-    own = arrange(where, (after(packed[0], far[0]), *parts[1:]), local_rows, train)
-    near = inverse_block(where, corrected, block, 0, width, 2)
+    partial = left_part(query_ids, jnp.transpose(u_pool, (0, 2, 1)), basis_out, n_in)
+    own = arrange(where, (after(packed[0], far[0], partial), *parts[1:]), local_rows, train)
+
+    ahead, behind = [shift(own, 1)], [shift(own, -1)]
+    far[0] = swap(after(far[0], *parts[1:], partial), "xh")
+    spread, window = left_sum(after(exchange(partial, IN), far[1]))
+    near = inverse_block(after(where, spread), corrected, block, 0, width, 2)
+    far[1] = swap(after(far[1], ahead[0], near[0]), "xh")
     near = (near[0], swap(near[1], "c"))
-
-    partial = left_pair(where, partial, other, lax.axis_size("y"))
-    ahead, behind = [shift(own, 1)], [shift(own, -1)]
-    far[0] = swap(after(far[0], other), "xh")
-    up, down = after((ahead[0], behind[0]), far[0])
-    spread, window = left_sum(exchange(partial, "y"))
-    far[1] = swap(after(far[1], ahead[0]), "xh")
+    up, down = after((ahead[0], behind[0]), spread, far[0])
     ahead.append(shift(up, 1))
     behind.append(shift(down, -1))
-    left = exchange(spread, "y").reshape(-1, basis_out.shape[1])
-    up, down, left = after((ahead[1], behind[1], left), far[1])
+    left = exchange(spread, IN).reshape(-1, basis_out.shape[1])
+    up, down, left = after((ahead[1], behind[1], left), far[2])
     ahead.append(shift(up, 1))
     behind.append(shift(down, -1))
-    far[2] = swap(after(far[2], left), "xh")
+    far[2] = swap(after(far[2], ahead[1]), "xh")
     left_x, window_x = swap(left, "xh"), swap(window, "xh")
     lefts = (left, swap(left, "c"))
     windows = (window, swap(window, "c"))
-    up, left_x, window_x = after((ahead[2], left_x, window_x), behind[2])
+    up = after(ahead[2], behind[2], far[1])
     ahead.append(shift(up, 1))
     far = halves(where, far, width)
     last, *far = after((ahead[3], *far))
@@ -517,10 +488,9 @@
     basis, right, tokens, delta = rotate(
         where, query_ids, jnp.transpose(v_pool, (0, 2, 1)), chunks, block
     )
-    left_x, window_x, right_x = after((left_x, window_x, right))
-    left_d, window_d = swap(left_x, "c"), swap(window_x, "c")
-    so_far = back_first(right_x, lefts, windows, near, queries)
-    far = (left_x, left_d, window_x, window_d, far[0], swap(far[1], "c"))
+    so_far = back_first(right, lefts, windows, near, queries)
+    left_x, window_x = after((left_x, window_x), so_far)
+    far = (left_x, swap(left_x, "c"), window_x, swap(window_x, "c"), far[0], swap(far[1], "c"))
     parts, score = back(
         where, block_ids, so_far, factor_table, right, tokens, delta, far, n_z, train
     )

time: 162 us -> 156 us (0.963)
  blocking collectives: 16.8 us -> 8.88 us
  starting transfers between devices: 51.3 us -> 59 us
  local copies, waits for them, and re-layouts: 11.2 us -> 6.15 us
    all_to_all x2 -> x1, blocking collectives: 16.8 us -> 8.88 us  [exchange(): return lax.all_to_all(value, axis, split_axis=0, concat_axis=0, tiled=True)]
    ppermute x7, waiting for transfers between devices: 6.58 us -> 0.02 us  [shift(): lax.ppermute(value, 'z', [(i, (i + step) % size) for i in range(size)])]
    unnamed x43 -> x37, local copies, waits for them, and re-layouts: 11.2 us -> 6.15 us
    ppermute x23 -> x22, waiting for transfers between devices: 23.6 us -> 27.3 us  [swap(): return lax.ppermute(value, axis, [(i, i ^ mask) for i in range(size)])]
    ppermute x7, starting transfers between devices: 11.3 us -> 14.1 us  [shift(): lax.ppermute(value, 'z', [(i, (i + step) % size) for i in range(size)])]
    ppermute x23 -> x22, starting transfers between devices: 29.7 us -> 32.2 us  [swap(): return lax.ppermute(value, axis, [(i, i ^ mask) for i in range(size)])]
    all_to_all x2 -> x3, starting transfers between devices: 10.3 us -> 12.7 us  [exchange(): return lax.all_to_all(value, axis, split_axis=0, concat_axis=0, tiled=True)]
    all_to_all x2 -> x3, waiting for transfers between devices: 16 us -> 18 us  [exchange(): return lax.all_to_all(value, axis, split_axis=0, concat_axis=0, tiled=True)]
  transfers between devices with their start and end apart: 32 -> 32, of which waited for: 11 -> 13; matrix products, arithmetic and copies ran while one was open for 0% -> 0% of each run, Pallas kernels for 15% -> 16%
where the time goes in v7:
time: 156 us; the launch traced here: 155 us
  starting transfers between devices  59 us (38%)
  waiting for transfers between devices  45.3 us (29%)
  Pallas kernels  34.5 us (22%)
  blocking collectives  8.88 us (6%)
  local copies, waits for them, and re-layouts  6.15 us (4%)
    ppermute x22, starting transfers between devices, swap(): return lax.ppermute(value, axis, [(i, i ^ mask) for i in range(size)])  32.2 us
    ppermute x22, waiting for transfers between devices, swap(): return lax.ppermute(value, axis, [(i, i ^ mask) for i in range(size)])  27.3 us
    all_to_all x3, waiting for transfers between devices, exchange(): return lax.all_to_all(value, axis, split_axis=0, concat_axis=0, tiled=True)  18 us
    ppermute x7, starting transfers between devices, shift(): lax.ppermute(value, 'z', [(i, (i + step) % size) for i in range(size)])  14.1 us
    all_to_all x3, starting transfers between devices, exchange(): return lax.all_to_all(value, axis, split_axis=0, concat_axis=0, tiled=True)  12.7 us
    pallas_call x4, Pallas kernels, inverse_block(): pl.pallas_call(inverse_body, out_shape=tuple((jax.ShapeDtypeStruct((rows,...  12.5 us
    all_to_all x1, blocking collectives, exchange(): return lax.all_to_all(value, axis, split_axis=0, concat_axis=0, tiled=True)  8.88 us
    unnamed x37, local copies, waits for them, and re-layouts  6.15 us
  transfers between devices with their start and end apart: 32, of which 13 were waited for; matrix products, arithmetic and copies ran while one was open for 0% of the time, Pallas kernels for 16%

profile of v7, /device:TPU:1, one launch (start us, length us, event | category | flops | bytes accessed | tf_op | source)
XLA Modules:
  0.0 154.9 jit_solution(1010225579471597127)
XLA Ops:
  0.6 1.0 copy.13.basis
  1.8 0.8 copy-done.12
  2.6 0.7 copy-done.13
  3.2 0.7 copy-done.15
  3.9 0.7 pack.1
  4.7 3.3 %collective-permute-start = (bf16[60,896]{1,0:T(8,128)(2,1)S(1)}, bf16[60,896]{1,0:T(8,128)(2,1)S(1)}, u32[]{:S(2)}, u32[]{:S(2)}) collective-permute-start(bf16[60,896]{1,0:T(8,128)(2,1)S(1)} %get-tuple-element.43), channel_id=1, source_target_pairs={{0,8},{8,0},{1,9},{9,1},{2,10},{10,2},{3,11},{11,3},{4,12},{12,4},... | collective-permute-start | bytes 322568 | tf_op jit(solution)/shard_map/ppermute | solution.py:39
  8.0 1.0 collective-permute-start.1
  9.0 2.2 %collective-permute-start.2 = (bf16[60,896]{1,0:T(8,128)(2,1)S(1)}, bf16[60,896]{1,0:T(8,128)(2,1)S(1)}, u32[]{:S(2)}, u32[]{:S(2)}) collective-permute-start(bf16[60,896]{1,0:T(8,128)(2,1)S(1)} %get-tuple-element.45), channel_id=1, source_target_pairs={{0,24},{8,16},{16,8},{24,0},{1,25},{9,17},{17,9},{25,1},{2,26},{10... | collective-permute-start | bytes 322568 | tf_op jit(solution)/shard_map/ppermute | solution.py:39
  11.2 3.0 %inverse.4 = bf16[192,1664]{1,0:T(8,128)(2,1)} custom-call(s32[4]{0:T(128)} %copy-done.9, f32[512,3328]{1,0:T(8,128)} %corrected.7), custom_call_target="tpu_custom_call" | custom-call | tf_op jit(solution)/shard_map/inverse/pallas_call | solution.py:126
  14.2 2.3 %left.1 = bf16[8,48,512]{2,1,0:T(8,128)(2,1)} custom-call(s32[4]{0:T(128)S(1)} %copy-done.14, bf16[6,64,2048]{2,1,0:T(8,128)(2,1)S(1)} %bitcast.14, bf16[6,64,2048]{2,1,0:T(8,128)(2,1)S(1)} %bitcast.15, bf16[6,64,2048]{2,1,0:T(8,128)(2,1)S(1)} %bitcast.16, bf16[6,64,2048]{2,1,0:T(8,128)(2,1)S(1)} %bitcast.17, bf16[2048,512]{1,0:T(8,128)(2,1)S(1)} %copy-done.4), custom_call_target="tpu_custom_call" | custom-call | tf_op jit(solution)/shard_map/left/pallas_call | solution.py:71
  16.5 0.3 collective-permute-done.2.a3
  16.8 1.1 collective-permute-start.5
  18.0 1.2 arrange.1.refs_0_
  19.2 1.6 %collective-permute-start.3 = (bf16[240,896]{1,0:T(8,128)(2,1)S(1)}, bf16[240,896]{1,0:T(8,128)(2,1)}, u32[]{:S(2)}, u32[]{:S(2)}) collective-permute-start(bf16[240,896]{1,0:T(8,128)(2,1)S(1)} %arrange.1.refs_0_), channel_id=1, source_target_pairs={{0,32},{32,64},{64,96},{96,128},{128,160},{160,192},{192,224},{224... | collective-permute-start | bytes 1290248 | tf_op jit(solution)/shard_map/ppermute | solution.py:44
  20.8 4.0 %collective-permute-start.4 = (bf16[240,896]{1,0:T(8,128)(2,1)S(1)}, bf16[240,896]{1,0:T(8,128)(2,1)}, u32[]{:S(2)}, u32[]{:S(2)}) collective-permute-start(bf16[240,896]{1,0:T(8,128)(2,1)S(1)} %arrange.1.refs_0_), channel_id=1, source_target_pairs={{0,224},{32,0},{64,32},{96,64},{128,96},{160,128},{192,160},{224,1... | collective-permute-start | bytes 1290248 | tf_op jit(solution)/shard_map/ppermute | solution.py:44
  24.8 4.2 %all-to-all-start = ((bf16[8,48,512]{2,1,0:T(8,128)(2,1)}), bf16[8,48,512]{2,1,0:T(8,128)(2,1)S(1)}, u32[]{:S(2)}, u32[]{:S(2)}) async-start(bf16[8,48,512]{2,1,0:T(8,128)(2,1)} %left.1), calls=%async_computation | async-start | bytes 786432 | tf_op jit(solution)/shard_map/all_to_all | solution.py:34
  29.0 3.0 %inverse.5 = bf16[192,1664]{1,0:T(8,128)(2,1)} custom-call(s32[4]{0:T(128)} %copy-done.9, f32[512,3328]{1,0:T(8,128)} %corrected.7), custom_call_target="tpu_custom_call" | custom-call | tf_op jit(solution)/shard_map/inverse/pallas_call | solution.py:126
  32.0 6.8 %all-to-all-done.parts = bf16[8,48,512]{2,1,0:T(8,128)(2,1)S(1)} async-done(((bf16[8,48,512]{2,1,0:T(8,128)(2,1)}), bf16[8,48,512]{2,1,0:T(8,128)(2,1)S(1)}, u32[]{:S(2)}, u32[]{:S(2)}) %all-to-all-start) | async-done | bytes 393248 | tf_op jit(solution)/shard_map/all_to_all | solution.py:34
  38.8 0.7 left_sum.1
  39.6 1.7 %collective-permute-start.6 = (bf16[240,896]{1,0:T(8,128)(2,1)}, bf16[240,896]{1,0:T(8,128)(2,1)}, u32[]{:S(2)}, u32[]{:S(2)}) collective-permute-start(bf16[240,896]{1,0:T(8,128)(2,1)} %collective-permute-done.3.refs_1_), channel_id=1, source_target_pairs={{0,32},{32,64},{64,96},{96,128},{128,160},{160,192},{192,224},{224... | collective-permute-start | bytes 1290248 | tf_op jit(solution)/shard_map/ppermute | solution.py:44
  41.3 4.0 %collective-permute-start.7 = (bf16[240,896]{1,0:T(8,128)(2,1)}, bf16[240,896]{1,0:T(8,128)(2,1)}, u32[]{:S(2)}, u32[]{:S(2)}) collective-permute-start(bf16[240,896]{1,0:T(8,128)(2,1)} %collective-permute-done.4.refs_7_), channel_id=1, source_target_pairs={{0,224},{32,0},{64,32},{96,64},{128,96},{160,128},{192,160},{224,1... | collective-permute-start | bytes 1290248 | tf_op jit(solution)/shard_map/ppermute | solution.py:44
  45.4 3.4 %all-to-all-start.1 = ((bf16[8,32,512]{2,1,0:T(8,128)(2,1)}), bf16[8,32,512]{2,1,0:T(8,128)(2,1)S(1)}, u32[]{:S(2)}, u32[]{:S(2)}) async-start(bf16[8,32,512]{2,1,0:T(8,128)(2,1)} %get-tuple-element.47), calls=%async_computation.1 | async-start | bytes 524288 | tf_op jit(solution)/shard_map/all_to_all | solution.py:34
  48.8 3.7 %inverse.7 = (bf16[512,896]{1,0:T(8,128)(2,1)}, bf16[512,896]{1,0:T(8,128)(2,1)}) custom-call(s32[4]{0:T(128)} %copy-done.9, f32[512,3328]{1,0:T(8,128)} %corrected.7), custom_call_target="tpu_custom_call" | custom-call | tf_op jit(solution)/shard_map/inverse/pallas_call | solution.py:126
  52.5 1.6 %collective-permute-start.10 = (bf16[192,1664]{1,0:T(8,128)(2,1)}, bf16[192,1664]{1,0:T(8,128)(2,1)}, u32[]{:S(2)}, u32[]{:S(2)}) collective-permute-start(bf16[192,1664]{1,0:T(8,128)(2,1)} %inverse.5), channel_id=1, source_target_pairs={{0,16},{16,0},{1,17},{17,1},{2,18},{18,2},{3,19},{19,3},{4,20},{20... | collective-permute-start | bytes 1916936 | tf_op jit(solution)/shard_map/ppermute | solution.py:39
  54.1 2.8 %inverse.6 = bf16[128,1664]{1,0:T(8,128)(2,1)} custom-call(s32[4]{0:T(128)} %copy-done.9, f32[512,3328]{1,0:T(8,128)} %corrected.7), custom_call_target="tpu_custom_call" | custom-call | tf_op jit(solution)/shard_map/inverse/pallas_call | solution.py:126
  57.0 0.1 collective-permute-start.8
  57.0 2.7 %collective-permute-start.9 = (bf16[240,896]{1,0:T(8,128)(2,1)}, bf16[240,896]{1,0:T(8,128)(2,1)S(1)}, u32[]{:S(2)}, u32[]{:S(2)}) collective-permute-start(bf16[240,896]{1,0:T(8,128)(2,1)} %collective-permute-done.7.refs_6_), channel_id=1, source_target_pairs={{0,224},{32,0},{64,32},{96,64},{128,96},{160,128},{192,160},{224,1... | collective-permute-start | bytes 1290248 | tf_op jit(solution)/shard_map/ppermute | solution.py:44
  59.7 8.9 %collective-permute-done.10.refs_1_ = bf16[192,1664]{1,0:T(8,128)(2,1)} collective-permute-done((bf16[192,1664]{1,0:T(8,128)(2,1)}, bf16[192,1664]{1,0:T(8,128)(2,1)}, u32[]{:S(2)}, u32[]{:S(2)}) %collective-permute-start.10) | collective-permute-done | bytes 639008 | tf_op jit(solution)/shard_map/ppermute | solution.py:39
  68.7 1.5 collective-permute-start.12
  70.1 3.0 %collective-permute-start.15 = (bf16[512,896]{1,0:T(8,128)(2,1)}, bf16[512,896]{1,0:T(8,128)(2,1)S(1)}, u32[]{:S(2)}, u32[]{:S(2)}) collective-permute-start(bf16[512,896]{1,0:T(8,128)(2,1)} %get-tuple-element.64), channel_id=1, source_target_pairs={{0,8},{8,0},{1,9},{9,1},{2,10},{10,2},{3,11},{11,3},{4,12},{12,4},... | collective-permute-start | bytes 2752520 | tf_op jit(solution)/shard_map/ppermute | solution.py:39
  73.1 6.2 %collective-permute-done.12.refs_2_ = bf16[128,1664]{1,0:T(8,128)(2,1)S(1)} collective-permute-done((bf16[128,1664]{1,0:T(8,128)(2,1)}, bf16[128,1664]{1,0:T(8,128)(2,1)S(1)}, u32[]{:S(2)}, u32[]{:S(2)}) %collective-permute-start.12) | collective-permute-done | bytes 426016 | tf_op jit(solution)/shard_map/ppermute | solution.py:39
  79.3 1.1 copy-done.7
  80.3 1.2 halves.1
  81.6 3.7 %collective-permute-start.20 = (bf16[512,896]{1,0:T(8,128)(2,1)S(1)}, bf16[512,896]{1,0:T(8,128)(2,1)S(1)}, u32[]{:S(2)}, u32[]{:S(2)}) collective-permute-start(bf16[512,896]{1,0:T(8,128)(2,1)S(1)} %get-tuple-element.70), channel_id=1, source_target_pairs={{0,8},{8,0},{1,9},{9,1},{2,10},{10,2},{3,11},{11,3},{4,12},{12,4},... | collective-permute-start | bytes 2752520 | tf_op jit(solution)/shard_map/ppermute | solution.py:39
  85.3 0.1 collective-permute-start.13
  85.4 0.4 collective-permute-start.14
  85.8 1.4 collective-permute-start.16
  87.2 0.8 collective-permute-done.14.refs_3_
  88.0 1.4 collective-permute-start.17
  89.3 3.8 %rotate.1 = (bf16[1664,896]{1,0:T(8,128)(2,1)S(1)}, bf16[256,896]{1,0:T(8,128)(2,1)S(1)}, bf16[128,896]{1,0:T(8,128)(2,1)S(1)}, bf16[128,128]{1,0:T(8,128)(2,1)S(1)}) custom-call(s32[4]{0:T(128)S(1)} %copy-done.11, s32[4]{0:T(128)S(1)} %copy-done.14, bf16[6,64,3328]{2,1,0:T(8,128)(2,1)S(1)} %bitcast.10, bf16[6,64,3328]{2,1,0:T(8,128)(2,1)S(1)} %bitcast.11, ...), custom_call_target="tpu_custom_call" | custom-call | tf_op jit(solution)/shard_map/rotate/pallas_call | solution.py:273
  93.2 3.4 %back_first.1.so_far = f32[4,128,896]{2,1,0:T(8,128)S(1)} custom-call(bf16[256,896]{1,0:T(8,128)(2,1)S(1)} %get-tuple-element.61.right, bf16[256,512]{1,0:T(8,128)(2,1)S(1)} %bitcast.20, bf16[256,512]{1,0:T(8,128)(2,1)S(1)} %collective-permute-done.13.refs_1_, bf16[128,512]{1,0:T(8,128)(2,1)S(1)} %get-tuple-element.63.refs_2_, ...), custom_call_target="tpu_custom_call" | custom-call | tf_op jit(solution)/shard_map/back_first/pallas_call | solution.py:313
  96.6 1.4 collective-permute-done.17.refs_2_
  98.0 0.9 collective-permute-start.18
  98.9 1.3 collective-permute-done.19.refs_3_
  100.2 5.7 %back.1 = (bf16[8,64,896]{2,1,0:T(8,128)(2,1)}, f32[1,128]{1,0:T(1,128)S(1)}) custom-call(s32[4]{0:T(128)S(1)} %copy-done.11, s32[16]{0:T(128)S(1)} %copy-done.16, f32[4,128,896]{2,1,0:T(8,128)S(1)} %back_first.1.so_far, f32[32,1664]{1,0:T(8,128)S(1)} %copy-done.8, bf16[256,896]{1,0:T(8,128)(2,1)S(1)} %get-tuple-element.61.right, ...), custom_call_target="tpu_custom_call" | custom-call | tf_op jit(solution)/shard_map/back/pallas_call | solution.py:354
  105.9 5.1 %all-to-all-start.2 = ((bf16[8,64,896]{2,1,0:T(8,128)(2,1)}), bf16[8,64,896]{2,1,0:T(8,128)(2,1)S(1)}, u32[]{:S(2)}, u32[]{:S(2)}) async-start(bf16[8,64,896]{2,1,0:T(8,128)(2,1)} %get-tuple-element.71), calls=%async_computation.2 | async-start | bytes 1835008 | tf_op jit(solution)/shard_map/all_to_all | solution.py:34
  111.0 0.7 collective-permute-start.21
  111.7 0.8 collective-permute-done.21
  112.5 1.1 collective-permute-start.22
  113.6 1.6 %collective-permute-done.22 = f32[1,128]{1,0:T(1,128)S(1)} collective-permute-done((f32[1,128]{1,0:T(1,128)S(1)}, f32[1,128]{1,0:T(1,128)S(1)}, u32[]{:S(2)}, u32[]{:S(2)}) %collective-permute-start.22) | collective-permute-done | bytes 544 | tf_op jit(solution)/shard_map/ppermute | solution.py:39
  115.2 1.1 collective-permute-start.23
  116.3 1.6 %collective-permute-done.23 = f32[1,128]{1,0:T(1,128)S(1)} collective-permute-done((f32[1,128]{1,0:T(1,128)S(1)}, f32[1,128]{1,0:T(1,128)S(1)}, u32[]{:S(2)}, u32[]{:S(2)}) %collective-permute-start.23) | collective-permute-done | bytes 544 | tf_op jit(solution)/shard_map/ppermute | solution.py:39
  117.9 2.6 %collective-permute-start.24 = (f32[1,128]{1,0:T(1,128)S(1)}, f32[1,128]{1,0:T(1,128)S(1)}, u32[]{:S(2)}, u32[]{:S(2)}) collective-permute-start(f32[1,128]{1,0:T(1,128)S(1)} %add.21), channel_id=1, source_target_pairs={{0,4},{2,6},{4,0},{6,2},{1,5},{3,7},{5,1},{7,3},{8,12},{10,14},{12... | collective-permute-start | bytes 1544 | tf_op jit(solution)/shard_map/ppermute | solution.py:39
  120.5 1.6 %collective-permute-done.24 = f32[1,128]{1,0:T(1,128)S(1)} collective-permute-done((f32[1,128]{1,0:T(1,128)S(1)}, f32[1,128]{1,0:T(1,128)S(1)}, u32[]{:S(2)}, u32[]{:S(2)}) %collective-permute-start.24) | collective-permute-done | bytes 544 | tf_op jit(solution)/shard_map/ppermute | solution.py:39
  122.1 1.4 collective-permute-start.25
  123.4 2.8 %collective-permute-done.25 = f32[1,128]{1,0:T(1,128)S(1)} collective-permute-done((f32[1,128]{1,0:T(1,128)S(1)}, f32[1,128]{1,0:T(1,128)S(1)}, u32[]{:S(2)}, u32[]{:S(2)}) %collective-permute-start.25) | collective-permute-done | bytes 544 | tf_op jit(solution)/shard_map/ppermute | solution.py:39
  126.3 11.1 %all-to-all-done.2.parts = bf16[8,64,896]{2,1,0:T(8,128)(2,1)S(1)} async-done(((bf16[8,64,896]{2,1,0:T(8,128)(2,1)}), bf16[8,64,896]{2,1,0:T(8,128)(2,1)S(1)}, u32[]{:S(2)}, u32[]{:S(2)}) %all-to-all-start.2) | async-done | bytes 917536 | tf_op jit(solution)/shard_map/all_to_all | solution.py:34
  137.4 1.8 %copy-done.3 = bf16[1664,896]{1,0:T(8,128)(2,1)S(1)} copy-done((bf16[1664,896]{1,0:T(8,128)(2,1)S(1)}, bf16[1664,896]{1,0:T(8,128)(2,1)}, u32[]{:S(2)}) %copy-start.3) | copy-done | bytes 2981912
  139.2 1.7 %tile.1 = (bf16[16,1664]{1,0:T(8,128)(2,1)S(1)}, bf16[16,1664]{1,0:T(8,128)(2,1)S(1)}, bf16[16,1664]{1,0:T(8,128)(2,1)S(1)}, bf16[16,1664]{1,0:T(8,128)(2,1)S(1)}) custom-call(s32[4]{0:T(128)S(1)} %copy-done.11, bf16[8,64,896]{2,1,0:T(8,128)(2,1)S(1)} %all-to-all-done.2.parts, bf16[1664,896]{1,0:T(8,128)(2,1)S(1)} %copy-done.3), custom_call_target="tpu_custom_call" | custom-call | tf_op jit(solution)/shard_map/tile/pallas_call | solution.py:389
  140.9 0.6 collective-permute-start.26
  141.5 1.4 collective-permute-start.27
  142.9 1.8 %collective-permute-start.28 = (bf16[16,1664]{1,0:T(8,128)(2,1)S(1)}, bf16[16,1664]{1,0:T(8,128)(2,1)S(1)}, u32[]{:S(2)}, u32[]{:S(2)}) collective-permute-start(bf16[16,1664]{1,0:T(8,128)(2,1)S(1)} %get-tuple-element.78), channel_id=1, source_target_pairs={{0,24},{8,16},{16,8},{24,0},{1,25},{9,17},{17,9},{25,1},{2,26},{10... | collective-permute-start | bytes 159752 | tf_op jit(solution)/shard_map/ppermute | solution.py:39
  144.7 8.9 %all_to_all.20.score = f32[8,1,128]{2,1,0:T(1,128)S(1)} all-to-all(f32[8,1,128]{2,1,0:T(1,128)S(1)} %broadcast_in_dim.3), channel_id=1, replica_groups=mesh['z'=8,'xh'=2,'c'=2,'y'=4,'xl'=2] {'z'}, dimensions={0} | all-to-all | bytes 8192 | tf_op jit(solution)/shard_map/all_to_all | solution.py:34
  153.6 1.2 final.1
  (59 shorter events, 0.2 us)
Async XLA Ops:
  1.8 9.5 %copy-start.9 = (s32[4]{0:T(128)}, s32[4]{0:T(128)S(1)}, u32[]{:S(2)}) copy-start(s32[4]{0:T(128)S(1)} %pad_add_fusion.where) | copy-start | bytes 52
  1.8 0.8 copy-start.12
  2.6 0.7 copy-start.13
  3.2 0.7 copy-start.15
  4.7 11.9 %collective-permute-start = (bf16[60,896]{1,0:T(8,128)(2,1)S(1)}, bf16[60,896]{1,0:T(8,128)(2,1)S(1)}, u32[]{:S(2)}, u32[]{:S(2)}) collective-permute-start(bf16[60,896]{1,0:T(8,128)(2,1)S(1)} %get-tuple-element.43), channel_id=1, source_target_pairs={{0,8},{8,0},{1,9},{9,1},{2,10},{10,2},{3,11},{11,3},{4,12},{12,4},... | collective-permute-start | bytes 322568 | tf_op jit(solution)/shard_map/ppermute | solution.py:39
  8.0 8.6 %collective-permute-start.1 = (bf16[60,896]{1,0:T(8,128)(2,1)S(1)}, bf16[60,896]{1,0:T(8,128)(2,1)S(1)}, u32[]{:S(2)}, u32[]{:S(2)}) collective-permute-start(bf16[60,896]{1,0:T(8,128)(2,1)S(1)} %get-tuple-element.44), channel_id=1, source_target_pairs={{0,16},{16,0},{1,17},{17,1},{2,18},{18,2},{3,19},{19,3},{4,20},{20... | collective-permute-start | bytes 322568 | tf_op jit(solution)/shard_map/ppermute | solution.py:39
  9.0 5.2 %copy-start.1 = (bf16[6,2048,64]{1,2,0:T(8,128)(2,1)S(1)}, bf16[6,2048,64]{1,2,0:T(8,128)(2,1)}, u32[]{:S(2)}) copy-start(bf16[6,2048,64]{1,2,0:T(8,128)(2,1)} %param.17) | copy-start | bytes 4718596
  9.0 5.2 %copy-start.4 = (bf16[2048,512]{1,0:T(8,128)(2,1)S(1)}, bf16[2048,512]{1,0:T(8,128)(2,1)}, u32[]{:S(2)}) copy-start(bf16[2048,512]{1,0:T(8,128)(2,1)} %basis.2) | copy-start | bytes 6291460
  9.0 5.2 %copy-start.14 = (s32[4]{0:T(128)S(1)}, s32[4]{0:T(128)}, u32[]{:S(2)}) copy-start(s32[4]{0:T(128)} %ids.3) | copy-start | bytes 52
  9.0 7.8 %collective-permute-start.2 = (bf16[60,896]{1,0:T(8,128)(2,1)S(1)}, bf16[60,896]{1,0:T(8,128)(2,1)S(1)}, u32[]{:S(2)}, u32[]{:S(2)}) collective-permute-start(bf16[60,896]{1,0:T(8,128)(2,1)S(1)} %get-tuple-element.45), channel_id=1, source_target_pairs={{0,24},{8,16},{16,8},{24,0},{1,25},{9,17},{17,9},{25,1},{2,26},{10... | collective-permute-start | bytes 322568 | tf_op jit(solution)/shard_map/ppermute | solution.py:39
  14.2 2.6 %copy-start.17 = (bf16[192,1664]{1,0:T(8,128)(2,1)S(1)}, bf16[192,1664]{1,0:T(8,128)(2,1)}, u32[]{:S(2)}) copy-start(bf16[192,1664]{1,0:T(8,128)(2,1)} %inverse.4) | copy-start | bytes 1916932
  14.2 3.7 %copy-start.10 = (s32[4]{0:T(128)S(1)}, s32[4]{0:T(128)}, u32[]{:S(2)}) copy-start(s32[4]{0:T(128)} %copy-done.9) | copy-start | bytes 52
  16.8 22.8 %collective-permute-start.5 = (bf16[192,1664]{1,0:T(8,128)(2,1)S(1)}, bf16[192,1664]{1,0:T(8,128)(2,1)S(1)}, u32[]{:S(2)}, u32[]{:S(2)}) collective-permute-start(bf16[192,1664]{1,0:T(8,128)(2,1)S(1)} %copy-done.17), channel_id=1, source_target_pairs={{0,16},{16,0},{1,17},{17,1},{2,18},{18,2},{3,19},{19,3},{4,20},{20... | collective-permute-start | bytes 1916936 | tf_op jit(solution)/shard_map/ppermute | solution.py:39
  19.2 20.4 %collective-permute-start.3 = (bf16[240,896]{1,0:T(8,128)(2,1)S(1)}, bf16[240,896]{1,0:T(8,128)(2,1)}, u32[]{:S(2)}, u32[]{:S(2)}) collective-permute-start(bf16[240,896]{1,0:T(8,128)(2,1)S(1)} %arrange.1.refs_0_), channel_id=1, source_target_pairs={{0,32},{32,64},{64,96},{96,128},{128,160},{160,192},{192,224},{224... | collective-permute-start | bytes 1290248 | tf_op jit(solution)/shard_map/ppermute | solution.py:44
  20.8 18.8 %collective-permute-start.4 = (bf16[240,896]{1,0:T(8,128)(2,1)S(1)}, bf16[240,896]{1,0:T(8,128)(2,1)}, u32[]{:S(2)}, u32[]{:S(2)}) collective-permute-start(bf16[240,896]{1,0:T(8,128)(2,1)S(1)} %arrange.1.refs_0_), channel_id=1, source_target_pairs={{0,224},{32,0},{64,32},{96,64},{128,96},{160,128},{192,160},{224,1... | collective-permute-start | bytes 1290248 | tf_op jit(solution)/shard_map/ppermute | solution.py:44
  24.8 14.1 %all-to-all-start = ((bf16[8,48,512]{2,1,0:T(8,128)(2,1)}), bf16[8,48,512]{2,1,0:T(8,128)(2,1)S(1)}, u32[]{:S(2)}, u32[]{:S(2)}) async-start(bf16[8,48,512]{2,1,0:T(8,128)(2,1)} %left.1), calls=%async_computation | async-start | bytes 786432 | tf_op jit(solution)/shard_map/all_to_all | solution.py:34
  39.6 12.9 %copy-start.6 = (bf16[192,1664]{1,0:T(8,128)(2,1)}, bf16[192,1664]{1,0:T(8,128)(2,1)S(1)}, u32[]{:S(2)}) copy-start(bf16[192,1664]{1,0:T(8,128)(2,1)S(1)} %collective-permute-done.5.refs_0_) | copy-start | bytes 1916932
  39.6 17.3 %collective-permute-start.6 = (bf16[240,896]{1,0:T(8,128)(2,1)}, bf16[240,896]{1,0:T(8,128)(2,1)}, u32[]{:S(2)}, u32[]{:S(2)}) collective-permute-start(bf16[240,896]{1,0:T(8,128)(2,1)} %collective-permute-done.3.refs_1_), channel_id=1, source_target_pairs={{0,32},{32,64},{64,96},{96,128},{128,160},{160,192},{192,224},{224... | collective-permute-start | bytes 1290248 | tf_op jit(solution)/shard_map/ppermute | solution.py:44
  41.3 15.6 %collective-permute-start.7 = (bf16[240,896]{1,0:T(8,128)(2,1)}, bf16[240,896]{1,0:T(8,128)(2,1)}, u32[]{:S(2)}, u32[]{:S(2)}) collective-permute-start(bf16[240,896]{1,0:T(8,128)(2,1)} %collective-permute-done.4.refs_7_), channel_id=1, source_target_pairs={{0,224},{32,0},{64,32},{96,64},{128,96},{160,128},{192,160},{224,1... | collective-permute-start | bytes 1290248 | tf_op jit(solution)/shard_map/ppermute | solution.py:44
  45.4 11.6 %all-to-all-start.1 = ((bf16[8,32,512]{2,1,0:T(8,128)(2,1)}), bf16[8,32,512]{2,1,0:T(8,128)(2,1)S(1)}, u32[]{:S(2)}, u32[]{:S(2)}) async-start(bf16[8,32,512]{2,1,0:T(8,128)(2,1)} %get-tuple-element.47), calls=%async_computation.1 | async-start | bytes 524288 | tf_op jit(solution)/shard_map/all_to_all | solution.py:34
  52.5 26.8 %copy-start.11 = (s32[4]{0:T(128)S(1)}, s32[4]{0:T(128)}, u32[]{:S(2)}) copy-start(s32[4]{0:T(128)} %copy-done.9) | copy-start | bytes 52
  52.5 16.1 %collective-permute-start.10 = (bf16[192,1664]{1,0:T(8,128)(2,1)}, bf16[192,1664]{1,0:T(8,128)(2,1)}, u32[]{:S(2)}, u32[]{:S(2)}) collective-permute-start(bf16[192,1664]{1,0:T(8,128)(2,1)} %inverse.5), channel_id=1, source_target_pairs={{0,16},{16,0},{1,17},{17,1},{2,18},{18,2},{3,19},{19,3},{4,20},{20... | collective-permute-start | bytes 1916936 | tf_op jit(solution)/shard_map/ppermute | solution.py:39
  54.1 35.2 %copy-start = (bf16[6,3328,64]{1,2,0:T(8,128)(2,1)S(1)}, bf16[6,3328,64]{1,2,0:T(8,128)(2,1)}, u32[]{:S(2)}) copy-start(bf16[6,3328,64]{1,2,0:T(8,128)(2,1)} %param.18) | copy-start | bytes 7667716
  57.0 11.7 %collective-permute-start.8 = (bf16[240,896]{1,0:T(8,128)(2,1)}, bf16[240,896]{1,0:T(8,128)(2,1)S(1)}, u32[]{:S(2)}, u32[]{:S(2)}) collective-permute-start(bf16[240,896]{1,0:T(8,128)(2,1)} %collective-permute-done.6.refs_2_), channel_id=1, source_target_pairs={{0,32},{32,64},{64,96},{96,128},{128,160},{160,192},{192,224},{224... | collective-permute-start | bytes 1290248 | tf_op jit(solution)/shard_map/ppermute | solution.py:44
  57.0 11.6 %collective-permute-start.9 = (bf16[240,896]{1,0:T(8,128)(2,1)}, bf16[240,896]{1,0:T(8,128)(2,1)S(1)}, u32[]{:S(2)}, u32[]{:S(2)}) collective-permute-start(bf16[240,896]{1,0:T(8,128)(2,1)} %collective-permute-done.7.refs_6_), channel_id=1, source_target_pairs={{0,224},{32,0},{64,32},{96,64},{128,96},{160,128},{192,160},{224,1... | collective-permute-start | bytes 1290248 | tf_op jit(solution)/shard_map/ppermute | solution.py:44
  68.7 12.9 %collective-permute-start.11 = (bf16[240,896]{1,0:T(8,128)(2,1)S(1)}, bf16[240,896]{1,0:T(8,128)(2,1)S(1)}, u32[]{:S(2)}, u32[]{:S(2)}) collective-permute-start(bf16[240,896]{1,0:T(8,128)(2,1)S(1)} %collective-permute-done.8.refs_3_), channel_id=1, source_target_pairs={{0,32},{32,64},{64,96},{96,128},{128,160},{160,192},{192,224},{224... | collective-permute-start | bytes 1290248 | tf_op jit(solution)/shard_map/ppermute | solution.py:44
  68.7 10.6 %collective-permute-start.12 = (bf16[128,1664]{1,0:T(8,128)(2,1)}, bf16[128,1664]{1,0:T(8,128)(2,1)S(1)}, u32[]{:S(2)}, u32[]{:S(2)}) collective-permute-start(bf16[128,1664]{1,0:T(8,128)(2,1)} %inverse.6), channel_id=1, source_target_pairs={{0,16},{16,0},{1,17},{17,1},{2,18},{18,2},{3,19},{19,3},{4,20},{20... | collective-permute-start | bytes 1277960 | tf_op jit(solution)/shard_map/ppermute | solution.py:39
  70.1 23.1 %collective-permute-start.15 = (bf16[512,896]{1,0:T(8,128)(2,1)}, bf16[512,896]{1,0:T(8,128)(2,1)S(1)}, u32[]{:S(2)}, u32[]{:S(2)}) collective-permute-start(bf16[512,896]{1,0:T(8,128)(2,1)} %get-tuple-element.64), channel_id=1, source_target_pairs={{0,8},{8,0},{1,9},{9,1},{2,10},{10,2},{3,11},{11,3},{4,12},{12,4},... | collective-permute-start | bytes 2752520 | tf_op jit(solution)/shard_map/ppermute | solution.py:39
  79.3 1.1 copy-start.7
  81.6 18.6 %collective-permute-start.20 = (bf16[512,896]{1,0:T(8,128)(2,1)S(1)}, bf16[512,896]{1,0:T(8,128)(2,1)S(1)}, u32[]{:S(2)}, u32[]{:S(2)}) collective-permute-start(bf16[512,896]{1,0:T(8,128)(2,1)S(1)} %get-tuple-element.70), channel_id=1, source_target_pairs={{0,8},{8,0},{1,9},{9,1},{2,10},{10,2},{3,11},{11,3},{4,12},{12,4},... | collective-permute-start | bytes 2752520 | tf_op jit(solution)/shard_map/ppermute | solution.py:39
  85.3 7.9 %collective-permute-start.13 = (bf16[256,512]{1,0:T(8,128)(2,1)S(1)}, bf16[256,512]{1,0:T(8,128)(2,1)S(1)}, u32[]{:S(2)}, u32[]{:S(2)}) collective-permute-start(bf16[256,512]{1,0:T(8,128)(2,1)S(1)} %bitcast.18), channel_id=1, source_target_pairs={{0,8},{8,0},{1,9},{9,1},{2,10},{10,2},{3,11},{11,3},{4,12},{12,4},... | collective-permute-start | bytes 786440 | tf_op jit(solution)/shard_map/ppermute | solution.py:39
  85.4 2.6 %collective-permute-start.14 = (bf16[128,512]{1,0:T(8,128)(2,1)S(1)}, bf16[128,512]{1,0:T(8,128)(2,1)S(1)}, u32[]{:S(2)}, u32[]{:S(2)}) collective-permute-start(bf16[128,512]{1,0:T(8,128)(2,1)S(1)} %get-tuple-element.63.refs_2_), channel_id=1, source_target_pairs={{0,8},{8,0},{1,9},{9,1},{2,10},{10,2},{3,11},{11,3},{4,12},{12,4},... | collective-permute-start | bytes 393224 | tf_op jit(solution)/shard_map/ppermute | solution.py:39
  85.8 12.2 %collective-permute-start.16 = (bf16[256,512]{1,0:T(8,128)(2,1)S(1)}, bf16[256,512]{1,0:T(8,128)(2,1)S(1)}, u32[]{:S(2)}, u32[]{:S(2)}) collective-permute-start(bf16[256,512]{1,0:T(8,128)(2,1)S(1)} %bitcast.19), channel_id=1, source_target_pairs={{0,16},{16,0},{1,17},{17,1},{2,18},{18,2},{3,19},{19,3},{4,20},{20... | collective-permute-start | bytes 786440 | tf_op jit(solution)/shard_map/ppermute | solution.py:39
  88.0 10.0 %collective-permute-start.17 = (bf16[128,512]{1,0:T(8,128)(2,1)S(1)}, bf16[128,512]{1,0:T(8,128)(2,1)S(1)}, u32[]{:S(2)}, u32[]{:S(2)}) collective-permute-start(bf16[128,512]{1,0:T(8,128)(2,1)S(1)} %get-tuple-element.63.refs_2_), channel_id=1, source_target_pairs={{0,16},{16,0},{1,17},{17,1},{2,18},{18,2},{3,19},{19,3},{4,20},{20... | collective-permute-start | bytes 393224 | tf_op jit(solution)/shard_map/ppermute | solution.py:39
  89.3 3.9 %copy-start.5 = (bf16[512,896]{1,0:T(8,128)(2,1)S(1)}, bf16[512,896]{1,0:T(8,128)(2,1)}, u32[]{:S(2)}) copy-start(bf16[512,896]{1,0:T(8,128)(2,1)} %get-tuple-element.54.refs_4_) | copy-start | bytes 2752516
  93.1 12.8 %copy-start.2 = (bf16[1664,896]{1,0:T(8,128)(2,1)}, bf16[1664,896]{1,0:T(8,128)(2,1)S(1)}, u32[]{:S(2)}) copy-start(bf16[1664,896]{1,0:T(8,128)(2,1)S(1)} %get-tuple-element.74.basis) | copy-start | bytes 8945668
  93.2 7.1 %copy-start.8 = (f32[32,1664]{1,0:T(8,128)S(1)}, f32[32,1664]{1,0:T(8,128)}, u32[]{:S(2)}) copy-start(f32[32,1664]{1,0:T(8,128)} %factors.1) | copy-start | bytes 638980
  93.2 7.1 %copy-start.16 = (s32[16]{0:T(128)S(1)}, s32[16]{0:T(128)}, u32[]{:S(2)}) copy-start(s32[16]{0:T(128)} %block_ids.1) | copy-start | bytes 196
  98.0 2.2 %collective-permute-start.18 = (bf16[256,512]{1,0:T(8,128)(2,1)S(1)}, bf16[256,512]{1,0:T(8,128)(2,1)S(1)}, u32[]{:S(2)}, u32[]{:S(2)}) collective-permute-start(bf16[256,512]{1,0:T(8,128)(2,1)S(1)} %collective-permute-done.16.refs_0_), channel_id=1, source_target_pairs={{0,8},{8,0},{1,9},{9,1},{2,10},{10,2},{3,11},{11,3},{4,12},{12,4},... | collective-permute-start | bytes 786440 | tf_op jit(solution)/shard_map/ppermute | solution.py:39
  98.9 1.3 collective-permute-start.19
  105.9 31.5 %all-to-all-start.2 = ((bf16[8,64,896]{2,1,0:T(8,128)(2,1)}), bf16[8,64,896]{2,1,0:T(8,128)(2,1)S(1)}, u32[]{:S(2)}, u32[]{:S(2)}) async-start(bf16[8,64,896]{2,1,0:T(8,128)(2,1)} %get-tuple-element.71), calls=%async_computation.2 | async-start | bytes 1835008 | tf_op jit(solution)/shard_map/all_to_all | solution.py:34
  111.0 1.5 collective-permute-start.21
  112.5 2.7 %collective-permute-start.22 = (f32[1,128]{1,0:T(1,128)S(1)}, f32[1,128]{1,0:T(1,128)S(1)}, u32[]{:S(2)}, u32[]{:S(2)}) collective-permute-start(f32[1,128]{1,0:T(1,128)S(1)} %add.19), channel_id=1, source_target_pairs={{0,1},{1,0},{2,3},{3,2},{4,5},{5,4},{6,7},{7,6},{8,9},{9,8},{10,11... | collective-permute-start | bytes 1544 | tf_op jit(solution)/shard_map/ppermute | solution.py:39
  115.2 2.7 %collective-permute-start.23 = (f32[1,128]{1,0:T(1,128)S(1)}, f32[1,128]{1,0:T(1,128)S(1)}, u32[]{:S(2)}, u32[]{:S(2)}) collective-permute-start(f32[1,128]{1,0:T(1,128)S(1)} %add.20), channel_id=1, source_target_pairs={{0,2},{2,0},{4,6},{6,4},{1,3},{3,1},{5,7},{7,5},{8,10},{10,8},{12,... | collective-permute-start | bytes 1544 | tf_op jit(solution)/shard_map/ppermute | solution.py:39
  117.9 4.2 %collective-permute-start.24 = (f32[1,128]{1,0:T(1,128)S(1)}, f32[1,128]{1,0:T(1,128)S(1)}, u32[]{:S(2)}, u32[]{:S(2)}) collective-permute-start(f32[1,128]{1,0:T(1,128)S(1)} %add.21), channel_id=1, source_target_pairs={{0,4},{2,6},{4,0},{6,2},{1,5},{3,7},{5,1},{7,3},{8,12},{10,14},{12... | collective-permute-start | bytes 1544 | tf_op jit(solution)/shard_map/ppermute | solution.py:39
  122.1 4.2 %collective-permute-start.25 = (f32[1,128]{1,0:T(1,128)S(1)}, f32[1,128]{1,0:T(1,128)S(1)}, u32[]{:S(2)}, u32[]{:S(2)}) collective-permute-start(f32[1,128]{1,0:T(1,128)S(1)} %add.22), channel_id=1, source_target_pairs={{0,16},{16,0},{1,17},{17,1},{2,18},{18,2},{3,19},{19,3},{4,20},{20... | collective-permute-start | bytes 1544 | tf_op jit(solution)/shard_map/ppermute | solution.py:39
  137.4 1.8 %copy-start.3 = (bf16[1664,896]{1,0:T(8,128)(2,1)S(1)}, bf16[1664,896]{1,0:T(8,128)(2,1)}, u32[]{:S(2)}) copy-start(bf16[1664,896]{1,0:T(8,128)(2,1)} %copy-done.2) | copy-start | bytes 8945668
  140.9 12.7 %collective-permute-start.26 = (bf16[16,1664]{1,0:T(8,128)(2,1)S(1)}, bf16[16,1664]{1,0:T(8,128)(2,1)S(1)}, u32[]{:S(2)}, u32[]{:S(2)}) collective-permute-start(bf16[16,1664]{1,0:T(8,128)(2,1)S(1)} %get-tuple-element.76), channel_id=1, source_target_pairs={{0,8},{8,0},{1,9},{9,1},{2,10},{10,2},{3,11},{11,3},{4,12},{12,4},... | collective-permute-start | bytes 159752 | tf_op jit(solution)/shard_map/ppermute | solution.py:39
  141.5 12.1 %collective-permute-start.27 = (bf16[16,1664]{1,0:T(8,128)(2,1)S(1)}, bf16[16,1664]{1,0:T(8,128)(2,1)S(1)}, u32[]{:S(2)}, u32[]{:S(2)}) collective-permute-start(bf16[16,1664]{1,0:T(8,128)(2,1)S(1)} %get-tuple-element.77), channel_id=1, source_target_pairs={{0,16},{16,0},{1,17},{17,1},{2,18},{18,2},{3,19},{19,3},{4,20},{20... | collective-permute-start | bytes 159752 | tf_op jit(solution)/shard_map/ppermute | solution.py:39
  142.9 10.7 %collective-permute-start.28 = (bf16[16,1664]{1,0:T(8,128)(2,1)S(1)}, bf16[16,1664]{1,0:T(8,128)(2,1)S(1)}, u32[]{:S(2)}, u32[]{:S(2)}) collective-permute-start(bf16[16,1664]{1,0:T(8,128)(2,1)S(1)} %get-tuple-element.78), channel_id=1, source_target_pairs={{0,24},{8,16},{16,8},{24,0},{1,25},{9,17},{17,9},{25,1},{2,26},{10... | collective-permute-start | bytes 159752 | tf_op jit(solution)/shard_map/ppermute | solution.py:39

commit v8 on v7

--- a/solution.py
+++ b/solution.py
@@ -461,35 +461,34 @@
     ]
     partial = left_part(query_ids, jnp.transpose(u_pool, (0, 2, 1)), basis_out, n_in)
     own = arrange(where, (after(packed[0], far[0], partial), *parts[1:]), local_rows, train)
+    near = inverse_block(where, corrected, block, 0, width, 2)
+    near = (near[0], swap(near[1], "c"))
 
     ahead, behind = [shift(own, 1)], [shift(own, -1)]
-    far[0] = swap(after(far[0], *parts[1:], partial), "xh")
-    spread, window = left_sum(after(exchange(partial, IN), far[1]))
-    near = inverse_block(after(where, spread), corrected, block, 0, width, 2)
-    far[1] = swap(after(far[1], ahead[0], near[0]), "xh")
-    near = (near[0], swap(near[1], "c"))
-    up, down = after((ahead[0], behind[0]), spread, far[0])
+    far[0] = swap(far[0], "xh")
+    spread, window = left_sum(exchange(partial, IN))
+    up, down = after((ahead[0], behind[0]), spread)
+    far[1] = swap(after(far[1], ahead[0], spread), "xh")
     ahead.append(shift(up, 1))
     behind.append(shift(down, -1))
     left = exchange(spread, IN).reshape(-1, basis_out.shape[1])
-    up, down, left = after((ahead[1], behind[1], left), far[2])
+    up, down, left = after((ahead[1], behind[1], left), far[0])
     ahead.append(shift(up, 1))
     behind.append(shift(down, -1))
-    far[2] = swap(after(far[2], ahead[1]), "xh")
+    up = after(ahead[2], behind[2], far[1])
+    ahead.append(shift(up, 1))
+    far[2] = swap(after(far[2], left), "xh")
     left_x, window_x = swap(left, "xh"), swap(window, "xh")
     lefts = (left, swap(left, "c"))
     windows = (window, swap(window, "c"))
-    up = after(ahead[2], behind[2], far[1])
-    ahead.append(shift(up, 1))
-    far = halves(where, far, width)
-    last, *far = after((ahead[3], *far))
-    chunks = (own, *ahead[:3], last, *behind[::-1])
+    chunks = (own, *ahead, *behind[::-1])
 
     basis, right, tokens, delta = rotate(
         where, query_ids, jnp.transpose(v_pool, (0, 2, 1)), chunks, block
     )
     so_far = back_first(right, lefts, windows, near, queries)
-    left_x, window_x = after((left_x, window_x), so_far)
+    left_x, window_x, *far = after((left_x, window_x, *far), so_far)
+    far = halves(where, far, width)
     far = (left_x, swap(left_x, "c"), window_x, swap(window_x, "c"), far[0], swap(far[1], "c"))
     parts, score = back(
         where, block_ids, so_far, factor_table, right, tokens, delta, far, n_z, train

time: 156 us -> 148 us (0.949)
  waiting for transfers between devices: 45.3 us -> 39.3 us
    ppermute x22, waiting for transfers between devices: 27.3 us -> 17.5 us  [swap(): return lax.ppermute(value, axis, [(i, i ^ mask) for i in range(size)])]
    ppermute x7, starting transfers between devices: 14.1 us -> 10 us  [shift(): lax.ppermute(value, 'z', [(i, (i + step) % size) for i in range(size)])]
    all_to_all x3, waiting for transfers between devices: 18 us -> 20.5 us  [exchange(): return lax.all_to_all(value, axis, split_axis=0, concat_axis=0, tiled=True)]
    ppermute x22, starting transfers between devices: 32.2 us -> 34.4 us  [swap(): return lax.ppermute(value, axis, [(i, i ^ mask) for i in range(size)])]
    unnamed x37 -> x35, local copies, waits for them, and re-layouts: 6.15 us -> 6.07 us
  transfers between devices with their start and end apart: 32 -> 32, of which waited for: 13 -> 14; matrix products, arithmetic and copies ran while one was open for 0% -> 0% of each run, Pallas kernels for 16% -> 15%
where the time goes in v8:
time: 148 us; the launch traced here: 147 us
  starting transfers between devices  57.8 us (39%)
  waiting for transfers between devices  39.3 us (27%)
  Pallas kernels  34 us (23%)
  blocking collectives  8.88 us (6%)
  local copies, waits for them, and re-layouts  6.08 us (4%)
    ppermute x22, starting transfers between devices, swap(): return lax.ppermute(value, axis, [(i, i ^ mask) for i in range(size)])  34.4 us
    all_to_all x3, waiting for transfers between devices, exchange(): return lax.all_to_all(value, axis, split_axis=0, concat_axis=0, tiled=True)  20.5 us
    ppermute x22, waiting for transfers between devices, swap(): return lax.ppermute(value, axis, [(i, i ^ mask) for i in range(size)])  17.5 us
    all_to_all x3, starting transfers between devices, exchange(): return lax.all_to_all(value, axis, split_axis=0, concat_axis=0, tiled=True)  13.4 us
    pallas_call x4, Pallas kernels, inverse_block(): pl.pallas_call(inverse_body, out_shape=tuple((jax.ShapeDtypeStruct((rows,...  12.4 us
    ppermute x7, starting transfers between devices, shift(): lax.ppermute(value, 'z', [(i, (i + step) % size) for i in range(size)])  10 us
    all_to_all x1, blocking collectives, exchange(): return lax.all_to_all(value, axis, split_axis=0, concat_axis=0, tiled=True)  8.88 us
    unnamed x35, local copies, waits for them, and re-layouts  6.07 us
  transfers between devices with their start and end apart: 32, of which 14 were waited for; matrix products, arithmetic and copies ran while one was open for 0% of the time, Pallas kernels for 15%

profile of v8, /device:TPU:1, one launch (start us, length us, event | category | flops | bytes accessed | tf_op | source)
XLA Modules:
  0.0 147.1 jit_solution(11653994095858998054)
XLA Ops:
  0.6 1.0 copy.13.basis
  1.8 0.8 copy-done.12
  2.6 0.7 copy-done.13
  3.2 0.7 copy-done.15
  3.9 0.7 pack.1
  4.7 3.3 %collective-permute-start = (bf16[60,896]{1,0:T(8,128)(2,1)S(1)}, bf16[60,896]{1,0:T(8,128)(2,1)S(1)}, u32[]{:S(2)}, u32[]{:S(2)}) collective-permute-start(bf16[60,896]{1,0:T(8,128)(2,1)S(1)} %get-tuple-element.40), channel_id=1, source_target_pairs={{0,8},{8,0},{1,9},{9,1},{2,10},{10,2},{3,11},{11,3},{4,12},{12,4},... | collective-permute-start | bytes 322568 | tf_op jit(solution)/shard_map/ppermute | solution.py:39
  8.0 1.0 collective-permute-start.1
  9.0 2.2 %collective-permute-start.2 = (bf16[60,896]{1,0:T(8,128)(2,1)S(1)}, bf16[60,896]{1,0:T(8,128)(2,1)S(1)}, u32[]{:S(2)}, u32[]{:S(2)}) collective-permute-start(bf16[60,896]{1,0:T(8,128)(2,1)S(1)} %get-tuple-element.42), channel_id=1, source_target_pairs={{0,24},{8,16},{16,8},{24,0},{1,25},{9,17},{17,9},{25,1},{2,26},{10... | collective-permute-start | bytes 322568 | tf_op jit(solution)/shard_map/ppermute | solution.py:39
  11.2 3.0 %inverse.4 = bf16[192,1664]{1,0:T(8,128)(2,1)} custom-call(s32[4]{0:T(128)} %copy-done.9, f32[512,3328]{1,0:T(8,128)} %corrected.7), custom_call_target="tpu_custom_call" | custom-call | tf_op jit(solution)/shard_map/inverse/pallas_call | solution.py:126
  14.2 2.3 %left.1 = bf16[8,48,512]{2,1,0:T(8,128)(2,1)} custom-call(s32[4]{0:T(128)S(1)} %copy-done.14, bf16[6,64,2048]{2,1,0:T(8,128)(2,1)S(1)} %bitcast.14, bf16[6,64,2048]{2,1,0:T(8,128)(2,1)S(1)} %bitcast.15, bf16[6,64,2048]{2,1,0:T(8,128)(2,1)S(1)} %bitcast.16, bf16[6,64,2048]{2,1,0:T(8,128)(2,1)S(1)} %bitcast.17, bf16[2048,512]{1,0:T(8,128)(2,1)S(1)} %copy-done.4), custom_call_target="tpu_custom_call" | custom-call | tf_op jit(solution)/shard_map/left/pallas_call | solution.py:71
  16.6 0.3 collective-permute-done.2.a3
  16.8 1.2 arrange.1.refs_0_
  18.0 0.5 collective-permute-start.3
  18.5 4.0 %collective-permute-start.4 = (bf16[240,896]{1,0:T(8,128)(2,1)S(1)}, bf16[240,896]{1,0:T(8,128)(2,1)S(1)}, u32[]{:S(2)}, u32[]{:S(2)}) collective-permute-start(bf16[240,896]{1,0:T(8,128)(2,1)S(1)} %arrange.1.refs_0_), channel_id=1, source_target_pairs={{0,224},{32,0},{64,32},{96,64},{128,96},{160,128},{192,160},{224,1... | collective-permute-start | bytes 1290248 | tf_op jit(solution)/shard_map/ppermute | solution.py:44
  22.6 4.6 %all-to-all-start = ((bf16[8,48,512]{2,1,0:T(8,128)(2,1)}), bf16[8,48,512]{2,1,0:T(8,128)(2,1)S(1)}, u32[]{:S(2)}, u32[]{:S(2)}) async-start(bf16[8,48,512]{2,1,0:T(8,128)(2,1)} %left.1), calls=%async_computation | async-start | bytes 786432 | tf_op jit(solution)/shard_map/all_to_all | solution.py:34
  27.2 2.4 %collective-permute-start.7 = (bf16[192,1664]{1,0:T(8,128)(2,1)}, bf16[192,1664]{1,0:T(8,128)(2,1)S(1)}, u32[]{:S(2)}, u32[]{:S(2)}) collective-permute-start(bf16[192,1664]{1,0:T(8,128)(2,1)} %inverse.4), channel_id=1, source_target_pairs={{0,16},{16,0},{1,17},{17,1},{2,18},{18,2},{3,19},{19,3},{4,20},{20... | collective-permute-start | bytes 1916936 | tf_op jit(solution)/shard_map/ppermute | solution.py:39
  29.6 5.3 %all-to-all-done.parts = bf16[8,48,512]{2,1,0:T(8,128)(2,1)S(1)} async-done(((bf16[8,48,512]{2,1,0:T(8,128)(2,1)}), bf16[8,48,512]{2,1,0:T(8,128)(2,1)S(1)}, u32[]{:S(2)}, u32[]{:S(2)}) %all-to-all-start) | async-done | bytes 393248 | tf_op jit(solution)/shard_map/all_to_all | solution.py:34
  34.9 0.7 left_sum.1
  35.7 0.1 collective-permute-start.5
  35.8 2.7 %collective-permute-start.6 = (bf16[240,896]{1,0:T(8,128)(2,1)S(1)}, bf16[240,896]{1,0:T(8,128)(2,1)}, u32[]{:S(2)}, u32[]{:S(2)}) collective-permute-start(bf16[240,896]{1,0:T(8,128)(2,1)S(1)} %collective-permute-done.4.refs_7_), channel_id=1, source_target_pairs={{0,224},{32,0},{64,32},{96,64},{128,96},{160,128},{192,160},{224,1... | collective-permute-start | bytes 1290248 | tf_op jit(solution)/shard_map/ppermute | solution.py:44
  38.5 3.4 %all-to-all-start.1 = ((bf16[8,32,512]{2,1,0:T(8,128)(2,1)}), bf16[8,32,512]{2,1,0:T(8,128)(2,1)S(1)}, u32[]{:S(2)}, u32[]{:S(2)}) async-start(bf16[8,32,512]{2,1,0:T(8,128)(2,1)} %get-tuple-element.43), calls=%async_computation.1 | async-start | bytes 524288 | tf_op jit(solution)/shard_map/all_to_all | solution.py:34
  41.9 3.0 %inverse.5 = bf16[192,1664]{1,0:T(8,128)(2,1)} custom-call(s32[4]{0:T(128)} %copy-done.9, f32[512,3328]{1,0:T(8,128)} %corrected.7), custom_call_target="tpu_custom_call" | custom-call | tf_op jit(solution)/shard_map/inverse/pallas_call | solution.py:126
  44.9 2.6 %collective-permute-start.10 = (bf16[192,1664]{1,0:T(8,128)(2,1)}, bf16[192,1664]{1,0:T(8,128)(2,1)S(1)}, u32[]{:S(2)}, u32[]{:S(2)}) collective-permute-start(bf16[192,1664]{1,0:T(8,128)(2,1)} %inverse.5), channel_id=1, source_target_pairs={{0,16},{16,0},{1,17},{17,1},{2,18},{18,2},{3,19},{19,3},{4,20},{20... | collective-permute-start | bytes 1916936 | tf_op jit(solution)/shard_map/ppermute | solution.py:39
  47.5 4.0 %all-to-all-done.1 = bf16[8,32,512]{2,1,0:T(8,128)(2,1)S(1)} async-done(((bf16[8,32,512]{2,1,0:T(8,128)(2,1)}), bf16[8,32,512]{2,1,0:T(8,128)(2,1)S(1)}, u32[]{:S(2)}, u32[]{:S(2)}) %all-to-all-start.1) | async-done | bytes 262176 | tf_op jit(solution)/shard_map/all_to_all | solution.py:34
  51.5 0.1 collective-permute-start.8
  51.6 2.7 %collective-permute-start.9 = (bf16[240,896]{1,0:T(8,128)(2,1)}, bf16[240,896]{1,0:T(8,128)(2,1)}, u32[]{:S(2)}, u32[]{:S(2)}) collective-permute-start(bf16[240,896]{1,0:T(8,128)(2,1)} %collective-permute-done.6.refs_6_), channel_id=1, source_target_pairs={{0,224},{32,0},{64,32},{96,64},{128,96},{160,128},{192,160},{224,1... | collective-permute-start | bytes 1290248 | tf_op jit(solution)/shard_map/ppermute | solution.py:44
  54.2 3.8 %inverse.6 = (bf16[512,896]{1,0:T(8,128)(2,1)}, bf16[512,896]{1,0:T(8,128)(2,1)}) custom-call(s32[4]{0:T(128)} %copy-done.9, f32[512,3328]{1,0:T(8,128)} %corrected.7), custom_call_target="tpu_custom_call" | custom-call | tf_op jit(solution)/shard_map/inverse/pallas_call | solution.py:126
  58.0 3.5 %collective-permute-start.14 = (bf16[512,896]{1,0:T(8,128)(2,1)}, bf16[512,896]{1,0:T(8,128)(2,1)S(1)}, u32[]{:S(2)}, u32[]{:S(2)}) collective-permute-start(bf16[512,896]{1,0:T(8,128)(2,1)} %get-tuple-element.54), channel_id=1, source_target_pairs={{0,8},{8,0},{1,9},{9,1},{2,10},{10,2},{3,11},{11,3},{4,12},{12,4},... | collective-permute-start | bytes 2752520 | tf_op jit(solution)/shard_map/ppermute | solution.py:39
  61.4 2.1 %collective-permute-done.10.refs_1_ = bf16[192,1664]{1,0:T(8,128)(2,1)S(1)} collective-permute-done((bf16[192,1664]{1,0:T(8,128)(2,1)}, bf16[192,1664]{1,0:T(8,128)(2,1)S(1)}, u32[]{:S(2)}, u32[]{:S(2)}) %collective-permute-start.10) | collective-permute-done | bytes 639008 | tf_op jit(solution)/shard_map/ppermute | solution.py:39
  63.6 2.7 %inverse.7 = bf16[128,1664]{1,0:T(8,128)(2,1)} custom-call(s32[4]{0:T(128)} %copy-done.9, f32[512,3328]{1,0:T(8,128)} %corrected.7), custom_call_target="tpu_custom_call" | custom-call | tf_op jit(solution)/shard_map/inverse/pallas_call | solution.py:126
  66.3 0.6 collective-permute-start.17
  66.9 3.8 %collective-permute-start.13 = (bf16[128,512]{1,0:T(8,128)(2,1)S(1)}, bf16[128,512]{1,0:T(8,128)(2,1)S(1)}, u32[]{:S(2)}, u32[]{:S(2)}) collective-permute-start(bf16[128,512]{1,0:T(8,128)(2,1)S(1)} %get-tuple-element.52.refs_2_), channel_id=1, source_target_pairs={{0,8},{8,0},{1,9},{9,1},{2,10},{10,2},{3,11},{11,3},{4,12},{12,4},... | collective-permute-start | bytes 393224 | tf_op jit(solution)/shard_map/ppermute | solution.py:39
  70.7 1.0 collective-permute-done.13.refs_3_
  71.7 1.1 collective-permute-start.15
  72.8 1.3 collective-permute-done.11.refs_4_
  74.2 0.5 collective-permute-start.16
  74.7 1.0 copy-done.7
  75.7 3.9 %rotate.1 = (bf16[1664,896]{1,0:T(8,128)(2,1)S(1)}, bf16[256,896]{1,0:T(8,128)(2,1)S(1)}, bf16[128,896]{1,0:T(8,128)(2,1)S(1)}, bf16[128,128]{1,0:T(8,128)(2,1)S(1)}) custom-call(s32[4]{0:T(128)S(1)} %copy-done.11, s32[4]{0:T(128)S(1)} %copy-done.14, bf16[6,64,3328]{2,1,0:T(8,128)(2,1)S(1)} %bitcast.10, bf16[6,64,3328]{2,1,0:T(8,128)(2,1)S(1)} %bitcast.11, ...), custom_call_target="tpu_custom_call" | custom-call | tf_op jit(solution)/shard_map/rotate/pallas_call | solution.py:273
  79.7 3.4 %back_first.1.so_far = f32[4,128,896]{2,1,0:T(8,128)S(1)} custom-call(bf16[256,896]{1,0:T(8,128)(2,1)S(1)} %get-tuple-element.50.right, bf16[256,512]{1,0:T(8,128)(2,1)S(1)} %bitcast.20, bf16[256,512]{1,0:T(8,128)(2,1)S(1)} %collective-permute-done.12.refs_1_, bf16[128,512]{1,0:T(8,128)(2,1)S(1)} %get-tuple-element.52.refs_2_, ...), custom_call_target="tpu_custom_call" | custom-call | tf_op jit(solution)/shard_map/back_first/pallas_call | solution.py:313
  83.0 2.4 %collective-permute-done.16.refs_2_ = bf16[128,512]{1,0:T(8,128)(2,1)S(1)} collective-permute-done((bf16[128,512]{1,0:T(8,128)(2,1)S(1)}, bf16[128,512]{1,0:T(8,128)(2,1)S(1)}, u32[]{:S(2)}, u32[]{:S(2)}) %collective-permute-start.16) | collective-permute-done | bytes 131104 | tf_op jit(solution)/shard_map/ppermute | solution.py:39
  85.4 0.7 halves.1
  86.1 3.3 %collective-permute-start.20 = (bf16[512,896]{1,0:T(8,128)(2,1)S(1)}, bf16[512,896]{1,0:T(8,128)(2,1)S(1)}, u32[]{:S(2)}, u32[]{:S(2)}) collective-permute-start(bf16[512,896]{1,0:T(8,128)(2,1)S(1)} %get-tuple-element.64), channel_id=1, source_target_pairs={{0,8},{8,0},{1,9},{9,1},{2,10},{10,2},{3,11},{11,3},{4,12},{12,4},... | collective-permute-start | bytes 2752520 | tf_op jit(solution)/shard_map/ppermute | solution.py:39
  89.5 0.1 collective-permute-start.18
  89.6 0.4 collective-permute-start.19
  90.0 2.2 %collective-permute-done.19.refs_3_ = bf16[128,512]{1,0:T(8,128)(2,1)S(1)} collective-permute-done((bf16[128,512]{1,0:T(8,128)(2,1)S(1)}, bf16[128,512]{1,0:T(8,128)(2,1)S(1)}, u32[]{:S(2)}, u32[]{:S(2)}) %collective-permute-start.19) | collective-permute-done | bytes 131104 | tf_op jit(solution)/shard_map/ppermute | solution.py:39
  92.1 5.7 %back.1 = (bf16[8,64,896]{2,1,0:T(8,128)(2,1)}, f32[1,128]{1,0:T(1,128)S(1)}) custom-call(s32[4]{0:T(128)S(1)} %copy-done.11, s32[16]{0:T(128)S(1)} %copy-done.16, f32[4,128,896]{2,1,0:T(8,128)S(1)} %back_first.1.so_far, f32[32,1664]{1,0:T(8,128)S(1)} %copy-done.8, bf16[256,896]{1,0:T(8,128)(2,1)S(1)} %get-tuple-element.50.right, ...), custom_call_target="tpu_custom_call" | custom-call | tf_op jit(solution)/shard_map/back/pallas_call | solution.py:354
  97.9 5.4 %all-to-all-start.2 = ((bf16[8,64,896]{2,1,0:T(8,128)(2,1)}), bf16[8,64,896]{2,1,0:T(8,128)(2,1)S(1)}, u32[]{:S(2)}, u32[]{:S(2)}) async-start(bf16[8,64,896]{2,1,0:T(8,128)(2,1)} %get-tuple-element.65), calls=%async_computation.2 | async-start | bytes 1835008 | tf_op jit(solution)/shard_map/all_to_all | solution.py:34
  103.2 0.7 collective-permute-start.21
  103.9 0.8 collective-permute-done.21
  104.8 2.6 %collective-permute-done.22 = f32[1,128]{1,0:T(1,128)S(1)} collective-permute-done((f32[1,128]{1,0:T(1,128)S(1)}, f32[1,128]{1,0:T(1,128)S(1)}, u32[]{:S(2)}, u32[]{:S(2)}) %collective-permute-start.22) | collective-permute-done | bytes 544 | tf_op jit(solution)/shard_map/ppermute | solution.py:39
  107.4 1.1 collective-permute-start.23
  108.5 1.5 %collective-permute-done.23 = f32[1,128]{1,0:T(1,128)S(1)} collective-permute-done((f32[1,128]{1,0:T(1,128)S(1)}, f32[1,128]{1,0:T(1,128)S(1)}, u32[]{:S(2)}, u32[]{:S(2)}) %collective-permute-start.23) | collective-permute-done | bytes 544 | tf_op jit(solution)/shard_map/ppermute | solution.py:39
  110.1 2.7 %collective-permute-start.24 = (f32[1,128]{1,0:T(1,128)S(1)}, f32[1,128]{1,0:T(1,128)S(1)}, u32[]{:S(2)}, u32[]{:S(2)}) collective-permute-start(f32[1,128]{1,0:T(1,128)S(1)} %add.21), channel_id=1, source_target_pairs={{0,4},{2,6},{4,0},{6,2},{1,5},{3,7},{5,1},{7,3},{8,12},{10,14},{12... | collective-permute-start | bytes 1544 | tf_op jit(solution)/shard_map/ppermute | solution.py:39
  112.8 1.5 collective-permute-done.24
  114.3 1.1 collective-permute-start.25
  115.3 3.1 %collective-permute-done.25 = f32[1,128]{1,0:T(1,128)S(1)} collective-permute-done((f32[1,128]{1,0:T(1,128)S(1)}, f32[1,128]{1,0:T(1,128)S(1)}, u32[]{:S(2)}, u32[]{:S(2)}) %collective-permute-start.25) | collective-permute-done | bytes 544 | tf_op jit(solution)/shard_map/ppermute | solution.py:39
  118.5 11.1 %all-to-all-done.2.parts = bf16[8,64,896]{2,1,0:T(8,128)(2,1)S(1)} async-done(((bf16[8,64,896]{2,1,0:T(8,128)(2,1)}), bf16[8,64,896]{2,1,0:T(8,128)(2,1)S(1)}, u32[]{:S(2)}, u32[]{:S(2)}) %all-to-all-start.2) | async-done | bytes 917536 | tf_op jit(solution)/shard_map/all_to_all | solution.py:34
  129.6 1.8 %copy-done.3 = bf16[1664,896]{1,0:T(8,128)(2,1)S(1)} copy-done((bf16[1664,896]{1,0:T(8,128)(2,1)S(1)}, bf16[1664,896]{1,0:T(8,128)(2,1)}, u32[]{:S(2)}) %copy-start.3) | copy-done | bytes 2981912
  131.4 1.7 %tile.1 = (bf16[16,1664]{1,0:T(8,128)(2,1)S(1)}, bf16[16,1664]{1,0:T(8,128)(2,1)S(1)}, bf16[16,1664]{1,0:T(8,128)(2,1)S(1)}, bf16[16,1664]{1,0:T(8,128)(2,1)S(1)}) custom-call(s32[4]{0:T(128)S(1)} %copy-done.11, bf16[8,64,896]{2,1,0:T(8,128)(2,1)S(1)} %all-to-all-done.2.parts, bf16[1664,896]{1,0:T(8,128)(2,1)S(1)} %copy-done.3), custom_call_target="tpu_custom_call" | custom-call | tf_op jit(solution)/shard_map/tile/pallas_call | solution.py:389
  133.1 0.6 collective-permute-start.26
  133.7 1.1 collective-permute-start.27
  134.8 2.2 %collective-permute-start.28 = (bf16[16,1664]{1,0:T(8,128)(2,1)S(1)}, bf16[16,1664]{1,0:T(8,128)(2,1)S(1)}, u32[]{:S(2)}, u32[]{:S(2)}) collective-permute-start(bf16[16,1664]{1,0:T(8,128)(2,1)S(1)} %get-tuple-element.72), channel_id=1, source_target_pairs={{0,24},{8,16},{16,8},{24,0},{1,25},{9,17},{17,9},{25,1},{2,26},{10... | collective-permute-start | bytes 159752 | tf_op jit(solution)/shard_map/ppermute | solution.py:39
  136.9 8.9 %all_to_all.20.score = f32[8,1,128]{2,1,0:T(1,128)S(1)} all-to-all(f32[8,1,128]{2,1,0:T(1,128)S(1)} %broadcast_in_dim.3), channel_id=1, replica_groups=mesh['z'=8,'xh'=2,'c'=2,'y'=4,'xl'=2] {'z'}, dimensions={0} | all-to-all | bytes 8192 | tf_op jit(solution)/shard_map/all_to_all | solution.py:34
  145.8 1.2 final.1
  (57 shorter events, 0.3 us)
Async XLA Ops:
  1.8 9.5 %copy-start.9 = (s32[4]{0:T(128)}, s32[4]{0:T(128)S(1)}, u32[]{:S(2)}) copy-start(s32[4]{0:T(128)S(1)} %pad_add_fusion.where) | copy-start | bytes 52
  1.8 0.8 copy-start.12
  2.6 0.7 copy-start.13
  3.2 0.7 copy-start.15
  4.7 11.9 %collective-permute-start = (bf16[60,896]{1,0:T(8,128)(2,1)S(1)}, bf16[60,896]{1,0:T(8,128)(2,1)S(1)}, u32[]{:S(2)}, u32[]{:S(2)}) collective-permute-start(bf16[60,896]{1,0:T(8,128)(2,1)S(1)} %get-tuple-element.40), channel_id=1, source_target_pairs={{0,8},{8,0},{1,9},{9,1},{2,10},{10,2},{3,11},{11,3},{4,12},{12,4},... | collective-permute-start | bytes 322568 | tf_op jit(solution)/shard_map/ppermute | solution.py:39
  8.0 8.6 %collective-permute-start.1 = (bf16[60,896]{1,0:T(8,128)(2,1)S(1)}, bf16[60,896]{1,0:T(8,128)(2,1)S(1)}, u32[]{:S(2)}, u32[]{:S(2)}) collective-permute-start(bf16[60,896]{1,0:T(8,128)(2,1)S(1)} %get-tuple-element.41), channel_id=1, source_target_pairs={{0,16},{16,0},{1,17},{17,1},{2,18},{18,2},{3,19},{19,3},{4,20},{20... | collective-permute-start | bytes 322568 | tf_op jit(solution)/shard_map/ppermute | solution.py:39
  9.0 5.2 %copy-start.1 = (bf16[6,2048,64]{1,2,0:T(8,128)(2,1)S(1)}, bf16[6,2048,64]{1,2,0:T(8,128)(2,1)}, u32[]{:S(2)}) copy-start(bf16[6,2048,64]{1,2,0:T(8,128)(2,1)} %param.17) | copy-start | bytes 4718596
  9.0 5.2 %copy-start.4 = (bf16[2048,512]{1,0:T(8,128)(2,1)S(1)}, bf16[2048,512]{1,0:T(8,128)(2,1)}, u32[]{:S(2)}) copy-start(bf16[2048,512]{1,0:T(8,128)(2,1)} %basis.2) | copy-start | bytes 6291460
  9.0 5.2 %copy-start.14 = (s32[4]{0:T(128)S(1)}, s32[4]{0:T(128)}, u32[]{:S(2)}) copy-start(s32[4]{0:T(128)} %ids.3) | copy-start | bytes 52
  9.0 7.8 %collective-permute-start.2 = (bf16[60,896]{1,0:T(8,128)(2,1)S(1)}, bf16[60,896]{1,0:T(8,128)(2,1)S(1)}, u32[]{:S(2)}, u32[]{:S(2)}) collective-permute-start(bf16[60,896]{1,0:T(8,128)(2,1)S(1)} %get-tuple-element.42), channel_id=1, source_target_pairs={{0,24},{8,16},{16,8},{24,0},{1,25},{9,17},{17,9},{25,1},{2,26},{10... | collective-permute-start | bytes 322568 | tf_op jit(solution)/shard_map/ppermute | solution.py:39
  14.2 2.6 %copy-start.10 = (s32[4]{0:T(128)S(1)}, s32[4]{0:T(128)}, u32[]{:S(2)}) copy-start(s32[4]{0:T(128)} %copy-done.9) | copy-start | bytes 52
  18.0 17.7 %collective-permute-start.3 = (bf16[240,896]{1,0:T(8,128)(2,1)S(1)}, bf16[240,896]{1,0:T(8,128)(2,1)S(1)}, u32[]{:S(2)}, u32[]{:S(2)}) collective-permute-start(bf16[240,896]{1,0:T(8,128)(2,1)S(1)} %arrange.1.refs_0_), channel_id=1, source_target_pairs={{0,32},{32,64},{64,96},{96,128},{128,160},{160,192},{192,224},{224... | collective-permute-start | bytes 1290248 | tf_op jit(solution)/shard_map/ppermute | solution.py:44
  18.5 17.1 %collective-permute-start.4 = (bf16[240,896]{1,0:T(8,128)(2,1)S(1)}, bf16[240,896]{1,0:T(8,128)(2,1)S(1)}, u32[]{:S(2)}, u32[]{:S(2)}) collective-permute-start(bf16[240,896]{1,0:T(8,128)(2,1)S(1)} %arrange.1.refs_0_), channel_id=1, source_target_pairs={{0,224},{32,0},{64,32},{96,64},{128,96},{160,128},{192,160},{224,1... | collective-permute-start | bytes 1290248 | tf_op jit(solution)/shard_map/ppermute | solution.py:44
  22.6 12.4 %all-to-all-start = ((bf16[8,48,512]{2,1,0:T(8,128)(2,1)}), bf16[8,48,512]{2,1,0:T(8,128)(2,1)S(1)}, u32[]{:S(2)}, u32[]{:S(2)}) async-start(bf16[8,48,512]{2,1,0:T(8,128)(2,1)} %left.1), calls=%async_computation | async-start | bytes 786432 | tf_op jit(solution)/shard_map/all_to_all | solution.py:34
  27.2 24.3 %collective-permute-start.7 = (bf16[192,1664]{1,0:T(8,128)(2,1)}, bf16[192,1664]{1,0:T(8,128)(2,1)S(1)}, u32[]{:S(2)}, u32[]{:S(2)}) collective-permute-start(bf16[192,1664]{1,0:T(8,128)(2,1)} %inverse.4), channel_id=1, source_target_pairs={{0,16},{16,0},{1,17},{17,1},{2,18},{18,2},{3,19},{19,3},{4,20},{20... | collective-permute-start | bytes 1916936 | tf_op jit(solution)/shard_map/ppermute | solution.py:39
  35.7 9.2 %copy-start.6 = (bf16[240,896]{1,0:T(8,128)(2,1)}, bf16[240,896]{1,0:T(8,128)(2,1)S(1)}, u32[]{:S(2)}) copy-start(bf16[240,896]{1,0:T(8,128)(2,1)S(1)} %collective-permute-done.4.refs_7_) | copy-start | bytes 1290244
  35.7 15.8 %collective-permute-start.5 = (bf16[240,896]{1,0:T(8,128)(2,1)S(1)}, bf16[240,896]{1,0:T(8,128)(2,1)}, u32[]{:S(2)}, u32[]{:S(2)}) collective-permute-start(bf16[240,896]{1,0:T(8,128)(2,1)S(1)} %collective-permute-done.3.refs_1_), channel_id=1, source_target_pairs={{0,32},{32,64},{64,96},{96,128},{128,160},{160,192},{192,224},{224... | collective-permute-start | bytes 1290248 | tf_op jit(solution)/shard_map/ppermute | solution.py:44
  35.8 15.7 %collective-permute-start.6 = (bf16[240,896]{1,0:T(8,128)(2,1)S(1)}, bf16[240,896]{1,0:T(8,128)(2,1)}, u32[]{:S(2)}, u32[]{:S(2)}) collective-permute-start(bf16[240,896]{1,0:T(8,128)(2,1)S(1)} %collective-permute-done.4.refs_7_), channel_id=1, source_target_pairs={{0,224},{32,0},{64,32},{96,64},{128,96},{160,128},{192,160},{224,1... | collective-permute-start | bytes 1290248 | tf_op jit(solution)/shard_map/ppermute | solution.py:44
  38.5 13.0 %all-to-all-start.1 = ((bf16[8,32,512]{2,1,0:T(8,128)(2,1)}), bf16[8,32,512]{2,1,0:T(8,128)(2,1)S(1)}, u32[]{:S(2)}, u32[]{:S(2)}) async-start(bf16[8,32,512]{2,1,0:T(8,128)(2,1)} %get-tuple-element.43), calls=%async_computation.1 | async-start | bytes 524288 | tf_op jit(solution)/shard_map/all_to_all | solution.py:34
  44.9 18.7 %collective-permute-start.10 = (bf16[192,1664]{1,0:T(8,128)(2,1)}, bf16[192,1664]{1,0:T(8,128)(2,1)S(1)}, u32[]{:S(2)}, u32[]{:S(2)}) collective-permute-start(bf16[192,1664]{1,0:T(8,128)(2,1)} %inverse.5), channel_id=1, source_target_pairs={{0,16},{16,0},{1,17},{17,1},{2,18},{18,2},{3,19},{19,3},{4,20},{20... | collective-permute-start | bytes 1916936 | tf_op jit(solution)/shard_map/ppermute | solution.py:39
  51.5 12.1 %collective-permute-start.8 = (bf16[240,896]{1,0:T(8,128)(2,1)}, bf16[240,896]{1,0:T(8,128)(2,1)}, u32[]{:S(2)}, u32[]{:S(2)}) collective-permute-start(bf16[240,896]{1,0:T(8,128)(2,1)} %collective-permute-done.5.refs_2_), channel_id=1, source_target_pairs={{0,32},{32,64},{64,96},{96,128},{128,160},{160,192},{192,224},{224... | collective-permute-start | bytes 1290248 | tf_op jit(solution)/shard_map/ppermute | solution.py:44
  51.6 12.0 %collective-permute-start.9 = (bf16[240,896]{1,0:T(8,128)(2,1)}, bf16[240,896]{1,0:T(8,128)(2,1)}, u32[]{:S(2)}, u32[]{:S(2)}) collective-permute-start(bf16[240,896]{1,0:T(8,128)(2,1)} %collective-permute-done.6.refs_6_), channel_id=1, source_target_pairs={{0,224},{32,0},{64,32},{96,64},{128,96},{160,128},{192,160},{224,1... | collective-permute-start | bytes 1290248 | tf_op jit(solution)/shard_map/ppermute | solution.py:44
  58.0 16.7 %copy-start = (bf16[6,3328,64]{1,2,0:T(8,128)(2,1)S(1)}, bf16[6,3328,64]{1,2,0:T(8,128)(2,1)}, u32[]{:S(2)}) copy-start(bf16[6,3328,64]{1,2,0:T(8,128)(2,1)} %param.18) | copy-start | bytes 7667716
  58.0 16.7 %copy-start.11 = (s32[4]{0:T(128)S(1)}, s32[4]{0:T(128)}, u32[]{:S(2)}) copy-start(s32[4]{0:T(128)} %copy-done.9) | copy-start | bytes 52
  58.0 21.7 %collective-permute-start.14 = (bf16[512,896]{1,0:T(8,128)(2,1)}, bf16[512,896]{1,0:T(8,128)(2,1)S(1)}, u32[]{:S(2)}, u32[]{:S(2)}) collective-permute-start(bf16[512,896]{1,0:T(8,128)(2,1)} %get-tuple-element.54), channel_id=1, source_target_pairs={{0,8},{8,0},{1,9},{9,1},{2,10},{10,2},{3,11},{11,3},{4,12},{12,4},... | collective-permute-start | bytes 2752520 | tf_op jit(solution)/shard_map/ppermute | solution.py:39
  63.6 10.6 %collective-permute-start.11 = (bf16[240,896]{1,0:T(8,128)(2,1)}, bf16[240,896]{1,0:T(8,128)(2,1)}, u32[]{:S(2)}, u32[]{:S(2)}) collective-permute-start(bf16[240,896]{1,0:T(8,128)(2,1)} %collective-permute-done.8.refs_3_), channel_id=1, source_target_pairs={{0,32},{32,64},{64,96},{96,128},{128,160},{160,192},{192,224},{224... | collective-permute-start | bytes 1290248 | tf_op jit(solution)/shard_map/ppermute | solution.py:44
  66.3 19.1 %collective-permute-start.17 = (bf16[128,1664]{1,0:T(8,128)(2,1)}, bf16[128,1664]{1,0:T(8,128)(2,1)S(1)}, u32[]{:S(2)}, u32[]{:S(2)}) collective-permute-start(bf16[128,1664]{1,0:T(8,128)(2,1)} %inverse.7), channel_id=1, source_target_pairs={{0,16},{16,0},{1,17},{17,1},{2,18},{18,2},{3,19},{19,3},{4,20},{20... | collective-permute-start | bytes 1277960 | tf_op jit(solution)/shard_map/ppermute | solution.py:39
  66.9 4.8 %collective-permute-start.13 = (bf16[128,512]{1,0:T(8,128)(2,1)S(1)}, bf16[128,512]{1,0:T(8,128)(2,1)S(1)}, u32[]{:S(2)}, u32[]{:S(2)}) collective-permute-start(bf16[128,512]{1,0:T(8,128)(2,1)S(1)} %get-tuple-element.52.refs_2_), channel_id=1, source_target_pairs={{0,8},{8,0},{1,9},{9,1},{2,10},{10,2},{3,11},{11,3},{4,12},{12,4},... | collective-permute-start | bytes 393224 | tf_op jit(solution)/shard_map/ppermute | solution.py:39
  70.7 8.9 %collective-permute-start.12 = (bf16[256,512]{1,0:T(8,128)(2,1)S(1)}, bf16[256,512]{1,0:T(8,128)(2,1)S(1)}, u32[]{:S(2)}, u32[]{:S(2)}) collective-permute-start(bf16[256,512]{1,0:T(8,128)(2,1)S(1)} %bitcast.18), channel_id=1, source_target_pairs={{0,8},{8,0},{1,9},{9,1},{2,10},{10,2},{3,11},{11,3},{4,12},{12,4},... | collective-permute-start | bytes 786440 | tf_op jit(solution)/shard_map/ppermute | solution.py:39
  71.7 13.7 %collective-permute-start.15 = (bf16[256,512]{1,0:T(8,128)(2,1)S(1)}, bf16[256,512]{1,0:T(8,128)(2,1)S(1)}, u32[]{:S(2)}, u32[]{:S(2)}) collective-permute-start(bf16[256,512]{1,0:T(8,128)(2,1)S(1)} %bitcast.19), channel_id=1, source_target_pairs={{0,16},{16,0},{1,17},{17,1},{2,18},{18,2},{3,19},{19,3},{4,20},{20... | collective-permute-start | bytes 786440 | tf_op jit(solution)/shard_map/ppermute | solution.py:39
  74.2 11.3 %collective-permute-start.16 = (bf16[128,512]{1,0:T(8,128)(2,1)S(1)}, bf16[128,512]{1,0:T(8,128)(2,1)S(1)}, u32[]{:S(2)}, u32[]{:S(2)}) collective-permute-start(bf16[128,512]{1,0:T(8,128)(2,1)S(1)} %get-tuple-element.52.refs_2_), channel_id=1, source_target_pairs={{0,16},{16,0},{1,17},{17,1},{2,18},{18,2},{3,19},{19,3},{4,20},{20... | collective-permute-start | bytes 393224 | tf_op jit(solution)/shard_map/ppermute | solution.py:39
  74.7 1.0 copy-start.7
  75.7 4.0 %copy-start.5 = (bf16[512,896]{1,0:T(8,128)(2,1)S(1)}, bf16[512,896]{1,0:T(8,128)(2,1)}, u32[]{:S(2)}) copy-start(bf16[512,896]{1,0:T(8,128)(2,1)} %get-tuple-element.53.refs_4_) | copy-start | bytes 2752516
  79.6 6.5 %copy-start.2 = (bf16[1664,896]{1,0:T(8,128)(2,1)}, bf16[1664,896]{1,0:T(8,128)(2,1)S(1)}, u32[]{:S(2)}) copy-start(bf16[1664,896]{1,0:T(8,128)(2,1)S(1)} %get-tuple-element.68.basis) | copy-start | bytes 8945668
  79.7 12.5 %copy-start.8 = (f32[32,1664]{1,0:T(8,128)S(1)}, f32[32,1664]{1,0:T(8,128)}, u32[]{:S(2)}) copy-start(f32[32,1664]{1,0:T(8,128)} %factors.1) | copy-start | bytes 638980
  79.7 12.5 %copy-start.16 = (s32[16]{0:T(128)S(1)}, s32[16]{0:T(128)}, u32[]{:S(2)}) copy-start(s32[16]{0:T(128)} %block_ids.1) | copy-start | bytes 196
  86.1 6.0 %collective-permute-start.20 = (bf16[512,896]{1,0:T(8,128)(2,1)S(1)}, bf16[512,896]{1,0:T(8,128)(2,1)S(1)}, u32[]{:S(2)}, u32[]{:S(2)}) collective-permute-start(bf16[512,896]{1,0:T(8,128)(2,1)S(1)} %get-tuple-element.64), channel_id=1, source_target_pairs={{0,8},{8,0},{1,9},{9,1},{2,10},{10,2},{3,11},{11,3},{4,12},{12,4},... | collective-permute-start | bytes 2752520 | tf_op jit(solution)/shard_map/ppermute | solution.py:39
  89.5 2.7 %collective-permute-start.18 = (bf16[256,512]{1,0:T(8,128)(2,1)S(1)}, bf16[256,512]{1,0:T(8,128)(2,1)S(1)}, u32[]{:S(2)}, u32[]{:S(2)}) collective-permute-start(bf16[256,512]{1,0:T(8,128)(2,1)S(1)} %collective-permute-done.15.refs_0_), channel_id=1, source_target_pairs={{0,8},{8,0},{1,9},{9,1},{2,10},{10,2},{3,11},{11,3},{4,12},{12,4},... | collective-permute-start | bytes 786440 | tf_op jit(solution)/shard_map/ppermute | solution.py:39
  89.6 2.6 %collective-permute-start.19 = (bf16[128,512]{1,0:T(8,128)(2,1)S(1)}, bf16[128,512]{1,0:T(8,128)(2,1)S(1)}, u32[]{:S(2)}, u32[]{:S(2)}) collective-permute-start(bf16[128,512]{1,0:T(8,128)(2,1)S(1)} %collective-permute-done.16.refs_2_), channel_id=1, source_target_pairs={{0,8},{8,0},{1,9},{9,1},{2,10},{10,2},{3,11},{11,3},{4,12},{12,4},... | collective-permute-start | bytes 393224 | tf_op jit(solution)/shard_map/ppermute | solution.py:39
  97.9 31.7 %all-to-all-start.2 = ((bf16[8,64,896]{2,1,0:T(8,128)(2,1)}), bf16[8,64,896]{2,1,0:T(8,128)(2,1)S(1)}, u32[]{:S(2)}, u32[]{:S(2)}) async-start(bf16[8,64,896]{2,1,0:T(8,128)(2,1)} %get-tuple-element.65), calls=%async_computation.2 | async-start | bytes 1835008 | tf_op jit(solution)/shard_map/all_to_all | solution.py:34
  103.2 1.5 %collective-permute-start.21 = (f32[1,128]{1,0:T(1,128)S(1)}, f32[1,128]{1,0:T(1,128)S(1)}, u32[]{:S(2)}, u32[]{:S(2)}) collective-permute-start(f32[1,128]{1,0:T(1,128)S(1)} %get-tuple-element.66), channel_id=1, source_target_pairs={{0,8},{8,0},{1,9},{9,1},{2,10},{10,2},{3,11},{11,3},{4,12},{12,4},... | collective-permute-start | bytes 1544 | tf_op jit(solution)/shard_map/ppermute | solution.py:39
  104.7 2.7 %collective-permute-start.22 = (f32[1,128]{1,0:T(1,128)S(1)}, f32[1,128]{1,0:T(1,128)S(1)}, u32[]{:S(2)}, u32[]{:S(2)}) collective-permute-start(f32[1,128]{1,0:T(1,128)S(1)} %add.19), channel_id=1, source_target_pairs={{0,1},{1,0},{2,3},{3,2},{4,5},{5,4},{6,7},{7,6},{8,9},{9,8},{10,11... | collective-permute-start | bytes 1544 | tf_op jit(solution)/shard_map/ppermute | solution.py:39
  107.4 2.7 %collective-permute-start.23 = (f32[1,128]{1,0:T(1,128)S(1)}, f32[1,128]{1,0:T(1,128)S(1)}, u32[]{:S(2)}, u32[]{:S(2)}) collective-permute-start(f32[1,128]{1,0:T(1,128)S(1)} %add.20), channel_id=1, source_target_pairs={{0,2},{2,0},{4,6},{6,4},{1,3},{3,1},{5,7},{7,5},{8,10},{10,8},{12,... | collective-permute-start | bytes 1544 | tf_op jit(solution)/shard_map/ppermute | solution.py:39
  110.1 4.2 %collective-permute-start.24 = (f32[1,128]{1,0:T(1,128)S(1)}, f32[1,128]{1,0:T(1,128)S(1)}, u32[]{:S(2)}, u32[]{:S(2)}) collective-permute-start(f32[1,128]{1,0:T(1,128)S(1)} %add.21), channel_id=1, source_target_pairs={{0,4},{2,6},{4,0},{6,2},{1,5},{3,7},{5,1},{7,3},{8,12},{10,14},{12... | collective-permute-start | bytes 1544 | tf_op jit(solution)/shard_map/ppermute | solution.py:39
  114.3 4.2 %collective-permute-start.25 = (f32[1,128]{1,0:T(1,128)S(1)}, f32[1,128]{1,0:T(1,128)S(1)}, u32[]{:S(2)}, u32[]{:S(2)}) collective-permute-start(f32[1,128]{1,0:T(1,128)S(1)} %add.22), channel_id=1, source_target_pairs={{0,16},{16,0},{1,17},{17,1},{2,18},{18,2},{3,19},{19,3},{4,20},{20... | collective-permute-start | bytes 1544 | tf_op jit(solution)/shard_map/ppermute | solution.py:39
  129.6 1.8 %copy-start.3 = (bf16[1664,896]{1,0:T(8,128)(2,1)S(1)}, bf16[1664,896]{1,0:T(8,128)(2,1)}, u32[]{:S(2)}) copy-start(bf16[1664,896]{1,0:T(8,128)(2,1)} %copy-done.2) | copy-start | bytes 8945668
  133.1 12.7 %collective-permute-start.26 = (bf16[16,1664]{1,0:T(8,128)(2,1)S(1)}, bf16[16,1664]{1,0:T(8,128)(2,1)S(1)}, u32[]{:S(2)}, u32[]{:S(2)}) collective-permute-start(bf16[16,1664]{1,0:T(8,128)(2,1)S(1)} %get-tuple-element.70), channel_id=1, source_target_pairs={{0,8},{8,0},{1,9},{9,1},{2,10},{10,2},{3,11},{11,3},{4,12},{12,4},... | collective-permute-start | bytes 159752 | tf_op jit(solution)/shard_map/ppermute | solution.py:39
  133.7 12.1 %collective-permute-start.27 = (bf16[16,1664]{1,0:T(8,128)(2,1)S(1)}, bf16[16,1664]{1,0:T(8,128)(2,1)S(1)}, u32[]{:S(2)}, u32[]{:S(2)}) collective-permute-start(bf16[16,1664]{1,0:T(8,128)(2,1)S(1)} %get-tuple-element.71), channel_id=1, source_target_pairs={{0,16},{16,0},{1,17},{17,1},{2,18},{18,2},{3,19},{19,3},{4,20},{20... | collective-permute-start | bytes 159752 | tf_op jit(solution)/shard_map/ppermute | solution.py:39
  134.8 11.1 %collective-permute-start.28 = (bf16[16,1664]{1,0:T(8,128)(2,1)S(1)}, bf16[16,1664]{1,0:T(8,128)(2,1)S(1)}, u32[]{:S(2)}, u32[]{:S(2)}) collective-permute-start(bf16[16,1664]{1,0:T(8,128)(2,1)S(1)} %get-tuple-element.72), channel_id=1, source_target_pairs={{0,24},{8,16},{16,8},{24,0},{1,25},{9,17},{17,9},{25,1},{2,26},{10... | collective-permute-start | bytes 159752 | tf_op jit(solution)/shard_map/ppermute | solution.py:39

commit v9 on v8

--- a/solution.py
+++ b/solution.py
@@ -320,8 +320,8 @@
     )(right, *lefts, *windows, *inverses)
 
 
-def back_body(where, block_ids, so_far, factors, right, tokens, delta, *refs, train):
-    refs, (out, score) = refs[:-2], refs[-2:]
+def back_body(where, block_ids, so_far, factors, right, *refs):
+    refs, out = refs[:-1], refs[-1]
     queries = so_far.shape[0]
     n_z, rows, width = out.shape
     per = rows // queries
@@ -334,34 +334,49 @@
     first = where[3] * (width - valid)
     mine = jnp.logical_and(lane >= first, lane < first + valid)
     scale = jnp.where(mine, 1.0 / row, 0.0)
+    for q in range(queries):
+        total = so_far[q] + back_terms(right, refs[:2], refs[2:4], refs[4:], rank, q)
+        total = (total * scale).astype(BF)
+        out[:, q * per : (q + 1) * per, :] = total.reshape(n_z, per, width)
+
+
+def back(where, block_ids, so_far, factors, right, far, n_z):
+    queries, win, width = so_far.shape
+    return pl.pallas_call(
+        back_body,
+        out_shape=jax.ShapeDtypeStruct((n_z, queries * win // n_z, width), BF),
+        in_specs=[SMEM_SPEC, SMEM_SPEC, *([VMEM_SPEC] * (3 + len(far)))],
+        out_specs=VMEM_SPEC,
+        compiler_params=params(12),
+        name="back",
+    )(where, block_ids, so_far, factors, right, *far)
+
+
+def score_body(parts, tokens, delta, score, *, queries, train):
+    n_z, rows, width = parts.shape
+    per = rows // queries
     which = lax.rem(lax.broadcasted_iota(jnp.int32, (tokens.shape[0], 1), 0), train)
     place = lax.broadcasted_iota(jnp.int32, (1, LANES), 1)
     table = jnp.zeros((1, LANES), F32)
     for q in range(queries):
-        total = so_far[q] + back_terms(right, refs[:2], refs[2:4], refs[4:], rank, q)
-        total = (total * scale).astype(BF)
-        out[:, q * per : (q + 1) * per, :] = total.reshape(n_z, per, width)
-        projected = dot(tokens[...], total, 1, 1) * delta[...].astype(F32)
+        part = parts[:, q * per : (q + 1) * per, :].reshape(n_z * per, width)
+        projected = dot(tokens[...], part, 1, 1) * delta[...].astype(F32)
         for b in range(train):
-            part = jnp.sum(jnp.where(which == b, projected, 0.0), axis=0, keepdims=True)
-            part = jnp.sum(part, axis=1, keepdims=True)
-            table = jnp.where(place == q * train + b, part, table)
+            line = jnp.sum(jnp.where(which == b, projected, 0.0), axis=0, keepdims=True)
+            value = jnp.sum(line, axis=1, keepdims=True)
+            table = jnp.where(place == q * train + b, value, table)
     score[...] = table
 
 
-def back(where, block_ids, so_far, factors, right, tokens, delta, far, n_z, train):
-    queries, win, width = so_far.shape
-    return pl.pallas_call(
-        functools.partial(back_body, train=train),
-        out_shape=(
-            jax.ShapeDtypeStruct((n_z, queries * win // n_z, width), BF),
-            jax.ShapeDtypeStruct((1, LANES), F32),
-        ),
-        in_specs=[SMEM_SPEC, SMEM_SPEC, *([VMEM_SPEC] * (5 + len(far)))],
-        out_specs=(VMEM_SPEC, VMEM_SPEC),
-        compiler_params=params(12),
-        name="back",
-    )(where, block_ids, so_far, factors, right, tokens, delta, *far)
+def score_part(parts, tokens, delta, queries, train):
+    return pl.pallas_call(
+        functools.partial(score_body, queries=queries, train=train),
+        out_shape=jax.ShapeDtypeStruct((1, LANES), F32),
+        in_specs=[VMEM_SPEC] * 3,
+        out_specs=VMEM_SPEC,
+        compiler_params=params(4),
+        name="score",
+    )(parts, tokens, delta)
 
 
 def tile_body(where, parts, basis, *outs, queries):
@@ -404,7 +419,7 @@
         at = pl.multiple_of((where[1] ^ r) * block, LANES)
         for q in range(queries):
             tiles[q, :, pl.ds(at, block)] = total[q * per : (q + 1) * per]
-    sums = jnp.sum(score[...], axis=0)
+    sums = jnp.sum(score[:, :1, :], axis=0)
     train = scores.shape[1]
     for q in range(queries):
         scores[q : q + 1, :] = sums[:, q * train : (q + 1) * train]
@@ -490,14 +505,13 @@
     left_x, window_x, *far = after((left_x, window_x, *far), so_far)
     far = halves(where, far, width)
     far = (left_x, swap(left_x, "c"), window_x, swap(window_x, "c"), far[0], swap(far[1], "c"))
-    parts, score = back(
-        where, block_ids, so_far, factor_table, right, tokens, delta, far, n_z, train
-    )
+    parts = back(where, block_ids, so_far, factor_table, right, far, n_z)
+    score = score_part(parts, tokens, delta, queries, train)
     for axis, mask in (("c", 1), ("xl", 1), ("y", 1), ("y", 2), ("xh", 1)):
         score = score + swap(score, axis, mask)
     parts, score = after((exchange(parts, "z"), score))
     parts = tile_part(where, parts, basis, queries)
-    score = exchange(jnp.broadcast_to(score, (n_z, *score.shape)), "z")
+    score = exchange(jnp.broadcast_to(score, (n_z, 8, LANES)), "z")
     parts = (
         parts[0],
         swap(parts[1], "c"),

time: 148 us -> 145 us (0.980)
  blocking collectives: 8.88 us -> 0 us
  starting transfers between devices: 57.8 us -> 62 us
  Pallas kernels: 34 us -> 36.1 us
    all_to_all x1 -> x0, blocking collectives: 8.88 us -> none  [exchange(): return lax.all_to_all(value, axis, split_axis=0, concat_axis=0, tiled=True)]
    all_to_all x3 -> x4, starting transfers between devices: 13.4 us -> 16.7 us  [exchange(): return lax.all_to_all(value, axis, split_axis=0, concat_axis=0, tiled=True)]
    all_to_all x3 -> x4, waiting for transfers between devices: 20.5 us -> 18.5 us  [exchange(): return lax.all_to_all(value, axis, split_axis=0, concat_axis=0, tiled=True)]
    ppermute x22, waiting for transfers between devices: 17.5 us -> 19.3 us  [swap(): return lax.ppermute(value, axis, [(i, i ^ mask) for i in range(size)])]
    pallas_call x1 -> x2, Pallas kernels: 5.71 us -> 6.57 us  [the longest x1 4.82 us: back(): pl.pallas_call(back_body, out_shape=jax.ShapeDtypeStruct((n_z, queries *...]
    unnamed x35 -> x39, local copies, waits for them, and re-layouts: 6.07 us -> 6.08 us
  transfers between devices with their start and end apart: 32 -> 33, of which waited for: 14 -> 16; matrix products, arithmetic and copies ran while one was open for 0% -> 0% of each run, Pallas kernels for 15% -> 19%
where the time goes in v9:
time: 145 us
  starting transfers between devices  62 us (43%)
  waiting for transfers between devices  38.7 us (27%)
  Pallas kernels  36.1 us (25%)
  local copies, waits for them, and re-layouts  6.7 us (5%)
    ppermute x22, starting transfers between devices, swap(): return lax.ppermute(value, axis, [(i, i ^ mask) for i in range(size)])  35.2 us
    ppermute x22, waiting for transfers between devices, swap(): return lax.ppermute(value, axis, [(i, i ^ mask) for i in range(size)])  19.3 us
    all_to_all x4, waiting for transfers between devices, exchange(): return lax.all_to_all(value, axis, split_axis=0, concat_axis=0, tiled=True)  18.5 us
    all_to_all x4, starting transfers between devices, exchange(): return lax.all_to_all(value, axis, split_axis=0, concat_axis=0, tiled=True)  16.7 us
    pallas_call x4, Pallas kernels, inverse_block(): pl.pallas_call(inverse_body, out_shape=tuple((jax.ShapeDtypeStruct((rows,...  12.5 us
    ppermute x7, starting transfers between devices, shift(): lax.ppermute(value, 'z', [(i, (i + step) % size) for i in range(size)])  10 us
    unnamed x39, local copies, waits for them, and re-layouts  6.08 us
    pallas_call x1, Pallas kernels, back(): pl.pallas_call(back_body, out_shape=jax.ShapeDtypeStruct((n_z, queries *...  4.82 us
  transfers between devices with their start and end apart: 33, of which 16 were waited for; matrix products, arithmetic and copies ran while one was open for 0% of the time, Pallas kernels for 19%

profile of v9, /device:TPU:1, one launch (start us, length us, event | category | flops | bytes accessed | tf_op | source)
XLA Modules:
  0.0 144.5 jit_solution(17010141643467152296)
XLA Ops:
  0.6 1.0 copy.13.basis
  1.8 0.8 copy-done.12
  2.6 0.7 copy-done.15
  3.2 0.7 copy-done.17
  3.9 0.7 pack.1
  4.7 3.3 %collective-permute-start = (bf16[60,896]{1,0:T(8,128)(2,1)S(1)}, bf16[60,896]{1,0:T(8,128)(2,1)S(1)}, u32[]{:S(2)}, u32[]{:S(2)}) collective-permute-start(bf16[60,896]{1,0:T(8,128)(2,1)S(1)} %get-tuple-element.38), channel_id=1, source_target_pairs={{0,8},{8,0},{1,9},{9,1},{2,10},{10,2},{3,11},{11,3},{4,12},{12,4},... | collective-permute-start | bytes 322568 | tf_op jit(solution)/shard_map/ppermute | solution.py:39
  8.0 1.0 collective-permute-start.1
  9.0 2.2 %collective-permute-start.2 = (bf16[60,896]{1,0:T(8,128)(2,1)S(1)}, bf16[60,896]{1,0:T(8,128)(2,1)S(1)}, u32[]{:S(2)}, u32[]{:S(2)}) collective-permute-start(bf16[60,896]{1,0:T(8,128)(2,1)S(1)} %get-tuple-element.40), channel_id=1, source_target_pairs={{0,24},{8,16},{16,8},{24,0},{1,25},{9,17},{17,9},{25,1},{2,26},{10... | collective-permute-start | bytes 322568 | tf_op jit(solution)/shard_map/ppermute | solution.py:39
  11.2 3.0 %inverse.4 = bf16[192,1664]{1,0:T(8,128)(2,1)} custom-call(s32[4]{0:T(128)} %copy-done.9, f32[512,3328]{1,0:T(8,128)} %corrected.7), custom_call_target="tpu_custom_call" | custom-call | tf_op jit(solution)/shard_map/inverse/pallas_call | solution.py:126
  14.2 2.3 %left.1 = bf16[8,48,512]{2,1,0:T(8,128)(2,1)} custom-call(s32[4]{0:T(128)S(1)} %copy-done.16, bf16[6,64,2048]{2,1,0:T(8,128)(2,1)S(1)} %bitcast.14, bf16[6,64,2048]{2,1,0:T(8,128)(2,1)S(1)} %bitcast.15, bf16[6,64,2048]{2,1,0:T(8,128)(2,1)S(1)} %bitcast.16, bf16[6,64,2048]{2,1,0:T(8,128)(2,1)S(1)} %bitcast.17, bf16[2048,512]{1,0:T(8,128)(2,1)S(1)} %copy-done.4), custom_call_target="tpu_custom_call" | custom-call | tf_op jit(solution)/shard_map/left/pallas_call | solution.py:71
  16.8 1.2 arrange.1.refs_0_
  18.0 0.5 collective-permute-start.3
  18.5 4.0 %collective-permute-start.4 = (bf16[240,896]{1,0:T(8,128)(2,1)S(1)}, bf16[240,896]{1,0:T(8,128)(2,1)S(1)}, u32[]{:S(2)}, u32[]{:S(2)}) collective-permute-start(bf16[240,896]{1,0:T(8,128)(2,1)S(1)} %arrange.1.refs_0_), channel_id=1, source_target_pairs={{0,224},{32,0},{64,32},{96,64},{128,96},{160,128},{192,160},{224,1... | collective-permute-start | bytes 1290248 | tf_op jit(solution)/shard_map/ppermute | solution.py:44
  22.6 4.6 %all-to-all-start = ((bf16[8,48,512]{2,1,0:T(8,128)(2,1)}), bf16[8,48,512]{2,1,0:T(8,128)(2,1)S(1)}, u32[]{:S(2)}, u32[]{:S(2)}) async-start(bf16[8,48,512]{2,1,0:T(8,128)(2,1)} %left.1), calls=%async_computation | async-start | bytes 786432 | tf_op jit(solution)/shard_map/all_to_all | solution.py:34
  27.2 2.4 %collective-permute-start.7 = (bf16[192,1664]{1,0:T(8,128)(2,1)}, bf16[192,1664]{1,0:T(8,128)(2,1)S(1)}, u32[]{:S(2)}, u32[]{:S(2)}) collective-permute-start(bf16[192,1664]{1,0:T(8,128)(2,1)} %inverse.4), channel_id=1, source_target_pairs={{0,16},{16,0},{1,17},{17,1},{2,18},{18,2},{3,19},{19,3},{4,20},{20... | collective-permute-start | bytes 1916936 | tf_op jit(solution)/shard_map/ppermute | solution.py:39
  29.6 5.3 %all-to-all-done.parts = bf16[8,48,512]{2,1,0:T(8,128)(2,1)S(1)} async-done(((bf16[8,48,512]{2,1,0:T(8,128)(2,1)}), bf16[8,48,512]{2,1,0:T(8,128)(2,1)S(1)}, u32[]{:S(2)}, u32[]{:S(2)}) %all-to-all-start) | async-done | bytes 393248 | tf_op jit(solution)/shard_map/all_to_all | solution.py:34
  34.9 0.8 left_sum.1
  35.8 2.7 %collective-permute-start.6 = (bf16[240,896]{1,0:T(8,128)(2,1)S(1)}, bf16[240,896]{1,0:T(8,128)(2,1)}, u32[]{:S(2)}, u32[]{:S(2)}) collective-permute-start(bf16[240,896]{1,0:T(8,128)(2,1)S(1)} %collective-permute-done.4.refs_7_), channel_id=1, source_target_pairs={{0,224},{32,0},{64,32},{96,64},{128,96},{160,128},{192,160},{224,1... | collective-permute-start | bytes 1290248 | tf_op jit(solution)/shard_map/ppermute | solution.py:44
  38.5 3.4 %all-to-all-start.1 = ((bf16[8,32,512]{2,1,0:T(8,128)(2,1)}), bf16[8,32,512]{2,1,0:T(8,128)(2,1)S(1)}, u32[]{:S(2)}, u32[]{:S(2)}) async-start(bf16[8,32,512]{2,1,0:T(8,128)(2,1)} %get-tuple-element.41), calls=%async_computation.1 | async-start | bytes 524288 | tf_op jit(solution)/shard_map/all_to_all | solution.py:34
  41.9 3.0 %inverse.5 = bf16[192,1664]{1,0:T(8,128)(2,1)} custom-call(s32[4]{0:T(128)} %copy-done.9, f32[512,3328]{1,0:T(8,128)} %corrected.7), custom_call_target="tpu_custom_call" | custom-call | tf_op jit(solution)/shard_map/inverse/pallas_call | solution.py:126
  44.9 2.6 %collective-permute-start.10 = (bf16[192,1664]{1,0:T(8,128)(2,1)}, bf16[192,1664]{1,0:T(8,128)(2,1)S(1)}, u32[]{:S(2)}, u32[]{:S(2)}) collective-permute-start(bf16[192,1664]{1,0:T(8,128)(2,1)} %inverse.5), channel_id=1, source_target_pairs={{0,16},{16,0},{1,17},{17,1},{2,18},{18,2},{3,19},{19,3},{4,20},{20... | collective-permute-start | bytes 1916936 | tf_op jit(solution)/shard_map/ppermute | solution.py:39
  47.5 3.9 %all-to-all-done.1 = bf16[8,32,512]{2,1,0:T(8,128)(2,1)S(1)} async-done(((bf16[8,32,512]{2,1,0:T(8,128)(2,1)}), bf16[8,32,512]{2,1,0:T(8,128)(2,1)S(1)}, u32[]{:S(2)}, u32[]{:S(2)}) %all-to-all-start.1) | async-done | bytes 262176 | tf_op jit(solution)/shard_map/all_to_all | solution.py:34
  51.6 2.7 %collective-permute-start.9 = (bf16[240,896]{1,0:T(8,128)(2,1)}, bf16[240,896]{1,0:T(8,128)(2,1)}, u32[]{:S(2)}, u32[]{:S(2)}) collective-permute-start(bf16[240,896]{1,0:T(8,128)(2,1)} %collective-permute-done.6.refs_6_), channel_id=1, source_target_pairs={{0,224},{32,0},{64,32},{96,64},{128,96},{160,128},{192,160},{224,1... | collective-permute-start | bytes 1290248 | tf_op jit(solution)/shard_map/ppermute | solution.py:44
  54.2 3.8 %inverse.6 = (bf16[512,896]{1,0:T(8,128)(2,1)}, bf16[512,896]{1,0:T(8,128)(2,1)}) custom-call(s32[4]{0:T(128)} %copy-done.9, f32[512,3328]{1,0:T(8,128)} %corrected.7), custom_call_target="tpu_custom_call" | custom-call | tf_op jit(solution)/shard_map/inverse/pallas_call | solution.py:126
  58.0 3.4 %collective-permute-start.14 = (bf16[512,896]{1,0:T(8,128)(2,1)}, bf16[512,896]{1,0:T(8,128)(2,1)S(1)}, u32[]{:S(2)}, u32[]{:S(2)}) collective-permute-start(bf16[512,896]{1,0:T(8,128)(2,1)} %get-tuple-element.52), channel_id=1, source_target_pairs={{0,8},{8,0},{1,9},{9,1},{2,10},{10,2},{3,11},{11,3},{4,12},{12,4},... | collective-permute-start | bytes 2752520 | tf_op jit(solution)/shard_map/ppermute | solution.py:39
  61.4 2.1 %collective-permute-done.10.refs_1_ = bf16[192,1664]{1,0:T(8,128)(2,1)S(1)} collective-permute-done((bf16[192,1664]{1,0:T(8,128)(2,1)}, bf16[192,1664]{1,0:T(8,128)(2,1)S(1)}, u32[]{:S(2)}, u32[]{:S(2)}) %collective-permute-start.10) | collective-permute-done | bytes 639008 | tf_op jit(solution)/shard_map/ppermute | solution.py:39
  63.5 2.7 %inverse.7 = bf16[128,1664]{1,0:T(8,128)(2,1)} custom-call(s32[4]{0:T(128)} %copy-done.9, f32[512,3328]{1,0:T(8,128)} %corrected.7), custom_call_target="tpu_custom_call" | custom-call | tf_op jit(solution)/shard_map/inverse/pallas_call | solution.py:126
  66.2 0.7 collective-permute-start.17
  66.9 3.8 %collective-permute-start.13 = (bf16[128,512]{1,0:T(8,128)(2,1)}, bf16[128,512]{1,0:T(8,128)(2,1)S(1)}, u32[]{:S(2)}, u32[]{:S(2)}) collective-permute-start(bf16[128,512]{1,0:T(8,128)(2,1)} %get-tuple-element.50.refs_2_), channel_id=1, source_target_pairs={{0,8},{8,0},{1,9},{9,1},{2,10},{10,2},{3,11},{11,3},{4,12},{12,4},... | collective-permute-start | bytes 393224 | tf_op jit(solution)/shard_map/ppermute | solution.py:39
  70.7 1.3 collective-permute-done.13.refs_3_
  72.0 1.1 collective-permute-start.15
  73.2 0.9 collective-permute-done.11.refs_4_
  74.1 0.9 collective-permute-start.16
  75.0 1.0 copy-done.7
  76.0 3.9 %rotate.1 = (bf16[1664,896]{1,0:T(8,128)(2,1)S(1)}, bf16[256,896]{1,0:T(8,128)(2,1)S(1)}, bf16[128,896]{1,0:T(8,128)(2,1)S(1)}, bf16[128,128]{1,0:T(8,128)(2,1)S(1)}) custom-call(s32[4]{0:T(128)S(1)} %copy-done.11, s32[4]{0:T(128)S(1)} %copy-done.16, bf16[6,64,3328]{2,1,0:T(8,128)(2,1)S(1)} %bitcast.10, bf16[6,64,3328]{2,1,0:T(8,128)(2,1)S(1)} %bitcast.11, ...), custom_call_target="tpu_custom_call" | custom-call | tf_op jit(solution)/shard_map/rotate/pallas_call | solution.py:273
  80.0 4.6 %back_first.1.so_far = f32[4,128,896]{2,1,0:T(8,128)S(1)} custom-call(bf16[256,896]{1,0:T(8,128)(2,1)S(1)} %get-tuple-element.48.right, bf16[256,512]{1,0:T(8,128)(2,1)S(1)} %bitcast.20, bf16[256,512]{1,0:T(8,128)(2,1)S(1)} %collective-permute-done.12.refs_1_, bf16[128,512]{1,0:T(8,128)(2,1)} %get-tuple-element.50.refs_2_, ...), custom_call_target="tpu_custom_call" | custom-call | tf_op jit(solution)/shard_map/back_first/pallas_call | solution.py:313
  84.6 0.7 collective-permute-done.16.refs_2_
  85.4 0.7 halves.1
  86.1 3.4 %collective-permute-start.20 = (bf16[512,896]{1,0:T(8,128)(2,1)S(1)}, bf16[512,896]{1,0:T(8,128)(2,1)S(1)}, u32[]{:S(2)}, u32[]{:S(2)}) collective-permute-start(bf16[512,896]{1,0:T(8,128)(2,1)S(1)} %get-tuple-element.60), channel_id=1, source_target_pairs={{0,8},{8,0},{1,9},{9,1},{2,10},{10,2},{3,11},{11,3},{4,12},{12,4},... | collective-permute-start | bytes 2752520 | tf_op jit(solution)/shard_map/ppermute | solution.py:39
  89.5 0.4 collective-permute-start.19
  89.9 2.2 %collective-permute-done.19.refs_3_ = bf16[128,512]{1,0:T(8,128)(2,1)S(1)} collective-permute-done((bf16[128,512]{1,0:T(8,128)(2,1)S(1)}, bf16[128,512]{1,0:T(8,128)(2,1)S(1)}, u32[]{:S(2)}, u32[]{:S(2)}) %collective-permute-start.19) | collective-permute-done | bytes 131104 | tf_op jit(solution)/shard_map/ppermute | solution.py:39
  92.1 4.8 %back.1.parts = bf16[8,64,896]{2,1,0:T(8,128)(2,1)} custom-call(s32[4]{0:T(128)S(1)} %copy-done.11, s32[16]{0:T(128)S(1)} %copy-done.18, f32[4,128,896]{2,1,0:T(8,128)S(1)} %back_first.1.so_far, f32[32,1664]{1,0:T(8,128)S(1)} %copy-done.8, bf16[256,896]{1,0:T(8,128)(2,1)S(1)} %get-tuple-element.48.right, ...), custom_call_target="tpu_custom_call" | custom-call | tf_op jit(solution)/shard_map/back/pallas_call | solution.py:345
  96.9 5.4 %all-to-all-start.2 = ((bf16[8,64,896]{2,1,0:T(8,128)(2,1)}), bf16[8,64,896]{2,1,0:T(8,128)(2,1)S(1)}, u32[]{:S(2)}, u32[]{:S(2)}) async-start(bf16[8,64,896]{2,1,0:T(8,128)(2,1)} %back.1.parts), calls=%async_computation.2 | async-start | bytes 1835008 | tf_op jit(solution)/shard_map/all_to_all | solution.py:34
  102.3 1.8 %score.1 = f32[1,128]{1,0:T(1,128)S(1)} custom-call(bf16[8,64,896]{2,1,0:T(8,128)(2,1)} %back.1.parts, bf16[128,896]{1,0:T(8,128)(2,1)S(1)} %get-tuple-element.61.tokens, bf16[128,128]{1,0:T(8,128)(2,1)S(1)} %copy-done.14), custom_call_target="tpu_custom_call" | custom-call | tf_op jit(solution)/shard_map/score/pallas_call | solution.py:372
  104.1 0.9 collective-permute-start.21
  105.0 0.8 collective-permute-done.21
  105.9 2.7 %collective-permute-done.22 = f32[1,128]{1,0:T(1,128)S(1)} collective-permute-done((f32[1,128]{1,0:T(1,128)S(1)}, f32[1,128]{1,0:T(1,128)S(1)}, u32[]{:S(2)}, u32[]{:S(2)}) %collective-permute-start.22) | collective-permute-done | bytes 544 | tf_op jit(solution)/shard_map/ppermute | solution.py:39
  108.5 1.1 collective-permute-start.23
  109.7 1.5 %collective-permute-done.23 = f32[1,128]{1,0:T(1,128)S(1)} collective-permute-done((f32[1,128]{1,0:T(1,128)S(1)}, f32[1,128]{1,0:T(1,128)S(1)}, u32[]{:S(2)}, u32[]{:S(2)}) %collective-permute-start.23) | collective-permute-done | bytes 544 | tf_op jit(solution)/shard_map/ppermute | solution.py:39
  111.2 2.7 %collective-permute-start.24 = (f32[1,128]{1,0:T(1,128)S(1)}, f32[1,128]{1,0:T(1,128)S(1)}, u32[]{:S(2)}, u32[]{:S(2)}) collective-permute-start(f32[1,128]{1,0:T(1,128)S(1)} %add.21), channel_id=1, source_target_pairs={{0,4},{2,6},{4,0},{6,2},{1,5},{3,7},{5,1},{7,3},{8,12},{10,14},{12... | collective-permute-start | bytes 1544 | tf_op jit(solution)/shard_map/ppermute | solution.py:39
  113.9 1.4 collective-permute-done.24
  115.3 1.2 collective-permute-start.25
  116.5 3.0 %collective-permute-done.25 = f32[1,128]{1,0:T(1,128)S(1)} collective-permute-done((f32[1,128]{1,0:T(1,128)S(1)}, f32[1,128]{1,0:T(1,128)S(1)}, u32[]{:S(2)}, u32[]{:S(2)}) %collective-permute-start.25) | collective-permute-done | bytes 544 | tf_op jit(solution)/shard_map/ppermute | solution.py:39
  119.5 9.2 %all-to-all-done.2.parts = bf16[8,64,896]{2,1,0:T(8,128)(2,1)S(1)} async-done(((bf16[8,64,896]{2,1,0:T(8,128)(2,1)}), bf16[8,64,896]{2,1,0:T(8,128)(2,1)S(1)}, u32[]{:S(2)}, u32[]{:S(2)}) %all-to-all-start.2) | async-done | bytes 917536 | tf_op jit(solution)/shard_map/all_to_all | solution.py:34
  128.7 0.6 broadcast_in_dim.2
  129.3 3.3 %all-to-all-start.3 = ((f32[8,8,128]{2,1,0:T(8,128)}), f32[8,8,128]{2,1,0:T(8,128)S(1)}, u32[]{:S(2)}, u32[]{:S(2)}) async-start(f32[8,8,128]{2,1,0:T(8,128)} %broadcast_in_dim.2), calls=%async_computation.3 | async-start | bytes 65536 | tf_op jit(solution)/shard_map/all_to_all | solution.py:34
  132.7 1.8 %copy-done.3 = bf16[1664,896]{1,0:T(8,128)(2,1)S(1)} copy-done((bf16[1664,896]{1,0:T(8,128)(2,1)S(1)}, bf16[1664,896]{1,0:T(8,128)(2,1)}, u32[]{:S(2)}) %copy-start.3) | copy-done | bytes 2981912
  134.5 1.7 %tile.1 = (bf16[16,1664]{1,0:T(8,128)(2,1)S(1)}, bf16[16,1664]{1,0:T(8,128)(2,1)S(1)}, bf16[16,1664]{1,0:T(8,128)(2,1)S(1)}, bf16[16,1664]{1,0:T(8,128)(2,1)S(1)}) custom-call(s32[4]{0:T(128)S(1)} %copy-done.11, bf16[8,64,896]{2,1,0:T(8,128)(2,1)S(1)} %all-to-all-done.2.parts, bf16[1664,896]{1,0:T(8,128)(2,1)S(1)} %copy-done.3), custom_call_target="tpu_custom_call" | custom-call | tf_op jit(solution)/shard_map/tile/pallas_call | solution.py:404
  136.2 0.6 collective-permute-start.26
  136.8 1.2 collective-permute-start.27
  138.0 2.0 %collective-permute-start.28 = (bf16[16,1664]{1,0:T(8,128)(2,1)S(1)}, bf16[16,1664]{1,0:T(8,128)(2,1)S(1)}, u32[]{:S(2)}, u32[]{:S(2)}) collective-permute-start(bf16[16,1664]{1,0:T(8,128)(2,1)S(1)} %get-tuple-element.68), channel_id=1, source_target_pairs={{0,24},{8,16},{16,8},{24,0},{1,25},{9,17},{17,9},{25,1},{2,26},{10... | collective-permute-start | bytes 159752 | tf_op jit(solution)/shard_map/ppermute | solution.py:39
  140.0 1.7 %collective-permute-done.27.t2 = bf16[16,1664]{1,0:T(8,128)(2,1)S(1)} collective-permute-done((bf16[16,1664]{1,0:T(8,128)(2,1)S(1)}, bf16[16,1664]{1,0:T(8,128)(2,1)S(1)}, u32[]{:S(2)}, u32[]{:S(2)}) %collective-permute-start.27) | collective-permute-done | bytes 53280 | tf_op jit(solution)/shard_map/ppermute | solution.py:39
  141.7 1.6 %collective-permute-done.28.t3 = bf16[16,1664]{1,0:T(8,128)(2,1)S(1)} collective-permute-done((bf16[16,1664]{1,0:T(8,128)(2,1)S(1)}, bf16[16,1664]{1,0:T(8,128)(2,1)S(1)}, u32[]{:S(2)}, u32[]{:S(2)}) %collective-permute-start.28) | collective-permute-done | bytes 53280 | tf_op jit(solution)/shard_map/ppermute | solution.py:39
  143.3 1.2 final.1
  (63 shorter events, 0.8 us)
Async XLA Ops:
  1.8 9.5 %copy-start.9 = (s32[4]{0:T(128)}, s32[4]{0:T(128)S(1)}, u32[]{:S(2)}) copy-start(s32[4]{0:T(128)S(1)} %pad_add_fusion.where) | copy-start | bytes 52
  1.8 0.8 copy-start.12
  2.6 0.7 copy-start.15
  3.2 0.7 copy-start.17
  4.7 11.9 %collective-permute-start = (bf16[60,896]{1,0:T(8,128)(2,1)S(1)}, bf16[60,896]{1,0:T(8,128)(2,1)S(1)}, u32[]{:S(2)}, u32[]{:S(2)}) collective-permute-start(bf16[60,896]{1,0:T(8,128)(2,1)S(1)} %get-tuple-element.38), channel_id=1, source_target_pairs={{0,8},{8,0},{1,9},{9,1},{2,10},{10,2},{3,11},{11,3},{4,12},{12,4},... | collective-permute-start | bytes 322568 | tf_op jit(solution)/shard_map/ppermute | solution.py:39
  8.0 8.6 %collective-permute-start.1 = (bf16[60,896]{1,0:T(8,128)(2,1)S(1)}, bf16[60,896]{1,0:T(8,128)(2,1)S(1)}, u32[]{:S(2)}, u32[]{:S(2)}) collective-permute-start(bf16[60,896]{1,0:T(8,128)(2,1)S(1)} %get-tuple-element.39), channel_id=1, source_target_pairs={{0,16},{16,0},{1,17},{17,1},{2,18},{18,2},{3,19},{19,3},{4,20},{20... | collective-permute-start | bytes 322568 | tf_op jit(solution)/shard_map/ppermute | solution.py:39
  9.0 5.2 %copy-start.1 = (bf16[6,2048,64]{1,2,0:T(8,128)(2,1)S(1)}, bf16[6,2048,64]{1,2,0:T(8,128)(2,1)}, u32[]{:S(2)}) copy-start(bf16[6,2048,64]{1,2,0:T(8,128)(2,1)} %param.17) | copy-start | bytes 4718596
  9.0 5.2 %copy-start.4 = (bf16[2048,512]{1,0:T(8,128)(2,1)S(1)}, bf16[2048,512]{1,0:T(8,128)(2,1)}, u32[]{:S(2)}) copy-start(bf16[2048,512]{1,0:T(8,128)(2,1)} %basis.2) | copy-start | bytes 6291460
  9.0 5.2 %copy-start.16 = (s32[4]{0:T(128)S(1)}, s32[4]{0:T(128)}, u32[]{:S(2)}) copy-start(s32[4]{0:T(128)} %ids.3) | copy-start | bytes 52
  9.0 7.8 %collective-permute-start.2 = (bf16[60,896]{1,0:T(8,128)(2,1)S(1)}, bf16[60,896]{1,0:T(8,128)(2,1)S(1)}, u32[]{:S(2)}, u32[]{:S(2)}) collective-permute-start(bf16[60,896]{1,0:T(8,128)(2,1)S(1)} %get-tuple-element.40), channel_id=1, source_target_pairs={{0,24},{8,16},{16,8},{24,0},{1,25},{9,17},{17,9},{25,1},{2,26},{10... | collective-permute-start | bytes 322568 | tf_op jit(solution)/shard_map/ppermute | solution.py:39
  14.2 2.6 %copy-start.10 = (s32[4]{0:T(128)S(1)}, s32[4]{0:T(128)}, u32[]{:S(2)}) copy-start(s32[4]{0:T(128)} %copy-done.9) | copy-start | bytes 52
  18.0 17.7 %collective-permute-start.3 = (bf16[240,896]{1,0:T(8,128)(2,1)S(1)}, bf16[240,896]{1,0:T(8,128)(2,1)S(1)}, u32[]{:S(2)}, u32[]{:S(2)}) collective-permute-start(bf16[240,896]{1,0:T(8,128)(2,1)S(1)} %arrange.1.refs_0_), channel_id=1, source_target_pairs={{0,32},{32,64},{64,96},{96,128},{128,160},{160,192},{192,224},{224... | collective-permute-start | bytes 1290248 | tf_op jit(solution)/shard_map/ppermute | solution.py:44
  18.5 17.2 %collective-permute-start.4 = (bf16[240,896]{1,0:T(8,128)(2,1)S(1)}, bf16[240,896]{1,0:T(8,128)(2,1)S(1)}, u32[]{:S(2)}, u32[]{:S(2)}) collective-permute-start(bf16[240,896]{1,0:T(8,128)(2,1)S(1)} %arrange.1.refs_0_), channel_id=1, source_target_pairs={{0,224},{32,0},{64,32},{96,64},{128,96},{160,128},{192,160},{224,1... | collective-permute-start | bytes 1290248 | tf_op jit(solution)/shard_map/ppermute | solution.py:44
  22.6 12.4 %all-to-all-start = ((bf16[8,48,512]{2,1,0:T(8,128)(2,1)}), bf16[8,48,512]{2,1,0:T(8,128)(2,1)S(1)}, u32[]{:S(2)}, u32[]{:S(2)}) async-start(bf16[8,48,512]{2,1,0:T(8,128)(2,1)} %left.1), calls=%async_computation | async-start | bytes 786432 | tf_op jit(solution)/shard_map/all_to_all | solution.py:34
  27.2 24.3 %collective-permute-start.7 = (bf16[192,1664]{1,0:T(8,128)(2,1)}, bf16[192,1664]{1,0:T(8,128)(2,1)S(1)}, u32[]{:S(2)}, u32[]{:S(2)}) collective-permute-start(bf16[192,1664]{1,0:T(8,128)(2,1)} %inverse.4), channel_id=1, source_target_pairs={{0,16},{16,0},{1,17},{17,1},{2,18},{18,2},{3,19},{19,3},{4,20},{20... | collective-permute-start | bytes 1916936 | tf_op jit(solution)/shard_map/ppermute | solution.py:39
  35.7 9.2 %copy-start.6 = (bf16[240,896]{1,0:T(8,128)(2,1)}, bf16[240,896]{1,0:T(8,128)(2,1)S(1)}, u32[]{:S(2)}) copy-start(bf16[240,896]{1,0:T(8,128)(2,1)S(1)} %collective-permute-done.4.refs_7_) | copy-start | bytes 1290244
  35.7 15.7 %collective-permute-start.5 = (bf16[240,896]{1,0:T(8,128)(2,1)S(1)}, bf16[240,896]{1,0:T(8,128)(2,1)}, u32[]{:S(2)}, u32[]{:S(2)}) collective-permute-start(bf16[240,896]{1,0:T(8,128)(2,1)S(1)} %collective-permute-done.3.refs_1_), channel_id=1, source_target_pairs={{0,32},{32,64},{64,96},{96,128},{128,160},{160,192},{192,224},{224... | collective-permute-start | bytes 1290248 | tf_op jit(solution)/shard_map/ppermute | solution.py:44
  35.8 15.6 %collective-permute-start.6 = (bf16[240,896]{1,0:T(8,128)(2,1)S(1)}, bf16[240,896]{1,0:T(8,128)(2,1)}, u32[]{:S(2)}, u32[]{:S(2)}) collective-permute-start(bf16[240,896]{1,0:T(8,128)(2,1)S(1)} %collective-permute-done.4.refs_7_), channel_id=1, source_target_pairs={{0,224},{32,0},{64,32},{96,64},{128,96},{160,128},{192,160},{224,1... | collective-permute-start | bytes 1290248 | tf_op jit(solution)/shard_map/ppermute | solution.py:44
  38.5 13.0 %all-to-all-start.1 = ((bf16[8,32,512]{2,1,0:T(8,128)(2,1)}), bf16[8,32,512]{2,1,0:T(8,128)(2,1)S(1)}, u32[]{:S(2)}, u32[]{:S(2)}) async-start(bf16[8,32,512]{2,1,0:T(8,128)(2,1)} %get-tuple-element.41), calls=%async_computation.1 | async-start | bytes 524288 | tf_op jit(solution)/shard_map/all_to_all | solution.py:34
  44.9 18.6 %collective-permute-start.10 = (bf16[192,1664]{1,0:T(8,128)(2,1)}, bf16[192,1664]{1,0:T(8,128)(2,1)S(1)}, u32[]{:S(2)}, u32[]{:S(2)}) collective-permute-start(bf16[192,1664]{1,0:T(8,128)(2,1)} %inverse.5), channel_id=1, source_target_pairs={{0,16},{16,0},{1,17},{17,1},{2,18},{18,2},{3,19},{19,3},{4,20},{20... | collective-permute-start | bytes 1916936 | tf_op jit(solution)/shard_map/ppermute | solution.py:39
  51.5 12.1 %collective-permute-start.8 = (bf16[240,896]{1,0:T(8,128)(2,1)}, bf16[240,896]{1,0:T(8,128)(2,1)}, u32[]{:S(2)}, u32[]{:S(2)}) collective-permute-start(bf16[240,896]{1,0:T(8,128)(2,1)} %collective-permute-done.5.refs_2_), channel_id=1, source_target_pairs={{0,32},{32,64},{64,96},{96,128},{128,160},{160,192},{192,224},{224... | collective-permute-start | bytes 1290248 | tf_op jit(solution)/shard_map/ppermute | solution.py:44
  51.6 12.0 %collective-permute-start.9 = (bf16[240,896]{1,0:T(8,128)(2,1)}, bf16[240,896]{1,0:T(8,128)(2,1)}, u32[]{:S(2)}, u32[]{:S(2)}) collective-permute-start(bf16[240,896]{1,0:T(8,128)(2,1)} %collective-permute-done.6.refs_6_), channel_id=1, source_target_pairs={{0,224},{32,0},{64,32},{96,64},{128,96},{160,128},{192,160},{224,1... | collective-permute-start | bytes 1290248 | tf_op jit(solution)/shard_map/ppermute | solution.py:44
  58.0 17.0 %copy-start = (bf16[6,3328,64]{1,2,0:T(8,128)(2,1)S(1)}, bf16[6,3328,64]{1,2,0:T(8,128)(2,1)}, u32[]{:S(2)}) copy-start(bf16[6,3328,64]{1,2,0:T(8,128)(2,1)} %param.18) | copy-start | bytes 7667716
  58.0 17.0 %copy-start.11 = (s32[4]{0:T(128)S(1)}, s32[4]{0:T(128)}, u32[]{:S(2)}) copy-start(s32[4]{0:T(128)} %copy-done.9) | copy-start | bytes 52
  58.0 22.0 %collective-permute-start.14 = (bf16[512,896]{1,0:T(8,128)(2,1)}, bf16[512,896]{1,0:T(8,128)(2,1)S(1)}, u32[]{:S(2)}, u32[]{:S(2)}) collective-permute-start(bf16[512,896]{1,0:T(8,128)(2,1)} %get-tuple-element.52), channel_id=1, source_target_pairs={{0,8},{8,0},{1,9},{9,1},{2,10},{10,2},{3,11},{11,3},{4,12},{12,4},... | collective-permute-start | bytes 2752520 | tf_op jit(solution)/shard_map/ppermute | solution.py:39
  63.5 10.6 %collective-permute-start.11 = (bf16[240,896]{1,0:T(8,128)(2,1)}, bf16[240,896]{1,0:T(8,128)(2,1)}, u32[]{:S(2)}, u32[]{:S(2)}) collective-permute-start(bf16[240,896]{1,0:T(8,128)(2,1)} %collective-permute-done.8.refs_3_), channel_id=1, source_target_pairs={{0,32},{32,64},{64,96},{96,128},{128,160},{160,192},{192,224},{224... | collective-permute-start | bytes 1290248 | tf_op jit(solution)/shard_map/ppermute | solution.py:44
  66.2 19.1 %collective-permute-start.17 = (bf16[128,1664]{1,0:T(8,128)(2,1)}, bf16[128,1664]{1,0:T(8,128)(2,1)S(1)}, u32[]{:S(2)}, u32[]{:S(2)}) collective-permute-start(bf16[128,1664]{1,0:T(8,128)(2,1)} %inverse.7), channel_id=1, source_target_pairs={{0,16},{16,0},{1,17},{17,1},{2,18},{18,2},{3,19},{19,3},{4,20},{20... | collective-permute-start | bytes 1277960 | tf_op jit(solution)/shard_map/ppermute | solution.py:39
  66.9 5.1 %collective-permute-start.13 = (bf16[128,512]{1,0:T(8,128)(2,1)}, bf16[128,512]{1,0:T(8,128)(2,1)S(1)}, u32[]{:S(2)}, u32[]{:S(2)}) collective-permute-start(bf16[128,512]{1,0:T(8,128)(2,1)} %get-tuple-element.50.refs_2_), channel_id=1, source_target_pairs={{0,8},{8,0},{1,9},{9,1},{2,10},{10,2},{3,11},{11,3},{4,12},{12,4},... | collective-permute-start | bytes 393224 | tf_op jit(solution)/shard_map/ppermute | solution.py:39
  70.7 9.3 %collective-permute-start.12 = (bf16[256,512]{1,0:T(8,128)(2,1)S(1)}, bf16[256,512]{1,0:T(8,128)(2,1)S(1)}, u32[]{:S(2)}, u32[]{:S(2)}) collective-permute-start(bf16[256,512]{1,0:T(8,128)(2,1)S(1)} %bitcast.18), channel_id=1, source_target_pairs={{0,8},{8,0},{1,9},{9,1},{2,10},{10,2},{3,11},{11,3},{4,12},{12,4},... | collective-permute-start | bytes 786440 | tf_op jit(solution)/shard_map/ppermute | solution.py:39
  72.0 13.3 %collective-permute-start.15 = (bf16[256,512]{1,0:T(8,128)(2,1)S(1)}, bf16[256,512]{1,0:T(8,128)(2,1)S(1)}, u32[]{:S(2)}, u32[]{:S(2)}) collective-permute-start(bf16[256,512]{1,0:T(8,128)(2,1)S(1)} %bitcast.19), channel_id=1, source_target_pairs={{0,16},{16,0},{1,17},{17,1},{2,18},{18,2},{3,19},{19,3},{4,20},{20... | collective-permute-start | bytes 786440 | tf_op jit(solution)/shard_map/ppermute | solution.py:39
  74.1 11.2 %collective-permute-start.16 = (bf16[128,512]{1,0:T(8,128)(2,1)}, bf16[128,512]{1,0:T(8,128)(2,1)S(1)}, u32[]{:S(2)}, u32[]{:S(2)}) collective-permute-start(bf16[128,512]{1,0:T(8,128)(2,1)} %get-tuple-element.50.refs_2_), channel_id=1, source_target_pairs={{0,16},{16,0},{1,17},{17,1},{2,18},{18,2},{3,19},{19,3},{4,20},{20... | collective-permute-start | bytes 393224 | tf_op jit(solution)/shard_map/ppermute | solution.py:39
  75.0 1.0 copy-start.7
  76.0 4.0 %copy-start.5 = (bf16[512,896]{1,0:T(8,128)(2,1)S(1)}, bf16[512,896]{1,0:T(8,128)(2,1)}, u32[]{:S(2)}) copy-start(bf16[512,896]{1,0:T(8,128)(2,1)} %get-tuple-element.51.refs_4_) | copy-start | bytes 2752516
  80.0 6.1 %copy-start.2 = (bf16[1664,896]{1,0:T(8,128)(2,1)}, bf16[1664,896]{1,0:T(8,128)(2,1)S(1)}, u32[]{:S(2)}) copy-start(bf16[1664,896]{1,0:T(8,128)(2,1)S(1)} %get-tuple-element.64.basis) | copy-start | bytes 8945668
  80.0 6.1 %copy-start.13 = (bf16[128,128]{1,0:T(8,128)(2,1)}, bf16[128,128]{1,0:T(8,128)(2,1)S(1)}, u32[]{:S(2)}) copy-start(bf16[128,128]{1,0:T(8,128)(2,1)S(1)} %get-tuple-element.62.delta) | copy-start | bytes 98308
  80.0 12.1 %copy-start.8 = (f32[32,1664]{1,0:T(8,128)S(1)}, f32[32,1664]{1,0:T(8,128)}, u32[]{:S(2)}) copy-start(f32[32,1664]{1,0:T(8,128)} %factors.1) | copy-start | bytes 638980
  80.0 12.1 %copy-start.18 = (s32[16]{0:T(128)S(1)}, s32[16]{0:T(128)}, u32[]{:S(2)}) copy-start(s32[16]{0:T(128)} %block_ids.1) | copy-start | bytes 196
  86.1 6.0 %collective-permute-start.20 = (bf16[512,896]{1,0:T(8,128)(2,1)S(1)}, bf16[512,896]{1,0:T(8,128)(2,1)S(1)}, u32[]{:S(2)}, u32[]{:S(2)}) collective-permute-start(bf16[512,896]{1,0:T(8,128)(2,1)S(1)} %get-tuple-element.60), channel_id=1, source_target_pairs={{0,8},{8,0},{1,9},{9,1},{2,10},{10,2},{3,11},{11,3},{4,12},{12,4},... | collective-permute-start | bytes 2752520 | tf_op jit(solution)/shard_map/ppermute | solution.py:39
  89.4 2.7 %collective-permute-start.18 = (bf16[256,512]{1,0:T(8,128)(2,1)S(1)}, bf16[256,512]{1,0:T(8,128)(2,1)S(1)}, u32[]{:S(2)}, u32[]{:S(2)}) collective-permute-start(bf16[256,512]{1,0:T(8,128)(2,1)S(1)} %collective-permute-done.15.refs_0_), channel_id=1, source_target_pairs={{0,8},{8,0},{1,9},{9,1},{2,10},{10,2},{3,11},{11,3},{4,12},{12,4},... | collective-permute-start | bytes 786440 | tf_op jit(solution)/shard_map/ppermute | solution.py:39
  89.5 2.6 %collective-permute-start.19 = (bf16[128,512]{1,0:T(8,128)(2,1)S(1)}, bf16[128,512]{1,0:T(8,128)(2,1)S(1)}, u32[]{:S(2)}, u32[]{:S(2)}) collective-permute-start(bf16[128,512]{1,0:T(8,128)(2,1)S(1)} %collective-permute-done.16.refs_2_), channel_id=1, source_target_pairs={{0,8},{8,0},{1,9},{9,1},{2,10},{10,2},{3,11},{11,3},{4,12},{12,4},... | collective-permute-start | bytes 393224 | tf_op jit(solution)/shard_map/ppermute | solution.py:39
  92.1 10.2 %copy-start.14 = (bf16[128,128]{1,0:T(8,128)(2,1)S(1)}, bf16[128,128]{1,0:T(8,128)(2,1)}, u32[]{:S(2)}) copy-start(bf16[128,128]{1,0:T(8,128)(2,1)} %copy-done.13) | copy-start | bytes 98308
  96.9 31.8 %all-to-all-start.2 = ((bf16[8,64,896]{2,1,0:T(8,128)(2,1)}), bf16[8,64,896]{2,1,0:T(8,128)(2,1)S(1)}, u32[]{:S(2)}, u32[]{:S(2)}) async-start(bf16[8,64,896]{2,1,0:T(8,128)(2,1)} %back.1.parts), calls=%async_computation.2 | async-start | bytes 1835008 | tf_op jit(solution)/shard_map/all_to_all | solution.py:34
  104.1 1.7 %collective-permute-start.21 = (f32[1,128]{1,0:T(1,128)S(1)}, f32[1,128]{1,0:T(1,128)S(1)}, u32[]{:S(2)}, u32[]{:S(2)}) collective-permute-start(f32[1,128]{1,0:T(1,128)S(1)} %score.1), channel_id=1, source_target_pairs={{0,8},{8,0},{1,9},{9,1},{2,10},{10,2},{3,11},{11,3},{4,12},{12,4},... | collective-permute-start | bytes 1544 | tf_op jit(solution)/shard_map/ppermute | solution.py:39
  105.8 2.7 %collective-permute-start.22 = (f32[1,128]{1,0:T(1,128)S(1)}, f32[1,128]{1,0:T(1,128)S(1)}, u32[]{:S(2)}, u32[]{:S(2)}) collective-permute-start(f32[1,128]{1,0:T(1,128)S(1)} %add.19), channel_id=1, source_target_pairs={{0,1},{1,0},{2,3},{3,2},{4,5},{5,4},{6,7},{7,6},{8,9},{9,8},{10,11... | collective-permute-start | bytes 1544 | tf_op jit(solution)/shard_map/ppermute | solution.py:39
  108.5 2.7 %collective-permute-start.23 = (f32[1,128]{1,0:T(1,128)S(1)}, f32[1,128]{1,0:T(1,128)S(1)}, u32[]{:S(2)}, u32[]{:S(2)}) collective-permute-start(f32[1,128]{1,0:T(1,128)S(1)} %add.20), channel_id=1, source_target_pairs={{0,2},{2,0},{4,6},{6,4},{1,3},{3,1},{5,7},{7,5},{8,10},{10,8},{12,... | collective-permute-start | bytes 1544 | tf_op jit(solution)/shard_map/ppermute | solution.py:39
  111.2 4.1 %collective-permute-start.24 = (f32[1,128]{1,0:T(1,128)S(1)}, f32[1,128]{1,0:T(1,128)S(1)}, u32[]{:S(2)}, u32[]{:S(2)}) collective-permute-start(f32[1,128]{1,0:T(1,128)S(1)} %add.21), channel_id=1, source_target_pairs={{0,4},{2,6},{4,0},{6,2},{1,5},{3,7},{5,1},{7,3},{8,12},{10,14},{12... | collective-permute-start | bytes 1544 | tf_op jit(solution)/shard_map/ppermute | solution.py:39
  115.3 4.2 %collective-permute-start.25 = (f32[1,128]{1,0:T(1,128)S(1)}, f32[1,128]{1,0:T(1,128)S(1)}, u32[]{:S(2)}, u32[]{:S(2)}) collective-permute-start(f32[1,128]{1,0:T(1,128)S(1)} %add.22), channel_id=1, source_target_pairs={{0,16},{16,0},{1,17},{17,1},{2,18},{18,2},{3,19},{19,3},{4,20},{20... | collective-permute-start | bytes 1544 | tf_op jit(solution)/shard_map/ppermute | solution.py:39
  129.3 13.9 %all-to-all-start.3 = ((f32[8,8,128]{2,1,0:T(8,128)}), f32[8,8,128]{2,1,0:T(8,128)S(1)}, u32[]{:S(2)}, u32[]{:S(2)}) async-start(f32[8,8,128]{2,1,0:T(8,128)} %broadcast_in_dim.2), calls=%async_computation.3 | async-start | bytes 65536 | tf_op jit(solution)/shard_map/all_to_all | solution.py:34
  132.7 1.8 %copy-start.3 = (bf16[1664,896]{1,0:T(8,128)(2,1)S(1)}, bf16[1664,896]{1,0:T(8,128)(2,1)}, u32[]{:S(2)}) copy-start(bf16[1664,896]{1,0:T(8,128)(2,1)} %copy-done.2) | copy-start | bytes 8945668
  136.2 3.8 %collective-permute-start.26 = (bf16[16,1664]{1,0:T(8,128)(2,1)S(1)}, bf16[16,1664]{1,0:T(8,128)(2,1)S(1)}, u32[]{:S(2)}, u32[]{:S(2)}) collective-permute-start(bf16[16,1664]{1,0:T(8,128)(2,1)S(1)} %get-tuple-element.66), channel_id=1, source_target_pairs={{0,8},{8,0},{1,9},{9,1},{2,10},{10,2},{3,11},{11,3},{4,12},{12,4},... | collective-permute-start | bytes 159752 | tf_op jit(solution)/shard_map/ppermute | solution.py:39
  136.8 4.9 %collective-permute-start.27 = (bf16[16,1664]{1,0:T(8,128)(2,1)S(1)}, bf16[16,1664]{1,0:T(8,128)(2,1)S(1)}, u32[]{:S(2)}, u32[]{:S(2)}) collective-permute-start(bf16[16,1664]{1,0:T(8,128)(2,1)S(1)} %get-tuple-element.67), channel_id=1, source_target_pairs={{0,16},{16,0},{1,17},{17,1},{2,18},{18,2},{3,19},{19,3},{4,20},{20... | collective-permute-start | bytes 159752 | tf_op jit(solution)/shard_map/ppermute | solution.py:39
  138.0 5.3 %collective-permute-start.28 = (bf16[16,1664]{1,0:T(8,128)(2,1)S(1)}, bf16[16,1664]{1,0:T(8,128)(2,1)S(1)}, u32[]{:S(2)}, u32[]{:S(2)}) collective-permute-start(bf16[16,1664]{1,0:T(8,128)(2,1)S(1)} %get-tuple-element.68), channel_id=1, source_target_pairs={{0,24},{8,16},{16,8},{24,0},{1,25},{9,17},{17,9},{25,1},{2,26},{10... | collective-permute-start | bytes 159752 | tf_op jit(solution)/shard_map/ppermute | solution.py:39

commit v10 on v9

--- a/solution.py
+++ b/solution.py
@@ -411,6 +411,21 @@
     )(where, parts, basis)
 
 
+def stage_body(score, basis, out):
+    out[...] = basis[...]
+
+
+def stage(score, basis):
+    return pl.pallas_call(
+        stage_body,
+        out_shape=jax.ShapeDtypeStruct(basis.shape, basis.dtype),
+        in_specs=[VMEM_SPEC, VMEM_SPEC],
+        out_specs=VMEM_SPEC,
+        compiler_params=params(8),
+        name="stage",
+    )(score, basis)
+
+
 def final_body(where, t0, t1, t2, t3, score, tiles, scores):
     queries, per, columns = tiles.shape
     block = columns // 2
@@ -509,9 +524,10 @@
     score = score_part(parts, tokens, delta, queries, train)
     for axis, mask in (("c", 1), ("xl", 1), ("y", 1), ("y", 2), ("xh", 1)):
         score = score + swap(score, axis, mask)
-    parts, score = after((exchange(parts, "z"), score))
+    score = jnp.broadcast_to(score, (n_z, 8, LANES))
+    parts, score, basis = after((exchange(parts, "z"), score, stage(score, basis)))
     parts = tile_part(where, parts, basis, queries)
-    score = exchange(jnp.broadcast_to(score, (n_z, 8, LANES)), "z")
+    score = exchange(score, "z")
     parts = (
         parts[0],
         swap(parts[1], "c"),

time: 145 us -> 145 us (level)
  waiting for transfers between devices: 38.7 us -> 35.4 us
  Pallas kernels: 36.1 us -> 37.8 us
    all_to_all x4, waiting for transfers between devices: 18.5 us -> 14.8 us  [exchange(): return lax.all_to_all(value, axis, split_axis=0, concat_axis=0, tiled=True)]
  transfers between devices with their start and end apart: 33 -> 33, of which waited for: 16 -> 16; matrix products, arithmetic and copies ran while one was open for 0% -> 0% of each run, Pallas kernels for 19% -> 20%
where the time goes in v10:
time: 145 us; the launch traced here: 144 us
  starting transfers between devices  63.3 us (44%)
  Pallas kernels  37.8 us (26%)
  waiting for transfers between devices  35.4 us (24%)
  local copies, waits for them, and re-layouts  6.7 us (5%)
    ppermute x22, starting transfers between devices, swap(): return lax.ppermute(value, axis, [(i, i ^ mask) for i in range(size)])  36.6 us
    ppermute x22, waiting for transfers between devices, swap(): return lax.ppermute(value, axis, [(i, i ^ mask) for i in range(size)])  19.7 us
    all_to_all x4, starting transfers between devices, exchange(): return lax.all_to_all(value, axis, split_axis=0, concat_axis=0, tiled=True)  16.7 us
    all_to_all x4, waiting for transfers between devices, exchange(): return lax.all_to_all(value, axis, split_axis=0, concat_axis=0, tiled=True)  14.8 us
    pallas_call x4, Pallas kernels, inverse_block(): pl.pallas_call(inverse_body, out_shape=tuple((jax.ShapeDtypeStruct((rows,...  12.5 us
    ppermute x7, starting transfers between devices, shift(): lax.ppermute(value, 'z', [(i, (i + step) % size) for i in range(size)])  10 us
    unnamed x39, local copies, waits for them, and re-layouts  6.08 us
    pallas_call x1, Pallas kernels, back(): pl.pallas_call(back_body, out_shape=jax.ShapeDtypeStruct((n_z, queries *...  4.85 us
  transfers between devices with their start and end apart: 33, of which 16 were waited for; matrix products, arithmetic and copies ran while one was open for 0% of the time, Pallas kernels for 20%

profile of v10, /device:TPU:1, one launch (start us, length us, event | category | flops | bytes accessed | tf_op | source)
XLA Modules:
  0.0 144.2 jit_solution(4993648630629133063)
XLA Ops:
  0.6 1.0 copy.13.basis
  1.8 0.8 copy-done.12
  2.6 0.7 copy-done.15
  3.2 0.7 copy-done.17
  3.9 0.7 pack.1
  4.7 3.3 %collective-permute-start = (bf16[60,896]{1,0:T(8,128)(2,1)S(1)}, bf16[60,896]{1,0:T(8,128)(2,1)S(1)}, u32[]{:S(2)}, u32[]{:S(2)}) collective-permute-start(bf16[60,896]{1,0:T(8,128)(2,1)S(1)} %get-tuple-element.39), channel_id=1, source_target_pairs={{0,8},{8,0},{1,9},{9,1},{2,10},{10,2},{3,11},{11,3},{4,12},{12,4},... | collective-permute-start | bytes 322568 | tf_op jit(solution)/shard_map/ppermute | solution.py:39
  8.0 1.0 collective-permute-start.1
  9.0 2.2 %collective-permute-start.2 = (bf16[60,896]{1,0:T(8,128)(2,1)S(1)}, bf16[60,896]{1,0:T(8,128)(2,1)S(1)}, u32[]{:S(2)}, u32[]{:S(2)}) collective-permute-start(bf16[60,896]{1,0:T(8,128)(2,1)S(1)} %get-tuple-element.41), channel_id=1, source_target_pairs={{0,24},{8,16},{16,8},{24,0},{1,25},{9,17},{17,9},{25,1},{2,26},{10... | collective-permute-start | bytes 322568 | tf_op jit(solution)/shard_map/ppermute | solution.py:39
  11.2 3.0 %inverse.4 = bf16[192,1664]{1,0:T(8,128)(2,1)} custom-call(s32[4]{0:T(128)} %copy-done.9, f32[512,3328]{1,0:T(8,128)} %corrected.7), custom_call_target="tpu_custom_call" | custom-call | tf_op jit(solution)/shard_map/inverse/pallas_call | solution.py:126
  14.2 2.3 %left.1 = bf16[8,48,512]{2,1,0:T(8,128)(2,1)} custom-call(s32[4]{0:T(128)S(1)} %copy-done.16, bf16[6,64,2048]{2,1,0:T(8,128)(2,1)S(1)} %bitcast.15, bf16[6,64,2048]{2,1,0:T(8,128)(2,1)S(1)} %bitcast.16, bf16[6,64,2048]{2,1,0:T(8,128)(2,1)S(1)} %bitcast.17, bf16[6,64,2048]{2,1,0:T(8,128)(2,1)S(1)} %bitcast.18, bf16[2048,512]{1,0:T(8,128)(2,1)S(1)} %copy-done.4), custom_call_target="tpu_custom_call" | custom-call | tf_op jit(solution)/shard_map/left/pallas_call | solution.py:71
  16.8 1.2 arrange.1.refs_0_
  18.0 0.5 collective-permute-start.3
  18.5 4.0 %collective-permute-start.4 = (bf16[240,896]{1,0:T(8,128)(2,1)S(1)}, bf16[240,896]{1,0:T(8,128)(2,1)S(1)}, u32[]{:S(2)}, u32[]{:S(2)}) collective-permute-start(bf16[240,896]{1,0:T(8,128)(2,1)S(1)} %arrange.1.refs_0_), channel_id=1, source_target_pairs={{0,224},{32,0},{64,32},{96,64},{128,96},{160,128},{192,160},{224,1... | collective-permute-start | bytes 1290248 | tf_op jit(solution)/shard_map/ppermute | solution.py:44
  22.6 4.6 %all-to-all-start = ((bf16[8,48,512]{2,1,0:T(8,128)(2,1)}), bf16[8,48,512]{2,1,0:T(8,128)(2,1)S(1)}, u32[]{:S(2)}, u32[]{:S(2)}) async-start(bf16[8,48,512]{2,1,0:T(8,128)(2,1)} %left.1), calls=%async_computation | async-start | bytes 786432 | tf_op jit(solution)/shard_map/all_to_all | solution.py:34
  27.2 2.4 %collective-permute-start.7 = (bf16[192,1664]{1,0:T(8,128)(2,1)}, bf16[192,1664]{1,0:T(8,128)(2,1)S(1)}, u32[]{:S(2)}, u32[]{:S(2)}) collective-permute-start(bf16[192,1664]{1,0:T(8,128)(2,1)} %inverse.4), channel_id=1, source_target_pairs={{0,16},{16,0},{1,17},{17,1},{2,18},{18,2},{3,19},{19,3},{4,20},{20... | collective-permute-start | bytes 1916936 | tf_op jit(solution)/shard_map/ppermute | solution.py:39
  29.6 5.3 %all-to-all-done.parts = bf16[8,48,512]{2,1,0:T(8,128)(2,1)S(1)} async-done(((bf16[8,48,512]{2,1,0:T(8,128)(2,1)}), bf16[8,48,512]{2,1,0:T(8,128)(2,1)S(1)}, u32[]{:S(2)}, u32[]{:S(2)}) %all-to-all-start) | async-done | bytes 393248 | tf_op jit(solution)/shard_map/all_to_all | solution.py:34
  34.9 0.8 left_sum.1
  35.8 2.7 %collective-permute-start.6 = (bf16[240,896]{1,0:T(8,128)(2,1)S(1)}, bf16[240,896]{1,0:T(8,128)(2,1)}, u32[]{:S(2)}, u32[]{:S(2)}) collective-permute-start(bf16[240,896]{1,0:T(8,128)(2,1)S(1)} %collective-permute-done.4.refs_7_), channel_id=1, source_target_pairs={{0,224},{32,0},{64,32},{96,64},{128,96},{160,128},{192,160},{224,1... | collective-permute-start | bytes 1290248 | tf_op jit(solution)/shard_map/ppermute | solution.py:44
  38.5 3.4 %all-to-all-start.1 = ((bf16[8,32,512]{2,1,0:T(8,128)(2,1)}), bf16[8,32,512]{2,1,0:T(8,128)(2,1)S(1)}, u32[]{:S(2)}, u32[]{:S(2)}) async-start(bf16[8,32,512]{2,1,0:T(8,128)(2,1)} %get-tuple-element.42), calls=%async_computation.1 | async-start | bytes 524288 | tf_op jit(solution)/shard_map/all_to_all | solution.py:34
  41.9 3.0 %inverse.5 = bf16[192,1664]{1,0:T(8,128)(2,1)} custom-call(s32[4]{0:T(128)} %copy-done.9, f32[512,3328]{1,0:T(8,128)} %corrected.7), custom_call_target="tpu_custom_call" | custom-call | tf_op jit(solution)/shard_map/inverse/pallas_call | solution.py:126
  44.9 2.6 %collective-permute-start.10 = (bf16[192,1664]{1,0:T(8,128)(2,1)}, bf16[192,1664]{1,0:T(8,128)(2,1)S(1)}, u32[]{:S(2)}, u32[]{:S(2)}) collective-permute-start(bf16[192,1664]{1,0:T(8,128)(2,1)} %inverse.5), channel_id=1, source_target_pairs={{0,16},{16,0},{1,17},{17,1},{2,18},{18,2},{3,19},{19,3},{4,20},{20... | collective-permute-start | bytes 1916936 | tf_op jit(solution)/shard_map/ppermute | solution.py:39
  47.5 3.9 %all-to-all-done.1 = bf16[8,32,512]{2,1,0:T(8,128)(2,1)S(1)} async-done(((bf16[8,32,512]{2,1,0:T(8,128)(2,1)}), bf16[8,32,512]{2,1,0:T(8,128)(2,1)S(1)}, u32[]{:S(2)}, u32[]{:S(2)}) %all-to-all-start.1) | async-done | bytes 262176 | tf_op jit(solution)/shard_map/all_to_all | solution.py:34
  51.6 2.7 %collective-permute-start.9 = (bf16[240,896]{1,0:T(8,128)(2,1)}, bf16[240,896]{1,0:T(8,128)(2,1)}, u32[]{:S(2)}, u32[]{:S(2)}) collective-permute-start(bf16[240,896]{1,0:T(8,128)(2,1)} %collective-permute-done.6.refs_6_), channel_id=1, source_target_pairs={{0,224},{32,0},{64,32},{96,64},{128,96},{160,128},{192,160},{224,1... | collective-permute-start | bytes 1290248 | tf_op jit(solution)/shard_map/ppermute | solution.py:44
  54.2 3.8 %inverse.6 = (bf16[512,896]{1,0:T(8,128)(2,1)}, bf16[512,896]{1,0:T(8,128)(2,1)}) custom-call(s32[4]{0:T(128)} %copy-done.9, f32[512,3328]{1,0:T(8,128)} %corrected.7), custom_call_target="tpu_custom_call" | custom-call | tf_op jit(solution)/shard_map/inverse/pallas_call | solution.py:126
  58.0 3.4 %collective-permute-start.14 = (bf16[512,896]{1,0:T(8,128)(2,1)}, bf16[512,896]{1,0:T(8,128)(2,1)S(1)}, u32[]{:S(2)}, u32[]{:S(2)}) collective-permute-start(bf16[512,896]{1,0:T(8,128)(2,1)} %get-tuple-element.53), channel_id=1, source_target_pairs={{0,8},{8,0},{1,9},{9,1},{2,10},{10,2},{3,11},{11,3},{4,12},{12,4},... | collective-permute-start | bytes 2752520 | tf_op jit(solution)/shard_map/ppermute | solution.py:39
  61.4 2.1 %collective-permute-done.10.refs_1_ = bf16[192,1664]{1,0:T(8,128)(2,1)S(1)} collective-permute-done((bf16[192,1664]{1,0:T(8,128)(2,1)}, bf16[192,1664]{1,0:T(8,128)(2,1)S(1)}, u32[]{:S(2)}, u32[]{:S(2)}) %collective-permute-start.10) | collective-permute-done | bytes 639008 | tf_op jit(solution)/shard_map/ppermute | solution.py:39
  63.5 2.7 %inverse.7 = bf16[128,1664]{1,0:T(8,128)(2,1)} custom-call(s32[4]{0:T(128)} %copy-done.9, f32[512,3328]{1,0:T(8,128)} %corrected.7), custom_call_target="tpu_custom_call" | custom-call | tf_op jit(solution)/shard_map/inverse/pallas_call | solution.py:126
  66.2 0.7 collective-permute-start.17
  66.9 3.8 %collective-permute-start.13 = (bf16[128,512]{1,0:T(8,128)(2,1)}, bf16[128,512]{1,0:T(8,128)(2,1)S(1)}, u32[]{:S(2)}, u32[]{:S(2)}) collective-permute-start(bf16[128,512]{1,0:T(8,128)(2,1)} %get-tuple-element.51.refs_2_), channel_id=1, source_target_pairs={{0,8},{8,0},{1,9},{9,1},{2,10},{10,2},{3,11},{11,3},{4,12},{12,4},... | collective-permute-start | bytes 393224 | tf_op jit(solution)/shard_map/ppermute | solution.py:39
  70.7 1.3 collective-permute-done.13.refs_3_
  72.0 1.1 collective-permute-start.15
  73.2 0.9 collective-permute-done.11.refs_4_
  74.1 0.9 collective-permute-start.16
  75.0 1.0 copy-done.7
  76.0 3.9 %rotate.1 = (bf16[1664,896]{1,0:T(8,128)(2,1)S(1)}, bf16[256,896]{1,0:T(8,128)(2,1)S(1)}, bf16[128,896]{1,0:T(8,128)(2,1)S(1)}, bf16[128,128]{1,0:T(8,128)(2,1)S(1)}) custom-call(s32[4]{0:T(128)S(1)} %copy-done.11, s32[4]{0:T(128)S(1)} %copy-done.16, bf16[6,64,3328]{2,1,0:T(8,128)(2,1)S(1)} %bitcast.11, bf16[6,64,3328]{2,1,0:T(8,128)(2,1)S(1)} %bitcast.12, ...), custom_call_target="tpu_custom_call" | custom-call | tf_op jit(solution)/shard_map/rotate/pallas_call | solution.py:273
  80.0 4.6 %back_first.1.so_far = f32[4,128,896]{2,1,0:T(8,128)S(1)} custom-call(bf16[256,896]{1,0:T(8,128)(2,1)S(1)} %get-tuple-element.49.right, bf16[256,512]{1,0:T(8,128)(2,1)S(1)} %bitcast.21, bf16[256,512]{1,0:T(8,128)(2,1)S(1)} %collective-permute-done.12.refs_1_, bf16[128,512]{1,0:T(8,128)(2,1)} %get-tuple-element.51.refs_2_, ...), custom_call_target="tpu_custom_call" | custom-call | tf_op jit(solution)/shard_map/back_first/pallas_call | solution.py:313
  84.6 0.7 collective-permute-done.16.refs_2_
  85.4 0.7 halves.1
  86.1 3.4 %collective-permute-start.20 = (bf16[512,896]{1,0:T(8,128)(2,1)S(1)}, bf16[512,896]{1,0:T(8,128)(2,1)S(1)}, u32[]{:S(2)}, u32[]{:S(2)}) collective-permute-start(bf16[512,896]{1,0:T(8,128)(2,1)S(1)} %get-tuple-element.61), channel_id=1, source_target_pairs={{0,8},{8,0},{1,9},{9,1},{2,10},{10,2},{3,11},{11,3},{4,12},{12,4},... | collective-permute-start | bytes 2752520 | tf_op jit(solution)/shard_map/ppermute | solution.py:39
  89.9 2.2 %collective-permute-done.19.refs_3_ = bf16[128,512]{1,0:T(8,128)(2,1)S(1)} collective-permute-done((bf16[128,512]{1,0:T(8,128)(2,1)S(1)}, bf16[128,512]{1,0:T(8,128)(2,1)S(1)}, u32[]{:S(2)}, u32[]{:S(2)}) %collective-permute-start.19) | collective-permute-done | bytes 131104 | tf_op jit(solution)/shard_map/ppermute | solution.py:39
  92.1 4.9 %back.1.parts = bf16[8,64,896]{2,1,0:T(8,128)(2,1)} custom-call(s32[4]{0:T(128)S(1)} %copy-done.11, s32[16]{0:T(128)S(1)} %copy-done.18, f32[4,128,896]{2,1,0:T(8,128)S(1)} %back_first.1.so_far, f32[32,1664]{1,0:T(8,128)S(1)} %copy-done.8, bf16[256,896]{1,0:T(8,128)(2,1)S(1)} %get-tuple-element.49.right, ...), custom_call_target="tpu_custom_call" | custom-call | tf_op jit(solution)/shard_map/back/pallas_call | solution.py:345
  97.0 5.4 %all-to-all-start.2 = ((bf16[8,64,896]{2,1,0:T(8,128)(2,1)}), bf16[8,64,896]{2,1,0:T(8,128)(2,1)}, u32[]{:S(2)}, u32[]{:S(2)}) async-start(bf16[8,64,896]{2,1,0:T(8,128)(2,1)} %back.1.parts), calls=%async_computation.2 | async-start | bytes 1835008 | tf_op jit(solution)/shard_map/all_to_all | solution.py:34
  102.4 1.7 %score.1 = f32[1,128]{1,0:T(1,128)S(1)} custom-call(bf16[8,64,896]{2,1,0:T(8,128)(2,1)} %back.1.parts, bf16[128,896]{1,0:T(8,128)(2,1)S(1)} %get-tuple-element.62.tokens, bf16[128,128]{1,0:T(8,128)(2,1)S(1)} %copy-done.14), custom_call_target="tpu_custom_call" | custom-call | tf_op jit(solution)/shard_map/score/pallas_call | solution.py:372
  104.1 0.9 collective-permute-start.21
  105.0 0.8 collective-permute-done.21
  105.9 2.8 %collective-permute-done.22 = f32[1,128]{1,0:T(1,128)S(1)} collective-permute-done((f32[1,128]{1,0:T(1,128)S(1)}, f32[1,128]{1,0:T(1,128)S(1)}, u32[]{:S(2)}, u32[]{:S(2)}) %collective-permute-start.22) | collective-permute-done | bytes 544 | tf_op jit(solution)/shard_map/ppermute | solution.py:39
  108.7 1.1 collective-permute-start.23
  109.8 1.6 %collective-permute-done.23 = f32[1,128]{1,0:T(1,128)S(1)} collective-permute-done((f32[1,128]{1,0:T(1,128)S(1)}, f32[1,128]{1,0:T(1,128)S(1)}, u32[]{:S(2)}, u32[]{:S(2)}) %collective-permute-start.23) | collective-permute-done | bytes 544 | tf_op jit(solution)/shard_map/ppermute | solution.py:39
  111.5 2.7 %collective-permute-start.24 = (f32[1,128]{1,0:T(1,128)S(1)}, f32[1,128]{1,0:T(1,128)S(1)}, u32[]{:S(2)}, u32[]{:S(2)}) collective-permute-start(f32[1,128]{1,0:T(1,128)S(1)} %add.23), channel_id=1, source_target_pairs={{0,4},{2,6},{4,0},{6,2},{1,5},{3,7},{5,1},{7,3},{8,12},{10,14},{12... | collective-permute-start | bytes 1544 | tf_op jit(solution)/shard_map/ppermute | solution.py:39
  114.2 1.4 collective-permute-done.24
  115.6 1.2 collective-permute-start.25
  116.8 3.1 %collective-permute-done.25 = f32[1,128]{1,0:T(1,128)S(1)} collective-permute-done((f32[1,128]{1,0:T(1,128)S(1)}, f32[1,128]{1,0:T(1,128)S(1)}, u32[]{:S(2)}, u32[]{:S(2)}) %collective-permute-start.25) | collective-permute-done | bytes 544 | tf_op jit(solution)/shard_map/ppermute | solution.py:39
  119.9 0.6 broadcast_in_dim.2.score
  120.5 1.8 %copy-done.3 = bf16[1664,896]{1,0:T(8,128)(2,1)S(1)} copy-done((bf16[1664,896]{1,0:T(8,128)(2,1)S(1)}, bf16[1664,896]{1,0:T(8,128)(2,1)}, u32[]{:S(2)}) %copy-start.3) | copy-done | bytes 2981912
  122.4 1.0 stage.1.basis
  123.4 5.5 %all-to-all-done.2.parts = bf16[8,64,896]{2,1,0:T(8,128)(2,1)} async-done(((bf16[8,64,896]{2,1,0:T(8,128)(2,1)}), bf16[8,64,896]{2,1,0:T(8,128)(2,1)}, u32[]{:S(2)}, u32[]{:S(2)}) %all-to-all-start.2) | async-done | bytes 917536 | tf_op jit(solution)/shard_map/all_to_all | solution.py:34
  128.9 3.3 %all-to-all-start.3 = ((f32[8,8,128]{2,1,0:T(8,128)}), f32[8,8,128]{2,1,0:T(8,128)S(1)}, u32[]{:S(2)}, u32[]{:S(2)}) async-start(f32[8,8,128]{2,1,0:T(8,128)} %broadcast_in_dim.2.score), calls=%async_computation.3 | async-start | bytes 65536 | tf_op jit(solution)/shard_map/all_to_all | solution.py:34
  132.2 2.3 %tile.1 = (bf16[16,1664]{1,0:T(8,128)(2,1)S(1)}, bf16[16,1664]{1,0:T(8,128)(2,1)S(1)}, bf16[16,1664]{1,0:T(8,128)(2,1)S(1)}, bf16[16,1664]{1,0:T(8,128)(2,1)S(1)}) custom-call(s32[4]{0:T(128)S(1)} %copy-done.11, bf16[8,64,896]{2,1,0:T(8,128)(2,1)} %all-to-all-done.2.parts, bf16[1664,896]{1,0:T(8,128)(2,1)S(1)} %stage.1.basis), custom_call_target="tpu_custom_call" | custom-call | tf_op jit(solution)/shard_map/tile/pallas_call | solution.py:404
  134.5 1.9 %collective-permute-start.26 = (bf16[16,1664]{1,0:T(8,128)(2,1)S(1)}, bf16[16,1664]{1,0:T(8,128)(2,1)S(1)}, u32[]{:S(2)}, u32[]{:S(2)}) collective-permute-start(bf16[16,1664]{1,0:T(8,128)(2,1)S(1)} %get-tuple-element.68), channel_id=1, source_target_pairs={{0,8},{8,0},{1,9},{9,1},{2,10},{10,2},{3,11},{11,3},{4,12},{12,4},... | collective-permute-start | bytes 159752 | tf_op jit(solution)/shard_map/ppermute | solution.py:39
  136.4 1.2 collective-permute-start.27
  137.6 2.1 %collective-permute-start.28 = (bf16[16,1664]{1,0:T(8,128)(2,1)S(1)}, bf16[16,1664]{1,0:T(8,128)(2,1)S(1)}, u32[]{:S(2)}, u32[]{:S(2)}) collective-permute-start(bf16[16,1664]{1,0:T(8,128)(2,1)S(1)} %get-tuple-element.70), channel_id=1, source_target_pairs={{0,24},{8,16},{16,8},{24,0},{1,25},{9,17},{17,9},{25,1},{2,26},{10... | collective-permute-start | bytes 159752 | tf_op jit(solution)/shard_map/ppermute | solution.py:39
  139.7 1.7 %collective-permute-done.27.t2 = bf16[16,1664]{1,0:T(8,128)(2,1)S(1)} collective-permute-done((bf16[16,1664]{1,0:T(8,128)(2,1)S(1)}, bf16[16,1664]{1,0:T(8,128)(2,1)S(1)}, u32[]{:S(2)}, u32[]{:S(2)}) %collective-permute-start.27) | collective-permute-done | bytes 53280 | tf_op jit(solution)/shard_map/ppermute | solution.py:39
  141.3 1.6 %collective-permute-done.28.t3 = bf16[16,1664]{1,0:T(8,128)(2,1)S(1)} collective-permute-done((bf16[16,1664]{1,0:T(8,128)(2,1)S(1)}, bf16[16,1664]{1,0:T(8,128)(2,1)S(1)}, u32[]{:S(2)}, u32[]{:S(2)}) %collective-permute-start.28) | collective-permute-done | bytes 53280 | tf_op jit(solution)/shard_map/ppermute | solution.py:39
  142.9 1.2 final.1
  (64 shorter events, 1.2 us)
Async XLA Ops:
  1.8 9.5 %copy-start.9 = (s32[4]{0:T(128)}, s32[4]{0:T(128)S(1)}, u32[]{:S(2)}) copy-start(s32[4]{0:T(128)S(1)} %pad_add_fusion.where) | copy-start | bytes 52
  1.8 0.8 copy-start.12
  2.6 0.7 copy-start.15
  3.2 0.7 copy-start.17
  4.7 11.9 %collective-permute-start = (bf16[60,896]{1,0:T(8,128)(2,1)S(1)}, bf16[60,896]{1,0:T(8,128)(2,1)S(1)}, u32[]{:S(2)}, u32[]{:S(2)}) collective-permute-start(bf16[60,896]{1,0:T(8,128)(2,1)S(1)} %get-tuple-element.39), channel_id=1, source_target_pairs={{0,8},{8,0},{1,9},{9,1},{2,10},{10,2},{3,11},{11,3},{4,12},{12,4},... | collective-permute-start | bytes 322568 | tf_op jit(solution)/shard_map/ppermute | solution.py:39
  8.0 8.6 %collective-permute-start.1 = (bf16[60,896]{1,0:T(8,128)(2,1)S(1)}, bf16[60,896]{1,0:T(8,128)(2,1)S(1)}, u32[]{:S(2)}, u32[]{:S(2)}) collective-permute-start(bf16[60,896]{1,0:T(8,128)(2,1)S(1)} %get-tuple-element.40), channel_id=1, source_target_pairs={{0,16},{16,0},{1,17},{17,1},{2,18},{18,2},{3,19},{19,3},{4,20},{20... | collective-permute-start | bytes 322568 | tf_op jit(solution)/shard_map/ppermute | solution.py:39
  9.0 5.2 %copy-start.1 = (bf16[6,2048,64]{1,2,0:T(8,128)(2,1)S(1)}, bf16[6,2048,64]{1,2,0:T(8,128)(2,1)}, u32[]{:S(2)}) copy-start(bf16[6,2048,64]{1,2,0:T(8,128)(2,1)} %param.17) | copy-start | bytes 4718596
  9.0 5.2 %copy-start.4 = (bf16[2048,512]{1,0:T(8,128)(2,1)S(1)}, bf16[2048,512]{1,0:T(8,128)(2,1)}, u32[]{:S(2)}) copy-start(bf16[2048,512]{1,0:T(8,128)(2,1)} %basis.2) | copy-start | bytes 6291460
  9.0 5.2 %copy-start.16 = (s32[4]{0:T(128)S(1)}, s32[4]{0:T(128)}, u32[]{:S(2)}) copy-start(s32[4]{0:T(128)} %ids.3) | copy-start | bytes 52
  9.0 7.8 %collective-permute-start.2 = (bf16[60,896]{1,0:T(8,128)(2,1)S(1)}, bf16[60,896]{1,0:T(8,128)(2,1)S(1)}, u32[]{:S(2)}, u32[]{:S(2)}) collective-permute-start(bf16[60,896]{1,0:T(8,128)(2,1)S(1)} %get-tuple-element.41), channel_id=1, source_target_pairs={{0,24},{8,16},{16,8},{24,0},{1,25},{9,17},{17,9},{25,1},{2,26},{10... | collective-permute-start | bytes 322568 | tf_op jit(solution)/shard_map/ppermute | solution.py:39
  14.2 2.6 %copy-start.10 = (s32[4]{0:T(128)S(1)}, s32[4]{0:T(128)}, u32[]{:S(2)}) copy-start(s32[4]{0:T(128)} %copy-done.9) | copy-start | bytes 52
  18.0 17.7 %collective-permute-start.3 = (bf16[240,896]{1,0:T(8,128)(2,1)S(1)}, bf16[240,896]{1,0:T(8,128)(2,1)S(1)}, u32[]{:S(2)}, u32[]{:S(2)}) collective-permute-start(bf16[240,896]{1,0:T(8,128)(2,1)S(1)} %arrange.1.refs_0_), channel_id=1, source_target_pairs={{0,32},{32,64},{64,96},{96,128},{128,160},{160,192},{192,224},{224... | collective-permute-start | bytes 1290248 | tf_op jit(solution)/shard_map/ppermute | solution.py:44
  18.5 17.2 %collective-permute-start.4 = (bf16[240,896]{1,0:T(8,128)(2,1)S(1)}, bf16[240,896]{1,0:T(8,128)(2,1)S(1)}, u32[]{:S(2)}, u32[]{:S(2)}) collective-permute-start(bf16[240,896]{1,0:T(8,128)(2,1)S(1)} %arrange.1.refs_0_), channel_id=1, source_target_pairs={{0,224},{32,0},{64,32},{96,64},{128,96},{160,128},{192,160},{224,1... | collective-permute-start | bytes 1290248 | tf_op jit(solution)/shard_map/ppermute | solution.py:44
  22.6 12.4 %all-to-all-start = ((bf16[8,48,512]{2,1,0:T(8,128)(2,1)}), bf16[8,48,512]{2,1,0:T(8,128)(2,1)S(1)}, u32[]{:S(2)}, u32[]{:S(2)}) async-start(bf16[8,48,512]{2,1,0:T(8,128)(2,1)} %left.1), calls=%async_computation | async-start | bytes 786432 | tf_op jit(solution)/shard_map/all_to_all | solution.py:34
  27.2 24.3 %collective-permute-start.7 = (bf16[192,1664]{1,0:T(8,128)(2,1)}, bf16[192,1664]{1,0:T(8,128)(2,1)S(1)}, u32[]{:S(2)}, u32[]{:S(2)}) collective-permute-start(bf16[192,1664]{1,0:T(8,128)(2,1)} %inverse.4), channel_id=1, source_target_pairs={{0,16},{16,0},{1,17},{17,1},{2,18},{18,2},{3,19},{19,3},{4,20},{20... | collective-permute-start | bytes 1916936 | tf_op jit(solution)/shard_map/ppermute | solution.py:39
  35.7 9.2 %copy-start.6 = (bf16[240,896]{1,0:T(8,128)(2,1)}, bf16[240,896]{1,0:T(8,128)(2,1)S(1)}, u32[]{:S(2)}) copy-start(bf16[240,896]{1,0:T(8,128)(2,1)S(1)} %collective-permute-done.4.refs_7_) | copy-start | bytes 1290244
  35.7 15.7 %collective-permute-start.5 = (bf16[240,896]{1,0:T(8,128)(2,1)S(1)}, bf16[240,896]{1,0:T(8,128)(2,1)}, u32[]{:S(2)}, u32[]{:S(2)}) collective-permute-start(bf16[240,896]{1,0:T(8,128)(2,1)S(1)} %collective-permute-done.3.refs_1_), channel_id=1, source_target_pairs={{0,32},{32,64},{64,96},{96,128},{128,160},{160,192},{192,224},{224... | collective-permute-start | bytes 1290248 | tf_op jit(solution)/shard_map/ppermute | solution.py:44
  35.8 15.6 %collective-permute-start.6 = (bf16[240,896]{1,0:T(8,128)(2,1)S(1)}, bf16[240,896]{1,0:T(8,128)(2,1)}, u32[]{:S(2)}, u32[]{:S(2)}) collective-permute-start(bf16[240,896]{1,0:T(8,128)(2,1)S(1)} %collective-permute-done.4.refs_7_), channel_id=1, source_target_pairs={{0,224},{32,0},{64,32},{96,64},{128,96},{160,128},{192,160},{224,1... | collective-permute-start | bytes 1290248 | tf_op jit(solution)/shard_map/ppermute | solution.py:44
  38.5 13.0 %all-to-all-start.1 = ((bf16[8,32,512]{2,1,0:T(8,128)(2,1)}), bf16[8,32,512]{2,1,0:T(8,128)(2,1)S(1)}, u32[]{:S(2)}, u32[]{:S(2)}) async-start(bf16[8,32,512]{2,1,0:T(8,128)(2,1)} %get-tuple-element.42), calls=%async_computation.1 | async-start | bytes 524288 | tf_op jit(solution)/shard_map/all_to_all | solution.py:34
  44.9 18.6 %collective-permute-start.10 = (bf16[192,1664]{1,0:T(8,128)(2,1)}, bf16[192,1664]{1,0:T(8,128)(2,1)S(1)}, u32[]{:S(2)}, u32[]{:S(2)}) collective-permute-start(bf16[192,1664]{1,0:T(8,128)(2,1)} %inverse.5), channel_id=1, source_target_pairs={{0,16},{16,0},{1,17},{17,1},{2,18},{18,2},{3,19},{19,3},{4,20},{20... | collective-permute-start | bytes 1916936 | tf_op jit(solution)/shard_map/ppermute | solution.py:39
  51.5 12.1 %collective-permute-start.8 = (bf16[240,896]{1,0:T(8,128)(2,1)}, bf16[240,896]{1,0:T(8,128)(2,1)}, u32[]{:S(2)}, u32[]{:S(2)}) collective-permute-start(bf16[240,896]{1,0:T(8,128)(2,1)} %collective-permute-done.5.refs_2_), channel_id=1, source_target_pairs={{0,32},{32,64},{64,96},{96,128},{128,160},{160,192},{192,224},{224... | collective-permute-start | bytes 1290248 | tf_op jit(solution)/shard_map/ppermute | solution.py:44
  51.6 12.0 %collective-permute-start.9 = (bf16[240,896]{1,0:T(8,128)(2,1)}, bf16[240,896]{1,0:T(8,128)(2,1)}, u32[]{:S(2)}, u32[]{:S(2)}) collective-permute-start(bf16[240,896]{1,0:T(8,128)(2,1)} %collective-permute-done.6.refs_6_), channel_id=1, source_target_pairs={{0,224},{32,0},{64,32},{96,64},{128,96},{160,128},{192,160},{224,1... | collective-permute-start | bytes 1290248 | tf_op jit(solution)/shard_map/ppermute | solution.py:44
  58.0 17.0 %copy-start = (bf16[6,3328,64]{1,2,0:T(8,128)(2,1)S(1)}, bf16[6,3328,64]{1,2,0:T(8,128)(2,1)}, u32[]{:S(2)}) copy-start(bf16[6,3328,64]{1,2,0:T(8,128)(2,1)} %param.18) | copy-start | bytes 7667716
  58.0 17.0 %copy-start.11 = (s32[4]{0:T(128)S(1)}, s32[4]{0:T(128)}, u32[]{:S(2)}) copy-start(s32[4]{0:T(128)} %copy-done.9) | copy-start | bytes 52
  58.0 22.0 %collective-permute-start.14 = (bf16[512,896]{1,0:T(8,128)(2,1)}, bf16[512,896]{1,0:T(8,128)(2,1)S(1)}, u32[]{:S(2)}, u32[]{:S(2)}) collective-permute-start(bf16[512,896]{1,0:T(8,128)(2,1)} %get-tuple-element.53), channel_id=1, source_target_pairs={{0,8},{8,0},{1,9},{9,1},{2,10},{10,2},{3,11},{11,3},{4,12},{12,4},... | collective-permute-start | bytes 2752520 | tf_op jit(solution)/shard_map/ppermute | solution.py:39
  63.5 10.6 %collective-permute-start.11 = (bf16[240,896]{1,0:T(8,128)(2,1)}, bf16[240,896]{1,0:T(8,128)(2,1)}, u32[]{:S(2)}, u32[]{:S(2)}) collective-permute-start(bf16[240,896]{1,0:T(8,128)(2,1)} %collective-permute-done.8.refs_3_), channel_id=1, source_target_pairs={{0,32},{32,64},{64,96},{96,128},{128,160},{160,192},{192,224},{224... | collective-permute-start | bytes 1290248 | tf_op jit(solution)/shard_map/ppermute | solution.py:44
  66.2 19.1 %collective-permute-start.17 = (bf16[128,1664]{1,0:T(8,128)(2,1)}, bf16[128,1664]{1,0:T(8,128)(2,1)S(1)}, u32[]{:S(2)}, u32[]{:S(2)}) collective-permute-start(bf16[128,1664]{1,0:T(8,128)(2,1)} %inverse.7), channel_id=1, source_target_pairs={{0,16},{16,0},{1,17},{17,1},{2,18},{18,2},{3,19},{19,3},{4,20},{20... | collective-permute-start | bytes 1277960 | tf_op jit(solution)/shard_map/ppermute | solution.py:39
  66.9 5.1 %collective-permute-start.13 = (bf16[128,512]{1,0:T(8,128)(2,1)}, bf16[128,512]{1,0:T(8,128)(2,1)S(1)}, u32[]{:S(2)}, u32[]{:S(2)}) collective-permute-start(bf16[128,512]{1,0:T(8,128)(2,1)} %get-tuple-element.51.refs_2_), channel_id=1, source_target_pairs={{0,8},{8,0},{1,9},{9,1},{2,10},{10,2},{3,11},{11,3},{4,12},{12,4},... | collective-permute-start | bytes 393224 | tf_op jit(solution)/shard_map/ppermute | solution.py:39
  70.7 9.3 %collective-permute-start.12 = (bf16[256,512]{1,0:T(8,128)(2,1)S(1)}, bf16[256,512]{1,0:T(8,128)(2,1)S(1)}, u32[]{:S(2)}, u32[]{:S(2)}) collective-permute-start(bf16[256,512]{1,0:T(8,128)(2,1)S(1)} %bitcast.19), channel_id=1, source_target_pairs={{0,8},{8,0},{1,9},{9,1},{2,10},{10,2},{3,11},{11,3},{4,12},{12,4},... | collective-permute-start | bytes 786440 | tf_op jit(solution)/shard_map/ppermute | solution.py:39
  72.0 13.3 %collective-permute-start.15 = (bf16[256,512]{1,0:T(8,128)(2,1)S(1)}, bf16[256,512]{1,0:T(8,128)(2,1)S(1)}, u32[]{:S(2)}, u32[]{:S(2)}) collective-permute-start(bf16[256,512]{1,0:T(8,128)(2,1)S(1)} %bitcast.20), channel_id=1, source_target_pairs={{0,16},{16,0},{1,17},{17,1},{2,18},{18,2},{3,19},{19,3},{4,20},{20... | collective-permute-start | bytes 786440 | tf_op jit(solution)/shard_map/ppermute | solution.py:39
  74.1 11.2 %collective-permute-start.16 = (bf16[128,512]{1,0:T(8,128)(2,1)}, bf16[128,512]{1,0:T(8,128)(2,1)S(1)}, u32[]{:S(2)}, u32[]{:S(2)}) collective-permute-start(bf16[128,512]{1,0:T(8,128)(2,1)} %get-tuple-element.51.refs_2_), channel_id=1, source_target_pairs={{0,16},{16,0},{1,17},{17,1},{2,18},{18,2},{3,19},{19,3},{4,20},{20... | collective-permute-start | bytes 393224 | tf_op jit(solution)/shard_map/ppermute | solution.py:39
  75.0 1.0 copy-start.7
  76.0 4.0 %copy-start.5 = (bf16[512,896]{1,0:T(8,128)(2,1)S(1)}, bf16[512,896]{1,0:T(8,128)(2,1)}, u32[]{:S(2)}) copy-start(bf16[512,896]{1,0:T(8,128)(2,1)} %get-tuple-element.52.refs_4_) | copy-start | bytes 2752516
  80.0 6.1 %copy-start.2 = (bf16[1664,896]{1,0:T(8,128)(2,1)}, bf16[1664,896]{1,0:T(8,128)(2,1)S(1)}, u32[]{:S(2)}) copy-start(bf16[1664,896]{1,0:T(8,128)(2,1)S(1)} %get-tuple-element.64.basis) | copy-start | bytes 8945668
  80.0 6.1 %copy-start.13 = (bf16[128,128]{1,0:T(8,128)(2,1)}, bf16[128,128]{1,0:T(8,128)(2,1)S(1)}, u32[]{:S(2)}) copy-start(bf16[128,128]{1,0:T(8,128)(2,1)S(1)} %get-tuple-element.63.delta) | copy-start | bytes 98308
  80.0 12.1 %copy-start.8 = (f32[32,1664]{1,0:T(8,128)S(1)}, f32[32,1664]{1,0:T(8,128)}, u32[]{:S(2)}) copy-start(f32[32,1664]{1,0:T(8,128)} %factors.1) | copy-start | bytes 638980
  80.0 12.1 %copy-start.18 = (s32[16]{0:T(128)S(1)}, s32[16]{0:T(128)}, u32[]{:S(2)}) copy-start(s32[16]{0:T(128)} %block_ids.1) | copy-start | bytes 196
  86.1 6.0 %collective-permute-start.20 = (bf16[512,896]{1,0:T(8,128)(2,1)S(1)}, bf16[512,896]{1,0:T(8,128)(2,1)S(1)}, u32[]{:S(2)}, u32[]{:S(2)}) collective-permute-start(bf16[512,896]{1,0:T(8,128)(2,1)S(1)} %get-tuple-element.61), channel_id=1, source_target_pairs={{0,8},{8,0},{1,9},{9,1},{2,10},{10,2},{3,11},{11,3},{4,12},{12,4},... | collective-permute-start | bytes 2752520 | tf_op jit(solution)/shard_map/ppermute | solution.py:39
  89.4 2.7 %collective-permute-start.18 = (bf16[256,512]{1,0:T(8,128)(2,1)S(1)}, bf16[256,512]{1,0:T(8,128)(2,1)S(1)}, u32[]{:S(2)}, u32[]{:S(2)}) collective-permute-start(bf16[256,512]{1,0:T(8,128)(2,1)S(1)} %collective-permute-done.15.refs_0_), channel_id=1, source_target_pairs={{0,8},{8,0},{1,9},{9,1},{2,10},{10,2},{3,11},{11,3},{4,12},{12,4},... | collective-permute-start | bytes 786440 | tf_op jit(solution)/shard_map/ppermute | solution.py:39
  89.5 2.6 %collective-permute-start.19 = (bf16[128,512]{1,0:T(8,128)(2,1)S(1)}, bf16[128,512]{1,0:T(8,128)(2,1)S(1)}, u32[]{:S(2)}, u32[]{:S(2)}) collective-permute-start(bf16[128,512]{1,0:T(8,128)(2,1)S(1)} %collective-permute-done.16.refs_2_), channel_id=1, source_target_pairs={{0,8},{8,0},{1,9},{9,1},{2,10},{10,2},{3,11},{11,3},{4,12},{12,4},... | collective-permute-start | bytes 393224 | tf_op jit(solution)/shard_map/ppermute | solution.py:39
  92.1 10.3 %copy-start.14 = (bf16[128,128]{1,0:T(8,128)(2,1)S(1)}, bf16[128,128]{1,0:T(8,128)(2,1)}, u32[]{:S(2)}) copy-start(bf16[128,128]{1,0:T(8,128)(2,1)} %copy-done.13) | copy-start | bytes 98308
  97.0 31.9 %all-to-all-start.2 = ((bf16[8,64,896]{2,1,0:T(8,128)(2,1)}), bf16[8,64,896]{2,1,0:T(8,128)(2,1)}, u32[]{:S(2)}, u32[]{:S(2)}) async-start(bf16[8,64,896]{2,1,0:T(8,128)(2,1)} %back.1.parts), calls=%async_computation.2 | async-start | bytes 1835008 | tf_op jit(solution)/shard_map/all_to_all | solution.py:34
  104.1 1.7 %collective-permute-start.21 = (f32[1,128]{1,0:T(1,128)S(1)}, f32[1,128]{1,0:T(1,128)S(1)}, u32[]{:S(2)}, u32[]{:S(2)}) collective-permute-start(f32[1,128]{1,0:T(1,128)S(1)} %score.1), channel_id=1, source_target_pairs={{0,8},{8,0},{1,9},{9,1},{2,10},{10,2},{3,11},{11,3},{4,12},{12,4},... | collective-permute-start | bytes 1544 | tf_op jit(solution)/shard_map/ppermute | solution.py:39
  105.9 2.8 %collective-permute-start.22 = (f32[1,128]{1,0:T(1,128)S(1)}, f32[1,128]{1,0:T(1,128)S(1)}, u32[]{:S(2)}, u32[]{:S(2)}) collective-permute-start(f32[1,128]{1,0:T(1,128)S(1)} %add.21), channel_id=1, source_target_pairs={{0,1},{1,0},{2,3},{3,2},{4,5},{5,4},{6,7},{7,6},{8,9},{9,8},{10,11... | collective-permute-start | bytes 1544 | tf_op jit(solution)/shard_map/ppermute | solution.py:39
  108.7 2.8 %collective-permute-start.23 = (f32[1,128]{1,0:T(1,128)S(1)}, f32[1,128]{1,0:T(1,128)S(1)}, u32[]{:S(2)}, u32[]{:S(2)}) collective-permute-start(f32[1,128]{1,0:T(1,128)S(1)} %add.22), channel_id=1, source_target_pairs={{0,2},{2,0},{4,6},{6,4},{1,3},{3,1},{5,7},{7,5},{8,10},{10,8},{12,... | collective-permute-start | bytes 1544 | tf_op jit(solution)/shard_map/ppermute | solution.py:39
  111.5 4.2 %collective-permute-start.24 = (f32[1,128]{1,0:T(1,128)S(1)}, f32[1,128]{1,0:T(1,128)S(1)}, u32[]{:S(2)}, u32[]{:S(2)}) collective-permute-start(f32[1,128]{1,0:T(1,128)S(1)} %add.23), channel_id=1, source_target_pairs={{0,4},{2,6},{4,0},{6,2},{1,5},{3,7},{5,1},{7,3},{8,12},{10,14},{12... | collective-permute-start | bytes 1544 | tf_op jit(solution)/shard_map/ppermute | solution.py:39
  115.6 4.3 %collective-permute-start.25 = (f32[1,128]{1,0:T(1,128)S(1)}, f32[1,128]{1,0:T(1,128)S(1)}, u32[]{:S(2)}, u32[]{:S(2)}) collective-permute-start(f32[1,128]{1,0:T(1,128)S(1)} %add.24), channel_id=1, source_target_pairs={{0,16},{16,0},{1,17},{17,1},{2,18},{18,2},{3,19},{19,3},{4,20},{20... | collective-permute-start | bytes 1544 | tf_op jit(solution)/shard_map/ppermute | solution.py:39
  120.5 1.8 %copy-start.3 = (bf16[1664,896]{1,0:T(8,128)(2,1)S(1)}, bf16[1664,896]{1,0:T(8,128)(2,1)}, u32[]{:S(2)}) copy-start(bf16[1664,896]{1,0:T(8,128)(2,1)} %copy-done.2) | copy-start | bytes 8945668
  128.9 14.1 %all-to-all-start.3 = ((f32[8,8,128]{2,1,0:T(8,128)}), f32[8,8,128]{2,1,0:T(8,128)S(1)}, u32[]{:S(2)}, u32[]{:S(2)}) async-start(f32[8,8,128]{2,1,0:T(8,128)} %broadcast_in_dim.2.score), calls=%async_computation.3 | async-start | bytes 65536 | tf_op jit(solution)/shard_map/all_to_all | solution.py:34
  134.5 5.1 %collective-permute-start.26 = (bf16[16,1664]{1,0:T(8,128)(2,1)S(1)}, bf16[16,1664]{1,0:T(8,128)(2,1)S(1)}, u32[]{:S(2)}, u32[]{:S(2)}) collective-permute-start(bf16[16,1664]{1,0:T(8,128)(2,1)S(1)} %get-tuple-element.68), channel_id=1, source_target_pairs={{0,8},{8,0},{1,9},{9,1},{2,10},{10,2},{3,11},{11,3},{4,12},{12,4},... | collective-permute-start | bytes 159752 | tf_op jit(solution)/shard_map/ppermute | solution.py:39
  136.4 4.9 %collective-permute-start.27 = (bf16[16,1664]{1,0:T(8,128)(2,1)S(1)}, bf16[16,1664]{1,0:T(8,128)(2,1)S(1)}, u32[]{:S(2)}, u32[]{:S(2)}) collective-permute-start(bf16[16,1664]{1,0:T(8,128)(2,1)S(1)} %get-tuple-element.69), channel_id=1, source_target_pairs={{0,16},{16,0},{1,17},{17,1},{2,18},{18,2},{3,19},{19,3},{4,20},{20... | collective-permute-start | bytes 159752 | tf_op jit(solution)/shard_map/ppermute | solution.py:39
  137.6 5.3 %collective-permute-start.28 = (bf16[16,1664]{1,0:T(8,128)(2,1)S(1)}, bf16[16,1664]{1,0:T(8,128)(2,1)S(1)}, u32[]{:S(2)}, u32[]{:S(2)}) collective-permute-start(bf16[16,1664]{1,0:T(8,128)(2,1)S(1)} %get-tuple-element.70), channel_id=1, source_target_pairs={{0,24},{8,16},{16,8},{24,0},{1,25},{9,17},{17,9},{25,1},{2,26},{10... | collective-permute-start | bytes 159752 | tf_op jit(solution)/shard_map/ppermute | solution.py:39
